TPU v7x, 32 devices: a whole 2x2x4 slice. The times are simulated.
32 devices in a mesh: seq: 8 (over z, y), head: 4 (over x, core).
Axes of the slice: x: 2, y: 2, z: 4, core: 2. Of those that a mesh axis runs over, the one named last changes fastest.
Arguments:
- hidden: bfloat16 [16384, 768], P('seq'), may hold values from -6 to 6
- teacher: bfloat16 [16384, 768], P('seq'), may hold values from -6 to 6
- doc_starts: int32 [16], replicated, may hold values from 0 to 15872, as said below
- valid_mask: int32 [16384], P('seq'), may hold values from 0 to 1, as said below
- norm_gain: float32 [768], replicated, may hold values from 0.5 to 1.5
- w_gate: bfloat16 [768, 1536], P(None, 'head'), may hold values from -0.21875 to 0.21875
- w_inner: bfloat16 [768, 1536], P(None, 'head'), may hold values from -0.21875 to 0.21875
- w_pair: bfloat16 [768, 256], replicated, may hold values from -0.21875 to 0.21875
- w_step: bfloat16 [768, 24], P(None, 'head'), may hold values from -0.21875 to 0.21875
- conv_inner: bfloat16 [4, 1536], P(None, 'head'), may hold values from -3 to 3
- bias_inner: bfloat16 [1536], P('head'), may hold values from -1.5 to 1.5
- conv_pair: bfloat16 [4, 256], replicated, may hold values from -3 to 3
- bias_pair: bfloat16 [256], replicated, may hold values from -1.5 to 1.5
- step_bias: float32 [24], P('head'), may hold values from -4 to -1
- decay_log: float32 [24], P('head'), may hold values from -11 to 0
- skip_gain: float32 [24], P('head'), may hold values from 0.5 to 1.5
- gate_gain: float32 [1536], P('head'), may hold values from 0.5 to 1.5
- w_output: bfloat16 [1536, 768], P('head'), may hold values from -0.15625 to 0.15625
Outputs:
- output: bfloat16 [16384, 768], P('seq')
- loss: float32 [], replicated
- grad_hidden: bfloat16 [16384, 768], P('seq')
- grad_norm_gain: float32 [768], replicated
- grad_w_gate: float32 [768, 1536], P(None, 'head')
- grad_w_inner: float32 [768, 1536], P(None, 'head')
- grad_w_pair: float32 [768, 256], replicated
- grad_w_step: float32 [768, 24], P(None, 'head')
- grad_conv_inner: float32 [4, 1536], P(None, 'head')
- grad_bias_inner: float32 [1536], P('head')
- grad_conv_pair: float32 [4, 256], replicated
- grad_bias_pair: float32 [256], replicated
- grad_step_bias: float32 [24], P('head')
- grad_decay_log: float32 [24], P('head')
- grad_skip_gain: float32 [24], P('head')
- grad_gate_gain: float32 [1536], P('head')
- grad_w_output: float32 [1536, 768], P('head')
Inputs may be any that keep to these rules, and one draw needn't show every extreme that they name: `doc_starts`: strictly increasing; entry 0 is 0; entries 1 to 7 lie below 1024; entry 8 is 15360; entries 9 to 14 lie between entry 8 and entry 15; entry 15 is 15872. `valid_mask`: the last token is valid.
All inputs are finite; a program needn't handle non-finite values.
Results may differ from a plain program's by a relative error of at most 0.004.
The roundings to bfloat16 on the way count: a program that leaves them out, or rounds other values in their place, can miss the bound.
Values may be sent and summed in bfloat16 or wider, within the bound.
A program may use at most 192 MiB of HBM per device.

v0:
```python
from functools import partial

import jax
import jax.numpy as jnp
from jax import lax
from jax.sharding import PartitionSpec as P

HEAD_DIM = 64
STATE = 128
KERNEL = 4
GROUP = 256


EPSILON = 1e-05
PRECISE = lax.Precision.HIGHEST


def shifted(block, axis, distance):
    devices = range(lax.axis_size(axis))
    route = [(i - distance, i) for i in devices if i - distance in devices]
    return lax.ppermute(block, axis, route)


def carried_in(value, axis, join, neutral, backward):
    count, mine = (lax.axis_size(axis), lax.axis_index(axis))
    pieces = jax.tree.map(lambda part: lax.all_gather(part, axis), value)
    if backward:
        pieces = jax.tree.map(lambda part: part[::-1], pieces)
        mine = count - 1 - mine
    total = jax.tree.map(
        lambda part, zero: jnp.full_like(part, 0) + jnp.asarray(zero, part.dtype), value, neutral
    )

    def lap(position, total):
        longer = join(total, jax.tree.map(lambda part: part[position], pieces))
        return jax.tree.map(lambda new, old: jnp.where(position < mine, new, old), longer, total)

    return lax.fori_loop(0, count - 1, lap, total)


def doc_numbers(positions, starts):
    return jnp.sum((starts[None, :] <= positions[:, None]).astype(jnp.int32), axis=1) - 1


def left_dot(first_matrix, second_matrix):
    return lax.dot_general(
        first_matrix, second_matrix, (((0,), (0,)), ((), ())), preferred_element_type=jnp.float32
    )


def right_dot(first_matrix, second_matrix):
    return lax.dot_general(
        first_matrix, second_matrix, (((1,), (1,)), ((), ())), preferred_element_type=jnp.float32
    )


def convolve(padded, weight, conv_bias, allowed):
    length = allowed.shape[0]
    running = jnp.zeros((length, weight.shape[1]), jnp.float32) + conv_bias[None, :]
    for tap_index in range(weight.shape[0]):
        running = (
            running
            + padded[tap_index : tap_index + length]
            * weight[tap_index][None, :]
            * allowed[:, tap_index : tap_index + 1]
        )
    return jax.nn.silu(running)


def group_step(carry_state, pieces):
    values, keys_b, reads_c, step_size, log_decay, doc_index, before = pieces
    cum_log = jnp.cumsum(log_decay, axis=0)
    row_index = jnp.arange(doc_index.shape[0], dtype=jnp.int32)
    joined = (doc_index[:, None] == doc_index[None, :]) & (row_index[:, None] >= row_index[None, :])
    log_gaps = cum_log[:, None, :] - cum_log[None, :, :]
    weights = jnp.where(
        joined[:, :, None], jnp.exp(jnp.where(joined[:, :, None], log_gaps, 0.0)), 0.0
    )
    scores = jnp.dot(reads_c, keys_b.T, precision=PRECISE)
    scaled = values * step_size[:, :, None]
    intra_part = jnp.einsum("ijh,jhp->ihp", scores[:, :, None] * weights, scaled, precision=PRECISE)
    inflow = jnp.exp(cum_log) * (doc_index == before).astype(jnp.float32)[:, None]
    inter_part = (
        jnp.einsum("in,hpn->ihp", reads_c, carry_state, precision=PRECISE) * inflow[:, :, None]
    )
    tail_weight = (
        jnp.exp(cum_log[-1][None, :] - cum_log)
        * (doc_index == doc_index[-1]).astype(jnp.float32)[:, None]
    )
    keep_factor = jnp.exp(cum_log[-1]) * (doc_index[-1] == before).astype(jnp.float32)
    new_state = carry_state * keep_factor[:, None, None] + jnp.einsum(
        "jh,jhp,jn->hpn", tail_weight, scaled, keys_b, precision=PRECISE
    )
    return (new_state, intra_part + inter_part)


def local_pass(values, pair_out, step_size, log_decay, skip_gain, doc_index, before):
    local_rows = values.shape[0]
    local_heads = step_size.shape[1]
    group_count = local_rows // GROUP
    shaped = values.reshape(group_count, GROUP, local_heads, HEAD_DIM)
    before_group = jnp.concatenate([before[None], doc_index[GROUP - 1 :: GROUP][:-1]])
    pieces = (
        shaped,
        pair_out[:, :STATE].reshape(group_count, GROUP, STATE),
        pair_out[:, STATE:].reshape(group_count, GROUP, STATE),
        step_size.reshape(group_count, GROUP, local_heads),
        log_decay.reshape(group_count, GROUP, local_heads),
        doc_index.reshape(group_count, GROUP),
        before_group,
    )
    final_state, outs = lax.scan(
        jax.checkpoint(group_step), jnp.zeros((local_heads, HEAD_DIM, STATE), jnp.float32), pieces
    )
    device_decay = jnp.exp(jnp.sum(log_decay, axis=0)) * (doc_index[-1] == before).astype(
        jnp.float32
    )
    direct = values.reshape(local_rows, local_heads, HEAD_DIM) * skip_gain[None, :, None]
    mixer_out = outs.reshape(local_rows, local_heads * HEAD_DIM) + direct.reshape(
        local_rows, local_heads * HEAD_DIM
    )
    return (mixer_out, device_decay, final_state)


def inflow_term(pair_out, log_decay, incoming, doc_index, before):
    cum_log = jnp.cumsum(log_decay, axis=0)
    inflow = jnp.exp(cum_log) * (doc_index == before).astype(jnp.float32)[:, None]
    carried = (
        jnp.einsum("tn,hpn->thp", pair_out[:, STATE:], incoming, precision=PRECISE)
        * inflow[:, :, None]
    )
    return carried.reshape(pair_out.shape[0], incoming.shape[0] * HEAD_DIM)


def step_rates(step_raw, step_bias, decay_log):
    step_size = jax.nn.softplus(step_raw + step_bias[None, :])
    return (step_size, -step_size * jnp.exp(decay_log)[None, :])


def chain_join(earlier, later):
    return (earlier[0] * later[0], later[0][:, None, None] * earlier[1] + later[1])


def shards(
    hidden,
    teacher,
    doc_starts,
    valid_mask,
    norm_gain,
    w_gate,
    w_inner,
    w_pair,
    w_step,
    conv_inner,
    bias_inner,
    conv_pair,
    bias_pair,
    step_bias,
    decay_log,
    skip_gain,
    gate_gain,
    w_output,
):
    local_rows = hidden.shape[0]
    margin = KERNEL - 1
    offset = lax.axis_index("seq") * local_rows
    doc_index = doc_numbers(offset + jnp.arange(local_rows, dtype=jnp.int32), doc_starts)
    wide_docs = doc_numbers(
        offset - margin + jnp.arange(local_rows + margin, dtype=jnp.int32), doc_starts
    )
    before = wide_docs[margin - 1]
    allowed = jnp.stack(
        [
            (wide_docs[tap_index : tap_index + local_rows] == doc_index).astype(jnp.float32)
            for tap_index in range(KERNEL)
        ],
        axis=1,
    )
    mask_float = valid_mask.astype(jnp.float32)
    hidden_float = hidden.astype(jnp.float32)
    inv_rms = lax.rsqrt(jnp.mean(hidden_float * hidden_float, axis=1, keepdims=True) + EPSILON)
    lowered = (hidden_float * inv_rms * norm_gain[None, :]).astype(jnp.bfloat16)
    gate_pre = jnp.dot(lowered, w_gate, preferred_element_type=jnp.float32)
    inner_in = jnp.dot(lowered, w_inner, preferred_element_type=jnp.float32).astype(jnp.bfloat16)
    pair_in = jnp.dot(lowered, w_pair, preferred_element_type=jnp.float32).astype(jnp.bfloat16)
    step_raw = jnp.dot(lowered, w_step, preferred_element_type=jnp.float32)
    inner_prev, pair_prev = shifted(
        (inner_in[local_rows - margin :], pair_in[local_rows - margin :]), "seq", 1
    )
    inner_wide = jnp.concatenate([inner_prev, inner_in]).astype(jnp.float32)
    pair_wide = jnp.concatenate([pair_prev, pair_in]).astype(jnp.float32)

    def tap_conv(padded, weight, conv_bias):
        return convolve(padded, weight, conv_bias, allowed)

    values, inner_back = jax.vjp(
        tap_conv, inner_wide, conv_inner.astype(jnp.float32), bias_inner.astype(jnp.float32)
    )
    pair_out, pair_back = jax.vjp(
        tap_conv, pair_wide, conv_pair.astype(jnp.float32), bias_pair.astype(jnp.float32)
    )
    (step_size, log_decay), rate_back = jax.vjp(step_rates, step_raw, step_bias, decay_log)

    def mix_pass(values_in, pair_in_out, step_in, decay_in, skip_in):
        return local_pass(values_in, pair_in_out, step_in, decay_in, skip_in, doc_index, before)

    (local_mix, device_decay, final_state), pass_back = jax.vjp(
        mix_pass, values, pair_out, step_size, log_decay, skip_gain
    )
    identity = (jnp.ones_like(device_decay), jnp.zeros_like(final_state))
    incoming = carried_in((device_decay, final_state), "seq", chain_join, identity, False)[1]
    carried, carry_back = jax.vjp(
        partial(inflow_term, doc_index=doc_index, before=before), pair_out, log_decay, incoming
    )
    mixer_out = local_mix + carried
    gate_act = jax.nn.silu(gate_pre)
    gated_out = mixer_out * gate_act
    inner_total = gated_out.shape[1] * lax.axis_size("head")
    square_sum = lax.psum(jnp.sum(gated_out * gated_out, axis=1), "head")
    gate_scale = lax.rsqrt(square_sum / inner_total + EPSILON)
    normed_out = (gated_out * gate_scale[:, None] * gate_gain[None, :]).astype(jnp.bfloat16)
    branch = lax.psum(jnp.dot(normed_out, w_output, preferred_element_type=jnp.float32), "head")
    output_float = hidden_float + branch
    error_term = output_float - teacher.astype(jnp.float32)
    local_error = jnp.sum(mask_float[:, None] * error_term * error_term)
    valid_count, error_total = lax.psum((jnp.sum(mask_float), local_error), "seq")
    loss_value = error_total / (valid_count * hidden.shape[1])
    total_rows = local_rows * lax.axis_size("seq")
    d_output = mask_float[:, None] * error_term * (total_rows / valid_count)
    d_branch = d_output.astype(jnp.bfloat16)
    grad_w_output = left_dot(normed_out, d_branch)
    d_normed = right_dot(d_branch, w_output)
    weighted = d_normed * gate_gain[None, :]
    cross_sum = lax.psum(jnp.sum(weighted * gated_out, axis=1), "head")
    grad_gate_gain = jnp.sum(d_normed * gated_out * gate_scale[:, None], axis=0)
    d_gated = (
        gate_scale[:, None] * weighted
        - gated_out * (gate_scale * gate_scale * gate_scale * cross_sum / inner_total)[:, None]
    )
    d_mixer = d_gated * gate_act
    gate_sigmoid = jax.nn.sigmoid(gate_pre)
    d_gate = d_gated * mixer_out * gate_sigmoid * (1.0 + gate_pre * (1.0 - gate_sigmoid))
    d_pairs_carry, d_logs_carry, d_incoming = carry_back(d_mixer)
    flowback = carried_in((device_decay, d_incoming), "seq", chain_join, identity, True)[1]
    d_decay = jnp.sum(flowback * incoming, axis=(1, 2))
    d_values, d_pairs_local, d_steps, d_logs_local, grad_skip_gain = pass_back(
        (d_mixer, d_decay, flowback)
    )
    d_step_raw, grad_step_bias, grad_decay_log = rate_back((d_steps, d_logs_carry + d_logs_local))
    d_pairs = lax.psum(d_pairs_carry + d_pairs_local, "head")
    d_inner_wide, grad_conv_inner, grad_bias_inner = inner_back(d_values)
    d_pair_wide, grad_conv_pair, grad_bias_pair = pair_back(d_pairs)
    inner_next, pair_next = shifted((d_inner_wide[:margin], d_pair_wide[:margin]), "seq", -1)
    d_inner = d_inner_wide[margin:].at[local_rows - margin :].add(inner_next).astype(jnp.bfloat16)
    d_pair = d_pair_wide[margin:].at[local_rows - margin :].add(pair_next).astype(jnp.bfloat16)
    d_gate_low = d_gate.astype(jnp.bfloat16)
    d_step_low = d_step_raw.astype(jnp.bfloat16)
    grad_w_gate = left_dot(lowered, d_gate_low)
    grad_w_inner = left_dot(lowered, d_inner)
    grad_w_pair = left_dot(lowered, d_pair)
    grad_w_step = left_dot(lowered, d_step_low)
    partial_input = (
        right_dot(d_gate_low, w_gate) + right_dot(d_inner, w_inner) + right_dot(d_step_low, w_step)
    )
    d_lowered = lax.psum(partial_input, "head") + right_dot(d_pair, w_pair)
    grad_norm_gain = jnp.sum(d_lowered * hidden_float * inv_rms, axis=0)
    scaled_grad = d_lowered * norm_gain[None, :]
    d_hidden = inv_rms * scaled_grad - hidden_float * (inv_rms * inv_rms * inv_rms) * jnp.mean(
        scaled_grad * hidden_float, axis=1, keepdims=True
    )
    grad_hidden = (d_output + d_hidden).astype(jnp.bfloat16)
    summed = lax.psum(
        (
            grad_norm_gain,
            grad_w_gate,
            grad_w_inner,
            grad_w_pair,
            grad_w_step,
            grad_conv_inner,
            grad_bias_inner,
            grad_conv_pair,
            grad_bias_pair,
            grad_step_bias,
            grad_decay_log,
            grad_skip_gain,
            grad_gate_gain,
            grad_w_output,
        ),
        "seq",
    )
    return (
        output_float.astype(jnp.bfloat16),
        loss_value,
        grad_hidden,
        summed[0],
        summed[1],
        summed[2],
        summed[3],
        summed[4],
        summed[5],
        summed[6],
        summed[7],
        summed[8],
        summed[9],
        summed[10],
        summed[11],
        summed[12],
        summed[13],
    )


def solution(mesh):
    in_specs = (
        P("seq", None),
        P("seq", None),
        P(),
        P("seq"),
        P(),
        P(None, "head"),
        P(None, "head"),
        P(),
        P(None, "head"),
        P(None, "head"),
        P("head"),
        P(),
        P(),
        P("head"),
        P("head"),
        P("head"),
        P("head"),
        P("head", None),
    )
    out_specs = (
        P("seq", None),
        P(),
        P("seq", None),
        P(),
        P(None, "head"),
        P(None, "head"),
        P(),
        P(None, "head"),
        P(None, "head"),
        P("head"),
        P(),
        P(),
        P("head"),
        P("head"),
        P("head"),
        P("head"),
        P("head", None),
    )
    return jax.shard_map(shards, mesh=mesh, in_specs=in_specs, out_specs=out_specs, check_vma=False)
```

profile of v0, /device:TPU:0, one launch (start us, length us, event | category | flops | bytes accessed | tf_op | source)
XLA Modules:
  0.0 1271.9 jit_solution(3137778671468858795)
XLA Ops:
  57.5 202.5 %while.72 = (s32[]{:T(128)}, f32[6,64,128]{2,1,0:T(8,128)S(1)}, f32[8,256,6,64]{1,0,3,2:T(8,128)}, f32[8,6,64,128]{3,2,1,0:T(8,128)}, f32[8,256,6]{1,2,0:T(8,128...) while((s32[]{:T(128)}, f32[6,64,128]{2,1,0:T(8,128)S(1)}, ...), condition=%wide.region_6.7_spmd.clone, body=%wide.region_3.6_spmd.clone.sunk | while | flops 707352064 | bytes 5849507 | solution.py:112
  94.7 9.8 dynamic_update_slice.81
  120.0 9.8 dynamic_update_slice.81
  145.3 9.8 dynamic_update_slice.81
  170.7 9.8 dynamic_update_slice.81
  221.3 9.8 dynamic_update_slice.81
  266.6 19.3 %all-reduce.23 = (f32[48]{0:T(128)S(1)}, f32[]{:T(128)}) all-reduce(f32[48]{0:T(128)S(1)} %multiply_dynamic-update-slice_fusion, f32[]{:T(128)} %convert_reduce_fusion.2), channel_id=2, replica_groups=mesh['seq'=8,'head'=4] {'seq'}, use_global_device_ids=true, to_apply=%add.21 | all-reduce | flops 49 | bytes 392
  320.4 12.1 multiply_reduce_fusion.11
  348.9 116.6 %all-reduce.30.cloned.1.call-done = f32[2048,768]{1,0:T(8,128)} async-done(((f32[2048,768]{1,0:T(8,128)}), f32[2048,768]{1,0:T(8,128)}) %all-reduce.30.cloned.1.call-update) | async-done | bytes 6291472 | tf_op jit(solution)/shard_map/psum | solution.py:222
  527.8 17.3 %all-gather.8.cloned.1.call-done = f32[48,64,128]{2,1,0:T(8,128)} async-done(((f32[6,64,128]{2,1,0:T(8,128)}), f32[48,64,128]{2,1,0:T(8,128)}) %all-gather.8.cloned.1.call-update) | async-done | bytes 1572880 | tf_op jit(solution)/shard_map/all_gather | solution.py:26
  551.6 337.3 %while.71 = (s32[]{:T(128)}, f32[6,64,128]{2,1,0:T(8,128)S(1)}, f32[8,256,6,64]{1,0,3,2:T(8,128)}, f32[8,256,128]{2,1,0:T(8,128)}, f32[8,256,128]{2,1,0:T(8,128)...) while((s32[]{:T(128)}, f32[6,64,128]{2,1,0:T(8,128)S(1)}, ...), condition=%wide.region_35.36_spmd, body=%wide.region_23.35_spmd.sunk | while | flops 1669126144 | bytes 14528255 | solution.py:112
  575.8 9.9 dynamic_update_slice.79
  617.9 9.9 dynamic_update_slice.79
  660.0 9.9 dynamic_update_slice.79
  702.1 9.9 dynamic_update_slice.79
  744.2 9.9 dynamic_update_slice.79
  786.3 9.9 dynamic_update_slice.79
  828.4 9.9 dynamic_update_slice.79
  870.5 9.9 dynamic_update_slice.79
  939.9 140.3 %all-reduce.34.cloned.1.call-done = (f32[2048,768]{1,0:T(8,128)}, f32[2048,256]{1,0:T(8,128)}) async-done(((f32[2048,768]{1,0:T(8,128)}, f32[2048,256]{1,0:T(8,128)}), (f32[2048,768]{1,0:T(8,128)}, f32[2048,256]{1,0:T(8,128)})) %all-reduce.34.cloned.1.call-update) | async-done | bytes 8388624 | tf_op jit(solution)/shard_map/psum | solution.py:265
  1107.6 10.1 fusion.105
  1117.7 40.8 %all-reduce.22 = (f32[]{:T(128)}, f32[768]{0:T(1024)}, f32[768,6]{0,1:T(8,128)}, f32[4,384]{1,0:T(4,128)}, f32[384]{0:T(512)}, /*index=5*/f32[4,256]{1,0:T(4,128...) all-reduce(f32[]{:T(128)} %get-tuple-element.983, ...), channel_id=1, replica_groups=mesh['seq'=8,'head'=4] {'seq'}, use_global_device_ids=true, to_apply=%region_16.17 | all-reduce | flops 8979 | bytes 71832 | tf_op jit(solution)/shard_map/psum | solution.py:226
  1159.9 10.2 fusion.102
  1170.1 88.5 %all-reduce.32.cloned.1.call-done = (f32[768,384]{1,0:T(8,128)}, f32[768,384]{1,0:T(8,128)}, f32[768,256]{1,0:T(8,128)}, f32[384,768]{1,0:T(8,128)}) async-done(((f32[768,384]{1,0:T(8,128)}, f32[768,384]{1,0:T(8,128)}, f32[768,256]{1,0:T(8,128)}, f32[384,768]{1,0:T(8,128)}), (f32[768,384]{1,0:T(8,128)}, f32[768,384]{1,0:T(8,128)}, f32[768,256]{1,0:T(8,128)}, ...) | async-done | bytes 4325392 | tf_op jit(solution)/shard_map/psum | solution.py:272
  (954 shorter events, 653.2 us)
Async XLA Ops:
  7.2 313.2 %copy-start = (bf16[768,384]{1,0:T(8,128)(2,1)S(1)}, bf16[768,384]{1,0:T(8,128)(2,1)}, u32[]{:S(2)}) copy-start(bf16[768,384]{1,0:T(8,128)(2,1)} %param.35) | copy-start | bytes 1769476
  7.2 297.6 %all-gather.6.cloned.1.call-start = ((), (), s32[]{:S(2)}) async-start(), calls=%async_computation.1 | async-start | bytes 1769472 | tf_op jit(solution)/shard_map/all_gather | solution.py:26
  12.7 14.9 %copy-start.86 = (bf16[4,256]{1,0:T(4,128)(2,1)S(1)}, bf16[4,256]{1,0:T(4,128)(2,1)}, u32[]{:S(2)}) copy-start(bf16[4,256]{1,0:T(4,128)(2,1)} %param.41) | copy-start | bytes 6148
  12.7 15.5 %copy-start.92 = (bf16[4,384]{1,0:T(4,128)(2,1)S(1)}, bf16[4,384]{1,0:T(4,128)(2,1)}, u32[]{:S(2)}) copy-start(bf16[4,384]{1,0:T(4,128)(2,1)} %param.39) | copy-start | bytes 9220
  12.7 16.1 %copy-start.98 = (f32[6]{0:T(128)S(1)}, f32[6]{0:T(128)}, u32[]{:S(2)}) copy-start(f32[6]{0:T(128)} %param.44) | copy-start | bytes 76
  12.7 16.2 %copy-start.59 = (bf16[768,6]{0,1:T(8,128)(2,1)S(1)}, bf16[768,6]{0,1:T(8,128)(2,1)}, u32[]{:S(2)}) copy-start(bf16[768,6]{0,1:T(8,128)(2,1)} %param.38) | copy-start | bytes 27652
  12.7 16.2 %copy-start.93 = (f32[6]{0:T(128)S(1)}, f32[6]{0:T(128)}, u32[]{:S(2)}) copy-start(f32[6]{0:T(128)} %param.43) | copy-start | bytes 76
  12.7 21.6 %collective-permute-start.1 = (bf16[3,256]{1,0:T(4,128)(2,1)S(1)}, bf16[3,256]{1,0:T(4,128)(2,1)S(1)}, u32[]{:S(2)}, u32[]{:S(2)}) collective-permute-start(bf16[3,256]{1,0:T(4,128)(2,1)S(1)} %slice.291), channel_id=1, source_target_pairs={{0,4},{4,8},{8,12},{12,16},{16,20},{20,24},{24,28},{1,5},{5,9},{9,... | collective-permute-start | bytes 4616 | tf_op jit(solution)/shard_map/ppermute | solution.py:21
  20.7 13.0 %copy-start.97 = (bf16[256]{0:T(256)(128)(2,1)S(1)}, bf16[256]{0:T(256)(128)(2,1)}, u32[]{:S(2)}) copy-start(bf16[256]{0:T(256)(128)(2,1)} %param.42) | copy-start | bytes 1540
  20.7 13.5 %copy-start.96 = (bf16[384]{0:T(512)(128)(2,1)S(1)}, bf16[384]{0:T(512)(128)(2,1)}, u32[]{:S(2)}) copy-start(bf16[384]{0:T(512)(128)(2,1)} %param.40) | copy-start | bytes 2308
  21.3 18.3 %collective-permute-start = (bf16[3,384]{1,0:T(4,128)(2,1)}, bf16[3,384]{1,0:T(4,128)(2,1)}, u32[]{:S(2)}, u32[]{:S(2)}) collective-permute-start(bf16[3,384]{1,0:T(4,128)(2,1)} %slice.278), channel_id=1, source_target_pairs={{0,4},{4,8},{8,12},{12,16},{16,20},{20,24},{24,28},{1,5},{5,9},{9,... | collective-permute-start | bytes 6920 | tf_op jit(solution)/shard_map/ppermute | solution.py:21
  27.6 13.8 %copy-start.41 = (f32[2048]{0:T(1024)}, f32[2048]{0:T(1024)S(1)}, u32[]{:S(2)}) copy-start(f32[2048]{0:T(1024)S(1)} %get-tuple-element.1133) | copy-start | bytes 24580
  27.6 13.8 %copy-start.43 = (f32[2048]{0:T(1024)}, f32[2048]{0:T(1024)S(1)}, u32[]{:S(2)}) copy-start(f32[2048]{0:T(1024)S(1)} %get-tuple-element.1134) | copy-start | bytes 24580
  32.4 253.6 %copy-start.31 = (f32[2048,6]{0,1:T(8,128)}, f32[2048,6]{0,1:T(8,128)S(1)}, u32[]{:S(2)}) copy-start(f32[2048,6]{0,1:T(8,128)S(1)} %get-tuple-element.1142) | copy-start | bytes 147460
  260.7 204.8 %all-reduce.30.cloned.1.call-start = ((), (), s32[]{:S(2)}) async-start(), calls=%async_computation | async-start | bytes 12582912 | tf_op jit(solution)/shard_map/psum | solution.py:222
  320.4 20.1 %copy-start.34 = (bf16[384,768]{1,0:T(8,128)(2,1)S(1)}, bf16[384,768]{1,0:T(8,128)(2,1)}, u32[]{:S(2)}) copy-start(bf16[384,768]{1,0:T(8,128)(2,1)} %param.47) | copy-start | bytes 1769476
  346.9 198.2 %all-gather.8.cloned.1.call-start = ((), (), s32[]{:S(2)}) async-start(), calls=%async_computation.2 | async-start | bytes 1769472 | tf_op jit(solution)/shard_map/all_gather | solution.py:26
  500.5 579.7 %all-reduce.34.cloned.1.call-start = ((), (), s32[]{:S(2)}) async-start(), calls=%async_computation.4 | async-start | bytes 16777216 | tf_op jit(solution)/shard_map/psum | solution.py:265
  506.7 16.6 %copy-start.17 = (bf16[2048,384]{1,0:T(8,128)(2,1)S(1)}, bf16[2048,384]{1,0:T(8,128)(2,1)}, u32[]{:S(2)}) copy-start(bf16[2048,384]{1,0:T(8,128)(2,1)} %get-tuple-element.1116) | copy-start | bytes 4718596
  907.4 7.8 collective-permute-start.2
  925.9 332.7 %all-reduce.32.cloned.1.call-start = ((), (), s32[]{:S(2)}) async-start(), calls=%async_computation.3 | async-start | bytes 8650752 | tf_op jit(solution)/shard_map/psum | solution.py:272
  937.1 143.1 %copy-start.5 = (f32[2051,256]{1,0:T(8,128)S(1)}, f32[2051,256]{1,0:T(8,128)}, u32[]{:S(2)}) copy-start(f32[2051,256]{1,0:T(8,128)} %copy-done.4) | copy-start | bytes 6300676
  1086.9 5.5 collective-permute-start.3
  1107.6 52.3 %copy-start.13 = (bf16[2048,768]{1,0:T(8,128)(2,1)S(1)}, bf16[2048,768]{1,0:T(8,128)(2,1)}, u32[]{:S(2)}) copy-start(bf16[2048,768]{1,0:T(8,128)(2,1)} %param.30) | copy-start | bytes 9437188
  (84 other events, 394.4 us)
Sparse Core Ops, SparseCore 0:
  260.9 43.9 all-gather.5
  347.0 118.4 all-reduce.29
  500.6 44.3 all-gather.7
  926.0 154.1 all-reduce.33
  1097.0 161.6 all-reduce.31
where the time goes:
time: 1280 us; the launch traced here: 1270 us
  waiting for transfers between devices  370 us (29%)
  local copies, waits for them, and re-layouts  330 us (26%)
  matrix products  227 us (18%)
  other arithmetic  216 us (17%)
  blocking collectives  73.2 us (6%)
  loops' own time  23.6 us (2%)
  between operations  20.2 us (2%)
    dynamic_update_slice x48, local copies, waits for them, and re-layouts, local_pass(): lax.scan(jax.checkpoint(group_step), jnp.zeros((local_heads, HEAD_DIM, ST...  164 us
    psum x1, waiting for transfers between devices, shards(): d_lowered = lax.psum(partial_input, 'head') + right_dot(d_pair, w_pair)  140 us
    psum x1, waiting for transfers between devices, shards(): lax.psum(jnp.dot(normed_out, w_output, preferred_element_type=jnp.float32...  117 us
    another operation x60, other arithmetic  101 us
    psum x1, waiting for transfers between devices, shards(): lax.psum((grad_norm_gain, grad_w_gate, grad_w_inner, grad_w_pair, grad_w_...  88.5 us
    dot_general x24, matrix products, group_step(): jnp.einsum('ijh,jhp->ihp', scores[:, :, None] * weights, scaled, precisio...  53.5 us
    dynamic_slice x40, local copies, waits for them, and re-layouts, local_pass(): lax.scan(jax.checkpoint(group_step), jnp.zeros((local_heads, HEAD_DIM, ST...  42.9 us
    psum x1, blocking collectives, shards(): lax.psum((jnp.sum(mask_float), local_error), 'seq')  40.8 us
  transfers between devices with their start and end apart: 9, of which 6 were waited for; matrix products, arithmetic and copies ran while one was open for 9% of the time, Pallas kernels for 0%

commit v1 on v0

v1 whole, which is shorter than its diff:
```python
from functools import partial

import jax
import jax.numpy as jnp
from jax import lax
from jax.experimental import pallas as pl
from jax.experimental.pallas import tpu as pltpu
from jax.sharding import PartitionSpec as P

EPSILON = 1e-05
CHUNK = 128
BLOCK = 256
HEAD_DIM = 64
LANES = 128
FAR = float(1 << 24)
F32 = jnp.float32
BF16 = jnp.bfloat16
HIGHEST = lax.Precision.HIGHEST

DT, CUM, INFLOW, TAIL, RATE, START, END = 0, 8, 16, 24, 32, 40, 41


def dot(a, b, da=1, db=0):
    return lax.dot_general(a, b, (((da,), (db,)), ((), ())), preferred_element_type=F32)


def halves(v):
    high = v.astype(BF16)
    return high, (v - high.astype(F32)).astype(BF16)


def dot3(a, b, da=1, db=0):
    ah, al = halves(a)
    bh, bl = halves(b)
    return dot(ah, bh, da, db) + (dot(ah, bl, da, db) + dot(al, bh, da, db))


def column_sums(v):
    high, low = halves(v)
    ones = jnp.ones((8, v.shape[1]), BF16)
    return (dot(ones, high, 1, 1) + dot(ones, low, 1, 1))[:1]


def as_column(row):
    return jnp.transpose(jnp.broadcast_to(row, (8, row.shape[1])))[:, :1]


def expand(table, base, width):
    rows = table.shape[0]
    lane = lax.broadcasted_iota(jnp.int32, (rows, LANES), 1)
    parts = []
    for pair in range(width // LANES):
        first = jnp.broadcast_to(table[:, base + 2 * pair : base + 2 * pair + 1], (rows, LANES))
        second = jnp.broadcast_to(table[:, base + 2 * pair + 1 : base + 2 * pair + 2], (rows, LANES))
        parts.append(jnp.where(lane < HEAD_DIM, first, second))
    return jnp.concatenate(parts, axis=1)


def head_matrix(width):
    channel = lax.broadcasted_iota(jnp.int32, (width, LANES), 0)
    head = lax.broadcasted_iota(jnp.int32, (width, LANES), 1)
    return ((channel >> 6) == head).astype(BF16)


def head_sums(v):
    high, low = halves(v)
    matrix = head_matrix(v.shape[1])
    return dot(high, matrix) + dot(low, matrix)


def triangle(upper):
    row = lax.broadcasted_iota(jnp.int32, (CHUNK, CHUNK), 0)
    col = lax.broadcasted_iota(jnp.int32, (CHUNK, CHUNK), 1)
    return ((col >= row) if upper else (col <= row)).astype(F32)


def silu_parts(pre):
    gate = jax.nn.sigmoid(pre)
    return pre * gate, gate * (1.0 + pre * (1.0 - gate))


def project_kernel(
    idx, starts, hid, halo, tail, gain, wi, wp, ws, conv_i, conv_p, bias_i, bias_p, sbias, dlog,
    low, in_i, in_p, pre_i, pre_p, aux, halo_i, halo_p, sloc, pkl, fin, wide_i, wide_p, state, decay,
):
    step = pl.program_id(0)
    edge = tail.shape[0]
    width = wi.shape[1]

    @pl.when(step == 0)
    def _():
        state[...] = jnp.zeros_like(state)
        decay[...] = jnp.ones_like(decay)

    before = jnp.where(step == 0, tail[...].astype(F32), halo[...].astype(F32))
    rows = jnp.concatenate([before, hid[...].astype(F32)], axis=0)
    scale = lax.rsqrt(jnp.mean(rows * rows, axis=1, keepdims=True) + EPSILON)
    lowered = (rows * scale * gain[...]).astype(BF16)
    own = lowered[edge:]
    low[...] = own
    inner = dot(lowered, wi[...]).astype(BF16)
    pair = dot(lowered, wp[...]).astype(BF16)
    in_i[...] = inner[edge:]
    in_p[...] = pair[edge:]
    wide_i[...] = inner.astype(F32)
    wide_p[...] = pair.astype(F32)

    @pl.when(step == 0)
    def _():
        halo_i[...] = inner[:edge]
        halo_p[...] = pair[:edge]

    base = idx[1] + step * BLOCK
    pos = (base + lax.broadcasted_iota(jnp.int32, (BLOCK, LANES), 0)).astype(F32)
    begun = starts[...] <= pos
    start = jnp.max(jnp.where(begun, starts[...], -1.0), axis=1, keepdims=True)
    end = jnp.min(jnp.where(begun, FAR, starts[...]), axis=1, keepdims=True)
    within = pos[:, :1] - start
    keep = [(within >= float(3 - k)).astype(F32) for k in range(3)]

    def convolve(wide, weight, bias):
        total = bias[...] + wide[edge : edge + BLOCK] * weight[3:4]
        for k in range(3):
            total = total + wide[edge - 3 + k : edge - 3 + k + BLOCK] * weight[k : k + 1] * keep[k]
        return total

    conv_inner = convolve(wide_i, conv_i, bias_i)
    conv_pair = convolve(wide_p, conv_p, bias_p)
    pre_i[...] = conv_inner
    pre_p[...] = conv_pair
    values = conv_inner * jax.nn.sigmoid(conv_inner)
    maps = conv_pair[:, :LANES]
    maps = maps * jax.nn.sigmoid(maps)

    raw = dot(own, ws[...]) + sbias[...]
    dt = jnp.maximum(raw, 0.0) + jnp.log1p(jnp.exp(-jnp.abs(raw)))
    rate = jax.nn.sigmoid(raw)
    logs = -dt * jnp.exp(dlog[...])
    lane = lax.broadcasted_iota(jnp.int32, (CHUNK, LANES), 1)
    lower = triangle(False)
    for c in range(BLOCK // CHUNK):
        at = slice(c * CHUNK, (c + 1) * CHUNK)
        cum = jnp.dot(lower, logs[at], precision=HIGHEST, preferred_element_type=F32)
        last = cum[CHUNK - 1 :]
        first = (base + c * CHUNK).astype(F32)
        inflow = jnp.exp(cum) * (start[at] <= first - 1.0).astype(F32)
        outflow = jnp.exp(last - cum) * (end[at] > first + (CHUNK - 1.0)).astype(F32)
        table = jnp.where(lane < CUM, dt[at], pltpu.roll(cum, CUM, 1))
        table = jnp.where(lane < INFLOW, table, pltpu.roll(inflow, INFLOW, 1))
        table = jnp.where(lane < TAIL, table, pltpu.roll(outflow, TAIL, 1))
        table = jnp.where(lane < RATE, table, pltpu.roll(rate[at], RATE, 1))
        table = jnp.where(lane < START, table, jnp.where(lane < END, start[at], end[at]))
        aux[at, :] = table
        scaled = values[at] * expand(table, DT, width) * expand(table, TAIL, width)
        added = dot3(maps[at], scaled, 0, 0)
        kept = expand(jnp.broadcast_to(inflow[CHUNK - 1 :], (8, LANES)), 0, width)
        sloc[c] = state[...]
        pkl[c] = decay[...]
        state[...] = state[...] * kept[:1] + added
        decay[...] = decay[...] * kept
    fin[:CHUNK] = state[...]
    fin[CHUNK:] = decay[...]


def masks(table, first, transposed):
    row = lax.broadcasted_iota(jnp.int32, (CHUNK, CHUNK), 0)
    col = lax.broadcasted_iota(jnp.int32, (CHUNK, CHUNK), 1)
    at = (first + col).astype(F32)
    if transposed:
        return (col >= row) & (at < table[:, END : END + 1])
    return (col <= row) & (at >= table[:, START : START + 1])


def head_split(v, pair):
    lane = lax.broadcasted_iota(jnp.int32, (v.shape[0], LANES), 1)
    part = v[:, pair * LANES : (pair + 1) * LANES]
    return jnp.concatenate(
        [jnp.where(lane < HEAD_DIM, part, 0.0), jnp.where(lane < HEAD_DIM, 0.0, part)], axis=0
    ).astype(BF16)


def intra_kernel(idx, low, wg, pre_i, pre_p, aux, skip, gate, mixed):
    width = wg.shape[1]
    gate[...] = dot(low[...], wg[...])
    base = idx[1] + pl.program_id(0) * BLOCK
    maps, _ = silu_parts(pre_p[...])
    values, _ = silu_parts(pre_i[...])
    for c in range(BLOCK // CHUNK):
        at = slice(c * CHUNK, (c + 1) * CHUNK)
        table = aux[at, :]
        rows = jnp.transpose(table)
        joined = masks(table, base + c * CHUNK, False)
        scores = dot(maps[at, LANES:].astype(BF16), maps[at, :LANES].astype(BF16), 1, 1)
        scaled = values[at] * expand(table, DT, width)
        parts = []
        for pair in range(width // LANES):
            weights = []
            for h in (2 * pair, 2 * pair + 1):
                gap = table[:, CUM + h : CUM + h + 1] - rows[CUM + h : CUM + h + 1, :]
                weights.append((scores * jnp.exp(jnp.where(joined, gap, -1e30))).astype(BF16))
            parts.append(dot(jnp.concatenate(weights, axis=1), head_split(scaled, pair)))
        mixed[at, :] = jnp.concatenate(parts, axis=1) + values[at] * skip[...]


def mix_kernel(pre_c, aux, sloc, pkl, sin, local, gate, mixer, states, square):
    width = local.shape[1]
    reads, _ = silu_parts(pre_c[...])
    for c in range(BLOCK // CHUNK):
        at = slice(c * CHUNK, (c + 1) * CHUNK)
        state = sloc[c] + pkl[c, :1] * sin[...]
        states[c] = state
        mixer[at, :] = local[at, :] + expand(aux[at, :], INFLOW, width) * dot3(reads[at], state)
    act, _ = silu_parts(gate[...])
    gated = mixer[...] * act
    square[...] = column_sums(gated * gated)


def gate_scale(square, total):
    return as_column(lax.rsqrt(square / total + EPSILON))


def branch_kernel(idx, mixer, gate, square, gain, wo, send, stay, *, total):
    step = pl.program_id(0)
    act, _ = silu_parts(gate[...])
    gated = mixer[...] * act
    normed = (gated * gate_scale(square[...], total) * gain[...]).astype(BF16)
    part = dot(normed, wo[...])

    @pl.when(step < pl.num_programs(0) // 2)
    def _():
        send[...] = part.astype(send.dtype)

    @pl.when(step >= pl.num_programs(0) // 2)
    def _():
        stay[...] = part


def loss_kernel(idx, factor, hid, teacher, valid, mine, other, out, d_branch, d_out, error):
    @pl.when(pl.program_id(0) == 0)
    def _():
        error[...] = jnp.zeros_like(error)

    outf = hid[...].astype(F32) + (mine[...].astype(F32) + other[...].astype(F32))
    out[...] = outf.astype(BF16)
    term = outf - teacher[...].astype(F32)
    masked = as_column(valid[...].astype(F32)) * term
    error[...] += jnp.sum(masked * term, axis=0, keepdims=True)
    grad = masked * factor[0]
    d_out[...] = grad
    d_branch[...] = grad.astype(BF16)


def branch_back_kernel(idx, mine, other, mixer, gate, square, gain, wo, weighted, cross, g_gain, g_wo, *, total):
    step = pl.program_id(0)

    @pl.when(step == 0)
    def _():
        g_gain[...] = jnp.zeros_like(g_gain)
        g_wo[...] = jnp.zeros_like(g_wo)

    d_branch = jnp.where(step < pl.num_programs(0) // 2, mine[...], other[...])
    act, _ = silu_parts(gate[...])
    gated = mixer[...] * act
    scaled = gated * gate_scale(square[...], total)
    normed = (scaled * gain[...]).astype(BF16)
    g_wo[...] += dot(normed, d_branch, 0, 0)
    d_normed = dot(d_branch, wo[...], 1, 1)
    g_gain[...] += jnp.sum(d_normed * scaled, axis=0, keepdims=True)
    grad = d_normed * gain[...]
    weighted[...] = grad
    cross[...] = column_sums(grad * gated)


def gate_back_kernel(
    weighted, mixer, gate, square, cross, pre_c, aux, d_mixer, d_gate, gloc, pkl, fin, state, decay, *, total
):
    @pl.when(pl.program_id(0) == 0)
    def _():
        state[...] = jnp.zeros_like(state)
        decay[...] = jnp.ones_like(decay)

    width = mixer.shape[1]
    act, slope = silu_parts(gate[...])
    gated = mixer[...] * act
    row = lax.rsqrt(square[...] / total + EPSILON)
    scale = as_column(row)
    pull = as_column(row * row * row * cross[...] / total)
    d_gated = scale * weighted[...] - gated * pull
    dy = d_gated * act
    d_mixer[...] = dy
    d_gate[...] = (d_gated * mixer[...] * slope).astype(BF16)
    reads, _ = silu_parts(pre_c[...])
    for c in reversed(range(BLOCK // CHUNK)):
        at = slice(c * CHUNK, (c + 1) * CHUNK)
        inflow = expand(aux[at, :], INFLOW, width)
        gloc[c] = state[...]
        pkl[c] = decay[...]
        kept = inflow[CHUNK - 1 :]
        state[...] = state[...] * kept + dot3(reads[at], dy[at] * inflow, 0, 0)
        decay[...] = decay[...] * kept
    fin[:CHUNK] = state[...]
    fin[CHUNK:] = decay[...]


def intra_back_kernel(idx, d_mixer, pre_i, pre_p, aux, low, d_gate, d_scaled, d_maps, g_wg):
    @pl.when(pl.program_id(0) == 0)
    def _():
        g_wg[...] = jnp.zeros_like(g_wg)

    g_wg[...] += dot(low[...], d_gate[...], 0, 0)
    width = d_mixer.shape[1]
    base = idx[1] + pl.program_id(0) * BLOCK
    maps, _ = silu_parts(pre_p[...])
    values, _ = silu_parts(pre_i[...])
    for c in range(BLOCK // CHUNK):
        at = slice(c * CHUNK, (c + 1) * CHUNK)
        table = aux[at, :]
        rows = jnp.transpose(table)
        joined = masks(table, base + c * CHUNK, True)
        keys = maps[at, :LANES].astype(BF16)
        reads = maps[at, LANES:].astype(BF16)
        scores = dot(keys, reads, 1, 1)
        scaled = (values[at] * expand(table, DT, width)).astype(BF16)
        grads = d_mixer[at, :]
        d_scores = jnp.zeros((CHUNK, CHUNK), F32)
        parts = []
        for pair in range(width // LANES):
            split = head_split(grads, pair)
            d_weights = dot(scaled[:, pair * LANES : (pair + 1) * LANES], split, 1, 1)
            weights = []
            for side in range(2):
                h = 2 * pair + side
                gap = rows[CUM + h : CUM + h + 1, :] - table[:, CUM + h : CUM + h + 1]
                factor = jnp.exp(jnp.where(joined, gap, -1e30))
                weights.append((scores * factor).astype(BF16))
                d_scores = d_scores + factor * d_weights[:, side * CHUNK : (side + 1) * CHUNK]
            parts.append(dot(jnp.concatenate(weights, axis=1), split))
        d_scaled[at, :] = jnp.concatenate(parts, axis=1)
        low_scores = d_scores.astype(BF16)
        d_maps[at, :] = jnp.concatenate([dot(low_scores, reads), dot(low_scores, keys, 0, 0)], axis=1)


def conv_back(grad, within, inputs, edge_inputs, weight, shifted, first, last, acc):
    rows = grad.shape[0]

    @pl.when(first)
    def _():
        for ref in shifted:
            ref[...] = jnp.zeros_like(ref)

    total = grad * weight[3:4]
    edge = jnp.zeros((8, grad.shape[1]), F32)
    acc[3:4] += jnp.sum(grad * inputs, axis=0, keepdims=True)
    acc[4:5] += jnp.sum(grad, axis=0, keepdims=True)
    for k, ref in enumerate(shifted):
        ref[8 : 8 + rows] = grad * (within >= float(3 - k)).astype(F32)
        moved = ref[3 - k : 3 - k + 8 + rows]
        total = total + moved[8:] * weight[k : k + 1]
        edge = edge + moved[:8] * weight[k : k + 1]
        outer = jnp.where(last, edge_inputs, 0.0) * moved[:8]
        acc[k : k + 1] += jnp.sum(moved[8:] * inputs, axis=0, keepdims=True) + jnp.sum(outer, axis=0, keepdims=True)
        ref[8 + rows :] = ref[8:16]
    return total, edge


def scan_back_kernel(
    idx, d_scaled, d_maps, pre_i, pre_p, in_i, halo_i, aux, gloc, pkl, gin, states, d_mixer, mixer, skip, dlog, conv_i,
    d_inner, d_step, d_both, edge, tail, small, heads, *shifted,
):
    step = pl.program_id(0)
    blocks = pl.num_programs(0)
    first, last = step == 0, step == blocks - 1
    width = mixer.shape[1]

    @pl.when(first)
    def _():
        small[...] = jnp.zeros_like(small)
        heads[...] = jnp.zeros_like(heads)

    base = idx[1] + (blocks - 1 - step) * BLOCK
    maps, _ = silu_parts(pre_p[...])
    values, slope = silu_parts(pre_i[...])
    dy = d_mixer[...]
    upper = triangle(True)
    lane = lax.broadcasted_iota(jnp.int32, (CHUNK, LANES), 1)
    grown = jnp.exp(dlog[...])
    pieces = []
    for c in range(BLOCK // CHUNK):
        at = slice(c * CHUNK, (c + 1) * CHUNK)
        table = aux[at, :]
        sizes = expand(table, DT, width)
        inflow = expand(table, INFLOW, width)
        outflow = expand(table, TAIL, width)
        keys, reads = maps[at, :LANES], maps[at, LANES:]
        scaled = values[at] * sizes
        grad_state = gloc[c] + pkl[c, :1] * gin[...]
        state = states[c]
        passed = outflow * dot3(keys, grad_state)
        total = d_scaled[at, :] + passed
        d_reads = d_maps[at, LANES:] + dot3(dy[at] * inflow, state, 1, 1)
        d_keys = d_maps[at, :LANES] + dot3(scaled * outflow, grad_state, 1, 1)
        d_both[at, :] = jnp.concatenate([d_keys, d_reads], axis=1)
        plain = mixer[at, :] - skip[...] * values[at]
        d_cum = head_sums(dy[at] * plain - scaled * total)
        carried = jnp.sum(grad_state * state, axis=0, keepdims=True) * inflow[CHUNK - 1 :]
        carried = carried + jnp.sum(scaled * passed, axis=0, keepdims=True)
        after = head_sums(jnp.broadcast_to(carried, (8, width)))[:1]
        d_logs = jnp.dot(upper, d_cum, precision=HIGHEST, preferred_element_type=F32) + after
        d_raw = (head_sums(total * values[at]) - grown * d_logs) * pltpu.roll(table, LANES - RATE, 1)
        d_raw = jnp.where(lane < 8, d_raw, 0.0)
        d_step[at, :] = d_raw.astype(BF16)
        d_decay = jnp.where(lane < 8, -d_logs * table * grown, 0.0)
        heads[0:1] += jnp.sum(d_raw, axis=0, keepdims=True)
        heads[1:2] += jnp.sum(d_decay, axis=0, keepdims=True)
        pieces.append(total * sizes + dy[at] * skip[...])
    small[5:6] += jnp.sum(dy * values, axis=0, keepdims=True)
    grad = jnp.concatenate(pieces, axis=0) * slope
    pos = (base + lax.broadcasted_iota(jnp.int32, (BLOCK, 1), 0)).astype(F32)
    within = pos - aux[:, START : START + 1]
    edge_inputs = halo_i[8:].astype(F32)
    whole, outer = conv_back(
        grad, within, in_i[...].astype(F32), edge_inputs, conv_i, shifted, first, last, small
    )
    d_inner[...] = whole.astype(BF16)
    edge[...] = outer

    @pl.when(first)
    def _():
        tail[...] = whole[BLOCK - 16 :]


def pair_back_kernel(idx, d_maps, pre_p, in_p, halo_p, aux, conv_p, d_pair, edge, tail, small, *shifted):
    step = pl.program_id(0)
    blocks = pl.num_programs(0)
    first, last = step == 0, step == blocks - 1

    @pl.when(first)
    def _():
        small[...] = jnp.zeros_like(small)

    base = idx[1] + (blocks - 1 - step) * BLOCK
    _, slope = silu_parts(pre_p[...])
    grad = d_maps[...].astype(F32) * slope
    pos = (base + lax.broadcasted_iota(jnp.int32, (BLOCK, 1), 0)).astype(F32)
    within = pos - aux[:, START : START + 1]
    whole, outer = conv_back(
        grad, within, in_p[...].astype(F32), halo_p[8:].astype(F32), conv_p, shifted, first, last, small
    )
    d_pair[...] = whole.astype(BF16)
    edge[...] = outer

    @pl.when(first)
    def _():
        tail[...] = whole[BLOCK - 16 :]


def input_back_kernel(idx, d_gate, d_inner, d_step, wg, wi, ws, send, stay):
    part = dot(d_gate[...], wg[...], 1, 1) + dot(d_inner[...], wi[...], 1, 1) + dot(d_step[...], ws[...], 1, 1)

    @pl.when(pl.program_id(0) < pl.num_programs(0) // 2)
    def _():
        send[...] = part.astype(send.dtype)

    @pl.when(pl.program_id(0) >= pl.num_programs(0) // 2)
    def _():
        stay[...] = part


def weight_back_kernel(low, d_inner, d_step, d_pair, g_wi, g_ws, g_wp):
    @pl.when(pl.program_id(0) == 0)
    def _():
        g_wi[...] = jnp.zeros_like(g_wi)
        g_ws[...] = jnp.zeros_like(g_ws)
        g_wp[...] = jnp.zeros_like(g_wp)

    g_wi[...] += dot(low[...], d_inner[...], 0, 0)
    g_ws[...] += dot(low[...], d_step[...], 0, 0)
    g_wp[...] += dot(low[...], d_pair[...], 0, 0)


def norm_back_kernel(idx, mine, other, d_pair, wp, hid, d_out, gain, grad, g_norm):
    @pl.when(pl.program_id(0) == 0)
    def _():
        g_norm[...] = jnp.zeros_like(g_norm)

    d_low = (mine[...].astype(F32) + other[...].astype(F32)) + dot(d_pair[...], wp[...], 1, 1)
    rows = hid[...].astype(F32)
    scale = lax.rsqrt(jnp.mean(rows * rows, axis=1, keepdims=True) + EPSILON)
    g_norm[...] += jnp.sum(d_low * rows * scale, axis=0, keepdims=True)
    scaled = d_low * gain[...]
    pull = jnp.mean(scaled * rows, axis=1, keepdims=True) * (scale * scale * scale)
    grad[...] = (d_out[...] + scale * scaled - rows * pull).astype(BF16)


def call(kernel, grid, ins, outs, scratch=(), prefetch=0, flops=0, moved=0):
    def spec(shape, block, index):
        if block is None:
            return pl.BlockSpec(shape, lambda *_: (0,) * len(shape))
        return pl.BlockSpec(block, index)

    scalars = [a for a, *_ in ins[:prefetch]]
    arrays = ins[prefetch:]
    in_specs = [
        pl.BlockSpec(memory_space=pltpu.SMEM) if block == "smem" else spec(a.shape, block, index)
        for a, block, index in arrays
    ]
    out_specs = [spec(shape, block, index) for shape, _, block, index in outs]
    return pl.pallas_call(
        kernel,
        grid_spec=pltpu.PrefetchScalarGridSpec(
            num_scalar_prefetch=prefetch, grid=(grid,), in_specs=in_specs, out_specs=out_specs, scratch_shapes=list(scratch)
        ),
        out_shape=[jax.ShapeDtypeStruct(shape, dtype) for shape, dtype, _, _ in outs],
        compiler_params=pltpu.CompilerParams(
            dimension_semantics=("arbitrary",), vmem_limit_bytes=48 << 20
        ),
        cost_estimate=pl.CostEstimate(flops=int(flops), bytes_accessed=int(moved), transcendentals=0),
    )(*scalars, *[a for a, *_ in arrays])


def swap(value, axis, bit):
    route = [(i, i ^ bit) for i in range(lax.axis_size(axis))]
    return jax.tree.map(lambda v: lax.ppermute(v, axis, route), value)


def shifted(value, axis, distance):
    devices = range(lax.axis_size(axis))
    route = [(i - distance, i) for i in devices if i - distance in devices]
    return lax.ppermute(value, axis, route)


def bits(axis):
    size = lax.axis_size(axis)
    return [1 << b for b in range(size.bit_length() - 1)]


def total_over(value, axis):
    for bit in bits(axis):
        value = value + swap(value, axis, bit)
    return value


def carried(total, axis, backward):
    mine = lax.axis_index(axis)

    def join(early, late):
        decay = late[CHUNK : CHUNK + 1]
        return jnp.concatenate([late[:CHUNK] + decay * early[:CHUNK], late[CHUNK:] * early[CHUNK:]])

    reached = jnp.concatenate([jnp.zeros_like(total[:CHUNK]), jnp.ones_like(total[CHUNK:])])
    for bit in bits(axis):
        other = swap(total, axis, bit)
        later = ((mine & bit) == 0) if backward else ((mine & bit) != 0)
        reached = jnp.where(later, join(other, reached), reached)
        total = jnp.where(later, join(other, total), join(total, other))
    return reached[:CHUNK]


def sum_rows(value, axis, wire):
    mine = lax.axis_index(axis)
    order = bits(axis)
    for bit in order:
        half = value.shape[0] // 2
        upper = ((mine & bit) != 0).astype(jnp.int32)
        away = lax.dynamic_slice_in_dim(value, (1 - upper) * half, half)
        value = lax.dynamic_slice_in_dim(value, upper * half, half)
        value = value + swap(away.astype(wire), axis, bit).astype(F32)
    value = value.astype(wire)
    for bit in reversed(order):
        other = swap(value, axis, bit)
        upper = (mine & bit) != 0
        value = jnp.where(upper, jnp.concatenate([other, value]), jnp.concatenate([value, other]))
    return value.astype(F32)


def both_halves(mine, other, core):
    return jnp.where(core == 0, jnp.concatenate([mine, other]), jnp.concatenate([other, mine]))


def padded(row, lanes=LANES):
    return jnp.zeros((1, lanes), F32).at[0, : row.shape[0]].set(row)


def shards(
    hidden, teacher, doc_starts, valid_mask, norm_gain, w_gate, w_inner, w_pair, w_step, conv_inner, bias_inner,
    conv_pair, bias_pair, step_bias, decay_log, skip_gain, gate_gain, w_output,
):
    rows, model = hidden.shape
    width = w_inner.shape[1]
    pair_width = w_pair.shape[1]
    heads = step_bias.shape[0]
    blocks, chunks = rows // BLOCK, rows // CHUNK
    per = BLOCK // CHUNK
    half = blocks // 2
    inner_total = float(width * lax.axis_size("head"))
    core = lax.axis_index("head") & 1
    offset = lax.axis_index("seq") * rows
    idx = jnp.stack([core, offset]).astype(jnp.int32)
    edge_rows = 16

    starts = jnp.full((1, LANES), FAR, F32).at[0, : doc_starts.shape[0]].set(doc_starts.astype(F32))
    ws = jnp.zeros((model, LANES), BF16).at[:, :heads].set(w_step)
    sbias, dlog = padded(step_bias), padded(decay_log)
    skip = jnp.repeat(skip_gain, HEAD_DIM)[None, :]
    gain, out_gain = norm_gain[None, :], gate_gain[None, :]
    conv_i, conv_p = conv_inner.astype(F32), conv_pair.astype(F32)
    bias_i, bias_p = bias_inner.astype(F32)[None, :], bias_pair.astype(F32)[None, :]
    valid = valid_mask[None, :]

    tail = shifted(hidden[rows - edge_rows :], "seq", 1)
    count = total_over(jnp.full((8, LANES), jnp.sum(valid_mask.astype(F32))), "seq")[0, 0]
    factor = (rows * lax.axis_size("seq")) / count

    def by(w, column=0):
        return (BLOCK, w), lambda i, *_: (i, column)

    def back(w, column=0):
        return (BLOCK, w), lambda i, *_: (blocks - 1 - i, column)

    row = ((1, BLOCK), lambda i, *_: (0, i))
    row_back = ((1, BLOCK), lambda i, *_: (0, blocks - 1 - i))
    grid3 = lambda n: ((per, n, width), lambda i, *_: (i, 0, 0))
    back3 = lambda n: ((per, n, width), lambda i, *_: (blocks - 1 - i, 0, 0))
    whole = (None, None)

    def send_order(w):
        return (BLOCK, w), lambda i, s: (lax.rem(i + half * (1 - s[0]), blocks), 0)

    def own_order(w):
        return (BLOCK, w), lambda i, s: (lax.rem(i + half * s[0], blocks), 0)

    own_row = ((1, BLOCK), lambda i, s: (0, lax.rem(i + half * s[0], blocks)))
    send_row = ((1, BLOCK), lambda i, s: (0, lax.rem(i + half * (1 - s[0]), blocks)))
    head_half = lambda w: ((BLOCK, w), lambda i, s: (jnp.minimum(i, half - 1), 0))
    tail_half = lambda w: ((BLOCK, w), lambda i, s: (jnp.maximum(i - half, 0), 0))

    halo_block = ((edge_rows, model), lambda i, *_: (jnp.maximum(i * (BLOCK // edge_rows) - 1, 0), 0))
    (low, in_i, in_p, pre_i, pre_p, aux, halo_i, halo_p, sloc, pkl, fin) = call(
        project_kernel,
        blocks,
        [
            (idx, None, None), (starts, *whole), (hidden, *by(model)), (hidden, *halo_block), (tail, *whole),
            (gain, *whole), (w_inner, *whole), (w_pair, *whole), (ws, *whole), (conv_i, *whole), (conv_p, *whole),
            (bias_i, *whole), (bias_p, *whole), (sbias, *whole), (dlog, *whole),
        ],
        [
            ((rows, model), BF16, *by(model)), ((rows, width), BF16, *by(width)), ((rows, pair_width), BF16, *by(pair_width)),
            ((rows, width), F32, *by(width)), ((rows, pair_width), F32, *by(pair_width)), ((rows, LANES), F32, *by(LANES)),
            ((edge_rows, width), BF16, *whole), ((edge_rows, pair_width), BF16, *whole),
            ((chunks, CHUNK, width), F32, *grid3(CHUNK)), ((chunks, 8, width), F32, *grid3(8)),
            ((CHUNK + 8, width), F32, *whole),
        ],
        [
            pltpu.VMEM((BLOCK + edge_rows, width), F32), pltpu.VMEM((BLOCK + edge_rows, pair_width), F32),
            pltpu.VMEM((CHUNK, width), F32), pltpu.VMEM((8, width), F32),
        ],
        prefetch=1, flops=3e9, moved=2e7,
    )
    state_in = carried(fin, "seq", False)
    gate, local = call(
        intra_kernel,
        blocks,
        [
            (idx, None, None), (low, *by(model)), (w_gate, *whole), (pre_i, *by(width)), (pre_p, *by(pair_width)),
            (aux, *by(LANES)), (skip, *whole),
        ],
        [((rows, width), F32, *by(width)), ((rows, width), F32, *by(width))],
        prefetch=1, flops=4e9, moved=2e7,
    )
    mixer, states, square = call(
        mix_kernel,
        blocks,
        [
            (pre_p, *by(LANES, 1)), (aux, *by(LANES)), (sloc, *grid3(CHUNK)), (pkl, *grid3(8)), (state_in, *whole),
            (local, *by(width)), (gate, *by(width)),
        ],
        [((rows, width), F32, *by(width)), ((chunks, CHUNK, width), F32, *grid3(CHUNK)), ((1, rows), F32, *row)],
        flops=1e9, moved=2e7,
    )
    square = total_over(square, "head")
    send, stay = call(
        partial(branch_kernel, total=inner_total),
        blocks,
        [
            (idx, None, None), (mixer, *send_order(width)), (gate, *send_order(width)), (square, *send_row),
            (out_gain, *whole), (w_output, *whole),
        ],
        [((rows // 2, model), BF16, *head_half(model)), ((rows // 2, model), F32, *tail_half(model))],
        prefetch=1, flops=1.2e9, moved=1e7,
    )
    mine = (stay + swap(send, "head", 1).astype(F32)).astype(BF16)
    other = swap(mine, "head", 2)
    half_own = lambda w: ((BLOCK, w), lambda i, s: (i + half * s[0], 0))
    output_half, d_branch_half, d_out, error = call(
        loss_kernel,
        half,
        [
            (idx, None, None), (factor.reshape(1), "smem", None), (hidden, *half_own(model)), (teacher, *half_own(model)),
            (valid, (1, BLOCK), lambda i, s: (0, i + half * s[0])), (mine, *by(model)), (other, *by(model)),
        ],
        [
            ((rows // 2, model), BF16, *by(model)), ((rows // 2, model), BF16, *by(model)),
            ((rows // 2, model), F32, *by(model)), ((1, model), F32, *whole),
        ],
        prefetch=1, flops=1e8, moved=1.5e7,
    )
    d_branch_other = swap(d_branch_half, "head", 1)
    output = both_halves(output_half, swap(output_half, "head", 1), core)
    weighted, cross, g_gain, g_wo = call(
        partial(branch_back_kernel, total=inner_total),
        blocks,
        [
            (idx, None, None), (d_branch_half, *head_half(model)), (d_branch_other, *tail_half(model)),
            (mixer, *own_order(width)), (gate, *own_order(width)), (square, *own_row), (out_gain, *whole), (w_output, *whole),
        ],
        [
            ((rows, width), F32, *own_order(width)), ((1, rows), F32, *own_row), ((1, width), F32, *whole),
            ((width, model), F32, *whole),
        ],
        prefetch=1, flops=2.4e9, moved=1.5e7,
    )
    cross = total_over(cross, "head")
    d_mixer, d_gate, gloc, pkb, fin_back = call(
        partial(gate_back_kernel, total=inner_total),
        blocks,
        [
            (weighted, *back(width)), (mixer, *back(width)), (gate, *back(width)), (square, *row_back), (cross, *row_back),
            (pre_p, *back(LANES, 1)), (aux, *back(LANES)),
        ],
        [
            ((rows, width), F32, *back(width)), ((rows, width), BF16, *back(width)),
            ((chunks, CHUNK, width), F32, *back3(CHUNK)), ((chunks, 8, width), F32, *back3(8)), ((CHUNK + 8, width), F32, *whole),
        ],
        [pltpu.VMEM((CHUNK, width), F32), pltpu.VMEM((8, width), F32)],
        flops=1e9, moved=2e7,
    )
    grad_in = carried(fin_back, "seq", True)
    d_scaled, d_maps, g_wg = call(
        intra_back_kernel,
        blocks,
        [
            (idx, None, None), (d_mixer, *by(width)), (pre_i, *by(width)), (pre_p, *by(pair_width)), (aux, *by(LANES)),
            (low, *by(model)), (d_gate, *by(width)),
        ],
        [((rows, width), F32, *by(width)), ((rows, pair_width), F32, *by(pair_width)), ((model, width), F32, *whole)],
        prefetch=1, flops=6e9, moved=2e7,
    )
    d_inner, d_step, d_both, edge_i, tail_i, small_i, head_small = call(
        scan_back_kernel,
        blocks,
        [
            (idx, None, None), (d_scaled, *back(width)), (d_maps, *back(pair_width)), (pre_i, *back(width)),
            (pre_p, *back(pair_width)), (in_i, *back(width)), (halo_i, *whole), (aux, *back(LANES)), (gloc, *back3(CHUNK)),
            (pkb, *back3(8)), (grad_in, *whole), (states, *back3(CHUNK)), (d_mixer, *back(width)), (mixer, *back(width)),
            (skip, *whole), (dlog, *whole), (conv_i, *whole),
        ],
        [
            ((rows, width), BF16, *back(width)), ((rows, LANES), BF16, *back(LANES)), ((rows, pair_width), F32, *back(pair_width)),
            ((8, width), F32, *whole), ((16, width), F32, *whole), ((8, width), F32, *whole), ((8, LANES), F32, *whole),
        ],
        [pltpu.VMEM((BLOCK + 16, width), F32)] * 3,
        prefetch=1, flops=3e9, moved=3e7,
    )

    def finish(grads, tail, edge):
        after = shifted(edge, "seq", -1)
        fixed = jnp.concatenate([tail[:8], tail[8:] + after]).astype(BF16)
        return lax.dynamic_update_slice(grads, fixed, (rows - 16, 0))

    d_inner = finish(d_inner, tail_i, edge_i)
    half_rows = rows // 2
    away = lax.dynamic_slice_in_dim(d_both, (1 - core) * half_rows, half_rows)
    kept = lax.dynamic_slice_in_dim(d_both, core * half_rows, half_rows)
    kept = kept + swap(away, "head", 1)
    kept = kept + swap(kept, "head", 2)
    d_both = both_halves(kept, swap(kept, "head", 1), core)
    d_pair, edge_p, tail_p, small_p = call(
        pair_back_kernel,
        blocks,
        [
            (idx, None, None), (d_both, *back(pair_width)), (pre_p, *back(pair_width)), (in_p, *back(pair_width)),
            (halo_p, *whole), (aux, *back(LANES)), (conv_p, *whole),
        ],
        [
            ((rows, pair_width), BF16, *back(pair_width)), ((8, pair_width), F32, *whole), ((16, pair_width), F32, *whole),
            ((8, pair_width), F32, *whole),
        ],
        [pltpu.VMEM((BLOCK + 16, pair_width), F32)] * 3,
        prefetch=1, flops=1e8, moved=1e7,
    )
    d_pair = finish(d_pair, tail_p, edge_p)
    send, stay = call(
        input_back_kernel,
        blocks,
        [
            (idx, None, None), (d_gate, *send_order(width)), (d_inner, *send_order(width)), (d_step, *send_order(LANES)),
            (w_gate, *whole), (w_inner, *whole), (ws, *whole),
        ],
        [((rows // 2, model), BF16, *head_half(model)), ((rows // 2, model), F32, *tail_half(model))],
        prefetch=1, flops=2.6e9, moved=1e7,
    )
    mine = (stay + swap(send, "head", 1).astype(F32)).astype(BF16)
    other = swap(mine, "head", 2)
    g_wi, g_ws, g_wp = call(
        weight_back_kernel,
        blocks,
        [(low, *by(model)), (d_inner, *by(width)), (d_step, *by(LANES)), (d_pair, *by(pair_width))],
        [((model, width), F32, *whole), ((model, LANES), F32, *whole), ((model, pair_width), F32, *whole)],
        flops=2.4e9, moved=1e7,
    )
    grad_half, g_norm = call(
        norm_back_kernel,
        half,
        [
            (idx, None, None), (mine, *by(model)), (other, *by(model)), (d_pair, *half_own(pair_width)), (w_pair, *whole),
            (hidden, *half_own(model)), (d_out, *by(model)), (gain, *whole),
        ],
        [((rows // 2, model), BF16, *by(model)), ((1, model), F32, *whole)],
        prefetch=1, flops=5e8, moved=1e7,
    )
    grad_hidden = both_halves(grad_half, swap(grad_half, "head", 1), core)

    g_wo = sum_rows(g_wo, "seq", BF16)
    g_wg = sum_rows(g_wg, "seq", BF16)
    g_wi = sum_rows(g_wi, "seq", BF16)
    g_wp = sum_rows(g_wp, "seq", F32)
    lane_small = jnp.concatenate([small_i[:6], g_gain, jnp.zeros((1, width), F32)])
    by_head = total_over(lane_small, "seq")
    head_small = total_over(head_small, "seq")
    g_ws = sum_rows(g_ws[:, :heads], "seq", F32)
    pair_small = total_over(small_p, "seq")
    sums = jnp.concatenate([g_norm, error, jnp.zeros((6, model), F32)])
    sums = total_over(sums + swap(sums, "head", 1), "seq")
    loss = jnp.sum(sums[1]) / (count * model)
    return (
        output, loss, grad_hidden, sums[0], g_wg, g_wi, g_wp, g_ws, by_head[:4], by_head[4], pair_small[:4], pair_small[4],
        head_small[0, :heads], head_small[1, :heads], jnp.sum(by_head[5].reshape(heads, HEAD_DIM), axis=1), by_head[6], g_wo,
    )


def solution(mesh):
    seq, head, wide = P("seq", None), P("head"), P(None, "head")
    in_specs = (
        seq, seq, P(), P("seq"), P(), wide, wide, P(), wide, wide, head, P(), P(), head, head, head, head, P("head", None),
    )
    out_specs = (
        seq, P(), seq, P(), wide, wide, P(), wide, wide, head, P(), P(), head, head, head, head, P("head", None),
    )
    return jax.shard_map(shards, mesh=mesh, in_specs=in_specs, out_specs=out_specs, check_vma=False)
```

time: 1280 us -> 428 us (0.33)
  local copies, waits for them, and re-layouts: 330 us -> 22.6 us
  waiting for transfers between devices: 370 us -> 133 us
  matrix products: 227 us -> 0 us
  other arithmetic: 216 us -> 39.9 us
  Pallas kernels: 0 us -> 145 us
  blocking collectives: 73.2 us -> 0 us
  starting transfers between devices: 11.9 us -> 79.9 us
  loops' own time: 23.6 us -> 0 us
  between operations: 20.2 us -> 4.58 us
    psum x3 -> x0, waiting for transfers between devices: 345 us -> none  [the longest x1 140 us: shards(): d_lowered = lax.psum(partial_input, 'head') + right_dot(d_pair, w_pair)]
    dot_general x130 -> x0, matrix products: 227 us -> none  [the longest x24 53.5 us: group_step(): jnp.einsum('ijh,jhp->ihp', scores[:, :, None] * weights, scaled, precisio...]
    dynamic_update_slice x48 -> x0, local copies, waits for them, and re-layouts: 164 us -> none  [local_pass(): lax.scan(jax.checkpoint(group_step), jnp.zeros((local_heads, HEAD_DIM, ST...]
    pallas_call x0 -> x13, Pallas kernels: none -> 145 us  [call(): pl.pallas_call(kernel, grid_spec=pltpu.PrefetchScalarGridSpec(num_scalar_...]
    ppermute x4 -> x69, waiting for transfers between devices: 2.28 us -> 133 us  [the longest x66 133 us: swap(): return jax.tree.map(lambda v: lax.ppermute(v, axis, route), value)]
    another operation x60 -> x8, other arithmetic: 101 us -> 5.32 us
    ppermute x4 -> x69, starting transfers between devices: 11.7 us -> 79.9 us  [the longest x66 72.5 us: swap(): return jax.tree.map(lambda v: lax.ppermute(v, axis, route), value)]
    psum x3 -> x0, blocking collectives: 53.8 us -> none  [the longest x1 40.8 us: shards(): lax.psum((jnp.sum(mask_float), local_error), 'seq')]
  transfers between devices with their start and end apart: 9 -> 69, of which waited for: 6 -> 36; matrix products, arithmetic and copies ran while one was open for 9% -> 12% of each run, Pallas kernels for 0% -> 23%
where the time goes in v1:
time: 428 us; the launch traced here: 425 us
  Pallas kernels  145 us (34%)
  waiting for transfers between devices  133 us (31%)
  starting transfers between devices  79.9 us (19%)
  other arithmetic  39.9 us (9%)
  local copies, waits for them, and re-layouts  22.6 us (5%)
  between operations  4.58 us (1%)
    pallas_call x13, Pallas kernels, call(): pl.pallas_call(kernel, grid_spec=pltpu.PrefetchScalarGridSpec(num_scalar_...  145 us
    ppermute x66, waiting for transfers between devices, swap(): return jax.tree.map(lambda v: lax.ppermute(v, axis, route), value)  133 us
    ppermute x66, starting transfers between devices, swap(): return jax.tree.map(lambda v: lax.ppermute(v, axis, route), value)  72.5 us
    select_n x3, other arithmetic, both_halves(): jnp.where(core == 0, jnp.concatenate([mine, other]), jnp.concatenate([oth...  10.3 us
    unnamed x53, local copies, waits for them, and re-layouts  8.97 us
  transfers between devices with their start and end apart: 69, of which 36 were waited for; matrix products, arithmetic and copies ran while one was open for 12% of the time, Pallas kernels for 23%

profile of v1, /device:TPU:0, one launch (start us, length us, event | category | flops | bytes accessed | tf_op | source)
XLA Modules:
  0.0 425.0 jit_solution(9506144689897725933)
XLA Ops:
  1.4 4.9 %collective-permute-start.3 = (bf16[16,768]{1,0:T(8,128)(2,1)S(1)}, bf16[16,768]{1,0:T(8,128)(2,1)S(1)}, u32[]{:S(2)}, u32[]{:S(2)}) collective-permute-start(bf16[16,768]{1,0:T(8,128)(2,1)S(1)} %slice.273), channel_id=1, source_target_pairs={{0,4},{4,8},{8,12},{12,16},{16,20},{20,24},{24,28},{1,5},{5,9},{9,... | collective-permute-start | bytes 73736 | tf_op jit(solution)/shard_map/ppermute | solution.py:529
  18.8 22.5 %shard_map.305 = (bf16[2048,768]{1,0:T(8,128)(2,1)}, bf16[2048,384]{1,0:T(8,128)(2,1)S(1)}, bf16[2048,256]{1,0:T(8,128)(2,1)S(1)}, f32[2048,384]{1,0:T(8,128)}, ...) custom-call(s32[2]{0:T(128)S(1)} %pad_add_fusion.idx, ...), custom_call_target="tpu_custom_call" | custom-call | flops 3000000000 | bytes 20000000 | tf_op jit(solution)/shard_map/pallas_call | solution.py:508
  46.7 10.5 %shard_map.306 = (f32[2048,384]{1,0:T(8,128)}, f32[2048,384]{1,0:T(8,128)}) custom-call(s32[2]{0:T(128)S(1)} %pad_add_fusion.idx, bf16[2048,768]{1,0:T(8,128)(2,1)} %get-tuple-element.122.low, bf16[768,384]{1,0:T(8,128)(2,1)S(1)} %copy-done.16, f32[2048,384]{1,0:T(8,128)} %get-tuple-element.123.pre_i, f32[2048,256]{1,0:T(8,128)S(1)} %copy-done, ...), custom_call_target="tpu_custom_call" | custom-call | flops 4000000000 | bytes 20000000 | tf_op jit(solution)/shard_map/pallas_call | solution.py:508
  59.0 4.7 %collective-permute-done.5 = f32[136,384]{1,0:T(8,128)S(1)} collective-permute-done((f32[136,384]{1,0:T(8,128)S(1)}, f32[136,384]{1,0:T(8,128)S(1)}, u32[]{:S(2)}, u32[]{:S(2)}) %collective-permute-start.5) | collective-permute-done | bytes 208928 | tf_op jit(solution)/shard_map/ppermute | solution.py:523
  66.5 8.1 %collective-permute-done.6 = f32[136,384]{1,0:T(8,128)S(1)} collective-permute-done((f32[136,384]{1,0:T(8,128)S(1)}, f32[136,384]{1,0:T(8,128)S(1)}, u32[]{:S(2)}, u32[]{:S(2)}) %collective-permute-start.6) | collective-permute-done | bytes 208928 | tf_op jit(solution)/shard_map/ppermute | solution.py:523
  74.8 9.7 %shard_map.307 = (f32[2048,384]{1,0:T(8,128)}, f32[16,128,384]{2,1,0:T(8,128)}, f32[1,2048]{1,0:T(1,128)S(1)}) custom-call(f32[2048,256]{1,0:T(8,128)S(1)} %copy-done.1, f32[2048,128]{1,0:T(8,128)S(1)} %get-tuple-element.118.aux, f32[16,128,384]{2,1,0:T(8,128)} %get-tuple-element.119.sloc, f32[16,8,384]{2,1,0:T(8,128)S(1)} %get-tuple-element.120.pkl, ...), custom_call_target="tpu_custom_call" | custom-call | flops 1000000000 | bytes 20000000 | tf_op jit(solution)/shard_map/pallas_call | solution.py:508
  89.4 8.4 %shard_map.308 = (bf16[1024,768]{1,0:T(8,128)(2,1)S(1)}, f32[1024,768]{1,0:T(8,128)S(1)}) custom-call(s32[2]{0:T(128)S(1)} %pad_add_fusion.idx, f32[2048,384]{1,0:T(8,128)} %get-tuple-element.126.mixer, f32[2048,384]{1,0:T(8,128)} %get-tuple-element.125.gate, f32[1,2048]{1,0:T(1,128)S(1)} %add.233.square, f32[1,384]{1,0:T(1,128)S(1)} %broadcast_in_dim.41.gain, ...), custom_call_target="tpu_custom_call" | custom-call | flops 1200000000 | bytes 10000000 | tf_op jit(solution)/shard_map/pallas_call | solution.py:508
  118.9 19.2 %collective-permute-done.10.other = bf16[1024,768]{1,0:T(8,128)(2,1)S(1)} collective-permute-done((bf16[1024,768]{1,0:T(8,128)(2,1)S(1)}, bf16[1024,768]{1,0:T(8,128)(2,1)S(1)}, u32[]{:S(2)}, u32[]{:S(2)}) %collective-permute-start.10) | collective-permute-done | bytes 1572896 | tf_op jit(solution)/shard_map/ppermute | solution.py:523
  139.3 6.6 %shard_map.309 = (bf16[1024,768]{1,0:T(8,128)(2,1)}, bf16[1024,768]{1,0:T(8,128)(2,1)}, f32[1024,768]{1,0:T(8,128)}, f32[1,768]{1,0:T(1,128)S(1)}) custom-call(s32[2]{0:T(128)S(1)} %pad_add_fusion.idx, f32[1]{0:T(128)} %bitcast.2.factor, bf16[2048,768]{1,0:T(8,128)(2,1)} %hid.5, bf16[2048,768]{1,0:T(8,128)(2,1)} %teacher.1, s32[1,2048]{1,0:T(1,128)S(1)} %bitcast.24, ...), custom_call_target="tpu_custom_call" | custom-call | flops 100000000 | bytes 15000000 | tf_op jit(solution)/shard_map/pallas_call | solution.py:508
  150.7 11.8 %shard_map.310 = (f32[2048,384]{1,0:T(8,128)}, f32[1,2048]{1,0:T(1,128)S(1)}, f32[1,384]{1,0:T(1,128)S(1)}, f32[384,768]{1,0:T(8,128)S(1)}) custom-call(s32[2]{0:T(128)S(1)} %pad_add_fusion.idx, bf16[1024,768]{1,0:T(8,128)(2,1)} %get-tuple-element.131.mine, bf16[1024,768]{1,0:T(8,128)(2,1)} %collective-permute-done.12.other, ...), custom_call_target="tpu_custom_call" | custom-call | flops 2400000000 | bytes 15000000 | tf_op jit(solution)/shard_map/pallas_call | solution.py:508
  169.7 10.2 %shard_map.311 = (f32[2048,384]{1,0:T(8,128)}, bf16[2048,384]{1,0:T(8,128)(2,1)S(1)}, f32[16,128,384]{2,1,0:T(8,128)}, f32[16,8,384]{2,1,0:T(8,128)S(1)}, f32[136,384]{1,0:T(8,128)S(1)}) custom-call(f32[2048,384]{1,0:T(8,128)} %get-tuple-element.132.weighted, f32[2048,384]{1,0:T(8,128)} %get-tuple-element.126.mixer, f32[2048,384]{1,0:T(8,128)} %get-tuple-element.125.gate, ...), custom_call_target="tpu_custom_call" | custom-call | flops 1000000000 | bytes 20000000 | tf_op jit(solution)/shard_map/pallas_call | solution.py:508
  181.0 12.7 %shard_map.312 = (f32[2048,384]{1,0:T(8,128)}, f32[2048,256]{1,0:T(8,128)S(1)}, f32[768,384]{1,0:T(8,128)S(1)}) custom-call(s32[2]{0:T(128)S(1)} %pad_add_fusion.idx, f32[2048,384]{1,0:T(8,128)} %get-tuple-element.135.d_mixer, f32[2048,384]{1,0:T(8,128)} %get-tuple-element.123.pre_i, f32[2048,256]{1,0:T(8,128)} %get-tuple-element.117.pre_p.pre_c, ...), custom_call_target="tpu_custom_call" | custom-call | flops 6000000000 | bytes 20000000 | tf_op jit(solution)/shard_map/pallas_call | solution.py:508
  195.4 6.0 %collective-permute-done.16 = f32[136,384]{1,0:T(8,128)S(1)} collective-permute-done((f32[136,384]{1,0:T(8,128)S(1)}, f32[136,384]{1,0:T(8,128)S(1)}, u32[]{:S(2)}, u32[]{:S(2)}) %collective-permute-start.16) | collective-permute-done | bytes 208928 | tf_op jit(solution)/shard_map/ppermute | solution.py:523
  203.5 9.0 %collective-permute-done.17 = f32[136,384]{1,0:T(8,128)S(1)} collective-permute-done((f32[136,384]{1,0:T(8,128)S(1)}, f32[136,384]{1,0:T(8,128)S(1)}, u32[]{:S(2)}, u32[]{:S(2)}) %collective-permute-start.17) | collective-permute-done | bytes 208928 | tf_op jit(solution)/shard_map/ppermute | solution.py:523
  212.5 23.1 %shard_map.313 = (bf16[2048,384]{1,0:T(8,128)(2,1)S(1)}, bf16[2048,128]{1,0:T(8,128)(2,1)S(1)}, f32[2048,256]{1,0:T(8,128)}, f32[8,384]{1,0:T(8,128)S(1)}, f32[1...) custom-call(s32[2]{0:T(128)S(1)} %pad_add_fusion.idx, f32[2048,384]{1,0:T(8,128)} %get-tuple-element.136.d_scaled, ...), custom_call_target="tpu_custom_call" | custom-call | flops 3000000000 | bytes 30000000 | tf_op jit(solution)/shard_map/pallas_call | solution.py:508
  256.4 9.2 %shard_map.314 = (bf16[1024,768]{1,0:T(8,128)(2,1)S(1)}, f32[1024,768]{1,0:T(8,128)}) custom-call(s32[2]{0:T(128)S(1)} %pad_add_fusion.idx, bf16[2048,384]{1,0:T(8,128)(2,1)S(1)} %get-tuple-element.134.d_gate, bf16[2048,384]{1,0:T(8,128)(2,1)} %maximum_dynamic-update-slice_fusion.d_inner, bf16[2048,128]{1,0:T(8,128)(2,1)S(1)} %get-tuple-element.147.d_step, ...), custom_call_target="tpu_custom_call" | custom-call | flops 2600000000 | bytes 10000000 | tf_op jit(solution)/shard_map/pallas_call | solution.py:508
  297.6 7.3 %shard_map.315 = (bf16[2048,256]{1,0:T(8,128)(2,1)S(1)}, f32[8,256]{1,0:T(8,128)S(1)}, f32[16,256]{1,0:T(8,128)S(1)}, f32[8,256]{1,0:T(8,128)S(1)}) custom-call(s32[2]{0:T(128)S(1)} %pad_add_fusion.idx, f32[2048,256]{1,0:T(8,128)S(1)} %maximum_select_fusion.2.d_maps, f32[2048,256]{1,0:T(8,128)} %get-tuple-element.117.pre_p.pre_c, ...), custom_call_target="tpu_custom_call" | custom-call | flops 100000000 | bytes 10000000 | tf_op jit(solution)/shard_map/pallas_call | solution.py:508
  312.4 7.5 %shard_map.317 = (f32[768,384]{1,0:T(8,128)S(1)}, f32[768,128]{1,0:T(8,128)S(1)}, f32[768,256]{1,0:T(8,128)S(1)}) custom-call(bf16[2048,768]{1,0:T(8,128)(2,1)} %get-tuple-element.122.low, bf16[2048,384]{1,0:T(8,128)(2,1)S(1)} %copy-done.13, bf16[2048,128]{1,0:T(8,128)(2,1)S(1)} %copy-done.19, bf16[2048,256]{1,0:T(8,128)(2,1)S(1)} %constant_dynamic-update-slice_fusion.d_pair), custom_call_target="tpu_custom_call" | custom-call | flops 2400000000 | bytes 10000000 | tf_op jit(solution)/shard_map/pallas_call | solution.py:508
  345.1 5.1 %shard_map.316 = (bf16[1024,768]{1,0:T(8,128)(2,1)S(1)}, f32[1,768]{1,0:T(1,128)S(1)}) custom-call(s32[2]{0:T(128)S(1)} %pad_add_fusion.idx, bf16[1024,768]{1,0:T(8,128)(2,1)S(1)} %add_convert_fusion.mine, bf16[1024,768]{1,0:T(8,128)(2,1)S(1)} %collective-permute-done.20.other, bf16[2048,256]{1,0:T(8,128)(2,1)S(1)} %constant_dynamic-update-slice_fusion.d_pair, ...), custom_call_target="tpu_custom_call" | custom-call | flops 500000000 | bytes 10000000 | tf_op jit(solution)/shard_map/pallas_call | solution.py:508
  367.3 4.8 %collective-permute-done.43 = f32[192,256]{1,0:T(8,128)S(1)} collective-permute-done((f32[192,256]{1,0:T(8,128)S(1)}, f32[192,256]{1,0:T(8,128)S(1)}, u32[]{:S(2)}, u32[]{:S(2)}) %collective-permute-start.43) | collective-permute-done | bytes 196640 | tf_op jit(solution)/shard_map/ppermute | solution.py:523
  373.3 6.4 %collective-permute-done.38 = bf16[96,384]{1,0:T(8,128)(2,1)S(1)} collective-permute-done((bf16[96,384]{1,0:T(8,128)(2,1)S(1)}, bf16[96,384]{1,0:T(8,128)(2,1)S(1)}, u32[]{:S(2)}, u32[]{:S(2)}) %collective-permute-start.38) | collective-permute-done | bytes 73760 | tf_op jit(solution)/shard_map/ppermute | solution.py:523
  379.7 6.7 %collective-permute-done.44 = f32[96,256]{1,0:T(8,128)S(1)} collective-permute-done((f32[96,256]{1,0:T(8,128)S(1)}, f32[96,256]{1,0:T(8,128)S(1)}, u32[]{:S(2)}, u32[]{:S(2)}) %collective-permute-start.44) | collective-permute-done | bytes 98336 | tf_op jit(solution)/shard_map/ppermute | solution.py:523
  386.4 6.2 %collective-permute-done.39 = bf16[96,384]{1,0:T(8,128)(2,1)S(1)} collective-permute-done((bf16[96,384]{1,0:T(8,128)(2,1)S(1)}, bf16[96,384]{1,0:T(8,128)(2,1)S(1)}, u32[]{:S(2)}, u32[]{:S(2)}) %collective-permute-start.39) | collective-permute-done | bytes 73760 | tf_op jit(solution)/shard_map/ppermute | solution.py:523
  392.7 6.1 %collective-permute-done.45 = f32[96,256]{1,0:T(8,128)S(1)} collective-permute-done((f32[96,256]{1,0:T(8,128)S(1)}, f32[96,256]{1,0:T(8,128)S(1)}, u32[]{:S(2)}, u32[]{:S(2)}) %collective-permute-start.45) | collective-permute-done | bytes 98336 | tf_op jit(solution)/shard_map/ppermute | solution.py:523
  (330 shorter events, 193.5 us)
Async XLA Ops:
  1.4 15.4 %collective-permute-start.3 = (bf16[16,768]{1,0:T(8,128)(2,1)S(1)}, bf16[16,768]{1,0:T(8,128)(2,1)S(1)}, u32[]{:S(2)}, u32[]{:S(2)}) collective-permute-start(bf16[16,768]{1,0:T(8,128)(2,1)S(1)} %slice.273), channel_id=1, source_target_pairs={{0,4},{4,8},{8,12},{12,16},{16,20},{20,24},{24,28},{1,5},{5,9},{9,... | collective-permute-start | bytes 73736 | tf_op jit(solution)/shard_map/ppermute | solution.py:529
  43.5 13.7 %collective-permute-start.4 = (f32[136,384]{1,0:T(8,128)S(1)}, f32[136,384]{1,0:T(8,128)S(1)}, u32[]{:S(2)}, u32[]{:S(2)}) collective-permute-start(f32[136,384]{1,0:T(8,128)S(1)} %get-tuple-element.121), channel_id=1, source_target_pairs={{0,4},{4,0},{8,12},{12,8},{16,20},{20,16},{24,28},{28,24},{1,5},{5... | collective-permute-start | bytes 626696 | tf_op jit(solution)/shard_map/ppermute | solution.py:523
  101.6 36.5 %collective-permute-start.10 = (bf16[1024,768]{1,0:T(8,128)(2,1)S(1)}, bf16[1024,768]{1,0:T(8,128)(2,1)S(1)}, u32[]{:S(2)}, u32[]{:S(2)}) collective-permute-start(bf16[1024,768]{1,0:T(8,128)(2,1)S(1)} %add_convert_fusion.1.mine), channel_id=1, source_target_pairs={{0,2},{1,3},{2,0},{3,1},{4,6},{5,7},{6,4},{7,5},{8,10},{9,11},{10,... | collective-permute-start | bytes 4718600 | tf_op jit(solution)/shard_map/ppermute | solution.py:523
  145.9 19.4 %collective-permute-start.11 = (bf16[1024,768]{1,0:T(8,128)(2,1)}, bf16[1024,768]{1,0:T(8,128)(2,1)}, u32[]{:S(2)}, u32[]{:S(2)}) collective-permute-start(bf16[1024,768]{1,0:T(8,128)(2,1)} %get-tuple-element.130), channel_id=1, source_target_pairs={{0,1},{1,0},{2,3},{3,2},{4,5},{5,4},{6,7},{7,6},{8,9},{9,8},{10,11... | collective-permute-start | bytes 4718600 | tf_op jit(solution)/shard_map/ppermute | solution.py:523
  162.6 32.6 %collective-permute-start.63 = (bf16[192,768]{1,0:T(8,128)(2,1)S(1)}, bf16[192,768]{1,0:T(8,128)(2,1)S(1)}, u32[]{:S(2)}, u32[]{:S(2)}) collective-permute-start(bf16[192,768]{1,0:T(8,128)(2,1)S(1)} %dynamic-slice_convert_fusion), channel_id=1, source_target_pairs={{0,4},{4,0},{8,12},{12,8},{16,20},{20,16},{24,28},{28,24},{1,5},{5... | collective-permute-start | bytes 884744 | tf_op jit(solution)/shard_map/ppermute | solution.py:523
  179.9 14.9 %collective-permute-start.15 = (f32[136,384]{1,0:T(8,128)S(1)}, f32[136,384]{1,0:T(8,128)S(1)}, u32[]{:S(2)}, u32[]{:S(2)}) collective-permute-start(f32[136,384]{1,0:T(8,128)S(1)} %get-tuple-element.142), channel_id=1, source_target_pairs={{0,4},{4,0},{8,12},{12,8},{16,20},{20,16},{24,28},{28,24},{1,5},{5... | collective-permute-start | bytes 626696 | tf_op jit(solution)/shard_map/ppermute | solution.py:523
  193.7 44.3 %collective-permute-start.30 = (bf16[384,384]{1,0:T(8,128)(2,1)S(1)}, bf16[384,384]{1,0:T(8,128)(2,1)S(1)}, u32[]{:S(2)}, u32[]{:S(2)}) collective-permute-start(bf16[384,384]{1,0:T(8,128)(2,1)S(1)} %dynamic-slice_convert_fusion.2), channel_id=1, source_target_pairs={{0,4},{4,0},{8,12},{12,8},{16,20},{20,16},{24,28},{28,24},{1,5},{5... | collective-permute-start | bytes 884744 | tf_op jit(solution)/shard_map/ppermute | solution.py:523
  247.5 24.8 %collective-permute-start.22 = (f32[1024,256]{1,0:T(8,128)S(1)}, f32[1024,256]{1,0:T(8,128)S(1)}, u32[]{:S(2)}, u32[]{:S(2)}) collective-permute-start(f32[1024,256]{1,0:T(8,128)S(1)} %dynamic-slice_add_fusion), channel_id=1, source_target_pairs={{0,2},{1,3},{2,0},{3,1},{4,6},{5,7},{6,4},{7,5},{8,10},{9,11},{10,... | collective-permute-start | bytes 3145736 | tf_op jit(solution)/shard_map/ppermute | solution.py:523
  248.1 17.5 %collective-permute-start.32 = (bf16[96,384]{1,0:T(8,128)(2,1)S(1)}, bf16[96,384]{1,0:T(8,128)(2,1)S(1)}, u32[]{:S(2)}, u32[]{:S(2)}) collective-permute-start(bf16[96,384]{1,0:T(8,128)(2,1)S(1)} %dynamic-slice_convert_fusion.8), channel_id=1, source_target_pairs={{0,16},{4,20},{8,24},{12,28},{16,0},{20,4},{24,8},{28,12},{1,17},{... | collective-permute-start | bytes 221192 | tf_op jit(solution)/shard_map/ppermute | solution.py:523
  251.5 23.0 %collective-permute-start.66 = (bf16[48,768]{1,0:T(8,128)(2,1)S(1)}, bf16[48,768]{1,0:T(8,128)(2,1)S(1)}, u32[]{:S(2)}, u32[]{:S(2)}) collective-permute-start(bf16[48,768]{1,0:T(8,128)(2,1)S(1)} %add_convert_fusion.2), channel_id=1, source_target_pairs={{0,16},{4,20},{8,24},{12,28},{16,0},{20,4},{24,8},{28,12},{1,17},{... | collective-permute-start | bytes 221192 | tf_op jit(solution)/shard_map/ppermute | solution.py:523
  265.6 40.6 %collective-permute-start.19 = (bf16[1024,768]{1,0:T(8,128)(2,1)S(1)}, bf16[1024,768]{1,0:T(8,128)(2,1)}, u32[]{:S(2)}, u32[]{:S(2)}) collective-permute-start(bf16[1024,768]{1,0:T(8,128)(2,1)S(1)} %get-tuple-element.149), channel_id=1, source_target_pairs={{0,1},{1,0},{2,3},{3,2},{4,5},{5,4},{6,7},{7,6},{8,9},{9,8},{10,11... | collective-permute-start | bytes 4718600 | tf_op jit(solution)/shard_map/ppermute | solution.py:523
  265.7 16.1 %collective-permute-start.33 = (bf16[96,384]{1,0:T(8,128)(2,1)S(1)}, bf16[96,384]{1,0:T(8,128)(2,1)S(1)}, u32[]{:S(2)}, u32[]{:S(2)}) collective-permute-start(bf16[96,384]{1,0:T(8,128)(2,1)S(1)} %add_convert_fusion.4), channel_id=1, source_target_pairs={{0,16},{4,20},{8,24},{12,28},{16,0},{20,4},{24,8},{28,12},{1,17},{... | collective-permute-start | bytes 221192 | tf_op jit(solution)/shard_map/ppermute | solution.py:523
  273.4 21.7 %collective-permute-start.23 = (f32[1024,256]{1,0:T(8,128)}, f32[1024,256]{1,0:T(8,128)}, u32[]{:S(2)}, u32[]{:S(2)}) collective-permute-start(f32[1024,256]{1,0:T(8,128)} %add.248), channel_id=1, source_target_pairs={{0,1},{1,0},{2,3},{3,2},{4,5},{5,4},{6,7},{7,6},{8,9},{9,8},{10,11... | collective-permute-start | bytes 3145736 | tf_op jit(solution)/shard_map/ppermute | solution.py:523
  278.2 14.0 %collective-permute-start.67 = (bf16[96,768]{1,0:T(8,128)(2,1)S(1)}, bf16[96,768]{1,0:T(8,128)(2,1)S(1)}, u32[]{:S(2)}, u32[]{:S(2)}) collective-permute-start(bf16[96,768]{1,0:T(8,128)(2,1)S(1)} %maximum_select_fusion.16), channel_id=1, source_target_pairs={{0,8},{4,12},{8,0},{12,4},{16,24},{20,28},{24,16},{28,20},{1,9},{5... | collective-permute-start | bytes 442376 | tf_op jit(solution)/shard_map/ppermute | solution.py:523
  292.2 27.9 %collective-permute-start.68 = (bf16[192,768]{1,0:T(8,128)(2,1)S(1)}, bf16[192,768]{1,0:T(8,128)(2,1)S(1)}, u32[]{:S(2)}, u32[]{:S(2)}) collective-permute-start(bf16[192,768]{1,0:T(8,128)(2,1)S(1)} %maximum_select_fusion.10), channel_id=1, source_target_pairs={{0,4},{4,0},{8,12},{12,8},{16,20},{20,16},{24,28},{28,24},{1,5},{5... | collective-permute-start | bytes 884744 | tf_op jit(solution)/shard_map/ppermute | solution.py:523
  294.1 112.5 %collective-permute-start.35 = (bf16[384,384]{1,0:T(8,128)(2,1)}, bf16[384,384]{1,0:T(8,128)(2,1)}, u32[]{:S(2)}, u32[]{:S(2)}) collective-permute-start(bf16[384,384]{1,0:T(8,128)(2,1)} %maximum_select_fusion.8), channel_id=1, source_target_pairs={{0,4},{4,0},{8,12},{12,8},{16,20},{20,16},{24,28},{28,24},{1,5},{5... | collective-permute-start | bytes 884744 | tf_op jit(solution)/shard_map/ppermute | solution.py:523
  309.1 32.5 %collective-permute-start.20 = (bf16[1024,768]{1,0:T(8,128)(2,1)S(1)}, bf16[1024,768]{1,0:T(8,128)(2,1)S(1)}, u32[]{:S(2)}, u32[]{:S(2)}) collective-permute-start(bf16[1024,768]{1,0:T(8,128)(2,1)S(1)} %add_convert_fusion.mine), channel_id=1, source_target_pairs={{0,2},{1,3},{2,0},{3,1},{4,6},{5,7},{6,4},{7,5},{8,10},{9,11},{10,... | collective-permute-start | bytes 4718600 | tf_op jit(solution)/shard_map/ppermute | solution.py:523
  321.8 31.8 %collective-permute-start.58 = (f32[8,256]{1,0:T(8,128)}, f32[8,256]{1,0:T(8,128)}, u32[]{:S(2)}, u32[]{:S(2)}) collective-permute-start(f32[8,256]{1,0:T(8,128)} %add.272), channel_id=1, source_target_pairs={{0,8},{4,12},{8,0},{12,4},{16,24},{20,28},{24,16},{28,20},{1,9},{5... | collective-permute-start | bytes 24584 | tf_op jit(solution)/shard_map/ppermute | solution.py:523
  329.3 31.7 %collective-permute-start.42 = (f32[384,256]{1,0:T(8,128)}, f32[384,256]{1,0:T(8,128)}, u32[]{:S(2)}, u32[]{:S(2)}) collective-permute-start(f32[384,256]{1,0:T(8,128)} %constant_dynamic-slice_fusion.5), channel_id=1, source_target_pairs={{0,4},{4,0},{8,12},{12,8},{16,20},{20,16},{24,28},{28,24},{1,5},{5... | collective-permute-start | bytes 1179656 | tf_op jit(solution)/shard_map/ppermute | solution.py:523
  336.4 22.7 %collective-permute-start.36 = (bf16[384,384]{1,0:T(8,128)(2,1)}, bf16[384,384]{1,0:T(8,128)(2,1)}, u32[]{:S(2)}, u32[]{:S(2)}) collective-permute-start(bf16[384,384]{1,0:T(8,128)(2,1)} %dynamic-slice_convert_fusion.1), channel_id=1, source_target_pairs={{0,4},{4,0},{8,12},{12,8},{16,20},{20,16},{24,28},{28,24},{1,5},{5... | collective-permute-start | bytes 884744 | tf_op jit(solution)/shard_map/ppermute | solution.py:523
  353.6 66.8 %collective-permute-start.29 = (bf16[1024,768]{1,0:T(8,128)(2,1)S(1)}, bf16[1024,768]{1,0:T(8,128)(2,1)}, u32[]{:S(2)}, u32[]{:S(2)}) collective-permute-start(bf16[1024,768]{1,0:T(8,128)(2,1)S(1)} %get-tuple-element.159), channel_id=1, source_target_pairs={{0,1},{1,0},{2,3},{3,2},{4,5},{5,4},{6,7},{7,6},{8,9},{9,8},{10,11... | collective-permute-start | bytes 4718600 | tf_op jit(solution)/shard_map/ppermute | solution.py:523
  357.0 51.1 %collective-permute-start.59 = (f32[8,256]{1,0:T(8,128)S(1)}, f32[8,256]{1,0:T(8,128)S(1)}, u32[]{:S(2)}, u32[]{:S(2)}) collective-permute-start(f32[8,256]{1,0:T(8,128)S(1)} %add.273), channel_id=1, source_target_pairs={{0,16},{4,20},{8,24},{12,28},{16,0},{20,4},{24,8},{28,12},{1,17},{... | collective-permute-start | bytes 24584 | tf_op jit(solution)/shard_map/ppermute | solution.py:523
  359.1 39.6 %collective-permute-start.26 = (f32[8,768]{1,0:T(8,128)S(1)}, f32[8,768]{1,0:T(8,128)S(1)}, u32[]{:S(2)}, u32[]{:S(2)}) collective-permute-start(f32[8,768]{1,0:T(8,128)S(1)} %fusion.14), channel_id=1, source_target_pairs={{0,4},{4,0},{8,12},{12,8},{16,20},{20,16},{24,28},{28,24},{1,5},{5... | collective-permute-start | bytes 73736 | tf_op jit(solution)/shard_map/ppermute | solution.py:523
  406.6 11.7 %collective-permute-start.41 = (bf16[384,384]{1,0:T(8,128)(2,1)S(1)}, bf16[384,384]{1,0:T(8,128)(2,1)S(1)}, u32[]{:S(2)}, u32[]{:S(2)}) collective-permute-start(bf16[384,384]{1,0:T(8,128)(2,1)S(1)} %maximum_select_fusion.9), channel_id=1, source_target_pairs={{0,4},{4,0},{8,12},{12,8},{16,20},{20,16},{24,28},{28,24},{1,5},{5... | collective-permute-start | bytes 884744 | tf_op jit(solution)/shard_map/ppermute | solution.py:523
  (71 other events, 549.0 us)

commit v2 on v1

--- a/solution.py
+++ b/solution.py
@@ -219,38 +219,113 @@
     return as_column(lax.rsqrt(square / total + EPSILON))
 
 
-def branch_kernel(idx, mixer, gate, square, gain, wo, send, stay, *, total):
+def core_bit():
+    return lax.rem(lax.axis_index("head"), 2)
+
+
+def core_peer():
+    return lax.axis_index("head") + 1 - 2 * core_bit()
+
+
+def enter(peers):
+    barrier = pltpu.get_barrier_semaphore()
+    for peer in peers:
+        pl.semaphore_signal(barrier, inc=1, device_id=peer, device_id_type=pl.DeviceIdType.MESH)
+    pl.semaphore_wait(barrier, len(peers))
+
+
+def to_peer(src, dst, sends, lands, slot):
+    return pltpu.make_async_remote_copy(
+        src_ref=src, dst_ref=dst, send_sem=sends.at[slot], recv_sem=lands.at[slot],
+        device_id={"head": core_peer()}, device_id_type=pl.DeviceIdType.MESH,
+    )
+
+
+def add_halves(part, mine, away, land, send_sem, land_sem):
     step = pl.program_id(0)
+    half = pl.num_programs(0) // 2
+
+    def copy(slot):
+        return to_peer(away.at[slot], land.at[slot], send_sem, land_sem, slot)
+
+    @pl.when(step < half)
+    def _():
+        away[step] = part.astype(away.dtype)
+        copy(step).start()
+
+    @pl.when(step >= half)
+    def _():
+        copy(step - half).wait_recv()
+        mine[...] = (part + land[step - half].astype(F32)).astype(mine.dtype)
+
+    @pl.when(step == 2 * half - 1)
+    def _():
+        def drain(slot, carry):
+            copy(slot).wait_send()
+            return carry
+
+        lax.fori_loop(0, half, drain, 0)
+
+
+def branch_kernel(mixer, gate, square, gain, wo, mine, away, land, send_sem, land_sem, *, total):
+    @pl.when(pl.program_id(0) == 0)
+    def _():
+        enter([{"head": core_peer()}])
+
     act, _ = silu_parts(gate[...])
     gated = mixer[...] * act
     normed = (gated * gate_scale(square[...], total) * gain[...]).astype(BF16)
-    part = dot(normed, wo[...])
-
-    @pl.when(step < pl.num_programs(0) // 2)
-    def _():
-        send[...] = part.astype(send.dtype)
-
-    @pl.when(step >= pl.num_programs(0) // 2)
-    def _():
-        stay[...] = part
-
-
-def loss_kernel(idx, factor, hid, teacher, valid, mine, other, out, d_branch, d_out, error):
-    @pl.when(pl.program_id(0) == 0)
+    add_halves(dot(normed, wo[...]), mine, away, land, send_sem, land_sem)
+
+
+def both_cores(buffers, wholes, sems):
+    step = pl.program_id(0)
+    half = pl.num_programs(0)
+    local, send, land = sems
+
+    def copies(k, slot):
+        rows = pl.ds(pl.multiple_of((core_bit() * half + slot) * BLOCK, BLOCK), BLOCK)
+        here = pltpu.make_async_copy(buffers[k].at[slot], wholes[k].at[rows], local.at[k * half + slot])
+        there = to_peer(buffers[k].at[slot], wholes[k].at[rows], send, land, k * half + slot)
+        return here, there
+
+    for k in range(len(wholes)):
+        for copy in copies(k, step):
+            copy.start()
+
+    @pl.when(step == half - 1)
+    def _():
+        for k in range(len(wholes)):
+
+            def drain(slot, carry, k=k):
+                here, there = copies(k, slot)
+                here.wait()
+                there.wait()
+                return carry
+
+            lax.fori_loop(0, half, drain, 0)
+
+
+def loss_kernel(factor, hid, teacher, valid, mine, other, out, d_branch, d_out, error, out_block, grad_block, *sems):
+    step = pl.program_id(0)
+
+    @pl.when(step == 0)
     def _():
         error[...] = jnp.zeros_like(error)
+        enter([{"head": core_peer()}])
 
     outf = hid[...].astype(F32) + (mine[...].astype(F32) + other[...].astype(F32))
-    out[...] = outf.astype(BF16)
     term = outf - teacher[...].astype(F32)
     masked = as_column(valid[...].astype(F32)) * term
     error[...] += jnp.sum(masked * term, axis=0, keepdims=True)
     grad = masked * factor[0]
     d_out[...] = grad
-    d_branch[...] = grad.astype(BF16)
-
-
-def branch_back_kernel(idx, mine, other, mixer, gate, square, gain, wo, weighted, cross, g_gain, g_wo, *, total):
+    out_block[step] = outf.astype(BF16)
+    grad_block[step] = grad.astype(BF16)
+    both_cores([out_block, grad_block], [out, d_branch], sems)
+
+
+def branch_back_kernel(d_branch, mixer, gate, square, gain, wo, weighted, cross, g_gain, g_wo, *, total):
     step = pl.program_id(0)
 
     @pl.when(step == 0)
@@ -258,13 +333,12 @@
         g_gain[...] = jnp.zeros_like(g_gain)
         g_wo[...] = jnp.zeros_like(g_wo)
 
-    d_branch = jnp.where(step < pl.num_programs(0) // 2, mine[...], other[...])
     act, _ = silu_parts(gate[...])
     gated = mixer[...] * act
     scaled = gated * gate_scale(square[...], total)
     normed = (scaled * gain[...]).astype(BF16)
-    g_wo[...] += dot(normed, d_branch, 0, 0)
-    d_normed = dot(d_branch, wo[...], 1, 1)
+    g_wo[...] += dot(normed, d_branch[...], 0, 0)
+    d_normed = dot(d_branch[...], wo[...], 1, 1)
     g_gain[...] += jnp.sum(d_normed * scaled, axis=0, keepdims=True)
     grad = d_normed * gain[...]
     weighted[...] = grad
@@ -364,8 +438,8 @@
 
 
 def scan_back_kernel(
-    idx, d_scaled, d_maps, pre_i, pre_p, in_i, halo_i, aux, gloc, pkl, gin, states, d_mixer, mixer, skip, dlog, conv_i,
-    d_inner, d_step, d_both, edge, tail, small, heads, *shifted,
+    idx, d_scaled, d_maps, pre_i, pre_p, in_i, in_p, halo_i, halo_p, aux, gloc, pkl, gin, states, d_mixer, mixer, skip, dlog,
+    conv_i, conv_p, d_inner, d_step, d_pair, edge, tail, small, small_p, heads, *shifted,
 ):
     step = pl.program_id(0)
     blocks = pl.num_programs(0)
@@ -375,16 +449,17 @@
     @pl.when(first)
     def _():
         small[...] = jnp.zeros_like(small)
+        small_p[...] = jnp.zeros_like(small_p)
         heads[...] = jnp.zeros_like(heads)
 
     base = idx[1] + (blocks - 1 - step) * BLOCK
-    maps, _ = silu_parts(pre_p[...])
+    maps, slope_p = silu_parts(pre_p[...])
     values, slope = silu_parts(pre_i[...])
     dy = d_mixer[...]
     upper = triangle(True)
     lane = lax.broadcasted_iota(jnp.int32, (CHUNK, LANES), 1)
     grown = jnp.exp(dlog[...])
-    pieces = []
+    pieces, pieces_p = [], []
     for c in range(BLOCK // CHUNK):
         at = slice(c * CHUNK, (c + 1) * CHUNK)
         table = aux[at, :]
@@ -399,7 +474,7 @@
         total = d_scaled[at, :] + passed
         d_reads = d_maps[at, LANES:] + dot3(dy[at] * inflow, state, 1, 1)
         d_keys = d_maps[at, :LANES] + dot3(scaled * outflow, grad_state, 1, 1)
-        d_both[at, :] = jnp.concatenate([d_keys, d_reads], axis=1)
+        pieces_p.append(jnp.concatenate([d_keys, d_reads], axis=1))
         plain = mixer[at, :] - skip[...] * values[at]
         d_cum = head_sums(dy[at] * plain - scaled * total)
         carried = jnp.sum(grad_state * state, axis=0, keepdims=True) * inflow[CHUNK - 1 :]
@@ -417,102 +492,178 @@
     grad = jnp.concatenate(pieces, axis=0) * slope
     pos = (base + lax.broadcasted_iota(jnp.int32, (BLOCK, 1), 0)).astype(F32)
     within = pos - aux[:, START : START + 1]
-    edge_inputs = halo_i[8:].astype(F32)
     whole, outer = conv_back(
-        grad, within, in_i[...].astype(F32), edge_inputs, conv_i, shifted, first, last, small
+        grad, within, in_i[...].astype(F32), halo_i[8:].astype(F32), conv_i, shifted[:3], first, last, small
+    )
+    grad_p = jnp.concatenate(pieces_p, axis=0) * slope_p
+    whole_p, outer_p = conv_back(
+        grad_p, within, in_p[...].astype(F32), halo_p[8:].astype(F32), conv_p, shifted[3:], first, last, small_p
     )
     d_inner[...] = whole.astype(BF16)
-    edge[...] = outer
+    d_pair[...] = whole_p
+    edge[...] = jnp.concatenate([outer, outer_p], axis=1)
 
     @pl.when(first)
     def _():
-        tail[...] = whole[BLOCK - 16 :]
-
-
-def pair_back_kernel(idx, d_maps, pre_p, in_p, halo_p, aux, conv_p, d_pair, edge, tail, small, *shifted):
+        tail[...] = jnp.concatenate([whole[BLOCK - 16 :], whole_p[BLOCK - 16 :]], axis=1)
+
+
+def dot_split(a, b, da=1, db=0):
+    high, low = halves(b)
+    return dot(a, high, da, db) + dot(a, low, da, db)
+
+
+def input_back_kernel(
+    d_gate, d_inner, d_step, d_pair, wg, wi, ws, wp, edge, tail, mine, fix_i, fix_p,
+    block_i, block_p, after, away, land, send_sem, land_sem, edge_send, edge_land,
+):
     step = pl.program_id(0)
     blocks = pl.num_programs(0)
-    first, last = step == 0, step == blocks - 1
-
-    @pl.when(first)
-    def _():
-        small[...] = jnp.zeros_like(small)
-
-    base = idx[1] + (blocks - 1 - step) * BLOCK
-    _, slope = silu_parts(pre_p[...])
-    grad = d_maps[...].astype(F32) * slope
-    pos = (base + lax.broadcasted_iota(jnp.int32, (BLOCK, 1), 0)).astype(F32)
-    within = pos - aux[:, START : START + 1]
-    whole, outer = conv_back(
-        grad, within, in_p[...].astype(F32), halo_p[8:].astype(F32), conv_p, shifted, first, last, small
-    )
-    d_pair[...] = whole.astype(BF16)
-    edge[...] = outer
-
-    @pl.when(first)
-    def _():
-        tail[...] = whole[BLOCK - 16 :]
-
-
-def input_back_kernel(idx, d_gate, d_inner, d_step, wg, wi, ws, send, stay):
-    part = dot(d_gate[...], wg[...], 1, 1) + dot(d_inner[...], wi[...], 1, 1) + dot(d_step[...], ws[...], 1, 1)
-
-    @pl.when(pl.program_id(0) < pl.num_programs(0) // 2)
-    def _():
-        send[...] = part.astype(send.dtype)
-
-    @pl.when(pl.program_id(0) >= pl.num_programs(0) // 2)
-    def _():
-        stay[...] = part
-
-
-def weight_back_kernel(low, d_inner, d_step, d_pair, g_wi, g_ws, g_wp):
-    @pl.when(pl.program_id(0) == 0)
-    def _():
-        g_wi[...] = jnp.zeros_like(g_wi)
+    seq, devices = lax.axis_index("seq"), lax.axis_size("seq")
+    behind, ahead = lax.rem(seq + devices - 1, devices), lax.rem(seq + 1, devices)
+    width = wi.shape[1]
+    moved = pltpu.make_async_remote_copy(
+        src_ref=edge, dst_ref=after, send_sem=edge_send, recv_sem=edge_land,
+        device_id={"seq": behind}, device_id_type=pl.DeviceIdType.MESH,
+    )
+
+    @pl.when(step == 0)
+    def _():
+        enter([{"head": core_peer()}, {"seq": behind}, {"seq": ahead}])
+        moved.start()
+
+    block_i[...] = d_inner[...]
+    block_p[...] = d_pair[...]
+    block = lax.rem(step + blocks // 2 * (1 - core_bit()), blocks)
+
+    @pl.when(block == blocks - 1)
+    def _():
+        moved.wait_recv()
+        more = jnp.where(seq == devices - 1, 0.0, after[...])
+        fixed = jnp.concatenate([tail[:8], tail[8:] + more], axis=0)
+        fix_i[...] = fixed[:, :width].astype(BF16)
+        fix_p[...] = fixed[:, width:]
+        block_i[BLOCK - 16 :] = fixed[:, :width].astype(BF16)
+        block_p[BLOCK - 16 :] = fixed[:, width:]
+
+    part = dot(d_gate[...], wg[...], 1, 1) + dot(block_i[...], wi[...], 1, 1) + dot(d_step[...], ws[...], 1, 1)
+    high, low = halves(block_p[...])
+    part = part + (dot(high, wp[...], 1, 1) + dot(low, wp[...], 1, 1))
+    add_halves(part, mine, away, land, send_sem, land_sem)
+
+    @pl.when(step == blocks - 1)
+    def _():
+        moved.wait_send()
+
+
+def pair_weight_kernel(low, d_step, d_pair, fix_p, g_ws, g_wp):
+    step = pl.program_id(0)
+
+    @pl.when(step == 0)
+    def _():
         g_ws[...] = jnp.zeros_like(g_ws)
         g_wp[...] = jnp.zeros_like(g_wp)
 
-    g_wi[...] += dot(low[...], d_inner[...], 0, 0)
-    g_ws[...] += dot(low[...], d_step[...], 0, 0)
-    g_wp[...] += dot(low[...], d_pair[...], 0, 0)
-
-
-def norm_back_kernel(idx, mine, other, d_pair, wp, hid, d_out, gain, grad, g_norm):
-    @pl.when(pl.program_id(0) == 0)
-    def _():
-        g_norm[...] = jnp.zeros_like(g_norm)
-
-    d_low = (mine[...].astype(F32) + other[...].astype(F32)) + dot(d_pair[...], wp[...], 1, 1)
+    grads = jnp.where(step == pl.num_programs(0) - 1, fix_p[...], d_pair[BLOCK - 16 :])
+    grads = jnp.concatenate([d_pair[: BLOCK - 16], grads], axis=0)
+    g_ws[...] += dot(d_step[...], low[...], 0, 0)[:8]
+    g_wp[...] += dot_split(low[...], grads, 0, 0)
+
+
+def inner_weight_kernel(low, d_inner, fix_i, g_wi):
+    step = pl.program_id(0)
+
+    @pl.when(step == 0)
+    def _():
+        g_wi[...] = jnp.zeros_like(g_wi)
+
+    grads = jnp.where(step == pl.num_programs(0) - 1, fix_i[...], d_inner[BLOCK - 16 :])
+    grads = jnp.concatenate([d_inner[: BLOCK - 16], grads], axis=0)
+    g_wi[...] += dot(low[...], grads, 0, 0)
+
+
+def norm_back_kernel(
+    mine, other, hid, d_out, gain, error, grad, sums, block, row, land, local, send, arrive, row_send, row_land
+):
+    step = pl.program_id(0)
+    seq, devices = lax.axis_index("seq"), lax.axis_size("seq")
+    head = lax.axis_index("head")
+    group = 2 * devices
+    me = 2 * seq + core_bit()
+
+    def device(distance):
+        to = lax.rem(me + distance, group)
+        return {"seq": to // 2, "head": head - core_bit() + lax.rem(to, 2)}
+
+    def hand(distance):
+        return pltpu.make_async_remote_copy(
+            src_ref=row, dst_ref=land.at[me], send_sem=row_send.at[distance], recv_sem=row_land.at[distance],
+            device_id=device(distance), device_id_type=pl.DeviceIdType.MESH,
+        )
+
+    def each(body):
+        def run(distance, carry):
+            body(distance)
+            return carry
+
+        lax.fori_loop(1, group, run, 0)
+
+    @pl.when(step == 0)
+    def _():
+        barrier = pltpu.get_barrier_semaphore()
+        each(
+            lambda d: pl.semaphore_signal(
+                barrier, inc=1, device_id=device(d), device_id_type=pl.DeviceIdType.MESH
+            )
+        )
+        pl.semaphore_wait(barrier, group - 1)
+        row[:1] = jnp.zeros_like(row[:1])
+        row[1:] = error[...]
+
+    d_low = mine[...].astype(F32) + other[...].astype(F32)
     rows = hid[...].astype(F32)
     scale = lax.rsqrt(jnp.mean(rows * rows, axis=1, keepdims=True) + EPSILON)
-    g_norm[...] += jnp.sum(d_low * rows * scale, axis=0, keepdims=True)
+    row[:1] += jnp.sum(d_low * rows * scale, axis=0, keepdims=True)
     scaled = d_low * gain[...]
     pull = jnp.mean(scaled * rows, axis=1, keepdims=True) * (scale * scale * scale)
-    grad[...] = (d_out[...] + scale * scaled - rows * pull).astype(BF16)
-
-
-def call(kernel, grid, ins, outs, scratch=(), prefetch=0, flops=0, moved=0):
+    block[step] = (d_out[...] + scale * scaled - rows * pull).astype(BF16)
+
+    @pl.when(step == pl.num_programs(0) - 1)
+    def _():
+        each(lambda d: hand(d).start())
+
+    both_cores([block], [grad], [local, send, arrive])
+
+    @pl.when(step == pl.num_programs(0) - 1)
+    def _():
+        land[me] = row[...]
+        each(lambda d: hand(d).wait())
+        sums[...] = lax.fori_loop(1, group, lambda d, total: total + land[d], land[0])
+
+
+def call(kernel, grid, ins, outs, scratch=(), prefetch=0, flops=0, moved=0, collective=None, vmem=14):
     def spec(shape, block, index):
         if block is None:
             return pl.BlockSpec(shape, lambda *_: (0,) * len(shape))
+        if isinstance(block, str):
+            return pl.BlockSpec(memory_space=pltpu.SMEM if block == "smem" else pl.ANY)
         return pl.BlockSpec(block, index)
 
     scalars = [a for a, *_ in ins[:prefetch]]
     arrays = ins[prefetch:]
-    in_specs = [
-        pl.BlockSpec(memory_space=pltpu.SMEM) if block == "smem" else spec(a.shape, block, index)
-        for a, block, index in arrays
-    ]
-    out_specs = [spec(shape, block, index) for shape, _, block, index in outs]
+    extra = {} if collective is None else {"collective_id": collective, "has_side_effects": True}
     return pl.pallas_call(
         kernel,
         grid_spec=pltpu.PrefetchScalarGridSpec(
-            num_scalar_prefetch=prefetch, grid=(grid,), in_specs=in_specs, out_specs=out_specs, scratch_shapes=list(scratch)
+            num_scalar_prefetch=prefetch,
+            grid=(grid,),
+            in_specs=[spec(a.shape, block, index) for a, block, index in arrays],
+            out_specs=[spec(shape, block, index) for shape, _, block, index in outs],
+            scratch_shapes=list(scratch),
         ),
         out_shape=[jax.ShapeDtypeStruct(shape, dtype) for shape, dtype, _, _ in outs],
         compiler_params=pltpu.CompilerParams(
-            dimension_semantics=("arbitrary",), vmem_limit_bytes=48 << 20
+            dimension_semantics=("arbitrary",), vmem_limit_bytes=vmem << 20, **extra
         ),
         cost_estimate=pl.CostEstimate(flops=int(flops), bytes_accessed=int(moved), transcendentals=0),
     )(*scalars, *[a for a, *_ in arrays])
@@ -556,25 +707,197 @@
     return reached[:CHUNK]
 
 
-def sum_rows(value, axis, wire):
-    mine = lax.axis_index(axis)
-    order = bits(axis)
-    for bit in order:
-        half = value.shape[0] // 2
-        upper = ((mine & bit) != 0).astype(jnp.int32)
-        away = lax.dynamic_slice_in_dim(value, (1 - upper) * half, half)
-        value = lax.dynamic_slice_in_dim(value, upper * half, half)
-        value = value + swap(away.astype(wire), axis, bit).astype(F32)
-    value = value.astype(wire)
-    for bit in reversed(order):
-        other = swap(value, axis, bit)
-        upper = (mine & bit) != 0
-        value = jnp.where(upper, jnp.concatenate([other, value]), jnp.concatenate([value, other]))
-    return value.astype(F32)
-
-
-def both_halves(mine, other, core):
-    return jnp.where(core == 0, jnp.concatenate([mine, other]), jnp.concatenate([other, mine]))
+def reduce_kernel(plain, wide, wires, axis, *refs):
+    count = plain + wide
+    take = iter(range(len(refs)))
+
+    def some(number):
+        return [refs[next(take)] for _ in range(number)]
+
+    ins, outs = some(count), some(count)
+    first, land1, second, land2, done = (some(count) for _ in range(5))
+    fold1, half, fold2, quarter = (some(wide) for _ in range(4))
+    sems = some(16)
+    members = first[0].shape[0]
+    me = lax.axis_index(axis)
+    side, place = lax.rem(me, 2), me // 2
+    partner = {axis: me + 1 - 2 * side}
+    head = lax.axis_index("head")
+    core, plane = lax.rem(head, 2), head // 2
+    beside, across = {"head": head + 1 - 2 * core}, {"head": head + 2 - 4 * plane}
+    source = ins[:plain] + quarter
+
+    def copy(src, dst, sem, slot, to):
+        return pltpu.make_async_remote_copy(
+            src_ref=src, dst_ref=dst, send_sem=sems[2 * sem].at[slot], recv_sem=sems[2 * sem + 1].at[slot],
+            device_id=to, device_id_type=pl.DeviceIdType.MESH,
+        )
+
+    def member(d):
+        return lax.rem(place + d, members)
+
+    def to_member(d):
+        return {axis: 2 * member(d) + side}
+
+    def halve(k):
+        return copy(first[k], land1[k], 0, k, partner)
+
+    def scatter(k, d):
+        return copy(second[k].at[member(d)], land2[k].at[d], 1, k * members + d, to_member(d))
+
+    def gather(k, d):
+        return copy(done[k].at[side, place], done[k].at[side, place], 2, k * members + d, to_member(d))
+
+    def gathered(k, d):
+        other = lax.rem(place + members - d, members)
+        return copy(done[k].at[side, other], done[k].at[side, other], 2, k * members + d, partner)
+
+    def widen(k):
+        return copy(done[k].at[side], done[k].at[side], 3, k, partner)
+
+    def widened(k):
+        return copy(done[k].at[1 - side], done[k].at[1 - side], 3, k, partner)
+
+    def fold_core(w):
+        return copy(ins[plain + w].at[1 - core], fold1[w], 4, w, beside)
+
+    def fold_plane(w):
+        return copy(half[w].at[1 - plane], fold2[w], 5, w, across)
+
+    def spread_plane(w, at):
+        ref = outs[plain + w].at[core, at]
+        return copy(ref, ref, 6, w, across)
+
+    def spread_core(w, at):
+        ref = outs[plain + w].at[at]
+        return copy(ref, ref, 7, w, beside)
+
+    def each(body):
+        def step(d, carry):
+            body(d)
+            return carry
+
+        lax.fori_loop(1, members, step, 0)
+
+    def split(k):
+        first[k][...] = source[k][1 - side].astype(wires[k])
+
+    def pass_on(k):
+        halve(k).wait_recv()
+        second[k][...] = (source[k][side] + land1[k][...].astype(F32)).astype(wires[k])
+        each(lambda d: scatter(k, d).start())
+
+    def finish(k):
+        def add(d, total):
+            scatter(k, d).wait_recv()
+            return total + land2[k][d].astype(F32)
+
+        total = lax.fori_loop(1, members, add, source[k][side, place] + land1[k][place].astype(F32))
+        done[k][side, place] = total.astype(wires[k])
+        each(lambda d: gather(k, d).start())
+
+    def collect(k):
+        each(lambda d: gathered(k, d).wait_recv())
+        widen(k).start()
+
+    def store(k, out):
+        out[side] = done[k][side].astype(F32)
+        widened(k).wait_recv()
+        out[1 - side] = done[k][1 - side].astype(F32)
+
+    barrier = pltpu.get_barrier_semaphore()
+
+    def greet(to):
+        pl.semaphore_signal(barrier, inc=1, device_id=to, device_id_type=pl.DeviceIdType.MESH)
+
+    for to in (partner, beside, across):
+        greet(to)
+    each(lambda d: greet(to_member(d)))
+    for k in range(plain):
+        split(k)
+    pl.semaphore_wait(barrier, members + 2)
+    for w in range(wide):
+        fold_core(w).start()
+    halve(0).start()
+    for k in range(plain):
+        if k + 1 < plain:
+            halve(k + 1).start()
+        pass_on(k)
+        if k == 0:
+            for w in range(wide):
+                fold_core(w).wait_recv()
+                half[w][...] = ins[plain + w][core] + fold1[w][...]
+                fold_plane(w).start()
+    for k in range(plain):
+        finish(k)
+    for w in range(wide):
+        fold_plane(w).wait_recv()
+        quarter[w][...] = half[w][plane] + fold2[w][...]
+        split(plain + w)
+        halve(plain + w).start()
+    for k in range(plain):
+        collect(k)
+    for w in range(wide):
+        pass_on(plain + w)
+    for k in range(plain):
+        store(k, outs[k])
+    for w in range(wide):
+        finish(plain + w)
+    for w in range(wide):
+        collect(plain + w)
+    for w in range(wide):
+        store(plain + w, outs[plain + w].at[core, plane])
+        spread_plane(w, plane).start()
+    for w in range(wide):
+        spread_plane(w, 1 - plane).wait_recv()
+        spread_core(w, core).start()
+    for w in range(wide):
+        spread_core(w, 1 - core).wait_recv()
+        fold_core(w).wait_send()
+        fold_plane(w).wait_send()
+        spread_plane(w, plane).wait_send()
+        spread_core(w, core).wait_send()
+    for k in range(count):
+        halve(k).wait_send()
+        widen(k).wait_send()
+
+        def drain(d, k=k):
+            scatter(k, d).wait_send()
+            gather(k, d).wait_send()
+
+        each(drain)
+
+
+def reduce_over(arrays, wires, wide_arrays, axis, collective):
+    size = lax.axis_size(axis)
+    members = size // 2
+    split = [a.reshape(2, members, a.shape[0] // size, a.shape[1]) for a in arrays]
+    split += [a.reshape(2, 2, 2, members, a.shape[0] // (4 * size), a.shape[1]) for a in wide_arrays]
+    plain, wide = len(arrays), len(wide_arrays)
+    wires = list(wires) + [F32] * wide
+    n = plain + wide
+    vmem = pl.BlockSpec(memory_space=pltpu.VMEM)
+    moved = sum(a.size * 4 for a in split)
+    tail = [a.shape[-3:] for a in split]
+    part = [pltpu.VMEM(shape, w) for shape, w in zip(tail, wires)]
+    last = [a.shape for a in split[plain:]]
+    dma = pltpu.SemaphoreType.DMA
+    outs = pl.pallas_call(
+        partial(reduce_kernel, plain, wide, wires, axis),
+        out_shape=[jax.ShapeDtypeStruct(a.shape, F32) for a in split],
+        in_specs=[vmem] * n,
+        out_specs=[vmem] * n,
+        scratch_shapes=part * 4
+        + [pltpu.VMEM((2,) + shape, w) for shape, w in zip(tail, wires)]
+        + [pltpu.VMEM(shape[1:], F32) for shape in last] * 2
+        + [pltpu.VMEM(shape[2:], F32) for shape in last] * 2
+        + [dma((n,))] * 2 + [dma((n * members,))] * 4 + [dma((n,))] * 2 + [dma((wide,))] * 8,
+        compiler_params=pltpu.CompilerParams(
+            collective_id=collective, has_side_effects=True, vmem_limit_bytes=24 << 20
+        ),
+        cost_estimate=pl.CostEstimate(flops=0, bytes_accessed=40 * moved, transcendentals=0),
+    )(*split)
+    return [o.reshape(a.shape) for o, a in zip(outs, list(arrays) + list(wide_arrays))]
 
 
 def padded(row, lanes=LANES):
@@ -624,15 +947,13 @@
     whole = (None, None)
 
     def send_order(w):
-        return (BLOCK, w), lambda i, s: (lax.rem(i + half * (1 - s[0]), blocks), 0)
-
-    def own_order(w):
-        return (BLOCK, w), lambda i, s: (lax.rem(i + half * s[0], blocks), 0)
-
-    own_row = ((1, BLOCK), lambda i, s: (0, lax.rem(i + half * s[0], blocks)))
-    send_row = ((1, BLOCK), lambda i, s: (0, lax.rem(i + half * (1 - s[0]), blocks)))
-    head_half = lambda w: ((BLOCK, w), lambda i, s: (jnp.minimum(i, half - 1), 0))
-    tail_half = lambda w: ((BLOCK, w), lambda i, s: (jnp.maximum(i - half, 0), 0))
+        return (BLOCK, w), lambda i: (lax.rem(i + half * (1 - core_bit()), blocks), 0)
+
+    send_row = ((1, BLOCK), lambda i: (0, lax.rem(i + half * (1 - core_bit()), blocks)))
+    half_own = lambda w: ((BLOCK, w), lambda i: (i + half * core_bit(), 0))
+    tail_half = lambda w: ((BLOCK, w), lambda i: (jnp.maximum(i - half, 0), 0))
+    dma = pltpu.SemaphoreType.DMA
+    swap_scratch = [pltpu.VMEM((half, BLOCK, model), BF16)] * 2 + [dma((half,))] * 2
 
     halo_block = ((edge_rows, model), lambda i, *_: (jnp.maximum(i * (BLOCK // edge_rows) - 1, 0), 0))
     (low, in_i, in_p, pre_i, pre_p, aux, halo_i, halo_p, sloc, pkl, fin) = call(
@@ -678,46 +999,43 @@
         flops=1e9, moved=2e7,
     )
     square = total_over(square, "head")
-    send, stay = call(
+    (mine,) = call(
         partial(branch_kernel, total=inner_total),
         blocks,
         [
-            (idx, None, None), (mixer, *send_order(width)), (gate, *send_order(width)), (square, *send_row),
-            (out_gain, *whole), (w_output, *whole),
-        ],
-        [((rows // 2, model), BF16, *head_half(model)), ((rows // 2, model), F32, *tail_half(model))],
-        prefetch=1, flops=1.2e9, moved=1e7,
-    )
-    mine = (stay + swap(send, "head", 1).astype(F32)).astype(BF16)
+            (mixer, *send_order(width)), (gate, *send_order(width)), (square, *send_row), (out_gain, *whole), (w_output, *whole),
+        ],
+        [((rows // 2, model), BF16, *tail_half(model))],
+        swap_scratch,
+        flops=1.2e9, moved=1e7, collective=2,
+    )
     other = swap(mine, "head", 2)
-    half_own = lambda w: ((BLOCK, w), lambda i, s: (i + half * s[0], 0))
-    output_half, d_branch_half, d_out, error = call(
+    output, d_branch, d_out, error = call(
         loss_kernel,
         half,
         [
-            (idx, None, None), (factor.reshape(1), "smem", None), (hidden, *half_own(model)), (teacher, *half_own(model)),
-            (valid, (1, BLOCK), lambda i, s: (0, i + half * s[0])), (mine, *by(model)), (other, *by(model)),
-        ],
-        [
-            ((rows // 2, model), BF16, *by(model)), ((rows // 2, model), BF16, *by(model)),
+            (factor.reshape(1), "smem", None), (hidden, *half_own(model)), (teacher, *half_own(model)),
+            (valid, (1, BLOCK), lambda i: (0, i + half * core_bit())), (mine, *by(model)), (other, *by(model)),
+        ],
+        [
+            ((rows, model), BF16, "any", None), ((rows, model), BF16, "any", None),
             ((rows // 2, model), F32, *by(model)), ((1, model), F32, *whole),
         ],
-        prefetch=1, flops=1e8, moved=1.5e7,
-    )
-    d_branch_other = swap(d_branch_half, "head", 1)
-    output = both_halves(output_half, swap(output_half, "head", 1), core)
+        [pltpu.VMEM((half, BLOCK, model), BF16)] * 2 + [dma((2 * half,))] * 3,
+        flops=1e8, moved=1.5e7, collective=3,
+    )
     weighted, cross, g_gain, g_wo = call(
         partial(branch_back_kernel, total=inner_total),
         blocks,
         [
-            (idx, None, None), (d_branch_half, *head_half(model)), (d_branch_other, *tail_half(model)),
-            (mixer, *own_order(width)), (gate, *own_order(width)), (square, *own_row), (out_gain, *whole), (w_output, *whole),
-        ],
-        [
-            ((rows, width), F32, *own_order(width)), ((1, rows), F32, *own_row), ((1, width), F32, *whole),
+            (d_branch, *by(model)), (mixer, *by(width)), (gate, *by(width)), (square, *row), (out_gain, *whole),
+            (w_output, *whole),
+        ],
+        [
+            ((rows, width), F32, *by(width)), ((1, rows), F32, *row), ((1, width), F32, *whole),
             ((width, model), F32, *whole),
         ],
-        prefetch=1, flops=2.4e9, moved=1.5e7,
+        flops=2.4e9, moved=1.5e7,
     )
     cross = total_over(cross, "head")
     d_mixer, d_gate, gloc, pkb, fin_back = call(
@@ -745,92 +1063,80 @@
         [((rows, width), F32, *by(width)), ((rows, pair_width), F32, *by(pair_width)), ((model, width), F32, *whole)],
         prefetch=1, flops=6e9, moved=2e7,
     )
-    d_inner, d_step, d_both, edge_i, tail_i, small_i, head_small = call(
+    both = width + pair_width
+    d_inner, d_step, d_pair, edge, tail, small_i, small_p, head_small = call(
         scan_back_kernel,
         blocks,
         [
             (idx, None, None), (d_scaled, *back(width)), (d_maps, *back(pair_width)), (pre_i, *back(width)),
-            (pre_p, *back(pair_width)), (in_i, *back(width)), (halo_i, *whole), (aux, *back(LANES)), (gloc, *back3(CHUNK)),
-            (pkb, *back3(8)), (grad_in, *whole), (states, *back3(CHUNK)), (d_mixer, *back(width)), (mixer, *back(width)),
-            (skip, *whole), (dlog, *whole), (conv_i, *whole),
+            (pre_p, *back(pair_width)), (in_i, *back(width)), (in_p, *back(pair_width)), (halo_i, *whole), (halo_p, *whole),
+            (aux, *back(LANES)), (gloc, *back3(CHUNK)), (pkb, *back3(8)), (grad_in, *whole), (states, *back3(CHUNK)),
+            (d_mixer, *back(width)), (mixer, *back(width)), (skip, *whole), (dlog, *whole), (conv_i, *whole), (conv_p, *whole),
         ],
         [
             ((rows, width), BF16, *back(width)), ((rows, LANES), BF16, *back(LANES)), ((rows, pair_width), F32, *back(pair_width)),
-            ((8, width), F32, *whole), ((16, width), F32, *whole), ((8, width), F32, *whole), ((8, LANES), F32, *whole),
-        ],
-        [pltpu.VMEM((BLOCK + 16, width), F32)] * 3,
-        prefetch=1, flops=3e9, moved=3e7,
-    )
-
-    def finish(grads, tail, edge):
-        after = shifted(edge, "seq", -1)
-        fixed = jnp.concatenate([tail[:8], tail[8:] + after]).astype(BF16)
-        return lax.dynamic_update_slice(grads, fixed, (rows - 16, 0))
-
-    d_inner = finish(d_inner, tail_i, edge_i)
-    half_rows = rows // 2
-    away = lax.dynamic_slice_in_dim(d_both, (1 - core) * half_rows, half_rows)
-    kept = lax.dynamic_slice_in_dim(d_both, core * half_rows, half_rows)
-    kept = kept + swap(away, "head", 1)
-    kept = kept + swap(kept, "head", 2)
-    d_both = both_halves(kept, swap(kept, "head", 1), core)
-    d_pair, edge_p, tail_p, small_p = call(
-        pair_back_kernel,
-        blocks,
-        [
-            (idx, None, None), (d_both, *back(pair_width)), (pre_p, *back(pair_width)), (in_p, *back(pair_width)),
-            (halo_p, *whole), (aux, *back(LANES)), (conv_p, *whole),
-        ],
-        [
-            ((rows, pair_width), BF16, *back(pair_width)), ((8, pair_width), F32, *whole), ((16, pair_width), F32, *whole),
-            ((8, pair_width), F32, *whole),
-        ],
-        [pltpu.VMEM((BLOCK + 16, pair_width), F32)] * 3,
-        prefetch=1, flops=1e8, moved=1e7,
-    )
-    d_pair = finish(d_pair, tail_p, edge_p)
-    send, stay = call(
+            ((8, both), F32, *whole), ((16, both), F32, *whole), ((8, width), F32, *whole), ((8, pair_width), F32, *whole),
+            ((8, LANES), F32, *whole),
+        ],
+        [pltpu.VMEM((BLOCK + 16, width), F32)] * 3 + [pltpu.VMEM((BLOCK + 16, pair_width), F32)] * 3,
+        prefetch=1, flops=3e9, moved=3e7, vmem=16,
+    )
+    mine, fix_i, fix_p = call(
         input_back_kernel,
         blocks,
         [
-            (idx, None, None), (d_gate, *send_order(width)), (d_inner, *send_order(width)), (d_step, *send_order(LANES)),
-            (w_gate, *whole), (w_inner, *whole), (ws, *whole),
-        ],
-        [((rows // 2, model), BF16, *head_half(model)), ((rows // 2, model), F32, *tail_half(model))],
-        prefetch=1, flops=2.6e9, moved=1e7,
-    )
-    mine = (stay + swap(send, "head", 1).astype(F32)).astype(BF16)
+            (d_gate, *send_order(width)), (d_inner, *send_order(width)), (d_step, *send_order(LANES)),
+            (d_pair, *send_order(pair_width)), (w_gate, *whole), (w_inner, *whole), (ws, *whole), (w_pair, *whole),
+            (edge, *whole), (tail, *whole),
+        ],
+        [
+            ((rows // 2, model), BF16, *tail_half(model)), ((16, width), BF16, *whole), ((16, pair_width), F32, *whole),
+        ],
+        [pltpu.VMEM((BLOCK, width), BF16), pltpu.VMEM((BLOCK, pair_width), F32), pltpu.VMEM((8, both), F32)]
+        + swap_scratch + [dma] * 2,
+        flops=2.6e9, moved=1e7, collective=4,
+    )
     other = swap(mine, "head", 2)
-    g_wi, g_ws, g_wp = call(
-        weight_back_kernel,
+    g_ws, g_wp = call(
+        pair_weight_kernel,
         blocks,
-        [(low, *by(model)), (d_inner, *by(width)), (d_step, *by(LANES)), (d_pair, *by(pair_width))],
-        [((model, width), F32, *whole), ((model, LANES), F32, *whole), ((model, pair_width), F32, *whole)],
-        flops=2.4e9, moved=1e7,
-    )
-    grad_half, g_norm = call(
+        [(low, *by(model)), (d_step, *by(LANES)), (d_pair, *by(pair_width)), (fix_p, *whole)],
+        [((8, model), F32, *whole), ((model, pair_width), F32, *whole)],
+        flops=1.6e9, moved=1e7,
+    )
+    (g_wi,) = call(
+        inner_weight_kernel,
+        blocks,
+        [(low, *by(model)), (d_inner, *by(width)), (fix_i, *whole)],
+        [((model, width), F32, *whole)],
+        flops=1.2e9, moved=1e7,
+    )
+    pack = jnp.concatenate([
+        small_i[:6], g_gain, jnp.zeros((1, width), F32), g_ws[:, :width], g_ws[:, width:],
+        jnp.pad(head_small, ((0, 32), (0, width - LANES))),
+    ])
+    quarters = 4 * lax.axis_size("seq")
+    small_p = jnp.pad(small_p, ((0, quarters - 8), (0, 0)))
+    g_wo, g_wg, g_wi, pack, g_wp, small_p = reduce_over(
+        [g_wo, g_wg, g_wi, pack], [BF16, BF16, BF16, F32], [g_wp, small_p], "seq", 1
+    )
+    grad_hidden, sums = call(
         norm_back_kernel,
         half,
         [
-            (idx, None, None), (mine, *by(model)), (other, *by(model)), (d_pair, *half_own(pair_width)), (w_pair, *whole),
-            (hidden, *half_own(model)), (d_out, *by(model)), (gain, *whole),
-        ],
-        [((rows // 2, model), BF16, *by(model)), ((1, model), F32, *whole)],
-        prefetch=1, flops=5e8, moved=1e7,
-    )
-    grad_hidden = both_halves(grad_half, swap(grad_half, "head", 1), core)
-
-    g_wo = sum_rows(g_wo, "seq", BF16)
-    g_wg = sum_rows(g_wg, "seq", BF16)
-    g_wi = sum_rows(g_wi, "seq", BF16)
-    g_wp = sum_rows(g_wp, "seq", F32)
-    lane_small = jnp.concatenate([small_i[:6], g_gain, jnp.zeros((1, width), F32)])
-    by_head = total_over(lane_small, "seq")
-    head_small = total_over(head_small, "seq")
-    g_ws = sum_rows(g_ws[:, :heads], "seq", F32)
-    pair_small = total_over(small_p, "seq")
-    sums = jnp.concatenate([g_norm, error, jnp.zeros((6, model), F32)])
-    sums = total_over(sums + swap(sums, "head", 1), "seq")
+            (mine, *by(model)), (other, *by(model)), (hidden, *half_own(model)), (d_out, *by(model)), (gain, *whole),
+            (error, *whole),
+        ],
+        [((rows, model), BF16, "any", None), ((2, model), F32, *whole)],
+        [
+            pltpu.VMEM((half, BLOCK, model), BF16), pltpu.VMEM((2, model), F32),
+            pltpu.VMEM((2 * lax.axis_size("seq"), 2, model), F32),
+        ]
+        + [dma((half,))] * 3 + [dma((2 * lax.axis_size("seq"),))] * 2,
+        flops=5e8, moved=1e7, collective=5,
+    )
+    by_head, g_ws = pack[:8], jnp.concatenate([pack[8:16], pack[16:24]], axis=1)[:heads].T
+    pair_small, head_small = small_p[:8], pack[24:32, :LANES]
     loss = jnp.sum(sums[1]) / (count * model)
     return (
         output, loss, grad_hidden, sums[0], g_wg, g_wi, g_wp, g_ws, by_head[:4], by_head[4], pair_small[:4], pair_small[4],

time: 428 us -> 354 us (0.83)
  waiting for transfers between devices: 133 us -> 61.9 us
  Pallas kernels: 145 us -> 203 us
  starting transfers between devices: 79.9 us -> 22.7 us
  other arithmetic: 39.9 us -> 11.1 us
  local copies, waits for them, and re-layouts: 22.6 us -> 49.5 us
    pallas_call x0 -> x1, Pallas kernels: none -> 76.4 us  [reduce_over(): pl.pallas_call(partial(reduce_kernel, plain, wide, wires, axis), out_shap...]
    ppermute x66 -> x15, waiting for transfers between devices: 133 us -> 61.9 us  [swap(): return jax.tree.map(lambda v: lax.ppermute(v, axis, route), value)]
    ppermute x66 -> x15, starting transfers between devices: 72.5 us -> 17.8 us  [swap(): return jax.tree.map(lambda v: lax.ppermute(v, axis, route), value)]
    unnamed x53 -> x129, local copies, waits for them, and re-layouts: 8.97 us -> 42.1 us
    pallas_call x13, Pallas kernels: 145 us -> 127 us  [call(): pl.pallas_call(kernel, grid_spec=pltpu.PrefetchScalarGridSpec(num_scalar_...]
    select_n x15 -> x0, other arithmetic: 13.1 us -> none  [the longest x3 10.3 us: both_halves(): jnp.where(core == 0, jnp.concatenate([mine, other]), jnp.concatenate([oth...]
    convert_element_type x8 -> x0, other arithmetic: 7.87 us -> none  [the longest x3 4.61 us: sum_rows(): return value.astype(F32)]
    add x15 -> x0, other arithmetic: 4.93 us -> none  [the longest x12 2.96 us: sum_rows(): value = value + swap(away.astype(wire), axis, bit).astype(F32)]
  transfers between devices with their start and end apart: 69 -> 16, of which waited for: 36 -> 12; matrix products, arithmetic and copies ran while one was open for 12% -> 5% of each run, Pallas kernels for 23% -> 28%
where the time goes in v2:
time: 354 us; the launch traced here: 353 us
  Pallas kernels  203 us (57%)
  waiting for transfers between devices  61.9 us (17%)
  local copies, waits for them, and re-layouts  49.5 us (14%)
  starting transfers between devices  22.7 us (6%)
  other arithmetic  11.1 us (3%)
  between operations  4.55 us (1%)
    pallas_call x13, Pallas kernels, call(): pl.pallas_call(kernel, grid_spec=pltpu.PrefetchScalarGridSpec(num_scalar_...  127 us
    pallas_call x1, Pallas kernels, reduce_over(): pl.pallas_call(partial(reduce_kernel, plain, wide, wires, axis), out_shap...  76.4 us
    ppermute x15, waiting for transfers between devices, swap(): return jax.tree.map(lambda v: lax.ppermute(v, axis, route), value)  61.9 us
    unnamed x129, local copies, waits for them, and re-layouts  42.1 us
    ppermute x15, starting transfers between devices, swap(): return jax.tree.map(lambda v: lax.ppermute(v, axis, route), value)  17.8 us
  transfers between devices with their start and end apart: 16, of which 12 were waited for; matrix products, arithmetic and copies ran while one was open for 5% of the time, Pallas kernels for 28%

profile of v2, /device:TPU:0, one launch (start us, length us, event | category | flops | bytes accessed | tf_op | source)
XLA Modules:
  0.0 353.2 jit_solution(2667503115412399587)
XLA Ops:
  1.4 4.9 %collective-permute-start.3 = (bf16[16,768]{1,0:T(8,128)(2,1)S(1)}, bf16[16,768]{1,0:T(8,128)(2,1)S(1)}, u32[]{:S(2)}, u32[]{:S(2)}) collective-permute-start(bf16[16,768]{1,0:T(8,128)(2,1)S(1)} %slice.282), channel_id=1, source_target_pairs={{0,4},{4,8},{8,12},{12,16},{16,20},{20,24},{24,28},{1,5},{5,9},{9,... | collective-permute-start | bytes 73736 | tf_op jit(solution)/shard_map/ppermute | solution.py:680
  20.1 20.5 %shard_map.305 = (bf16[2048,768]{1,0:T(8,128)(2,1)S(1)}, bf16[2048,384]{1,0:T(8,128)(2,1)S(1)}, bf16[2048,256]{1,0:T(8,128)(2,1)S(1)}, f32[2048,384]{1,0:T(8,128...) custom-call(s32[2]{0:T(128)S(1)} %pad_add_fusion.idx, ...), custom_call_target="tpu_custom_call" | custom-call | flops 3000000000 | bytes 20000000 | tf_op jit(solution)/shard_map/pallas_call | solution.py:655
  44.3 7.2 %shard_map.306 = (f32[2048,384]{1,0:T(8,128)S(1)}, f32[2048,384]{1,0:T(8,128)S(1)}) custom-call(s32[2]{0:T(128)S(1)} %pad_add_fusion.idx, bf16[2048,768]{1,0:T(8,128)(2,1)S(1)} %get-tuple-element.123.low, bf16[768,384]{1,0:T(8,128)(2,1)S(1)} %copy-done.52, f32[2048,384]{1,0:T(8,128)S(1)} %get-tuple-element.124.pre_i, ...), custom_call_target="tpu_custom_call" | custom-call | flops 4000000000 | bytes 20000000 | tf_op jit(solution)/shard_map/pallas_call | solution.py:655
  53.3 4.7 %collective-permute-done.5 = f32[136,384]{1,0:T(8,128)S(1)} collective-permute-done((f32[136,384]{1,0:T(8,128)S(1)}, f32[136,384]{1,0:T(8,128)S(1)}, u32[]{:S(2)}, u32[]{:S(2)}) %collective-permute-start.5) | collective-permute-done | bytes 208928 | tf_op jit(solution)/shard_map/ppermute | solution.py:674
  60.9 8.1 %collective-permute-done.6 = f32[136,384]{1,0:T(8,128)S(1)} collective-permute-done((f32[136,384]{1,0:T(8,128)S(1)}, f32[136,384]{1,0:T(8,128)S(1)}, u32[]{:S(2)}, u32[]{:S(2)}) %collective-permute-start.6) | collective-permute-done | bytes 208928 | tf_op jit(solution)/shard_map/ppermute | solution.py:674
  69.1 5.4 %shard_map.307 = (f32[2048,384]{1,0:T(8,128)S(1)}, f32[16,128,384]{2,1,0:T(8,128)S(1)}, f32[1,2048]{1,0:T(1,128)S(1)}) custom-call(f32[2048,256]{1,0:T(8,128)S(1)} %get-tuple-element.118.pre_p.pre_c, f32[2048,128]{1,0:T(8,128)S(1)} %get-tuple-element.119.aux, f32[16,128,384]{2,1,0:T(8,128)S(1)} %get-tuple-element.120.sloc, ...), custom_call_target="tpu_custom_call" | custom-call | flops 1000000000 | bytes 20000000 | tf_op jit(solution)/shard_map/pallas_call | solution.py:655
  81.2 5.4 %shard_map.308.mine = bf16[1024,768]{1,0:T(8,128)(2,1)S(1)} custom-call(f32[2048,384]{1,0:T(8,128)S(1)} %get-tuple-element.127.mixer, f32[2048,384]{1,0:T(8,128)S(1)} %get-tuple-element.126.gate, f32[1,2048]{1,0:T(1,128)S(1)} %add.87.square, f32[1,384]{1,0:T(1,128)S(1)} %broadcast_in_dim.38.gain, bf16[384,768]{1,0:T(8,128)(2,1)S(1)} %copy-done.26), custom_call_target="tpu_custom_call" | custom-call | flops 1200000000 | bytes 10000000 | tf_op jit(solution)/shard_map/pallas_call | solution.py:655
  90.0 3.1 collective-permute-done
  93.8 3.6 %collective-permute-done.1 = f32[8,128]{1,0:T(8,128)S(1)} collective-permute-done((f32[8,128]{1,0:T(8,128)S(1)}, f32[8,128]{1,0:T(8,128)S(1)}, u32[]{:S(2)}, u32[]{:S(2)}) %collective-permute-start.1) | collective-permute-done | bytes 4128 | tf_op jit(solution)/shard_map/ppermute | solution.py:674
  99.4 3.3 collective-permute-done.2
  103.8 19.6 %collective-permute-done.9.other = bf16[1024,768]{1,0:T(8,128)(2,1)S(1)} collective-permute-done((bf16[1024,768]{1,0:T(8,128)(2,1)S(1)}, bf16[1024,768]{1,0:T(8,128)(2,1)S(1)}, u32[]{:S(2)}, u32[]{:S(2)}) %collective-permute-start.9) | collective-permute-done | bytes 1572896 | tf_op jit(solution)/shard_map/ppermute | solution.py:674
  123.5 6.5 %shard_map.309 = (bf16[2048,768]{1,0:T(8,128)(2,1)S(1)}, bf16[2048,768]{1,0:T(8,128)(2,1)S(1)}, f32[1024,768]{1,0:T(8,128)S(1)}, f32[1,768]{1,0:T(1,128)S(1)}) custom-call(f32[1]{0:T(128)} %bitcast.factor, bf16[2048,768]{1,0:T(8,128)(2,1)S(1)} %copy-done.6, bf16[2048,768]{1,0:T(8,128)(2,1)S(1)} %copy-done.21, s32[1,2048]{1,0:T(1,128)S(1)} %bitcast.39, ...), custom_call_target="tpu_custom_call" | custom-call | flops 100000000 | bytes 15000000 | tf_op jit(solution)/shard_map/pallas_call | solution.py:655
  131.7 8.9 %shard_map.310 = (f32[2048,384]{1,0:T(8,128)S(1)}, f32[1,2048]{1,0:T(1,128)S(1)}, f32[1,384]{1,0:T(1,128)S(1)}, f32[384,768]{1,0:T(8,128)S(1)}) custom-call(bf16[2048,768]{1,0:T(8,128)(2,1)S(1)} %get-tuple-element.130.d_branch, f32[2048,384]{1,0:T(8,128)S(1)} %get-tuple-element.127.mixer, f32[2048,384]{1,0:T(8,128)S(1)} %get-tuple-element.126.gate, ...), custom_call_target="tpu_custom_call" | custom-call | flops 2400000000 | bytes 15000000 | tf_op jit(solution)/shard_map/pallas_call | solution.py:655
  154.8 7.3 %shard_map.311 = (f32[2048,384]{1,0:T(8,128)S(1)}, bf16[2048,384]{1,0:T(8,128)(2,1)S(1)}, f32[16,128,384]{2,1,0:T(8,128)S(1)}, f32[16,8,384]{2,1,0:T(8,128)S(1)}, f32[136,384]{1,0:T(8,128)S(1)}) custom-call(f32[2048,384]{1,0:T(8,128)S(1)} %copy-done.25, f32[2048,384]{1,0:T(8,128)S(1)} %get-tuple-element.127.mixer, f32[2048,384]{1,0:T(8,128)S(1)} %copy-done.1, ...), custom_call_target="tpu_custom_call" | custom-call | flops 1000000000 | bytes 20000000 | tf_op jit(solution)/shard_map/pallas_call | solution.py:655
  162.7 9.5 %shard_map.312 = (f32[2048,384]{1,0:T(8,128)S(1)}, f32[2048,256]{1,0:T(8,128)S(1)}, f32[768,384]{1,0:T(8,128)S(1)}) custom-call(s32[2]{0:T(128)S(1)} %pad_add_fusion.idx, f32[2048,384]{1,0:T(8,128)S(1)} %get-tuple-element.134.d_mixer, f32[2048,384]{1,0:T(8,128)S(1)} %copy-done.12, f32[2048,256]{1,0:T(8,128)S(1)} %copy-done.4, f32[2048,128]{1,0:T(8,128)S(1)} %copy-done.10, ...), custom_call_target="tpu_custom_call" | custom-call | flops 6000000000 | bytes 20000000 | tf_op jit(solution)/shard_map/pallas_call | solution.py:655
  173.2 5.1 %collective-permute-done.13 = f32[136,384]{1,0:T(8,128)S(1)} collective-permute-done((f32[136,384]{1,0:T(8,128)S(1)}, f32[136,384]{1,0:T(8,128)S(1)}, u32[]{:S(2)}, u32[]{:S(2)}) %collective-permute-start.13) | collective-permute-done | bytes 208928 | tf_op jit(solution)/shard_map/ppermute | solution.py:674
  180.8 7.8 %collective-permute-done.14 = f32[136,384]{1,0:T(8,128)S(1)} collective-permute-done((f32[136,384]{1,0:T(8,128)S(1)}, f32[136,384]{1,0:T(8,128)S(1)}, u32[]{:S(2)}, u32[]{:S(2)}) %collective-permute-start.14) | collective-permute-done | bytes 208928 | tf_op jit(solution)/shard_map/ppermute | solution.py:674
  188.8 24.4 %shard_map.313 = (bf16[2048,384]{1,0:T(8,128)(2,1)S(1)}, bf16[2048,128]{1,0:T(8,128)(2,1)S(1)}, f32[2048,256]{1,0:T(8,128)S(1)}, f32[8,640]{1,0:T(8,128)S(1)}, f...) custom-call(s32[2]{0:T(128)S(1)} %pad_add_fusion.idx, ...), custom_call_target="tpu_custom_call" | custom-call | flops 3000000000 | bytes 30000000 | tf_op jit(solution)/shard_map/pallas_call | solution.py:655
  213.3 12.7 %shard_map.314 = (bf16[1024,768]{1,0:T(8,128)(2,1)}, bf16[16,384]{1,0:T(8,128)(2,1)S(1)}, f32[16,256]{1,0:T(8,128)S(1)}) custom-call(bf16[2048,384]{1,0:T(8,128)(2,1)S(1)} %get-tuple-element.133.d_gate, bf16[2048,384]{1,0:T(8,128)(2,1)S(1)} %get-tuple-element.145.d_inner, bf16[2048,128]{1,0:T(8,128)(2,1)S(1)} %get-tuple-element.146.d_step, ...), custom_call_target="tpu_custom_call" | custom-call | flops 2600000000 | bytes 10000000 | tf_op jit(solution)/shard_map/pallas_call | solution.py:655
  230.9 3.8 %shard_map.317 = (f32[8,768]{1,0:T(8,128)S(1)}, f32[768,256]{1,0:T(8,128)S(1)}) custom-call(bf16[2048,768]{1,0:T(8,128)(2,1)S(1)} %copy-done.17, bf16[2048,128]{1,0:T(8,128)(2,1)S(1)} %copy-done.55, f32[2048,256]{1,0:T(8,128)S(1)} %copy-done.49, f32[16,256]{1,0:T(8,128)S(1)} %get-tuple-element.160.fix_p), custom_call_target="tpu_custom_call" | custom-call | flops 1600000000 | bytes 10000000 | tf_op jit(solution)/shard_map/pallas_call | solution.py:655
  237.0 3.3 shard_map.316
  240.3 76.4 %shard_map.318 = (f32[2,4,48,768]{3,2,1,0:T(8,128)S(1)}, f32[2,4,96,384]{3,2,1,0:T(8,128)S(1)}, f32[2,4,96,384]{3,2,1,0:T(8,128)S(1)}, f32[2,4,8,384]{3,2,1,0:T(...) custom-call(f32[2,4,48,768]{3,2,1,0:T(8,128)S(1)} %bitcast.34, ...), custom_call_target="tpu_custom_call" | custom-call | bytes 178257920 | tf_op jit(solution)/shard_map/pallas_call | solution.py:885
  326.8 12.4 %shard_map.315 = (bf16[2048,768]{1,0:T(8,128)(2,1)S(1)}, f32[2,768]{1,0:T(2,128)S(1)}) custom-call(bf16[1024,768]{1,0:T(8,128)(2,1)} %get-tuple-element.150.mine, bf16[1024,768]{1,0:T(8,128)(2,1)} %collective-permute-done.15.other, bf16[2048,768]{1,0:T(8,128)(2,1)S(1)} %copy-done.7, f32[1024,768]{1,0:T(8,128)S(1)} %copy-done.23, ...), custom_call_target="tpu_custom_call" | custom-call | flops 500000000 | bytes 10000000 | tf_op jit(solution)/shard_map/pallas_call | solution.py:655
  342.1 3.9 %copy.43 = bf16[2048,768]{1,0:T(8,128)(2,1)} copy(bf16[2048,768]{1,0:T(8,128)(2,1)} %copy-done.18) | data formatting | bytes 6291456
  (232 shorter events, 81.0 us)
Async XLA Ops:
  1.4 14.7 %collective-permute-start.3 = (bf16[16,768]{1,0:T(8,128)(2,1)S(1)}, bf16[16,768]{1,0:T(8,128)(2,1)S(1)}, u32[]{:S(2)}, u32[]{:S(2)}) collective-permute-start(bf16[16,768]{1,0:T(8,128)(2,1)S(1)} %slice.282), channel_id=1, source_target_pairs={{0,4},{4,8},{8,12},{12,16},{16,20},{20,24},{24,28},{1,5},{5,9},{9,... | collective-permute-start | bytes 73736 | tf_op jit(solution)/shard_map/ppermute | solution.py:680
  42.7 26.4 %copy-start.2 = (f32[2048,256]{1,0:T(8,128)}, f32[2048,256]{1,0:T(8,128)S(1)}, u32[]{:S(2)}) copy-start(f32[2048,256]{1,0:T(8,128)S(1)} %get-tuple-element.118.pre_p.pre_c) | copy-start | bytes 6291460
  42.7 26.4 %copy-start.8 = (f32[2048,128]{1,0:T(8,128)}, f32[2048,128]{1,0:T(8,128)S(1)}, u32[]{:S(2)}) copy-start(f32[2048,128]{1,0:T(8,128)S(1)} %get-tuple-element.119.aux) | copy-start | bytes 3145732
  42.7 8.8 %collective-permute-start.4 = (f32[136,384]{1,0:T(8,128)S(1)}, f32[136,384]{1,0:T(8,128)S(1)}, u32[]{:S(2)}, u32[]{:S(2)}) collective-permute-start(f32[136,384]{1,0:T(8,128)S(1)} %get-tuple-element.122), channel_id=1, source_target_pairs={{0,4},{4,0},{8,12},{12,8},{16,20},{20,16},{24,28},{28,24},{1,5},{5... | collective-permute-start | bytes 626696 | tf_op jit(solution)/shard_map/ppermute | solution.py:674
  51.5 80.2 %copy-start = (f32[2048,384]{1,0:T(8,128)}, f32[2048,384]{1,0:T(8,128)S(1)}, u32[]{:S(2)}) copy-start(f32[2048,384]{1,0:T(8,128)S(1)} %get-tuple-element.126.gate) | copy-start | bytes 9437188
  51.6 6.4 %collective-permute-start.5 = (f32[136,384]{1,0:T(8,128)S(1)}, f32[136,384]{1,0:T(8,128)S(1)}, u32[]{:S(2)}, u32[]{:S(2)}) collective-permute-start(f32[136,384]{1,0:T(8,128)S(1)} %fusion.3), channel_id=1, source_target_pairs={{0,8},{4,12},{8,0},{12,4},{16,24},{20,28},{24,16},{28,20},{1,9},{5... | collective-permute-start | bytes 626696 | tf_op jit(solution)/shard_map/ppermute | solution.py:674
  58.2 10.9 %collective-permute-start.6 = (f32[136,384]{1,0:T(8,128)S(1)}, f32[136,384]{1,0:T(8,128)S(1)}, u32[]{:S(2)}, u32[]{:S(2)}) collective-permute-start(f32[136,384]{1,0:T(8,128)S(1)} %fusion.2), channel_id=1, source_target_pairs={{0,16},{4,20},{8,24},{12,28},{16,0},{20,4},{24,8},{28,12},{1,17},{... | collective-permute-start | bytes 626696 | tf_op jit(solution)/shard_map/ppermute | solution.py:674
  76.2 1.2 collective-permute-start.7
  77.4 3.7 %collective-permute-start.8 = (f32[1,2048]{1,0:T(1,128)S(1)}, f32[1,2048]{1,0:T(1,128)S(1)}, u32[]{:S(2)}, u32[]{:S(2)}) collective-permute-start(f32[1,2048]{1,0:T(1,128)S(1)} %add.86), channel_id=1, source_target_pairs={{0,2},{1,3},{2,0},{3,1},{4,6},{5,7},{6,4},{7,5},{8,10},{9,11},{10,... | collective-permute-start | bytes 24584 | tf_op jit(solution)/shard_map/ppermute | solution.py:674
  81.2 42.3 %copy-start.6 = (bf16[2048,768]{1,0:T(8,128)(2,1)S(1)}, bf16[2048,768]{1,0:T(8,128)(2,1)}, u32[]{:S(2)}) copy-start(bf16[2048,768]{1,0:T(8,128)(2,1)} %hid.5) | copy-start | bytes 9437188
  81.2 42.3 %copy-start.21 = (bf16[2048,768]{1,0:T(8,128)(2,1)S(1)}, bf16[2048,768]{1,0:T(8,128)(2,1)}, u32[]{:S(2)}) copy-start(bf16[2048,768]{1,0:T(8,128)(2,1)} %teacher.1) | copy-start | bytes 9437188
  86.6 36.9 %collective-permute-start.9 = (bf16[1024,768]{1,0:T(8,128)(2,1)S(1)}, bf16[1024,768]{1,0:T(8,128)(2,1)S(1)}, u32[]{:S(2)}, u32[]{:S(2)}) collective-permute-start(bf16[1024,768]{1,0:T(8,128)(2,1)S(1)} %shard_map.308.mine), channel_id=1, source_target_pairs={{0,2},{1,3},{2,0},{3,1},{4,6},{5,7},{6,4},{7,5},{8,10},{9,11},{10,... | collective-permute-start | bytes 4718600 | tf_op jit(solution)/shard_map/ppermute | solution.py:674
  89.4 3.7 %collective-permute-start = (f32[8,128]{1,0:T(8,128)S(1)}, f32[8,128]{1,0:T(8,128)S(1)}, u32[]{:S(2)}, u32[]{:S(2)}) collective-permute-start(f32[8,128]{1,0:T(8,128)S(1)} %broadcast_in_dim.30), channel_id=1, source_target_pairs={{0,4},{4,0},{8,12},{12,8},{16,20},{20,16},{24,28},{28,24},{1,5},{5... | collective-permute-start | bytes 12296 | tf_op jit(solution)/shard_map/ppermute | solution.py:674
  93.7 3.7 %collective-permute-start.1 = (f32[8,128]{1,0:T(8,128)S(1)}, f32[8,128]{1,0:T(8,128)S(1)}, u32[]{:S(2)}, u32[]{:S(2)}) collective-permute-start(f32[8,128]{1,0:T(8,128)S(1)} %broadcast_add_fusion), channel_id=1, source_target_pairs={{0,8},{4,12},{8,0},{12,4},{16,24},{20,28},{24,16},{28,20},{1,9},{5... | collective-permute-start | bytes 12296 | tf_op jit(solution)/shard_map/ppermute | solution.py:674
  98.1 4.6 %collective-permute-start.2 = (f32[8,128]{1,0:T(8,128)S(1)}, f32[8,128]{1,0:T(8,128)S(1)}, u32[]{:S(2)}, u32[]{:S(2)}) collective-permute-start(f32[8,128]{1,0:T(8,128)S(1)} %fusion.14), channel_id=1, source_target_pairs={{0,16},{4,20},{8,24},{12,28},{16,0},{20,4},{24,8},{28,12},{1,17},{... | collective-permute-start | bytes 12296 | tf_op jit(solution)/shard_map/ppermute | solution.py:674
  143.2 1.2 collective-permute-start.10
  144.4 3.7 %collective-permute-start.11 = (f32[1,2048]{1,0:T(1,128)S(1)}, f32[1,2048]{1,0:T(1,128)S(1)}, u32[]{:S(2)}, u32[]{:S(2)}) collective-permute-start(f32[1,2048]{1,0:T(1,128)S(1)} %add.88), channel_id=1, source_target_pairs={{0,2},{1,3},{2,0},{3,1},{4,6},{5,7},{6,4},{7,5},{8,10},{9,11},{10,... | collective-permute-start | bytes 24584 | tf_op jit(solution)/shard_map/ppermute | solution.py:674
  162.1 10.2 %collective-permute-start.12 = (f32[136,384]{1,0:T(8,128)S(1)}, f32[136,384]{1,0:T(8,128)S(1)}, u32[]{:S(2)}, u32[]{:S(2)}) collective-permute-start(f32[136,384]{1,0:T(8,128)S(1)} %get-tuple-element.143), channel_id=1, source_target_pairs={{0,4},{4,0},{8,12},{12,8},{16,20},{20,16},{24,28},{28,24},{1,5},{5... | collective-permute-start | bytes 626696 | tf_op jit(solution)/shard_map/ppermute | solution.py:674
  172.4 5.9 %collective-permute-start.13 = (f32[136,384]{1,0:T(8,128)S(1)}, f32[136,384]{1,0:T(8,128)S(1)}, u32[]{:S(2)}, u32[]{:S(2)}) collective-permute-start(f32[136,384]{1,0:T(8,128)S(1)} %fusion.1), channel_id=1, source_target_pairs={{0,8},{4,12},{8,0},{12,4},{16,24},{20,28},{24,16},{28,20},{1,9},{5... | collective-permute-start | bytes 626696 | tf_op jit(solution)/shard_map/ppermute | solution.py:674
  178.4 10.2 %collective-permute-start.14 = (f32[136,384]{1,0:T(8,128)S(1)}, f32[136,384]{1,0:T(8,128)S(1)}, u32[]{:S(2)}, u32[]{:S(2)}) collective-permute-start(f32[136,384]{1,0:T(8,128)S(1)} %fusion), channel_id=1, source_target_pairs={{0,16},{4,20},{8,24},{12,28},{16,0},{20,4},{24,8},{28,12},{1,17},{... | collective-permute-start | bytes 626696 | tf_op jit(solution)/shard_map/ppermute | solution.py:674
  188.8 24.5 %copy-start.51 = (bf16[768,384]{1,0:T(8,128)(2,1)S(1)}, bf16[768,384]{1,0:T(8,128)(2,1)}, u32[]{:S(2)}) copy-start(bf16[768,384]{1,0:T(8,128)(2,1)} %wi.3) | copy-start | bytes 1769476
  188.8 24.5 %copy-start.53 = (bf16[768,384]{1,0:T(8,128)(2,1)S(1)}, bf16[768,384]{1,0:T(8,128)(2,1)}, u32[]{:S(2)}) copy-start(bf16[768,384]{1,0:T(8,128)(2,1)} %wg.3) | copy-start | bytes 1769476
  226.0 98.9 %collective-permute-start.15 = (bf16[1024,768]{1,0:T(8,128)(2,1)}, bf16[1024,768]{1,0:T(8,128)(2,1)}, u32[]{:S(2)}, u32[]{:S(2)}) collective-permute-start(bf16[1024,768]{1,0:T(8,128)(2,1)} %get-tuple-element.150.mine), channel_id=1, source_target_pairs={{0,2},{1,3},{2,0},{3,1},{4,6},{5,7},{6,4},{7,5},{8,10},{9,11},{10,... | collective-permute-start | bytes 4718600 | tf_op jit(solution)/shard_map/ppermute | solution.py:674
  240.3 84.7 %copy-start.7 = (bf16[2048,768]{1,0:T(8,128)(2,1)S(1)}, bf16[2048,768]{1,0:T(8,128)(2,1)}, u32[]{:S(2)}) copy-start(bf16[2048,768]{1,0:T(8,128)(2,1)} %hid.5) | copy-start | bytes 9437188
  (53 other events, 329.7 us)

commit v3 on v2

--- a/solution.py
+++ b/solution.py
@@ -513,132 +513,370 @@
     return dot(a, high, da, db) + dot(a, low, da, db)
 
 
-def input_back_kernel(
-    d_gate, d_inner, d_step, d_pair, wg, wi, ws, wp, edge, tail, mine, fix_i, fix_p,
-    block_i, block_p, after, away, land, send_sem, land_sem, edge_send, edge_land,
+def device_copy(src, dst, sems, slot, to):
+    return pltpu.make_async_remote_copy(
+        src_ref=src, dst_ref=dst, send_sem=sems[0].at[slot], recv_sem=sems[1].at[slot],
+        device_id=to, device_id_type=pl.DeviceIdType.MESH,
+    )
+
+
+def loop(start, stop, body):
+    def run(d, carry):
+        body(d)
+        return carry
+
+    lax.fori_loop(start, stop, run, 0)
+
+
+def rows_at(ref, index, size):
+    return ref.at[pl.ds(pl.multiple_of(index * size, size), size)]
+
+
+class SeqSum:
+    def __init__(self, source, first, land1, second, land2, done, sems):
+        self.source, self.first, self.land1, self.second, self.land2, self.done = source, first, land1, second, land2, done
+        self.sems = [sems[i : i + 2] for i in range(0, 8, 2)]
+        self.wire = first.dtype
+        self.members = land2.shape[0]
+        self.piece = first.shape[0] // self.members
+        me = lax.axis_index("seq")
+        self.side, self.place = lax.rem(me, 2), me // 2
+        self.partner = {"seq": me + 1 - 2 * self.side}
+
+    def half(self, ref, side):
+        return rows_at(ref, side, self.members * self.piece)
+
+    def member(self, d):
+        return lax.rem(self.place + d, self.members)
+
+    def to_member(self, d):
+        return {"seq": 2 * self.member(d) + self.side}
+
+    def halve(self):
+        return device_copy(self.first, self.land1, self.sems[0], 0, self.partner)
+
+    def scatter(self, d):
+        src = rows_at(self.second, self.member(d), self.piece)
+        return device_copy(src, self.land2.at[d], self.sems[1], d, self.to_member(d))
+
+    def part(self, place):
+        return rows_at(self.done, self.side * self.members + place, self.piece)
+
+    def gather(self, d):
+        ref = self.part(self.place)
+        return device_copy(ref, ref, self.sems[2], d, self.to_member(d))
+
+    def gathered(self, d):
+        ref = self.part(lax.rem(self.place + self.members - d, self.members))
+        return device_copy(ref, ref, self.sems[2], d, self.partner)
+
+    def widen(self, side):
+        ref = self.half(self.done, side)
+        return device_copy(ref, ref, self.sems[3], 0, self.partner)
+
+    def begin(self):
+        self.first[...] = self.half(self.source, 1 - self.side)[...].astype(self.wire)
+        self.halve().start()
+
+    def pass_on(self):
+        self.halve().wait_recv()
+        self.second[...] = (self.half(self.source, self.side)[...] + self.land1[...].astype(F32)).astype(self.wire)
+        loop(1, self.members, lambda d: self.scatter(d).start())
+
+    def finish(self):
+        own = rows_at(self.source, self.side * self.members + self.place, self.piece)[...]
+        own = own + rows_at(self.land1, self.place, self.piece)[...].astype(F32)
+
+        def add(d, total):
+            self.scatter(d).wait_recv()
+            return total + self.land2[d].astype(F32)
+
+        self.part(self.place)[...] = lax.fori_loop(1, self.members, add, own).astype(self.wire)
+        loop(1, self.members, lambda d: self.gather(d).start())
+
+    def collect(self):
+        loop(1, self.members, lambda d: self.gathered(d).wait_recv())
+        self.widen(self.side).start()
+
+    def store(self, out):
+        self.half(out, self.side)[...] = self.half(self.done, self.side)[...].astype(F32)
+        self.widen(1 - self.side).wait_recv()
+        self.half(out, 1 - self.side)[...] = self.half(self.done, 1 - self.side)[...].astype(F32)
+
+    def drain(self):
+        self.halve().wait_send()
+        self.widen(self.side).wait_send()
+
+        def both(d):
+            self.scatter(d).wait_send()
+            self.gather(d).wait_send()
+
+        loop(1, self.members, both)
+
+    @staticmethod
+    def scratch(rows, lanes, wire, size):
+        members = size // 2
+        half = pltpu.VMEM((members * rows, lanes), wire)
+        dma = pltpu.SemaphoreType.DMA
+        return [half, half, half, pltpu.VMEM((members, rows, lanes), wire), pltpu.VMEM((2 * members * rows, lanes), wire)] + [
+            dma((1,)), dma((1,)), dma((members,)), dma((members,)), dma((members,)), dma((members,)), dma((1,)), dma((1,)),
+        ]
+
+
+SUM_REFS = 13
+
+
+class HeadSum:
+    def __init__(self, source, out, fold1, half, fold2, quarter, sems):
+        self.source, self.out, self.fold1, self.held, self.fold2, self.quarter = source, out, fold1, half, fold2, quarter
+        self.sems = [sems[i : i + 2] for i in range(0, 8, 2)]
+        self.rows = source.shape[0]
+        head = lax.axis_index("head")
+        self.core, self.plane = lax.rem(head, 2), head // 2
+        self.beside, self.across = {"head": head + 1 - 2 * self.core}, {"head": head + 2 - 4 * self.plane}
+
+    def fold_core(self):
+        return device_copy(rows_at(self.source, 1 - self.core, self.rows // 2), self.fold1, self.sems[0], 0, self.beside)
+
+    def fold_plane(self):
+        return device_copy(rows_at(self.held, 1 - self.plane, self.rows // 4), self.fold2, self.sems[1], 0, self.across)
+
+    def spread_plane(self, plane):
+        ref = rows_at(self.out, 2 * self.core + plane, self.rows // 4)
+        return device_copy(ref, ref, self.sems[2], 0, self.across)
+
+    def spread_core(self, core):
+        ref = rows_at(self.out, core, self.rows // 2)
+        return device_copy(ref, ref, self.sems[3], 0, self.beside)
+
+    def fold(self):
+        self.fold_core().wait_recv()
+        self.held[...] = rows_at(self.source, self.core, self.rows // 2)[...] + self.fold1[...]
+        self.fold_plane().start()
+
+    def settle(self):
+        self.fold_plane().wait_recv()
+        self.quarter[...] = jnp.zeros_like(self.quarter)
+        self.quarter[: self.rows // 4] = rows_at(self.held, self.plane, self.rows // 4)[...] + self.fold2[...]
+
+    def spread(self, total):
+        rows_at(self.out, 2 * self.core + self.plane, self.rows // 4)[...] = total[: self.rows // 4]
+        self.spread_plane(self.plane).start()
+
+    def spread_more(self):
+        self.spread_plane(1 - self.plane).wait_recv()
+        self.spread_core(self.core).start()
+
+    def finish(self):
+        self.spread_core(1 - self.core).wait_recv()
+        self.fold_core().wait_send()
+        self.fold_plane().wait_send()
+        self.spread_plane(self.plane).wait_send()
+        self.spread_core(self.core).wait_send()
+
+    @staticmethod
+    def scratch(rows, lanes, padded_rows):
+        dma = pltpu.SemaphoreType.DMA
+        shapes = [(rows // 2, lanes), (rows // 2, lanes), (rows // 4, lanes), (padded_rows, lanes)]
+        return [pltpu.VMEM(shape, F32) for shape in shapes] + [dma((1,))] * 8
+
+
+HEAD_REFS = 12
+
+
+def dot_split(a, b, da=1, db=0):
+    high, low = halves(b)
+    return dot(a, high, da, db) + dot(a, low, da, db)
+
+
+def tail_kernel(
+    low, d_gate, d_inner, d_step, d_pair, wg, wi, ws, wp, edge, tail, hid, d_out, gain, error, g_wo, g_wg, small_i, g_gain,
+    small_p, heads,
+    grad, sums, out_wo, out_wg, out_wi, out_pack, out_wp, out_small,
+    block_i, block_p, after, away, land, mine, other, row, row_land, g_wi, g_ws, pack, g_wp, pair_small, sum_small, sum_wp,
+    spread_wp, spread_small, grad_own, grad_other,
+    core_send, core_land, x_send, x_land, edge_send, edge_land, grad_send, grad_land, row_send, row_arrive, *more,
 ):
     step = pl.program_id(0)
     blocks = pl.num_programs(0)
+    half = blocks // 2
     seq, devices = lax.axis_index("seq"), lax.axis_size("seq")
-    behind, ahead = lax.rem(seq + devices - 1, devices), lax.rem(seq + 1, devices)
+    head, core = lax.axis_index("head"), core_bit()
     width = wi.shape[1]
-    moved = pltpu.make_async_remote_copy(
-        src_ref=edge, dst_ref=after, send_sem=edge_send, recv_sem=edge_land,
-        device_id={"seq": behind}, device_id_type=pl.DeviceIdType.MESH,
-    )
+    behind = lax.rem(seq + devices - 1, devices)
+    group = 2 * devices
+    me = 2 * seq + core
+    beside, across = {"head": core_peer()}, {"head": lax.rem(head + 2, 4)}
+
+    more = list(more)
+
+    def take(number):
+        taken = more[:number]
+        del more[:number]
+        return taken
+
+    head_sums_ = []
+    for source, out in ((g_wp, spread_wp), (pair_small, spread_small)):
+        refs = take(HEAD_REFS)
+        head_sums_.append(HeadSum(source, out, *refs[:4], refs[4:]))
+    sources = [g_wo, g_wg, g_wi, pack, head_sums_[0].quarter, head_sums_[1].quarter]
+    seq_sums = []
+    for source in sources:
+        refs = take(SUM_REFS)
+        seq_sums.append(SeqSum(source, *refs[:5], refs[5:]))
+    s_wo, s_wg, s_wi, s_pack, s_wp, s_small = seq_sums
+    wide = list(zip(head_sums_, (s_wp, s_small), (sum_wp, sum_small)))
+
+    def device(distance):
+        to = lax.rem(me + distance, group)
+        return {"seq": to // 2, "head": head - core + lax.rem(to, 2)}
+
+    def hand(distance):
+        return device_copy(row, row_land.at[me], (row_send, row_arrive), distance, device(distance))
+
+    moved = device_copy(edge, after, (edge_send, edge_land), 0, {"seq": behind})
+
+    def core_copy(slot):
+        return device_copy(away.at[slot], land.at[slot], (core_send, core_land), slot, beside)
+
+    def x_copy(slot):
+        return device_copy(mine.at[slot], other.at[slot], (x_send, x_land), slot, across)
+
+    def grad_copy(slot):
+        return device_copy(grad_own.at[slot], grad_other.at[slot], (grad_send, grad_land), slot, beside)
 
     @pl.when(step == 0)
     def _():
-        enter([{"head": core_peer()}, {"seq": behind}, {"seq": ahead}])
+        barrier = pltpu.get_barrier_semaphore()
+
+        def greet(to):
+            pl.semaphore_signal(barrier, inc=1, device_id=to, device_id_type=pl.DeviceIdType.MESH)
+
+        loop(1, group, lambda d: greet(device(d)))
+        greet(across)
+        for ref in (g_wi, g_ws, pack, g_wp, pair_small):
+            ref[...] = jnp.zeros_like(ref)
+        pl.semaphore_wait(barrier, group)
         moved.start()
+        s_wo.begin()
+        s_wg.begin()
 
     block_i[...] = d_inner[...]
     block_p[...] = d_pair[...]
-    block = lax.rem(step + blocks // 2 * (1 - core_bit()), blocks)
+    block = lax.rem(step + half * (1 - core), blocks)
 
     @pl.when(block == blocks - 1)
     def _():
         moved.wait_recv()
-        more = jnp.where(seq == devices - 1, 0.0, after[...])
-        fixed = jnp.concatenate([tail[:8], tail[8:] + more], axis=0)
-        fix_i[...] = fixed[:, :width].astype(BF16)
-        fix_p[...] = fixed[:, width:]
+        extra = jnp.where(seq == devices - 1, 0.0, after[...])
+        fixed = jnp.concatenate([tail[:8], tail[8:] + extra], axis=0)
         block_i[BLOCK - 16 :] = fixed[:, :width].astype(BF16)
         block_p[BLOCK - 16 :] = fixed[:, width:]
 
     part = dot(d_gate[...], wg[...], 1, 1) + dot(block_i[...], wi[...], 1, 1) + dot(d_step[...], ws[...], 1, 1)
-    high, low = halves(block_p[...])
-    part = part + (dot(high, wp[...], 1, 1) + dot(low, wp[...], 1, 1))
-    add_halves(part, mine, away, land, send_sem, land_sem)
+    high, rest = halves(block_p[...])
+    part = part + (dot(high, wp[...], 1, 1) + dot(rest, wp[...], 1, 1))
+
+    @pl.when(step < half)
+    def _():
+        away[step] = part.astype(away.dtype)
+        core_copy(step).start()
+
+    @pl.when(step >= half)
+    def _():
+        core_copy(step - half).wait_recv()
+        mine[step - half] = (part + land[step - half].astype(F32)).astype(BF16)
+        x_copy(step - half).start()
+
+    g_ws[...] += dot(d_step[...], low[...], 0, 0)[:8]
+    g_wp[...] += dot_split(low[...], block_p[...], 0, 0)
+    g_wi[: low.shape[1]] += dot(low[...], block_i[...], 0, 0)
+
+    def norm_back(slot):
+        x_copy(slot).wait_recv()
+        at = pl.ds(slot * BLOCK, BLOCK)
+        d_low = mine[slot].astype(F32) + other[slot].astype(F32)
+        rows = hid[at, :].astype(F32)
+        scale = lax.rsqrt(jnp.mean(rows * rows, axis=1, keepdims=True) + EPSILON)
+        row[:1] += jnp.sum(d_low * rows * scale, axis=0, keepdims=True)
+        scaled = d_low * gain[...]
+        pull = jnp.mean(scaled * rows, axis=1, keepdims=True) * (scale * scale * scale)
+        block = (d_out[at, :] + scale * scaled - rows * pull).astype(BF16)
+        grad_own[slot] = block
+        grad_copy(slot).start()
+        rows_at(grad, core * half + slot, BLOCK)[...] = block
+
+    @pl.when(step == half + 1)
+    def _():
+        s_wo.pass_on()
 
     @pl.when(step == blocks - 1)
     def _():
-        moved.wait_send()
-
-
-def pair_weight_kernel(low, d_step, d_pair, fix_p, g_ws, g_wp):
-    step = pl.program_id(0)
-
-    @pl.when(step == 0)
-    def _():
-        g_ws[...] = jnp.zeros_like(g_ws)
-        g_wp[...] = jnp.zeros_like(g_wp)
-
-    grads = jnp.where(step == pl.num_programs(0) - 1, fix_p[...], d_pair[BLOCK - 16 :])
-    grads = jnp.concatenate([d_pair[: BLOCK - 16], grads], axis=0)
-    g_ws[...] += dot(d_step[...], low[...], 0, 0)[:8]
-    g_wp[...] += dot_split(low[...], grads, 0, 0)
-
-
-def inner_weight_kernel(low, d_inner, fix_i, g_wi):
-    step = pl.program_id(0)
-
-    @pl.when(step == 0)
-    def _():
-        g_wi[...] = jnp.zeros_like(g_wi)
-
-    grads = jnp.where(step == pl.num_programs(0) - 1, fix_i[...], d_inner[BLOCK - 16 :])
-    grads = jnp.concatenate([d_inner[: BLOCK - 16], grads], axis=0)
-    g_wi[...] += dot(low[...], grads, 0, 0)
-
-
-def norm_back_kernel(
-    mine, other, hid, d_out, gain, error, grad, sums, block, row, land, local, send, arrive, row_send, row_land
-):
-    step = pl.program_id(0)
-    seq, devices = lax.axis_index("seq"), lax.axis_size("seq")
-    head = lax.axis_index("head")
-    group = 2 * devices
-    me = 2 * seq + core_bit()
-
-    def device(distance):
-        to = lax.rem(me + distance, group)
-        return {"seq": to // 2, "head": head - core_bit() + lax.rem(to, 2)}
-
-    def hand(distance):
-        return pltpu.make_async_remote_copy(
-            src_ref=row, dst_ref=land.at[me], send_sem=row_send.at[distance], recv_sem=row_land.at[distance],
-            device_id=device(distance), device_id_type=pl.DeviceIdType.MESH,
-        )
-
-    def each(body):
-        def run(distance, carry):
-            body(distance)
-            return carry
-
-        lax.fori_loop(1, group, run, 0)
-
-    @pl.when(step == 0)
-    def _():
-        barrier = pltpu.get_barrier_semaphore()
-        each(
-            lambda d: pl.semaphore_signal(
-                barrier, inc=1, device_id=device(d), device_id_type=pl.DeviceIdType.MESH
-            )
-        )
-        pl.semaphore_wait(barrier, group - 1)
+        s_wi.begin()
+        pack[:6] = small_i[:6]
+        pack[6:7] = g_gain[...]
+        pack[8:16] = g_ws[:, :width]
+        pack[16:24] = g_ws[:, width:]
+        pack[24:32, : heads.shape[1]] = heads[...]
+        pair_small[:8] = small_p[...]
+        for h_sum, _, _ in wide:
+            h_sum.fold_core().start()
         row[:1] = jnp.zeros_like(row[:1])
         row[1:] = error[...]
-
-    d_low = mine[...].astype(F32) + other[...].astype(F32)
-    rows = hid[...].astype(F32)
-    scale = lax.rsqrt(jnp.mean(rows * rows, axis=1, keepdims=True) + EPSILON)
-    row[:1] += jnp.sum(d_low * rows * scale, axis=0, keepdims=True)
-    scaled = d_low * gain[...]
-    pull = jnp.mean(scaled * rows, axis=1, keepdims=True) * (scale * scale * scale)
-    block[step] = (d_out[...] + scale * scaled - rows * pull).astype(BF16)
-
-    @pl.when(step == pl.num_programs(0) - 1)
-    def _():
-        each(lambda d: hand(d).start())
-
-    both_cores([block], [grad], [local, send, arrive])
-
-    @pl.when(step == pl.num_programs(0) - 1)
-    def _():
-        land[me] = row[...]
-        each(lambda d: hand(d).wait())
-        sums[...] = lax.fori_loop(1, group, lambda d, total: total + land[d], land[0])
+        s_pack.begin()
+        s_wg.pass_on()
+        for h_sum, _, _ in wide:
+            h_sum.fold()
+        s_wo.finish()
+        norm_back(0)
+        s_wi.pass_on()
+        s_pack.pass_on()
+        s_wg.finish()
+        norm_back(1)
+        s_wo.collect()
+        s_wi.finish()
+        s_pack.finish()
+        norm_back(2)
+        s_wg.collect()
+        norm_back(3)
+        loop(1, group, lambda d: hand(d).start())
+        for h_sum, s_sum, _ in wide:
+            h_sum.settle()
+            s_sum.begin()
+        s_wi.collect()
+        for _, s_sum, _ in wide:
+            s_sum.pass_on()
+        s_wo.store(out_wo)
+        s_pack.collect()
+        for _, s_sum, _ in wide:
+            s_sum.finish()
+        s_wg.store(out_wg)
+        for _, s_sum, _ in wide:
+            s_sum.collect()
+        s_wi.store(out_wi)
+        for h_sum, s_sum, total in wide:
+            s_sum.store(total)
+            h_sum.spread(total)
+        s_pack.store(out_pack)
+        for h_sum, _, _ in wide:
+            h_sum.spread_more()
+        row_land[me] = row[...]
+        loop(1, group, lambda d: hand(d).wait())
+        sums[...] = lax.fori_loop(1, group, lambda d, total: total + row_land[d], row_land[0])
+        for (h_sum, _, _), out in zip(wide, (out_wp, out_small)):
+            h_sum.finish()
+            out[...] = h_sum.out[...]
+        for s_sum in seq_sums:
+            s_sum.drain()
+        moved.wait_send()
+
+        def drain(slot):
+            core_copy(slot).wait_send()
+            x_copy(slot).wait_send()
+            grad_copy(slot).wait()
+            rows_at(grad, (1 - core) * half + slot, BLOCK)[...] = grad_other[slot]
+
+        loop(0, half, drain)
 
 
 def call(kernel, grid, ins, outs, scratch=(), prefetch=0, flops=0, moved=0, collective=None, vmem=14):
@@ -646,7 +884,7 @@
         if block is None:
             return pl.BlockSpec(shape, lambda *_: (0,) * len(shape))
         if isinstance(block, str):
-            return pl.BlockSpec(memory_space=pltpu.SMEM if block == "smem" else pl.ANY)
+            return pl.BlockSpec(memory_space={"smem": pltpu.SMEM, "vmem": pltpu.VMEM, "any": pl.ANY}[block])
         return pl.BlockSpec(block, index)
 
     scalars = [a for a, *_ in ins[:prefetch]]
@@ -707,199 +945,6 @@
     return reached[:CHUNK]
 
 
-def reduce_kernel(plain, wide, wires, axis, *refs):
-    count = plain + wide
-    take = iter(range(len(refs)))
-
-    def some(number):
-        return [refs[next(take)] for _ in range(number)]
-
-    ins, outs = some(count), some(count)
-    first, land1, second, land2, done = (some(count) for _ in range(5))
-    fold1, half, fold2, quarter = (some(wide) for _ in range(4))
-    sems = some(16)
-    members = first[0].shape[0]
-    me = lax.axis_index(axis)
-    side, place = lax.rem(me, 2), me // 2
-    partner = {axis: me + 1 - 2 * side}
-    head = lax.axis_index("head")
-    core, plane = lax.rem(head, 2), head // 2
-    beside, across = {"head": head + 1 - 2 * core}, {"head": head + 2 - 4 * plane}
-    source = ins[:plain] + quarter
-
-    def copy(src, dst, sem, slot, to):
-        return pltpu.make_async_remote_copy(
-            src_ref=src, dst_ref=dst, send_sem=sems[2 * sem].at[slot], recv_sem=sems[2 * sem + 1].at[slot],
-            device_id=to, device_id_type=pl.DeviceIdType.MESH,
-        )
-
-    def member(d):
-        return lax.rem(place + d, members)
-
-    def to_member(d):
-        return {axis: 2 * member(d) + side}
-
-    def halve(k):
-        return copy(first[k], land1[k], 0, k, partner)
-
-    def scatter(k, d):
-        return copy(second[k].at[member(d)], land2[k].at[d], 1, k * members + d, to_member(d))
-
-    def gather(k, d):
-        return copy(done[k].at[side, place], done[k].at[side, place], 2, k * members + d, to_member(d))
-
-    def gathered(k, d):
-        other = lax.rem(place + members - d, members)
-        return copy(done[k].at[side, other], done[k].at[side, other], 2, k * members + d, partner)
-
-    def widen(k):
-        return copy(done[k].at[side], done[k].at[side], 3, k, partner)
-
-    def widened(k):
-        return copy(done[k].at[1 - side], done[k].at[1 - side], 3, k, partner)
-
-    def fold_core(w):
-        return copy(ins[plain + w].at[1 - core], fold1[w], 4, w, beside)
-
-    def fold_plane(w):
-        return copy(half[w].at[1 - plane], fold2[w], 5, w, across)
-
-    def spread_plane(w, at):
-        ref = outs[plain + w].at[core, at]
-        return copy(ref, ref, 6, w, across)
-
-    def spread_core(w, at):
-        ref = outs[plain + w].at[at]
-        return copy(ref, ref, 7, w, beside)
-
-    def each(body):
-        def step(d, carry):
-            body(d)
-            return carry
-
-        lax.fori_loop(1, members, step, 0)
-
-    def split(k):
-        first[k][...] = source[k][1 - side].astype(wires[k])
-
-    def pass_on(k):
-        halve(k).wait_recv()
-        second[k][...] = (source[k][side] + land1[k][...].astype(F32)).astype(wires[k])
-        each(lambda d: scatter(k, d).start())
-
-    def finish(k):
-        def add(d, total):
-            scatter(k, d).wait_recv()
-            return total + land2[k][d].astype(F32)
-
-        total = lax.fori_loop(1, members, add, source[k][side, place] + land1[k][place].astype(F32))
-        done[k][side, place] = total.astype(wires[k])
-        each(lambda d: gather(k, d).start())
-
-    def collect(k):
-        each(lambda d: gathered(k, d).wait_recv())
-        widen(k).start()
-
-    def store(k, out):
-        out[side] = done[k][side].astype(F32)
-        widened(k).wait_recv()
-        out[1 - side] = done[k][1 - side].astype(F32)
-
-    barrier = pltpu.get_barrier_semaphore()
-
-    def greet(to):
-        pl.semaphore_signal(barrier, inc=1, device_id=to, device_id_type=pl.DeviceIdType.MESH)
-
-    for to in (partner, beside, across):
-        greet(to)
-    each(lambda d: greet(to_member(d)))
-    for k in range(plain):
-        split(k)
-    pl.semaphore_wait(barrier, members + 2)
-    for w in range(wide):
-        fold_core(w).start()
-    halve(0).start()
-    for k in range(plain):
-        if k + 1 < plain:
-            halve(k + 1).start()
-        pass_on(k)
-        if k == 0:
-            for w in range(wide):
-                fold_core(w).wait_recv()
-                half[w][...] = ins[plain + w][core] + fold1[w][...]
-                fold_plane(w).start()
-    for k in range(plain):
-        finish(k)
-    for w in range(wide):
-        fold_plane(w).wait_recv()
-        quarter[w][...] = half[w][plane] + fold2[w][...]
-        split(plain + w)
-        halve(plain + w).start()
-    for k in range(plain):
-        collect(k)
-    for w in range(wide):
-        pass_on(plain + w)
-    for k in range(plain):
-        store(k, outs[k])
-    for w in range(wide):
-        finish(plain + w)
-    for w in range(wide):
-        collect(plain + w)
-    for w in range(wide):
-        store(plain + w, outs[plain + w].at[core, plane])
-        spread_plane(w, plane).start()
-    for w in range(wide):
-        spread_plane(w, 1 - plane).wait_recv()
-        spread_core(w, core).start()
-    for w in range(wide):
-        spread_core(w, 1 - core).wait_recv()
-        fold_core(w).wait_send()
-        fold_plane(w).wait_send()
-        spread_plane(w, plane).wait_send()
-        spread_core(w, core).wait_send()
-    for k in range(count):
-        halve(k).wait_send()
-        widen(k).wait_send()
-
-        def drain(d, k=k):
-            scatter(k, d).wait_send()
-            gather(k, d).wait_send()
-
-        each(drain)
-
-
-def reduce_over(arrays, wires, wide_arrays, axis, collective):
-    size = lax.axis_size(axis)
-    members = size // 2
-    split = [a.reshape(2, members, a.shape[0] // size, a.shape[1]) for a in arrays]
-    split += [a.reshape(2, 2, 2, members, a.shape[0] // (4 * size), a.shape[1]) for a in wide_arrays]
-    plain, wide = len(arrays), len(wide_arrays)
-    wires = list(wires) + [F32] * wide
-    n = plain + wide
-    vmem = pl.BlockSpec(memory_space=pltpu.VMEM)
-    moved = sum(a.size * 4 for a in split)
-    tail = [a.shape[-3:] for a in split]
-    part = [pltpu.VMEM(shape, w) for shape, w in zip(tail, wires)]
-    last = [a.shape for a in split[plain:]]
-    dma = pltpu.SemaphoreType.DMA
-    outs = pl.pallas_call(
-        partial(reduce_kernel, plain, wide, wires, axis),
-        out_shape=[jax.ShapeDtypeStruct(a.shape, F32) for a in split],
-        in_specs=[vmem] * n,
-        out_specs=[vmem] * n,
-        scratch_shapes=part * 4
-        + [pltpu.VMEM((2,) + shape, w) for shape, w in zip(tail, wires)]
-        + [pltpu.VMEM(shape[1:], F32) for shape in last] * 2
-        + [pltpu.VMEM(shape[2:], F32) for shape in last] * 2
-        + [dma((n,))] * 2 + [dma((n * members,))] * 4 + [dma((n,))] * 2 + [dma((wide,))] * 8,
-        compiler_params=pltpu.CompilerParams(
-            collective_id=collective, has_side_effects=True, vmem_limit_bytes=24 << 20
-        ),
-        cost_estimate=pl.CostEstimate(flops=0, bytes_accessed=40 * moved, transcendentals=0),
-    )(*split)
-    return [o.reshape(a.shape) for o, a in zip(outs, list(arrays) + list(wide_arrays))]
-
-
 def padded(row, lanes=LANES):
     return jnp.zeros((1, lanes), F32).at[0, : row.shape[0]].set(row)
 
@@ -953,7 +998,7 @@
     half_own = lambda w: ((BLOCK, w), lambda i: (i + half * core_bit(), 0))
     tail_half = lambda w: ((BLOCK, w), lambda i: (jnp.maximum(i - half, 0), 0))
     dma = pltpu.SemaphoreType.DMA
-    swap_scratch = [pltpu.VMEM((half, BLOCK, model), BF16)] * 2 + [dma((half,))] * 2
+    swap_scratch = [pltpu.VMEM((half, BLOCK, model), F32)] * 2 + [dma((half,))] * 2
 
     halo_block = ((edge_rows, model), lambda i, *_: (jnp.maximum(i * (BLOCK // edge_rows) - 1, 0), 0))
     (low, in_i, in_p, pre_i, pre_p, aux, halo_i, halo_p, sloc, pkl, fin) = call(
@@ -1081,60 +1126,53 @@
         [pltpu.VMEM((BLOCK + 16, width), F32)] * 3 + [pltpu.VMEM((BLOCK + 16, pair_width), F32)] * 3,
         prefetch=1, flops=3e9, moved=3e7, vmem=16,
     )
-    mine, fix_i, fix_p = call(
-        input_back_kernel,
+    size = lax.axis_size("seq")
+
+    def piece(total_rows, tile):
+        return -(-total_rows // (size * tile)) * tile
+
+    r_wo, r_w, r_pack, r_wp, r_small = piece(width, 16), piece(model, 16), 8, piece(model // 4, 8), 8
+    vmem = ("vmem", None)
+    core_wire = F32 if size <= 8 else BF16
+    once = lambda w: ((rows // 2, w), lambda i: (core_bit(), 0))
+    sums_shapes = [(r_wo, model, BF16), (r_w, width, BF16), (r_w, width, BF16), (r_pack, width, F32), (r_wp, pair_width, F32),
+                   (r_small, pair_width, F32)]
+    pad_rows = lambda a, r: a if a.shape[0] == r * size else jnp.pad(a, ((0, r * size - a.shape[0]), (0, 0)))
+    scratch = [
+        pltpu.VMEM((BLOCK, width), BF16), pltpu.VMEM((BLOCK, pair_width), F32), pltpu.VMEM((8, both), F32),
+        pltpu.VMEM((half, BLOCK, model), core_wire), pltpu.VMEM((half, BLOCK, model), core_wire),
+        pltpu.VMEM((half, BLOCK, model), BF16), pltpu.VMEM((half, BLOCK, model), BF16),
+        pltpu.VMEM((2, model), F32), pltpu.VMEM((2 * size, 2, model), F32),
+        pltpu.VMEM((r_w * size, width), F32), pltpu.VMEM((8, model), F32), pltpu.VMEM((r_pack * size, width), F32),
+        pltpu.VMEM((model, pair_width), F32), pltpu.VMEM((32, pair_width), F32),
+        pltpu.VMEM((r_small * size, pair_width), F32), pltpu.VMEM((r_wp * size, pair_width), F32),
+        pltpu.VMEM((model, pair_width), F32), pltpu.VMEM((32, pair_width), F32),
+        pltpu.VMEM((half, BLOCK, model), BF16), pltpu.VMEM((half, BLOCK, model), BF16),
+        dma((half,)), dma((half,)), dma((half,)), dma((half,)), dma((1,)), dma((1,)), dma((half,)), dma((half,)),
+        dma((2 * size,)), dma((2 * size,)),
+    ]
+    scratch += HeadSum.scratch(model, pair_width, r_wp * size) + HeadSum.scratch(32, pair_width, r_small * size)
+    for r, lanes, wire in sums_shapes:
+        scratch += SeqSum.scratch(r, lanes, wire, size)
+    grad_hidden, sums, g_wo, g_wg, g_wi, pack, g_wp, small_p = call(
+        tail_kernel,
         blocks,
         [
-            (d_gate, *send_order(width)), (d_inner, *send_order(width)), (d_step, *send_order(LANES)),
+            (low, *send_order(model)), (d_gate, *send_order(width)), (d_inner, *send_order(width)), (d_step, *send_order(LANES)),
             (d_pair, *send_order(pair_width)), (w_gate, *whole), (w_inner, *whole), (ws, *whole), (w_pair, *whole),
-            (edge, *whole), (tail, *whole),
-        ],
-        [
-            ((rows // 2, model), BF16, *tail_half(model)), ((16, width), BF16, *whole), ((16, pair_width), F32, *whole),
-        ],
-        [pltpu.VMEM((BLOCK, width), BF16), pltpu.VMEM((BLOCK, pair_width), F32), pltpu.VMEM((8, both), F32)]
-        + swap_scratch + [dma] * 2,
-        flops=2.6e9, moved=1e7, collective=4,
-    )
-    other = swap(mine, "head", 2)
-    g_ws, g_wp = call(
-        pair_weight_kernel,
-        blocks,
-        [(low, *by(model)), (d_step, *by(LANES)), (d_pair, *by(pair_width)), (fix_p, *whole)],
-        [((8, model), F32, *whole), ((model, pair_width), F32, *whole)],
-        flops=1.6e9, moved=1e7,
-    )
-    (g_wi,) = call(
-        inner_weight_kernel,
-        blocks,
-        [(low, *by(model)), (d_inner, *by(width)), (fix_i, *whole)],
-        [((model, width), F32, *whole)],
-        flops=1.2e9, moved=1e7,
-    )
-    pack = jnp.concatenate([
-        small_i[:6], g_gain, jnp.zeros((1, width), F32), g_ws[:, :width], g_ws[:, width:],
-        jnp.pad(head_small, ((0, 32), (0, width - LANES))),
-    ])
-    quarters = 4 * lax.axis_size("seq")
-    small_p = jnp.pad(small_p, ((0, quarters - 8), (0, 0)))
-    g_wo, g_wg, g_wi, pack, g_wp, small_p = reduce_over(
-        [g_wo, g_wg, g_wi, pack], [BF16, BF16, BF16, F32], [g_wp, small_p], "seq", 1
-    )
-    grad_hidden, sums = call(
-        norm_back_kernel,
-        half,
-        [
-            (mine, *by(model)), (other, *by(model)), (hidden, *half_own(model)), (d_out, *by(model)), (gain, *whole),
-            (error, *whole),
-        ],
-        [((rows, model), BF16, "any", None), ((2, model), F32, *whole)],
-        [
-            pltpu.VMEM((half, BLOCK, model), BF16), pltpu.VMEM((2, model), F32),
-            pltpu.VMEM((2 * lax.axis_size("seq"), 2, model), F32),
-        ]
-        + [dma((half,))] * 3 + [dma((2 * lax.axis_size("seq"),))] * 2,
-        flops=5e8, moved=1e7, collective=5,
-    )
+            (edge, *whole), (tail, *whole), (hidden, *once(model)), (d_out, *vmem), (gain, *whole), (error, *whole),
+            (pad_rows(g_wo, r_wo), *vmem), (pad_rows(g_wg, r_w), *vmem), (small_i, *whole), (g_gain, *whole), (small_p, *whole),
+            (head_small, *whole),
+        ],
+        [
+            ((rows, model), BF16, *vmem), ((2, model), F32, *vmem), ((r_wo * size, model), F32, *vmem),
+            ((r_w * size, width), F32, *vmem), ((r_w * size, width), F32, *vmem), ((r_pack * size, width), F32, *vmem),
+            ((model, pair_width), F32, *vmem), ((32, pair_width), F32, *vmem),
+        ],
+        scratch,
+        flops=6e9, moved=4e7, collective=4, vmem=40 if size <= 8 else 60,
+    )
+    g_wo, g_wg, g_wi = g_wo[:width], g_wg[:model], g_wi[:model]
     by_head, g_ws = pack[:8], jnp.concatenate([pack[8:16], pack[16:24]], axis=1)[:heads].T
     pair_small, head_small = small_p[:8], pack[24:32, :LANES]
     loss = jnp.sum(sums[1]) / (count * model)

time: 354 us -> 333 us (0.941)
  Pallas kernels: 203 us -> 189 us
    pallas_call x1 -> x0, Pallas kernels: 76.4 us -> none  [reduce_over(): pl.pallas_call(partial(reduce_kernel, plain, wide, wires, axis), out_shap...]
    pallas_call x13 -> x10, Pallas kernels: 127 us -> 189 us  [call(): pl.pallas_call(kernel, grid_spec=pltpu.PrefetchScalarGridSpec(num_scalar_...]
    unnamed x129 -> x115, local copies, waits for them, and re-layouts: 42.1 us -> 38.9 us
    ppermute x15 -> x14, starting transfers between devices: 17.8 us -> 16.2 us  [swap(): return jax.tree.map(lambda v: lax.ppermute(v, axis, route), value)]
    ppermute x15 -> x14, waiting for transfers between devices: 61.9 us -> 60.8 us  [swap(): return jax.tree.map(lambda v: lax.ppermute(v, axis, route), value)]
  transfers between devices with their start and end apart: 16 -> 15, of which waited for: 12 -> 12; matrix products, arithmetic and copies ran while one was open for 5% -> 4% of each run, Pallas kernels for 28% -> 5%
where the time goes in v3:
time: 333 us; the launch traced here: 332 us
  Pallas kernels  189 us (57%)
  waiting for transfers between devices  60.9 us (18%)
  local copies, waits for them, and re-layouts  46.3 us (14%)
  starting transfers between devices  21.1 us (6%)
  other arithmetic  11.1 us (3%)
  between operations  4.36 us (1%)
    pallas_call x10, Pallas kernels, call(): pl.pallas_call(kernel, grid_spec=pltpu.PrefetchScalarGridSpec(num_scalar_...  189 us
    ppermute x14, waiting for transfers between devices, swap(): return jax.tree.map(lambda v: lax.ppermute(v, axis, route), value)  60.8 us
    unnamed x115, local copies, waits for them, and re-layouts  38.9 us
    ppermute x14, starting transfers between devices, swap(): return jax.tree.map(lambda v: lax.ppermute(v, axis, route), value)  16.2 us
  transfers between devices with their start and end apart: 15, of which 12 were waited for; matrix products, arithmetic and copies ran while one was open for 4% of the time, Pallas kernels for 5%

profile of v3, /device:TPU:0, one launch (start us, length us, event | category | flops | bytes accessed | tf_op | source)
XLA Modules:
  0.0 332.3 jit_solution(17705646726949289387)
XLA Ops:
  1.4 4.9 %collective-permute-start.3 = (bf16[16,768]{1,0:T(8,128)(2,1)S(1)}, bf16[16,768]{1,0:T(8,128)(2,1)S(1)}, u32[]{:S(2)}, u32[]{:S(2)}) collective-permute-start(bf16[16,768]{1,0:T(8,128)(2,1)S(1)} %slice.273), channel_id=1, source_target_pairs={{0,4},{4,8},{8,12},{12,16},{16,20},{20,24},{24,28},{1,5},{5,9},{9,... | collective-permute-start | bytes 73736 | tf_op jit(solution)/shard_map/ppermute | solution.py:918
  16.1 1.9 copy-done.8
  20.1 20.6 %shard_map.305 = (bf16[2048,768]{1,0:T(8,128)(2,1)S(1)}, bf16[2048,384]{1,0:T(8,128)(2,1)S(1)}, bf16[2048,256]{1,0:T(8,128)(2,1)S(1)}, f32[2048,384]{1,0:T(8,128...) custom-call(s32[2]{0:T(128)S(1)} %pad_add_fusion.idx, ...), custom_call_target="tpu_custom_call" | custom-call | flops 3000000000 | bytes 20000000 | tf_op jit(solution)/shard_map/pallas_call | solution.py:893
  43.3 7.3 %shard_map.306 = (f32[2048,384]{1,0:T(8,128)S(1)}, f32[2048,384]{1,0:T(8,128)S(1)}) custom-call(s32[2]{0:T(128)S(1)} %pad_add_fusion.idx, bf16[2048,768]{1,0:T(8,128)(2,1)S(1)} %get-tuple-element.118.low, bf16[768,384]{1,0:T(8,128)(2,1)S(1)} %copy-done.40, f32[2048,384]{1,0:T(8,128)S(1)} %get-tuple-element.119.pre_i, ...), custom_call_target="tpu_custom_call" | custom-call | flops 4000000000 | bytes 20000000 | tf_op jit(solution)/shard_map/pallas_call | solution.py:893
  52.5 4.7 %collective-permute-done.5 = f32[136,384]{1,0:T(8,128)S(1)} collective-permute-done((f32[136,384]{1,0:T(8,128)S(1)}, f32[136,384]{1,0:T(8,128)S(1)}, u32[]{:S(2)}, u32[]{:S(2)}) %collective-permute-start.5) | collective-permute-done | bytes 208928 | tf_op jit(solution)/shard_map/ppermute | solution.py:912
  57.3 2.7 collective-permute-start.6
  60.0 8.2 %collective-permute-done.6 = f32[136,384]{1,0:T(8,128)S(1)} collective-permute-done((f32[136,384]{1,0:T(8,128)S(1)}, f32[136,384]{1,0:T(8,128)S(1)}, u32[]{:S(2)}, u32[]{:S(2)}) %collective-permute-start.6) | collective-permute-done | bytes 208928 | tf_op jit(solution)/shard_map/ppermute | solution.py:912
  68.3 5.5 %shard_map.307 = (f32[2048,384]{1,0:T(8,128)S(1)}, f32[16,128,384]{2,1,0:T(8,128)S(1)}, f32[1,2048]{1,0:T(1,128)S(1)}) custom-call(f32[2048,256]{1,0:T(8,128)S(1)} %get-tuple-element.113.pre_p.pre_c, f32[2048,128]{1,0:T(8,128)S(1)} %get-tuple-element.114.aux, f32[16,128,384]{2,1,0:T(8,128)S(1)} %get-tuple-element.115.sloc, ...), custom_call_target="tpu_custom_call" | custom-call | flops 1000000000 | bytes 20000000 | tf_op jit(solution)/shard_map/pallas_call | solution.py:893
  78.3 2.2 collective-permute-done.8
  80.5 6.5 %shard_map.308.mine = bf16[1024,768]{1,0:T(8,128)(2,1)S(1)} custom-call(f32[2048,384]{1,0:T(8,128)S(1)} %get-tuple-element.122.mixer, f32[2048,384]{1,0:T(8,128)S(1)} %get-tuple-element.121.gate, f32[1,2048]{1,0:T(1,128)S(1)} %add.83.square, f32[1,384]{1,0:T(1,128)S(1)} %broadcast_in_dim.35.gain, bf16[384,768]{1,0:T(8,128)(2,1)S(1)} %copy-done.19), custom_call_target="tpu_custom_call" | custom-call | flops 1200000000 | bytes 10000000 | tf_op jit(solution)/shard_map/pallas_call | solution.py:893
  90.4 3.1 collective-permute-done
  94.2 3.6 %collective-permute-done.1 = f32[8,128]{1,0:T(8,128)S(1)} collective-permute-done((f32[8,128]{1,0:T(8,128)S(1)}, f32[8,128]{1,0:T(8,128)S(1)}, u32[]{:S(2)}, u32[]{:S(2)}) %collective-permute-start.1) | collective-permute-done | bytes 4128 | tf_op jit(solution)/shard_map/ppermute | solution.py:912
  99.8 3.3 collective-permute-done.2
  104.3 19.2 %collective-permute-done.9.other = bf16[1024,768]{1,0:T(8,128)(2,1)S(1)} collective-permute-done((bf16[1024,768]{1,0:T(8,128)(2,1)S(1)}, bf16[1024,768]{1,0:T(8,128)(2,1)S(1)}, u32[]{:S(2)}, u32[]{:S(2)}) %collective-permute-start.9) | collective-permute-done | bytes 1572896 | tf_op jit(solution)/shard_map/ppermute | solution.py:912
  123.4 6.5 %shard_map.309 = (bf16[2048,768]{1,0:T(8,128)(2,1)S(1)}, bf16[2048,768]{1,0:T(8,128)(2,1)S(1)}, f32[1024,768]{1,0:T(8,128)S(1)}, f32[1,768]{1,0:T(1,128)S(1)}) custom-call(f32[1]{0:T(128)} %bitcast.factor, bf16[2048,768]{1,0:T(8,128)(2,1)S(1)} %copy-done.9, bf16[2048,768]{1,0:T(8,128)(2,1)S(1)} %copy-done.16, s32[1,2048]{1,0:T(1,128)S(1)} %bitcast.19, ...), custom_call_target="tpu_custom_call" | custom-call | flops 100000000 | bytes 15000000 | tf_op jit(solution)/shard_map/pallas_call | solution.py:893
  133.3 8.8 %shard_map.310 = (f32[2048,384]{1,0:T(8,128)S(1)}, f32[1,2048]{1,0:T(1,128)S(1)}, f32[1,384]{1,0:T(1,128)S(1)}, f32[384,768]{1,0:T(8,128)S(1)}) custom-call(bf16[2048,768]{1,0:T(8,128)(2,1)S(1)} %get-tuple-element.125.d_branch, f32[2048,384]{1,0:T(8,128)S(1)} %get-tuple-element.122.mixer, f32[2048,384]{1,0:T(8,128)S(1)} %get-tuple-element.121.gate, ...), custom_call_target="tpu_custom_call" | custom-call | flops 2400000000 | bytes 15000000 | tf_op jit(solution)/shard_map/pallas_call | solution.py:893
  154.4 1.9 copy-done.18
  156.3 7.4 %shard_map.311 = (f32[2048,384]{1,0:T(8,128)S(1)}, bf16[2048,384]{1,0:T(8,128)(2,1)S(1)}, f32[16,128,384]{2,1,0:T(8,128)S(1)}, f32[16,8,384]{2,1,0:T(8,128)S(1)}, f32[136,384]{1,0:T(8,128)S(1)}) custom-call(f32[2048,384]{1,0:T(8,128)S(1)} %copy-done.18, f32[2048,384]{1,0:T(8,128)S(1)} %get-tuple-element.122.mixer, f32[2048,384]{1,0:T(8,128)S(1)} %copy-done.1, ...), custom_call_target="tpu_custom_call" | custom-call | flops 1000000000 | bytes 20000000 | tf_op jit(solution)/shard_map/pallas_call | solution.py:893
  164.3 9.7 %shard_map.312 = (f32[2048,384]{1,0:T(8,128)S(1)}, f32[2048,256]{1,0:T(8,128)S(1)}, f32[768,384]{1,0:T(8,128)S(1)}) custom-call(s32[2]{0:T(128)S(1)} %pad_add_fusion.idx, f32[2048,384]{1,0:T(8,128)S(1)} %get-tuple-element.129.d_mixer, f32[2048,384]{1,0:T(8,128)S(1)} %copy-done.11, f32[2048,256]{1,0:T(8,128)S(1)} %copy-done.4, f32[2048,128]{1,0:T(8,128)S(1)} %copy-done.7, ...), custom_call_target="tpu_custom_call" | custom-call | flops 6000000000 | bytes 20000000 | tf_op jit(solution)/shard_map/pallas_call | solution.py:893
  174.9 5.1 %collective-permute-done.13 = f32[136,384]{1,0:T(8,128)S(1)} collective-permute-done((f32[136,384]{1,0:T(8,128)S(1)}, f32[136,384]{1,0:T(8,128)S(1)}, u32[]{:S(2)}, u32[]{:S(2)}) %collective-permute-start.13) | collective-permute-done | bytes 208928 | tf_op jit(solution)/shard_map/ppermute | solution.py:912
  180.1 2.3 collective-permute-start.14
  182.5 7.8 %collective-permute-done.14 = f32[136,384]{1,0:T(8,128)S(1)} collective-permute-done((f32[136,384]{1,0:T(8,128)S(1)}, f32[136,384]{1,0:T(8,128)S(1)}, u32[]{:S(2)}, u32[]{:S(2)}) %collective-permute-start.14) | collective-permute-done | bytes 208928 | tf_op jit(solution)/shard_map/ppermute | solution.py:912
  190.5 25.0 %shard_map.313 = (bf16[2048,384]{1,0:T(8,128)(2,1)S(1)}, bf16[2048,128]{1,0:T(8,128)(2,1)S(1)}, f32[2048,256]{1,0:T(8,128)S(1)}, f32[8,640]{1,0:T(8,128)S(1)}, f...) custom-call(s32[2]{0:T(128)S(1)} %pad_add_fusion.idx, ...), custom_call_target="tpu_custom_call" | custom-call | flops 3000000000 | bytes 30000000 | tf_op jit(solution)/shard_map/pallas_call | solution.py:893
  221.2 91.4 %shard_map.314 = (bf16[2048,768]{1,0:T(8,128)(2,1)}, f32[2,768]{1,0:T(2,128)S(1)}, f32[384,768]{1,0:T(8,128)S(1)}, f32[768,384]{1,0:T(8,128)S(1)}, f32[768,384]{...) custom-call(bf16[2048,768]{1,0:T(8,128)(2,1)} %copy-done.46, ...), custom_call_target="tpu_custom_call" | custom-call | flops 6000000000 | bytes 40000000 | tf_op jit(solution)/shard_map/pallas_call | solution.py:893
  (204 shorter events, 68.5 us)
Async XLA Ops:
  1.4 14.7 %collective-permute-start.3 = (bf16[16,768]{1,0:T(8,128)(2,1)S(1)}, bf16[16,768]{1,0:T(8,128)(2,1)S(1)}, u32[]{:S(2)}, u32[]{:S(2)}) collective-permute-start(bf16[16,768]{1,0:T(8,128)(2,1)S(1)} %slice.273), channel_id=1, source_target_pairs={{0,4},{4,8},{8,12},{12,16},{16,20},{20,24},{24,28},{1,5},{5,9},{9,... | collective-permute-start | bytes 73736 | tf_op jit(solution)/shard_map/ppermute | solution.py:918
  41.6 26.6 %copy-start.5 = (f32[2048,128]{1,0:T(8,128)}, f32[2048,128]{1,0:T(8,128)S(1)}, u32[]{:S(2)}) copy-start(f32[2048,128]{1,0:T(8,128)S(1)} %get-tuple-element.114.aux) | copy-start | bytes 3145732
  41.7 9.0 %collective-permute-start.4 = (f32[136,384]{1,0:T(8,128)S(1)}, f32[136,384]{1,0:T(8,128)S(1)}, u32[]{:S(2)}, u32[]{:S(2)}) collective-permute-start(f32[136,384]{1,0:T(8,128)S(1)} %get-tuple-element.117), channel_id=1, source_target_pairs={{0,4},{4,0},{8,12},{12,8},{16,20},{20,16},{24,28},{28,24},{1,5},{5... | collective-permute-start | bytes 626696 | tf_op jit(solution)/shard_map/ppermute | solution.py:912
  50.6 82.7 %copy-start = (f32[2048,384]{1,0:T(8,128)}, f32[2048,384]{1,0:T(8,128)S(1)}, u32[]{:S(2)}) copy-start(f32[2048,384]{1,0:T(8,128)S(1)} %get-tuple-element.121.gate) | copy-start | bytes 9437188
  50.7 6.4 %collective-permute-start.5 = (f32[136,384]{1,0:T(8,128)S(1)}, f32[136,384]{1,0:T(8,128)S(1)}, u32[]{:S(2)}, u32[]{:S(2)}) collective-permute-start(f32[136,384]{1,0:T(8,128)S(1)} %fusion.3), channel_id=1, source_target_pairs={{0,8},{4,12},{8,0},{12,4},{16,24},{20,28},{24,16},{28,20},{1,9},{5... | collective-permute-start | bytes 626696 | tf_op jit(solution)/shard_map/ppermute | solution.py:912
  57.3 10.9 %collective-permute-start.6 = (f32[136,384]{1,0:T(8,128)S(1)}, f32[136,384]{1,0:T(8,128)S(1)}, u32[]{:S(2)}, u32[]{:S(2)}) collective-permute-start(f32[136,384]{1,0:T(8,128)S(1)} %fusion.2), channel_id=1, source_target_pairs={{0,16},{4,20},{8,24},{12,28},{16,0},{20,4},{24,8},{28,12},{1,17},{... | collective-permute-start | bytes 626696 | tf_op jit(solution)/shard_map/ppermute | solution.py:912
  75.6 1.2 collective-permute-start.7
  76.7 3.7 %collective-permute-start.8 = (f32[1,2048]{1,0:T(1,128)S(1)}, f32[1,2048]{1,0:T(1,128)S(1)}, u32[]{:S(2)}, u32[]{:S(2)}) collective-permute-start(f32[1,2048]{1,0:T(1,128)S(1)} %add.82), channel_id=1, source_target_pairs={{0,2},{1,3},{2,0},{3,1},{4,6},{5,7},{6,4},{7,5},{8,10},{9,11},{10,... | collective-permute-start | bytes 24584 | tf_op jit(solution)/shard_map/ppermute | solution.py:912
  80.5 42.9 %copy-start.9 = (bf16[2048,768]{1,0:T(8,128)(2,1)S(1)}, bf16[2048,768]{1,0:T(8,128)(2,1)}, u32[]{:S(2)}) copy-start(bf16[2048,768]{1,0:T(8,128)(2,1)} %hid.5) | copy-start | bytes 9437188
  80.5 42.9 %copy-start.16 = (bf16[2048,768]{1,0:T(8,128)(2,1)S(1)}, bf16[2048,768]{1,0:T(8,128)(2,1)}, u32[]{:S(2)}) copy-start(bf16[2048,768]{1,0:T(8,128)(2,1)} %teacher.1) | copy-start | bytes 9437188
  87.0 36.4 %collective-permute-start.9 = (bf16[1024,768]{1,0:T(8,128)(2,1)S(1)}, bf16[1024,768]{1,0:T(8,128)(2,1)S(1)}, u32[]{:S(2)}, u32[]{:S(2)}) collective-permute-start(bf16[1024,768]{1,0:T(8,128)(2,1)S(1)} %shard_map.308.mine), channel_id=1, source_target_pairs={{0,2},{1,3},{2,0},{3,1},{4,6},{5,7},{6,4},{7,5},{8,10},{9,11},{10,... | collective-permute-start | bytes 4718600 | tf_op jit(solution)/shard_map/ppermute | solution.py:912
  89.8 3.7 %collective-permute-start = (f32[8,128]{1,0:T(8,128)S(1)}, f32[8,128]{1,0:T(8,128)S(1)}, u32[]{:S(2)}, u32[]{:S(2)}) collective-permute-start(f32[8,128]{1,0:T(8,128)S(1)} %broadcast_in_dim.27), channel_id=1, source_target_pairs={{0,4},{4,0},{8,12},{12,8},{16,20},{20,16},{24,28},{28,24},{1,5},{5... | collective-permute-start | bytes 12296 | tf_op jit(solution)/shard_map/ppermute | solution.py:912
  94.2 3.7 %collective-permute-start.1 = (f32[8,128]{1,0:T(8,128)S(1)}, f32[8,128]{1,0:T(8,128)S(1)}, u32[]{:S(2)}, u32[]{:S(2)}) collective-permute-start(f32[8,128]{1,0:T(8,128)S(1)} %broadcast_add_fusion), channel_id=1, source_target_pairs={{0,8},{4,12},{8,0},{12,4},{16,24},{20,28},{24,16},{28,20},{1,9},{5... | collective-permute-start | bytes 12296 | tf_op jit(solution)/shard_map/ppermute | solution.py:912
  98.5 4.6 %collective-permute-start.2 = (f32[8,128]{1,0:T(8,128)S(1)}, f32[8,128]{1,0:T(8,128)S(1)}, u32[]{:S(2)}, u32[]{:S(2)}) collective-permute-start(f32[8,128]{1,0:T(8,128)S(1)} %fusion.13), channel_id=1, source_target_pairs={{0,16},{4,20},{8,24},{12,28},{16,0},{20,4},{24,8},{28,12},{1,17},{... | collective-permute-start | bytes 12296 | tf_op jit(solution)/shard_map/ppermute | solution.py:912
  144.8 1.2 collective-permute-start.10
  145.9 3.7 %collective-permute-start.11 = (f32[1,2048]{1,0:T(1,128)S(1)}, f32[1,2048]{1,0:T(1,128)S(1)}, u32[]{:S(2)}, u32[]{:S(2)}) collective-permute-start(f32[1,2048]{1,0:T(1,128)S(1)} %add.84), channel_id=1, source_target_pairs={{0,2},{1,3},{2,0},{3,1},{4,6},{5,7},{6,4},{7,5},{8,10},{9,11},{10,... | collective-permute-start | bytes 24584 | tf_op jit(solution)/shard_map/ppermute | solution.py:912
  163.7 10.3 %collective-permute-start.12 = (f32[136,384]{1,0:T(8,128)S(1)}, f32[136,384]{1,0:T(8,128)S(1)}, u32[]{:S(2)}, u32[]{:S(2)}) collective-permute-start(f32[136,384]{1,0:T(8,128)S(1)} %get-tuple-element.138), channel_id=1, source_target_pairs={{0,4},{4,0},{8,12},{12,8},{16,20},{20,16},{24,28},{28,24},{1,5},{5... | collective-permute-start | bytes 626696 | tf_op jit(solution)/shard_map/ppermute | solution.py:912
  174.1 5.9 %collective-permute-start.13 = (f32[136,384]{1,0:T(8,128)S(1)}, f32[136,384]{1,0:T(8,128)S(1)}, u32[]{:S(2)}, u32[]{:S(2)}) collective-permute-start(f32[136,384]{1,0:T(8,128)S(1)} %fusion.1), channel_id=1, source_target_pairs={{0,8},{4,12},{8,0},{12,4},{16,24},{20,28},{24,16},{28,20},{1,9},{5... | collective-permute-start | bytes 626696 | tf_op jit(solution)/shard_map/ppermute | solution.py:912
  180.1 10.2 %collective-permute-start.14 = (f32[136,384]{1,0:T(8,128)S(1)}, f32[136,384]{1,0:T(8,128)S(1)}, u32[]{:S(2)}, u32[]{:S(2)}) collective-permute-start(f32[136,384]{1,0:T(8,128)S(1)} %fusion), channel_id=1, source_target_pairs={{0,16},{4,20},{8,24},{12,28},{16,0},{20,4},{24,8},{28,12},{1,17},{... | collective-permute-start | bytes 626696 | tf_op jit(solution)/shard_map/ppermute | solution.py:912
  190.5 27.0 %copy-start.37 = (f32[384,768]{1,0:T(8,128)S(1)}, f32[384,768]{1,0:T(8,128)}, u32[]{:S(2)}) copy-start(f32[384,768]{1,0:T(8,128)} %copy-done.36) | copy-start | bytes 3538948
  190.5 27.0 %copy-start.39 = (bf16[768,384]{1,0:T(8,128)(2,1)S(1)}, bf16[768,384]{1,0:T(8,128)(2,1)}, u32[]{:S(2)}) copy-start(bf16[768,384]{1,0:T(8,128)(2,1)} %wi.3) | copy-start | bytes 1769476
  190.5 27.0 %copy-start.41 = (bf16[768,384]{1,0:T(8,128)(2,1)S(1)}, bf16[768,384]{1,0:T(8,128)(2,1)}, u32[]{:S(2)}) copy-start(bf16[768,384]{1,0:T(8,128)(2,1)} %wg.3) | copy-start | bytes 1769476
  190.5 27.0 %copy-start.45 = (bf16[768,256]{1,0:T(8,128)(2,1)S(1)}, bf16[768,256]{1,0:T(8,128)(2,1)}, u32[]{:S(2)}) copy-start(bf16[768,256]{1,0:T(8,128)(2,1)} %wp.3) | copy-start | bytes 1179652
  221.2 100.9 %copy-start.15 = (bf16[2048,768]{1,0:T(8,128)(2,1)S(1)}, bf16[2048,768]{1,0:T(8,128)(2,1)}, u32[]{:S(2)}) copy-start(bf16[2048,768]{1,0:T(8,128)(2,1)} %copy-done.14) | copy-start | bytes 9437188
  (45 other events, 266.6 us)

commit v4 on v3

--- a/solution.py
+++ b/solution.py
@@ -81,7 +81,7 @@
 
 def project_kernel(
     idx, starts, hid, halo, tail, gain, wi, wp, ws, conv_i, conv_p, bias_i, bias_p, sbias, dlog,
-    low, in_i, in_p, pre_i, pre_p, aux, halo_i, halo_p, sloc, pkl, fin, wide_i, wide_p, state, decay,
+    low, in_i, in_p, pre_i, pre_p, aux, halo_low, halo_i, halo_p, sloc, pkl, fin, wide_i, wide_p, state, decay,
 ):
     step = pl.program_id(0)
     edge = tail.shape[0]
@@ -107,6 +107,7 @@
 
     @pl.when(step == 0)
     def _():
+        halo_low[...] = lowered[:edge]
         halo_i[...] = inner[:edge]
         halo_p[...] = pair[:edge]
 
@@ -437,29 +438,265 @@
     return total, edge
 
 
-def scan_back_kernel(
-    idx, d_scaled, d_maps, pre_i, pre_p, in_i, in_p, halo_i, halo_p, aux, gloc, pkl, gin, states, d_mixer, mixer, skip, dlog,
-    conv_i, conv_p, d_inner, d_step, d_pair, edge, tail, small, small_p, heads, *shifted,
+def device_copy(src, dst, sems, slot, to):
+    return pltpu.make_async_remote_copy(
+        src_ref=src, dst_ref=dst, send_sem=sems[0].at[slot], recv_sem=sems[1].at[slot],
+        device_id=to, device_id_type=pl.DeviceIdType.MESH,
+    )
+
+
+def loop(start, stop, body):
+    def run(d, carry):
+        body(d)
+        return carry
+
+    lax.fori_loop(start, stop, run, 0)
+
+
+def rows_at(ref, index, size):
+    return ref.at[pl.ds(pl.multiple_of(index * size, size), size)]
+
+
+class SeqSum:
+    def __init__(self, source, first, land1, second, land2, done, sems):
+        self.source, self.first, self.land1, self.second, self.land2, self.done = source, first, land1, second, land2, done
+        self.sems = [sems[i : i + 2] for i in range(0, 8, 2)]
+        self.wire = first.dtype
+        self.members = land2.shape[0]
+        self.piece = first.shape[0] // self.members
+        me = lax.axis_index("seq")
+        self.side, self.place = lax.rem(me, 2), me // 2
+        self.partner = {"seq": me + 1 - 2 * self.side}
+
+    def half(self, ref, side):
+        return rows_at(ref, side, self.members * self.piece)
+
+    def member(self, d):
+        return lax.rem(self.place + d, self.members)
+
+    def to_member(self, d):
+        return {"seq": 2 * self.member(d) + self.side}
+
+    def halve(self):
+        return device_copy(self.first, self.land1, self.sems[0], 0, self.partner)
+
+    def scatter(self, d):
+        src = rows_at(self.second, self.member(d), self.piece)
+        return device_copy(src, self.land2.at[d], self.sems[1], d, self.to_member(d))
+
+    def part(self, place):
+        return rows_at(self.done, self.side * self.members + place, self.piece)
+
+    def gather(self, d):
+        ref = self.part(self.place)
+        return device_copy(ref, ref, self.sems[2], d, self.to_member(d))
+
+    def gathered(self, d):
+        ref = self.part(lax.rem(self.place + self.members - d, self.members))
+        return device_copy(ref, ref, self.sems[2], d, self.partner)
+
+    def widen(self, side):
+        ref = self.half(self.done, side)
+        return device_copy(ref, ref, self.sems[3], 0, self.partner)
+
+    def begin(self):
+        self.first[...] = self.half(self.source, 1 - self.side)[...].astype(self.wire)
+        self.halve().start()
+
+    def pass_on(self):
+        self.halve().wait_recv()
+        self.second[...] = (self.half(self.source, self.side)[...] + self.land1[...].astype(F32)).astype(self.wire)
+        loop(1, self.members, lambda d: self.scatter(d).start())
+
+    def finish(self):
+        own = rows_at(self.source, self.side * self.members + self.place, self.piece)[...]
+        own = own + rows_at(self.land1, self.place, self.piece)[...].astype(F32)
+
+        def add(d, total):
+            self.scatter(d).wait_recv()
+            return total + self.land2[d].astype(F32)
+
+        self.part(self.place)[...] = lax.fori_loop(1, self.members, add, own).astype(self.wire)
+        loop(1, self.members, lambda d: self.gather(d).start())
+
+    def collect(self):
+        loop(1, self.members, lambda d: self.gathered(d).wait_recv())
+        self.widen(self.side).start()
+
+    def store(self, out):
+        self.half(out, self.side)[...] = self.half(self.done, self.side)[...].astype(F32)
+        self.widen(1 - self.side).wait_recv()
+        self.half(out, 1 - self.side)[...] = self.half(self.done, 1 - self.side)[...].astype(F32)
+
+    def drain(self):
+        self.halve().wait_send()
+        self.widen(self.side).wait_send()
+
+        def both(d):
+            self.scatter(d).wait_send()
+            self.gather(d).wait_send()
+
+        loop(1, self.members, both)
+
+    @staticmethod
+    def scratch(rows, lanes, wire, size):
+        members = size // 2
+        half = pltpu.VMEM((members * rows, lanes), wire)
+        dma = pltpu.SemaphoreType.DMA
+        return [half, half, half, pltpu.VMEM((members, rows, lanes), wire), pltpu.VMEM((2 * members * rows, lanes), wire)] + [
+            dma((1,)), dma((1,)), dma((members,)), dma((members,)), dma((members,)), dma((members,)), dma((1,)), dma((1,)),
+        ]
+
+
+SUM_REFS = 13
+
+
+class HeadSum:
+    def __init__(self, source, out, fold1, half, fold2, quarter, sems):
+        self.source, self.out, self.fold1, self.held, self.fold2, self.quarter = source, out, fold1, half, fold2, quarter
+        self.sems = [sems[i : i + 2] for i in range(0, 8, 2)]
+        self.rows = source.shape[0]
+        head = lax.axis_index("head")
+        self.core, self.plane = lax.rem(head, 2), head // 2
+        self.beside, self.across = {"head": head + 1 - 2 * self.core}, {"head": head + 2 - 4 * self.plane}
+
+    def fold_core(self):
+        return device_copy(rows_at(self.source, 1 - self.core, self.rows // 2), self.fold1, self.sems[0], 0, self.beside)
+
+    def fold_plane(self):
+        return device_copy(rows_at(self.held, 1 - self.plane, self.rows // 4), self.fold2, self.sems[1], 0, self.across)
+
+    def spread_plane(self, plane):
+        ref = rows_at(self.out, 2 * self.core + plane, self.rows // 4)
+        return device_copy(ref, ref, self.sems[2], 0, self.across)
+
+    def spread_core(self, core):
+        ref = rows_at(self.out, core, self.rows // 2)
+        return device_copy(ref, ref, self.sems[3], 0, self.beside)
+
+    def fold(self):
+        self.fold_core().wait_recv()
+        self.held[...] = rows_at(self.source, self.core, self.rows // 2)[...] + self.fold1[...]
+        self.fold_plane().start()
+
+    def settle(self):
+        self.fold_plane().wait_recv()
+        self.quarter[...] = jnp.zeros_like(self.quarter)
+        self.quarter[: self.rows // 4] = rows_at(self.held, self.plane, self.rows // 4)[...] + self.fold2[...]
+
+    def spread(self, total):
+        rows_at(self.out, 2 * self.core + self.plane, self.rows // 4)[...] = total[: self.rows // 4]
+        self.spread_plane(self.plane).start()
+
+    def spread_more(self):
+        self.spread_plane(1 - self.plane).wait_recv()
+        self.spread_core(self.core).start()
+
+    def finish(self):
+        self.spread_core(1 - self.core).wait_recv()
+        self.fold_core().wait_send()
+        self.fold_plane().wait_send()
+        self.spread_plane(self.plane).wait_send()
+        self.spread_core(self.core).wait_send()
+
+    @staticmethod
+    def scratch(rows, lanes, padded_rows):
+        dma = pltpu.SemaphoreType.DMA
+        shapes = [(rows // 2, lanes), (rows // 2, lanes), (rows // 4, lanes), (padded_rows, lanes)]
+        return [pltpu.VMEM(shape, F32) for shape in shapes] + [dma((1,))] * 8
+
+
+HEAD_REFS = 12
+
+
+def finale_kernel(
+    d_scaled, d_maps, pre_i, pre_p, in_i, in_p, halo_low, halo_i, halo_p, aux, gloc, pkl, gin, states, d_mixer, mixer, skip, dlog,
+    conv_i, conv_p, low, d_gate, wg, wi, ws, wp, hid, d_out, gain, error, g_wo, g_wg, g_gain,
+    grad_all, sums, out_wo, out_wg, out_wi, out_pack, out_wp, out_small,
+    shift_i0, shift_i1, shift_i2, shift_p0, shift_p1, shift_p2, small, small_p, heads,
+    parts, land, mine, other, row, row_land, g_wi, g_ws, pack, g_wp, pair_small, sum_small, sum_wp, spread_wp, spread_small,
+    grad_own, grad_other, edge, edge_core, edge_plane, edge_ahead,
+    core_send, core_land, x_send, x_land, edge_send, edge_land, grad_send, grad_land, row_send, row_arrive, *more,
 ):
+    shifted = (shift_i0, shift_i1, shift_i2, shift_p0, shift_p1, shift_p2)
     step = pl.program_id(0)
     blocks = pl.num_programs(0)
+    half = blocks // 2
     first, last = step == 0, step == blocks - 1
-    width = mixer.shape[1]
+    seq, devices = lax.axis_index("seq"), lax.axis_size("seq")
+    head, core = lax.axis_index("head"), core_bit()
+    width = wi.shape[1]
+    model = low.shape[1]
+    behind, ahead = lax.rem(seq + devices - 1, devices), lax.rem(seq + 1, devices)
+    group = 2 * devices
+    me = 2 * seq + core
+    beside, across = {"head": core_peer()}, {"head": lax.rem(head + 2, 4)}
+    summing = len(more) > 0
+
+    more = list(more)
+
+    def take(number):
+        taken = more[:number]
+        del more[:number]
+        return taken
+
+    seq_sums, wide = [], []
+    if summing:
+        head_parts = []
+        for source, out in ((g_wp, spread_wp), (pair_small, spread_small)):
+            refs = take(HEAD_REFS)
+            head_parts.append(HeadSum(source, out, *refs[:4], refs[4:]))
+        for source in (g_wo, g_wg, g_wi, pack, head_parts[0].quarter, head_parts[1].quarter):
+            refs = take(SUM_REFS)
+            seq_sums.append(SeqSum(source, *refs[:5], refs[5:]))
+        s_wo, s_wg, s_wi, s_pack, s_wp, s_small = seq_sums
+        wide = list(zip(head_parts, (s_wp, s_small), (sum_wp, sum_small)))
+
+    def device(distance):
+        to = lax.rem(me + distance, group)
+        return {"seq": to // 2, "head": head - core + lax.rem(to, 2)}
+
+    def hand(distance):
+        return device_copy(row, row_land.at[me], (row_send, row_arrive), distance, device(distance))
+
+    def edge_copy(slot, landing, to):
+        return device_copy(edge.at[slot], landing, (edge_send, edge_land), slot, to)
+
+    def core_copy(slot):
+        return device_copy(parts.at[slot], land.at[slot], (core_send, core_land), slot, beside)
+
+    def x_copy(slot):
+        return device_copy(mine.at[slot], other.at[slot], (x_send, x_land), slot, across)
+
+    def grad_copy(slot):
+        return device_copy(grad_own.at[slot], grad_other.at[slot], (grad_send, grad_land), slot, beside)
 
     @pl.when(first)
     def _():
-        small[...] = jnp.zeros_like(small)
-        small_p[...] = jnp.zeros_like(small_p)
-        heads[...] = jnp.zeros_like(heads)
-
-    base = idx[1] + (blocks - 1 - step) * BLOCK
+        barrier = pltpu.get_barrier_semaphore()
+
+        def greet(to):
+            pl.semaphore_signal(barrier, inc=1, device_id=to, device_id_type=pl.DeviceIdType.MESH)
+
+        loop(1, group, lambda d: greet(device(d)))
+        greet(across)
+        for ref in (g_wi, g_ws, pack, g_wp, pair_small, small, small_p, heads):
+            ref[...] = jnp.zeros_like(ref)
+        row[:1] = jnp.zeros_like(row[:1])
+        row[1:] = error[...]
+        pl.semaphore_wait(barrier, group)
+        if summing:
+            s_wo.begin()
+            s_wg.begin()
+
+    base = seq * (blocks * BLOCK) + (blocks - 1 - step) * BLOCK
     maps, slope_p = silu_parts(pre_p[...])
     values, slope = silu_parts(pre_i[...])
     dy = d_mixer[...]
     upper = triangle(True)
     lane = lax.broadcasted_iota(jnp.int32, (CHUNK, LANES), 1)
     grown = jnp.exp(dlog[...])
-    pieces, pieces_p = [], []
+    pieces, pieces_p, pieces_s = [], [], []
     for c in range(BLOCK // CHUNK):
         at = slice(c * CHUNK, (c + 1) * CHUNK)
         table = aux[at, :]
@@ -483,7 +720,7 @@
         d_logs = jnp.dot(upper, d_cum, precision=HIGHEST, preferred_element_type=F32) + after
         d_raw = (head_sums(total * values[at]) - grown * d_logs) * pltpu.roll(table, LANES - RATE, 1)
         d_raw = jnp.where(lane < 8, d_raw, 0.0)
-        d_step[at, :] = d_raw.astype(BF16)
+        pieces_s.append(d_raw.astype(BF16))
         d_decay = jnp.where(lane < 8, -d_logs * table * grown, 0.0)
         heads[0:1] += jnp.sum(d_raw, axis=0, keepdims=True)
         heads[1:2] += jnp.sum(d_decay, axis=0, keepdims=True)
@@ -499,382 +736,162 @@
     whole_p, outer_p = conv_back(
         grad_p, within, in_p[...].astype(F32), halo_p[8:].astype(F32), conv_p, shifted[3:], first, last, small_p
     )
-    d_inner[...] = whole.astype(BF16)
-    d_pair[...] = whole_p
-    edge[...] = jnp.concatenate([outer, outer_p], axis=1)
-
-    @pl.when(first)
-    def _():
-        tail[...] = jnp.concatenate([whole[BLOCK - 16 :], whole_p[BLOCK - 16 :]], axis=1)
-
-
-def dot_split(a, b, da=1, db=0):
-    high, low = halves(b)
-    return dot(a, high, da, db) + dot(a, low, da, db)
-
-
-def device_copy(src, dst, sems, slot, to):
-    return pltpu.make_async_remote_copy(
-        src_ref=src, dst_ref=dst, send_sem=sems[0].at[slot], recv_sem=sems[1].at[slot],
-        device_id=to, device_id_type=pl.DeviceIdType.MESH,
-    )
-
-
-def loop(start, stop, body):
-    def run(d, carry):
-        body(d)
-        return carry
-
-    lax.fori_loop(start, stop, run, 0)
-
-
-def rows_at(ref, index, size):
-    return ref.at[pl.ds(pl.multiple_of(index * size, size), size)]
-
-
-class SeqSum:
-    def __init__(self, source, first, land1, second, land2, done, sems):
-        self.source, self.first, self.land1, self.second, self.land2, self.done = source, first, land1, second, land2, done
-        self.sems = [sems[i : i + 2] for i in range(0, 8, 2)]
-        self.wire = first.dtype
-        self.members = land2.shape[0]
-        self.piece = first.shape[0] // self.members
-        me = lax.axis_index("seq")
-        self.side, self.place = lax.rem(me, 2), me // 2
-        self.partner = {"seq": me + 1 - 2 * self.side}
-
-    def half(self, ref, side):
-        return rows_at(ref, side, self.members * self.piece)
-
-    def member(self, d):
-        return lax.rem(self.place + d, self.members)
-
-    def to_member(self, d):
-        return {"seq": 2 * self.member(d) + self.side}
-
-    def halve(self):
-        return device_copy(self.first, self.land1, self.sems[0], 0, self.partner)
-
-    def scatter(self, d):
-        src = rows_at(self.second, self.member(d), self.piece)
-        return device_copy(src, self.land2.at[d], self.sems[1], d, self.to_member(d))
-
-    def part(self, place):
-        return rows_at(self.done, self.side * self.members + place, self.piece)
-
-    def gather(self, d):
-        ref = self.part(self.place)
-        return device_copy(ref, ref, self.sems[2], d, self.to_member(d))
-
-    def gathered(self, d):
-        ref = self.part(lax.rem(self.place + self.members - d, self.members))
-        return device_copy(ref, ref, self.sems[2], d, self.partner)
-
-    def widen(self, side):
-        ref = self.half(self.done, side)
-        return device_copy(ref, ref, self.sems[3], 0, self.partner)
-
-    def begin(self):
-        self.first[...] = self.half(self.source, 1 - self.side)[...].astype(self.wire)
-        self.halve().start()
-
-    def pass_on(self):
-        self.halve().wait_recv()
-        self.second[...] = (self.half(self.source, self.side)[...] + self.land1[...].astype(F32)).astype(self.wire)
-        loop(1, self.members, lambda d: self.scatter(d).start())
-
-    def finish(self):
-        own = rows_at(self.source, self.side * self.members + self.place, self.piece)[...]
-        own = own + rows_at(self.land1, self.place, self.piece)[...].astype(F32)
-
-        def add(d, total):
-            self.scatter(d).wait_recv()
-            return total + self.land2[d].astype(F32)
-
-        self.part(self.place)[...] = lax.fori_loop(1, self.members, add, own).astype(self.wire)
-        loop(1, self.members, lambda d: self.gather(d).start())
-
-    def collect(self):
-        loop(1, self.members, lambda d: self.gathered(d).wait_recv())
-        self.widen(self.side).start()
-
-    def store(self, out):
-        self.half(out, self.side)[...] = self.half(self.done, self.side)[...].astype(F32)
-        self.widen(1 - self.side).wait_recv()
-        self.half(out, 1 - self.side)[...] = self.half(self.done, 1 - self.side)[...].astype(F32)
-
-    def drain(self):
-        self.halve().wait_send()
-        self.widen(self.side).wait_send()
-
-        def both(d):
-            self.scatter(d).wait_send()
-            self.gather(d).wait_send()
-
-        loop(1, self.members, both)
-
-    @staticmethod
-    def scratch(rows, lanes, wire, size):
-        members = size // 2
-        half = pltpu.VMEM((members * rows, lanes), wire)
-        dma = pltpu.SemaphoreType.DMA
-        return [half, half, half, pltpu.VMEM((members, rows, lanes), wire), pltpu.VMEM((2 * members * rows, lanes), wire)] + [
-            dma((1,)), dma((1,)), dma((members,)), dma((members,)), dma((members,)), dma((members,)), dma((1,)), dma((1,)),
-        ]
-
-
-SUM_REFS = 13
-
-
-class HeadSum:
-    def __init__(self, source, out, fold1, half, fold2, quarter, sems):
-        self.source, self.out, self.fold1, self.held, self.fold2, self.quarter = source, out, fold1, half, fold2, quarter
-        self.sems = [sems[i : i + 2] for i in range(0, 8, 2)]
-        self.rows = source.shape[0]
-        head = lax.axis_index("head")
-        self.core, self.plane = lax.rem(head, 2), head // 2
-        self.beside, self.across = {"head": head + 1 - 2 * self.core}, {"head": head + 2 - 4 * self.plane}
-
-    def fold_core(self):
-        return device_copy(rows_at(self.source, 1 - self.core, self.rows // 2), self.fold1, self.sems[0], 0, self.beside)
-
-    def fold_plane(self):
-        return device_copy(rows_at(self.held, 1 - self.plane, self.rows // 4), self.fold2, self.sems[1], 0, self.across)
-
-    def spread_plane(self, plane):
-        ref = rows_at(self.out, 2 * self.core + plane, self.rows // 4)
-        return device_copy(ref, ref, self.sems[2], 0, self.across)
-
-    def spread_core(self, core):
-        ref = rows_at(self.out, core, self.rows // 2)
-        return device_copy(ref, ref, self.sems[3], 0, self.beside)
-
-    def fold(self):
-        self.fold_core().wait_recv()
-        self.held[...] = rows_at(self.source, self.core, self.rows // 2)[...] + self.fold1[...]
-        self.fold_plane().start()
-
-    def settle(self):
-        self.fold_plane().wait_recv()
-        self.quarter[...] = jnp.zeros_like(self.quarter)
-        self.quarter[: self.rows // 4] = rows_at(self.held, self.plane, self.rows // 4)[...] + self.fold2[...]
-
-    def spread(self, total):
-        rows_at(self.out, 2 * self.core + self.plane, self.rows // 4)[...] = total[: self.rows // 4]
-        self.spread_plane(self.plane).start()
-
-    def spread_more(self):
-        self.spread_plane(1 - self.plane).wait_recv()
-        self.spread_core(self.core).start()
-
-    def finish(self):
-        self.spread_core(1 - self.core).wait_recv()
-        self.fold_core().wait_send()
-        self.fold_plane().wait_send()
-        self.spread_plane(self.plane).wait_send()
-        self.spread_core(self.core).wait_send()
-
-    @staticmethod
-    def scratch(rows, lanes, padded_rows):
-        dma = pltpu.SemaphoreType.DMA
-        shapes = [(rows // 2, lanes), (rows // 2, lanes), (rows // 4, lanes), (padded_rows, lanes)]
-        return [pltpu.VMEM(shape, F32) for shape in shapes] + [dma((1,))] * 8
-
-
-HEAD_REFS = 12
-
-
-def dot_split(a, b, da=1, db=0):
-    high, low = halves(b)
-    return dot(a, high, da, db) + dot(a, low, da, db)
-
-
-def tail_kernel(
-    low, d_gate, d_inner, d_step, d_pair, wg, wi, ws, wp, edge, tail, hid, d_out, gain, error, g_wo, g_wg, small_i, g_gain,
-    small_p, heads,
-    grad, sums, out_wo, out_wg, out_wi, out_pack, out_wp, out_small,
-    block_i, block_p, after, away, land, mine, other, row, row_land, g_wi, g_ws, pack, g_wp, pair_small, sum_small, sum_wp,
-    spread_wp, spread_small, grad_own, grad_other,
-    core_send, core_land, x_send, x_land, edge_send, edge_land, grad_send, grad_land, row_send, row_arrive, *more,
-):
-    step = pl.program_id(0)
-    blocks = pl.num_programs(0)
-    half = blocks // 2
-    seq, devices = lax.axis_index("seq"), lax.axis_size("seq")
-    head, core = lax.axis_index("head"), core_bit()
-    width = wi.shape[1]
-    behind = lax.rem(seq + devices - 1, devices)
-    group = 2 * devices
-    me = 2 * seq + core
-    beside, across = {"head": core_peer()}, {"head": lax.rem(head + 2, 4)}
-
-    more = list(more)
-
-    def take(number):
-        taken = more[:number]
-        del more[:number]
-        return taken
-
-    head_sums_ = []
-    for source, out in ((g_wp, spread_wp), (pair_small, spread_small)):
-        refs = take(HEAD_REFS)
-        head_sums_.append(HeadSum(source, out, *refs[:4], refs[4:]))
-    sources = [g_wo, g_wg, g_wi, pack, head_sums_[0].quarter, head_sums_[1].quarter]
-    seq_sums = []
-    for source in sources:
-        refs = take(SUM_REFS)
-        seq_sums.append(SeqSum(source, *refs[:5], refs[5:]))
-    s_wo, s_wg, s_wi, s_pack, s_wp, s_small = seq_sums
-    wide = list(zip(head_sums_, (s_wp, s_small), (sum_wp, sum_small)))
-
-    def device(distance):
-        to = lax.rem(me + distance, group)
-        return {"seq": to // 2, "head": head - core + lax.rem(to, 2)}
-
-    def hand(distance):
-        return device_copy(row, row_land.at[me], (row_send, row_arrive), distance, device(distance))
-
-    moved = device_copy(edge, after, (edge_send, edge_land), 0, {"seq": behind})
-
-    def core_copy(slot):
-        return device_copy(away.at[slot], land.at[slot], (core_send, core_land), slot, beside)
-
-    def x_copy(slot):
-        return device_copy(mine.at[slot], other.at[slot], (x_send, x_land), slot, across)
-
-    def grad_copy(slot):
-        return device_copy(grad_own.at[slot], grad_other.at[slot], (grad_send, grad_land), slot, beside)
-
-    @pl.when(step == 0)
-    def _():
-        barrier = pltpu.get_barrier_semaphore()
-
-        def greet(to):
-            pl.semaphore_signal(barrier, inc=1, device_id=to, device_id_type=pl.DeviceIdType.MESH)
-
-        loop(1, group, lambda d: greet(device(d)))
-        greet(across)
-        for ref in (g_wi, g_ws, pack, g_wp, pair_small):
-            ref[...] = jnp.zeros_like(ref)
-        pl.semaphore_wait(barrier, group)
-        moved.start()
-        s_wo.begin()
-        s_wg.begin()
-
-    block_i[...] = d_inner[...]
-    block_p[...] = d_pair[...]
-    block = lax.rem(step + half * (1 - core), blocks)
-
-    @pl.when(block == blocks - 1)
-    def _():
-        moved.wait_recv()
-        extra = jnp.where(seq == devices - 1, 0.0, after[...])
-        fixed = jnp.concatenate([tail[:8], tail[8:] + extra], axis=0)
-        block_i[BLOCK - 16 :] = fixed[:, :width].astype(BF16)
-        block_p[BLOCK - 16 :] = fixed[:, width:]
-
-    part = dot(d_gate[...], wg[...], 1, 1) + dot(block_i[...], wi[...], 1, 1) + dot(d_step[...], ws[...], 1, 1)
-    high, rest = halves(block_p[...])
+
+    inner = whole.astype(BF16)
+    d_step = jnp.concatenate(pieces_s, axis=0)
+    part = dot(d_gate[...], wg[...], 1, 1) + dot(inner, wi[...], 1, 1) + dot(d_step, ws[...], 1, 1)
+    high, rest = halves(whole_p)
     part = part + (dot(high, wp[...], 1, 1) + dot(rest, wp[...], 1, 1))
-
-    @pl.when(step < half)
-    def _():
-        away[step] = part.astype(away.dtype)
-        core_copy(step).start()
-
-    @pl.when(step >= half)
-    def _():
-        core_copy(step - half).wait_recv()
-        mine[step - half] = (part + land[step - half].astype(F32)).astype(BF16)
-        x_copy(step - half).start()
-
-    g_ws[...] += dot(d_step[...], low[...], 0, 0)[:8]
-    g_wp[...] += dot_split(low[...], block_p[...], 0, 0)
-    g_wi[: low.shape[1]] += dot(low[...], block_i[...], 0, 0)
-
-    def norm_back(slot):
-        x_copy(slot).wait_recv()
-        at = pl.ds(slot * BLOCK, BLOCK)
-        d_low = mine[slot].astype(F32) + other[slot].astype(F32)
-        rows = hid[at, :].astype(F32)
+    upper = (step < half).astype(jnp.int32)
+    slot = half - 1 - lax.rem(step, half)
+    own = upper == core
+
+    def settle(at):
+        core_copy(at).wait_recv()
+        mine[at] = (parts[at].astype(F32) + land[at].astype(F32)).astype(BF16)
+        x_copy(at).start()
+
+    @pl.when((step > 0) & ((step - 1 < half).astype(jnp.int32) == core))
+    def _():
+        settle(half - 1 - lax.rem(step - 1, half))
+
+    @pl.when((step >= half) & (core == 0))
+    def _():
+        core_copy(slot).wait_send()
+
+    parts[slot] = part.astype(parts.dtype)
+
+    @pl.when(jnp.logical_not(own))
+    def _():
+        core_copy(slot).start()
+
+    g_ws[...] += dot(d_step, low[...], 0, 0)[:8]
+    g_wp[...] += dot(low[...], high, 0, 0) + dot(low[...], rest, 0, 0)
+    g_wi[:model] += dot(low[...], inner, 0, 0)
+
+    def norm_back(at):
+        x_copy(at).wait_recv()
+        block_rows = pl.ds(at * BLOCK, BLOCK)
+        d_low = mine[at].astype(F32) + other[at].astype(F32)
+        if at == half - 1:
+            edge_copy(2, edge_ahead, {"seq": behind}).wait_recv()
+            there = ((core == 1) & (seq < devices - 1)).astype(F32)
+            d_low = jnp.concatenate([d_low[: BLOCK - 8], d_low[BLOCK - 8 :] + there * edge_ahead[...]], axis=0)
+        rows = hid[block_rows, :].astype(F32)
         scale = lax.rsqrt(jnp.mean(rows * rows, axis=1, keepdims=True) + EPSILON)
         row[:1] += jnp.sum(d_low * rows * scale, axis=0, keepdims=True)
         scaled = d_low * gain[...]
         pull = jnp.mean(scaled * rows, axis=1, keepdims=True) * (scale * scale * scale)
-        block = (d_out[at, :] + scale * scaled - rows * pull).astype(BF16)
-        grad_own[slot] = block
-        grad_copy(slot).start()
-        rows_at(grad, core * half + slot, BLOCK)[...] = block
-
-    @pl.when(step == half + 1)
-    def _():
-        s_wo.pass_on()
-
-    @pl.when(step == blocks - 1)
-    def _():
-        s_wi.begin()
-        pack[:6] = small_i[:6]
+        block = (d_out[block_rows, :] + scale * scaled - rows * pull).astype(BF16)
+        grad_own[at] = block
+        grad_copy(at).start()
+        rows_at(grad_all, core * half + at, BLOCK)[...] = block
+
+    if summing:
+
+        @pl.when(step == half)
+        def _():
+            s_wo.pass_on()
+
+        @pl.when(step == blocks - 2)
+        def _():
+            s_wg.pass_on()
+
+    @pl.when(last)
+    def _():
+        before = jnp.concatenate([jnp.zeros_like(outer), outer], axis=0).astype(BF16)
+        g_wi[:model] += dot(halo_low[...], before, 0, 0)
+        before_p = jnp.concatenate([jnp.zeros_like(outer_p), outer_p], axis=0)
+        high_p, rest_p = halves(before_p)
+        g_wp[...] += dot(halo_low[...], high_p, 0, 0) + dot(halo_low[...], rest_p, 0, 0)
+        edge_part = dot(before, wi[...], 1, 1) + (dot(high_p, wp[...], 1, 1) + dot(rest_p, wp[...], 1, 1))
+        edge[0] = edge_part[8:]
+        edge_copy(0, edge_core, beside).start()
+        pack[:6] = small[:6]
         pack[6:7] = g_gain[...]
         pack[8:16] = g_ws[:, :width]
         pack[16:24] = g_ws[:, width:]
         pack[24:32, : heads.shape[1]] = heads[...]
         pair_small[:8] = small_p[...]
-        for h_sum, _, _ in wide:
-            h_sum.fold_core().start()
-        row[:1] = jnp.zeros_like(row[:1])
-        row[1:] = error[...]
-        s_pack.begin()
-        s_wg.pass_on()
-        for h_sum, _, _ in wide:
-            h_sum.fold()
-        s_wo.finish()
-        norm_back(0)
-        s_wi.pass_on()
-        s_pack.pass_on()
-        s_wg.finish()
-        norm_back(1)
-        s_wo.collect()
-        s_wi.finish()
-        s_pack.finish()
-        norm_back(2)
-        s_wg.collect()
-        norm_back(3)
-        loop(1, group, lambda d: hand(d).start())
+        if summing:
+            for h_sum, _, _ in wide:
+                h_sum.fold_core().start()
+            s_wi.begin()
+            s_pack.begin()
+
+        @pl.when(core == 0)
+        def _():
+            settle(0)
+
+        if summing:
+            for h_sum, _, _ in wide:
+                h_sum.fold()
+        edge_copy(0, edge_core, beside).wait_recv()
+        edge[1] = edge[0] + edge_core[...]
+        edge_copy(1, edge_plane, across).start()
+        if summing:
+            s_wo.finish()
+            s_wi.pass_on()
+            s_wg.finish()
+            s_pack.pass_on()
+        edge_copy(1, edge_plane, across).wait_recv()
+        edge[2] = edge[1] + edge_plane[...]
+        edge_copy(2, edge_ahead, {"seq": behind}).start()
         for h_sum, s_sum, _ in wide:
             h_sum.settle()
             s_sum.begin()
-        s_wi.collect()
+        norm_back(2)
+        norm_back(1)
+        if summing:
+            s_wo.collect()
+            s_wi.finish()
+            s_pack.finish()
         for _, s_sum, _ in wide:
             s_sum.pass_on()
-        s_wo.store(out_wo)
-        s_pack.collect()
-        for _, s_sum, _ in wide:
-            s_sum.finish()
-        s_wg.store(out_wg)
-        for _, s_sum, _ in wide:
-            s_sum.collect()
-        s_wi.store(out_wi)
-        for h_sum, s_sum, total in wide:
-            s_sum.store(total)
-            h_sum.spread(total)
-        s_pack.store(out_pack)
-        for h_sum, _, _ in wide:
-            h_sum.spread_more()
+        norm_back(0)
+        norm_back(3)
+        loop(1, group, lambda d: hand(d).start())
+        if summing:
+            s_wg.collect()
+            for _, s_sum, _ in wide:
+                s_sum.finish()
+            s_wo.store(out_wo)
+            for _, s_sum, _ in wide:
+                s_sum.collect()
+            s_wi.collect()
+            s_pack.collect()
+            for h_sum, s_sum, total in wide:
+                s_sum.store(total)
+                h_sum.spread(total)
+            s_wg.store(out_wg)
+            for h_sum, _, _ in wide:
+                h_sum.spread_more()
+            s_wi.store(out_wi)
+            s_pack.store(out_pack)
+            for (h_sum, _, _), out in zip(wide, (out_wp, out_small)):
+                h_sum.finish()
+                out[...] = h_sum.out[...]
+            for s_sum in seq_sums:
+                s_sum.drain()
+        else:
+            for out, ref in (
+                (out_wo, g_wo), (out_wg, g_wg), (out_wi, g_wi), (out_pack, pack), (out_wp, g_wp), (out_small, pair_small),
+            ):
+                out[...] = ref[...]
         row_land[me] = row[...]
         loop(1, group, lambda d: hand(d).wait())
         sums[...] = lax.fori_loop(1, group, lambda d, total: total + row_land[d], row_land[0])
-        for (h_sum, _, _), out in zip(wide, (out_wp, out_small)):
-            h_sum.finish()
-            out[...] = h_sum.out[...]
-        for s_sum in seq_sums:
-            s_sum.drain()
-        moved.wait_send()
-
-        def drain(slot):
-            core_copy(slot).wait_send()
-            x_copy(slot).wait_send()
-            grad_copy(slot).wait()
-            rows_at(grad, (1 - core) * half + slot, BLOCK)[...] = grad_other[slot]
+        for at, to in enumerate((beside, across, {"seq": behind})):
+            edge_copy(at, edge_core, to).wait_send()
+
+        @pl.when(core == 1)
+        def _():
+            loop(0, half, lambda at: core_copy(at).wait_send())
+
+        def drain(at):
+            x_copy(at).wait_send()
+            grad_copy(at).wait()
+            rows_at(grad_all, (1 - core) * half + at, BLOCK)[...] = grad_other[at]
 
         loop(0, half, drain)
 
@@ -1001,7 +1018,7 @@
     swap_scratch = [pltpu.VMEM((half, BLOCK, model), F32)] * 2 + [dma((half,))] * 2
 
     halo_block = ((edge_rows, model), lambda i, *_: (jnp.maximum(i * (BLOCK // edge_rows) - 1, 0), 0))
-    (low, in_i, in_p, pre_i, pre_p, aux, halo_i, halo_p, sloc, pkl, fin) = call(
+    (low, in_i, in_p, pre_i, pre_p, aux, halo_low, halo_i, halo_p, sloc, pkl, fin) = call(
         project_kernel,
         blocks,
         [
@@ -1012,7 +1029,7 @@
         [
             ((rows, model), BF16, *by(model)), ((rows, width), BF16, *by(width)), ((rows, pair_width), BF16, *by(pair_width)),
             ((rows, width), F32, *by(width)), ((rows, pair_width), F32, *by(pair_width)), ((rows, LANES), F32, *by(LANES)),
-            ((edge_rows, width), BF16, *whole), ((edge_rows, pair_width), BF16, *whole),
+            ((edge_rows, model), BF16, *whole), ((edge_rows, width), BF16, *whole), ((edge_rows, pair_width), BF16, *whole),
             ((chunks, CHUNK, width), F32, *grid3(CHUNK)), ((chunks, 8, width), F32, *grid3(8)),
             ((CHUNK + 8, width), F32, *whole),
         ],
@@ -1108,71 +1125,60 @@
         [((rows, width), F32, *by(width)), ((rows, pair_width), F32, *by(pair_width)), ((model, width), F32, *whole)],
         prefetch=1, flops=6e9, moved=2e7,
     )
-    both = width + pair_width
-    d_inner, d_step, d_pair, edge, tail, small_i, small_p, head_small = call(
-        scan_back_kernel,
-        blocks,
-        [
-            (idx, None, None), (d_scaled, *back(width)), (d_maps, *back(pair_width)), (pre_i, *back(width)),
-            (pre_p, *back(pair_width)), (in_i, *back(width)), (in_p, *back(pair_width)), (halo_i, *whole), (halo_p, *whole),
-            (aux, *back(LANES)), (gloc, *back3(CHUNK)), (pkb, *back3(8)), (grad_in, *whole), (states, *back3(CHUNK)),
-            (d_mixer, *back(width)), (mixer, *back(width)), (skip, *whole), (dlog, *whole), (conv_i, *whole), (conv_p, *whole),
-        ],
-        [
-            ((rows, width), BF16, *back(width)), ((rows, LANES), BF16, *back(LANES)), ((rows, pair_width), F32, *back(pair_width)),
-            ((8, both), F32, *whole), ((16, both), F32, *whole), ((8, width), F32, *whole), ((8, pair_width), F32, *whole),
-            ((8, LANES), F32, *whole),
-        ],
-        [pltpu.VMEM((BLOCK + 16, width), F32)] * 3 + [pltpu.VMEM((BLOCK + 16, pair_width), F32)] * 3,
-        prefetch=1, flops=3e9, moved=3e7, vmem=16,
-    )
     size = lax.axis_size("seq")
+    summing = size <= 8
 
     def piece(total_rows, tile):
         return -(-total_rows // (size * tile)) * tile
 
     r_wo, r_w, r_pack, r_wp, r_small = piece(width, 16), piece(model, 16), 8, piece(model // 4, 8), 8
     vmem = ("vmem", None)
-    core_wire = F32 if size <= 8 else BF16
+    core_wire = F32 if summing else BF16
     once = lambda w: ((rows // 2, w), lambda i: (core_bit(), 0))
-    sums_shapes = [(r_wo, model, BF16), (r_w, width, BF16), (r_w, width, BF16), (r_pack, width, F32), (r_wp, pair_width, F32),
-                   (r_small, pair_width, F32)]
-    pad_rows = lambda a, r: a if a.shape[0] == r * size else jnp.pad(a, ((0, r * size - a.shape[0]), (0, 0)))
-    scratch = [
-        pltpu.VMEM((BLOCK, width), BF16), pltpu.VMEM((BLOCK, pair_width), F32), pltpu.VMEM((8, both), F32),
+    sum_shapes = [(r_wo, model, BF16), (r_w, width, BF16), (r_w, width, BF16), (r_pack, width, F32), (r_wp, pair_width, F32),
+                  (r_small, pair_width, F32)]
+    n_wo, n_w, n_pack = (r_wo * size, r_w * size, r_pack * size) if summing else (width, model, 64)
+    scratch = [pltpu.VMEM((BLOCK + 16, width), F32)] * 3 + [pltpu.VMEM((BLOCK + 16, pair_width), F32)] * 3 + [
+        pltpu.VMEM((8, width), F32), pltpu.VMEM((8, pair_width), F32), pltpu.VMEM((8, LANES), F32),
         pltpu.VMEM((half, BLOCK, model), core_wire), pltpu.VMEM((half, BLOCK, model), core_wire),
         pltpu.VMEM((half, BLOCK, model), BF16), pltpu.VMEM((half, BLOCK, model), BF16),
         pltpu.VMEM((2, model), F32), pltpu.VMEM((2 * size, 2, model), F32),
-        pltpu.VMEM((r_w * size, width), F32), pltpu.VMEM((8, model), F32), pltpu.VMEM((r_pack * size, width), F32),
+        pltpu.VMEM((n_w, width), F32), pltpu.VMEM((8, model), F32), pltpu.VMEM((n_pack, width), F32),
         pltpu.VMEM((model, pair_width), F32), pltpu.VMEM((32, pair_width), F32),
         pltpu.VMEM((r_small * size, pair_width), F32), pltpu.VMEM((r_wp * size, pair_width), F32),
         pltpu.VMEM((model, pair_width), F32), pltpu.VMEM((32, pair_width), F32),
         pltpu.VMEM((half, BLOCK, model), BF16), pltpu.VMEM((half, BLOCK, model), BF16),
-        dma((half,)), dma((half,)), dma((half,)), dma((half,)), dma((1,)), dma((1,)), dma((half,)), dma((half,)),
+        pltpu.VMEM((3, 8, model), F32), pltpu.VMEM((8, model), F32), pltpu.VMEM((8, model), F32), pltpu.VMEM((8, model), F32),
+        dma((half,)), dma((half,)), dma((half,)), dma((half,)), dma((3,)), dma((3,)), dma((half,)), dma((half,)),
         dma((2 * size,)), dma((2 * size,)),
     ]
-    scratch += HeadSum.scratch(model, pair_width, r_wp * size) + HeadSum.scratch(32, pair_width, r_small * size)
-    for r, lanes, wire in sums_shapes:
-        scratch += SeqSum.scratch(r, lanes, wire, size)
+    if summing:
+        scratch += HeadSum.scratch(model, pair_width, r_wp * size) + HeadSum.scratch(32, pair_width, r_small * size)
+        for r, lanes, wire in sum_shapes:
+            scratch += SeqSum.scratch(r, lanes, wire, size)
     grad_hidden, sums, g_wo, g_wg, g_wi, pack, g_wp, small_p = call(
-        tail_kernel,
+        finale_kernel,
         blocks,
         [
-            (low, *send_order(model)), (d_gate, *send_order(width)), (d_inner, *send_order(width)), (d_step, *send_order(LANES)),
-            (d_pair, *send_order(pair_width)), (w_gate, *whole), (w_inner, *whole), (ws, *whole), (w_pair, *whole),
-            (edge, *whole), (tail, *whole), (hidden, *once(model)), (d_out, *vmem), (gain, *whole), (error, *whole),
-            (pad_rows(g_wo, r_wo), *vmem), (pad_rows(g_wg, r_w), *vmem), (small_i, *whole), (g_gain, *whole), (small_p, *whole),
-            (head_small, *whole),
-        ],
-        [
-            ((rows, model), BF16, *vmem), ((2, model), F32, *vmem), ((r_wo * size, model), F32, *vmem),
-            ((r_w * size, width), F32, *vmem), ((r_w * size, width), F32, *vmem), ((r_pack * size, width), F32, *vmem),
+            (d_scaled, *back(width)), (d_maps, *back(pair_width)), (pre_i, *back(width)), (pre_p, *back(pair_width)),
+            (in_i, *back(width)), (in_p, *back(pair_width)), (halo_low, *whole), (halo_i, *whole), (halo_p, *whole),
+            (aux, *back(LANES)), (gloc, *back3(CHUNK)), (pkb, *back3(8)), (grad_in, *whole), (states, *back3(CHUNK)),
+            (d_mixer, *back(width)), (mixer, *back(width)), (skip, *whole), (dlog, *whole), (conv_i, *whole), (conv_p, *whole),
+            (low, *back(model)), (d_gate, *back(width)), (w_gate, *whole), (w_inner, *whole), (ws, *whole), (w_pair, *whole),
+            (hidden, *once(model)), (d_out, *vmem), (gain, *whole), (error, *whole), (g_wo, *vmem), (g_wg, *vmem),
+            (g_gain, *whole),
+        ],
+        [
+            ((rows, model), BF16, *vmem), ((2, model), F32, *vmem), ((n_wo, model), F32, *vmem),
+            ((n_w, width), F32, *vmem), ((n_w, width), F32, *vmem), ((n_pack, width), F32, *vmem),
             ((model, pair_width), F32, *vmem), ((32, pair_width), F32, *vmem),
         ],
         scratch,
-        flops=6e9, moved=4e7, collective=4, vmem=40 if size <= 8 else 60,
-    )
-    g_wo, g_wg, g_wi = g_wo[:width], g_wg[:model], g_wi[:model]
+        flops=9e9, moved=8e7, collective=4, vmem=58,
+    )
+    if not summing:
+        g_wo, g_wg, g_wi, pack = lax.psum((g_wo, g_wg, g_wi, pack), "seq")
+        g_wp, small_p = lax.psum((g_wp, small_p), ("seq", "head"))
     by_head, g_ws = pack[:8], jnp.concatenate([pack[8:16], pack[16:24]], axis=1)[:heads].T
     pair_small, head_small = small_p[:8], pack[24:32, :LANES]
     loss = jnp.sum(sums[1]) / (count * model)

time: 333 us -> 322 us (0.967)
  Pallas kernels: 189 us -> 178 us
    pallas_call x10 -> x9, Pallas kernels: 189 us -> 178 us  [call(): pl.pallas_call(kernel, grid_spec=pltpu.PrefetchScalarGridSpec(num_scalar_...]
    unnamed x115 -> x119, local copies, waits for them, and re-layouts: 38.9 us -> 31.7 us
where the time goes in v4:
time: 322 us; the launch traced here: 321 us
  Pallas kernels  178 us (55%)
  waiting for transfers between devices  60.7 us (19%)
  local copies, waits for them, and re-layouts  43.5 us (14%)
  starting transfers between devices  21.1 us (7%)
  other arithmetic  12.5 us (4%)
  between operations  4.4 us (1%)
    pallas_call x9, Pallas kernels, call(): pl.pallas_call(kernel, grid_spec=pltpu.PrefetchScalarGridSpec(num_scalar_...  178 us
    ppermute x14, waiting for transfers between devices, swap(): return jax.tree.map(lambda v: lax.ppermute(v, axis, route), value)  60.7 us
    unnamed x119, local copies, waits for them, and re-layouts  31.7 us
    ppermute x14, starting transfers between devices, swap(): return jax.tree.map(lambda v: lax.ppermute(v, axis, route), value)  16.3 us
  transfers between devices with their start and end apart: 15, of which 12 were waited for; matrix products, arithmetic and copies ran while one was open for 4% of the time, Pallas kernels for 5%

profile of v4, /device:TPU:0, one launch (start us, length us, event | category | flops | bytes accessed | tf_op | source)
XLA Modules:
  0.0 320.7 jit_solution(12653950622783928569)
XLA Ops:
  1.4 4.9 %collective-permute-start.3 = (bf16[16,768]{1,0:T(8,128)(2,1)S(1)}, bf16[16,768]{1,0:T(8,128)(2,1)S(1)}, u32[]{:S(2)}, u32[]{:S(2)}) collective-permute-start(bf16[16,768]{1,0:T(8,128)(2,1)S(1)} %slice.273), channel_id=1, source_target_pairs={{0,4},{4,8},{8,12},{12,16},{16,20},{20,24},{24,28},{1,5},{5,9},{9,... | collective-permute-start | bytes 73736 | tf_op jit(solution)/shard_map/ppermute | solution.py:935
  16.2 1.9 copy-done.6
  20.2 20.6 %shard_map.305 = (bf16[2048,768]{1,0:T(8,128)(2,1)S(1)}, bf16[2048,384]{1,0:T(8,128)(2,1)S(1)}, bf16[2048,256]{1,0:T(8,128)(2,1)S(1)}, f32[2048,384]{1,0:T(8,128...) custom-call(s32[2]{0:T(128)S(1)} %pad_add_fusion.idx, ...), custom_call_target="tpu_custom_call" | custom-call | flops 3000000000 | bytes 20000000 | tf_op jit(solution)/shard_map/pallas_call | solution.py:910
  44.1 7.3 %shard_map.306 = (f32[2048,384]{1,0:T(8,128)S(1)}, f32[2048,384]{1,0:T(8,128)S(1)}) custom-call(s32[2]{0:T(128)S(1)} %pad_add_fusion.idx, bf16[2048,768]{1,0:T(8,128)(2,1)S(1)} %get-tuple-element.111.low, bf16[768,384]{1,0:T(8,128)(2,1)S(1)} %copy-done.34, f32[2048,384]{1,0:T(8,128)S(1)} %get-tuple-element.112.pre_i, ...), custom_call_target="tpu_custom_call" | custom-call | flops 4000000000 | bytes 20000000 | tf_op jit(solution)/shard_map/pallas_call | solution.py:910
  53.3 4.7 %collective-permute-done.5 = f32[136,384]{1,0:T(8,128)S(1)} collective-permute-done((f32[136,384]{1,0:T(8,128)S(1)}, f32[136,384]{1,0:T(8,128)S(1)}, u32[]{:S(2)}, u32[]{:S(2)}) %collective-permute-start.5) | collective-permute-done | bytes 208928 | tf_op jit(solution)/shard_map/ppermute | solution.py:929
  58.1 2.7 collective-permute-start.6
  60.8 8.2 %collective-permute-done.6 = f32[136,384]{1,0:T(8,128)S(1)} collective-permute-done((f32[136,384]{1,0:T(8,128)S(1)}, f32[136,384]{1,0:T(8,128)S(1)}, u32[]{:S(2)}, u32[]{:S(2)}) %collective-permute-start.6) | collective-permute-done | bytes 208928 | tf_op jit(solution)/shard_map/ppermute | solution.py:929
  69.1 5.5 %shard_map.307 = (f32[2048,384]{1,0:T(8,128)S(1)}, f32[16,128,384]{2,1,0:T(8,128)S(1)}, f32[1,2048]{1,0:T(1,128)S(1)}) custom-call(f32[2048,256]{1,0:T(8,128)S(1)} %get-tuple-element.106.pre_p.pre_c, f32[2048,128]{1,0:T(8,128)S(1)} %get-tuple-element.107.aux, f32[16,128,384]{2,1,0:T(8,128)S(1)} %get-tuple-element.108.sloc, ...), custom_call_target="tpu_custom_call" | custom-call | flops 1000000000 | bytes 20000000 | tf_op jit(solution)/shard_map/pallas_call | solution.py:910
  79.1 2.2 collective-permute-done.8
  81.3 6.5 %shard_map.308.mine = bf16[1024,768]{1,0:T(8,128)(2,1)S(1)} custom-call(f32[2048,384]{1,0:T(8,128)S(1)} %get-tuple-element.115.mixer, f32[2048,384]{1,0:T(8,128)S(1)} %get-tuple-element.114.gate, f32[1,2048]{1,0:T(1,128)S(1)} %add.83.square, f32[1,384]{1,0:T(1,128)S(1)} %broadcast_in_dim.35.gain, bf16[384,768]{1,0:T(8,128)(2,1)S(1)} %copy-done.25), custom_call_target="tpu_custom_call" | custom-call | flops 1200000000 | bytes 10000000 | tf_op jit(solution)/shard_map/pallas_call | solution.py:910
  91.2 3.1 collective-permute-done
  95.0 3.6 %collective-permute-done.1 = f32[8,128]{1,0:T(8,128)S(1)} collective-permute-done((f32[8,128]{1,0:T(8,128)S(1)}, f32[8,128]{1,0:T(8,128)S(1)}, u32[]{:S(2)}, u32[]{:S(2)}) %collective-permute-start.1) | collective-permute-done | bytes 4128 | tf_op jit(solution)/shard_map/ppermute | solution.py:929
  100.6 3.3 %collective-permute-done.2 = f32[8,128]{1,0:T(8,128)S(1)} collective-permute-done((f32[8,128]{1,0:T(8,128)S(1)}, f32[8,128]{1,0:T(8,128)S(1)}, u32[]{:S(2)}, u32[]{:S(2)}) %collective-permute-start.2) | collective-permute-done | bytes 4128 | tf_op jit(solution)/shard_map/ppermute | solution.py:929
  105.1 19.2 %collective-permute-done.9.other = bf16[1024,768]{1,0:T(8,128)(2,1)S(1)} collective-permute-done((bf16[1024,768]{1,0:T(8,128)(2,1)S(1)}, bf16[1024,768]{1,0:T(8,128)(2,1)S(1)}, u32[]{:S(2)}, u32[]{:S(2)}) %collective-permute-start.9) | collective-permute-done | bytes 1572896 | tf_op jit(solution)/shard_map/ppermute | solution.py:929
  124.2 6.5 %shard_map.309 = (bf16[2048,768]{1,0:T(8,128)(2,1)S(1)}, bf16[2048,768]{1,0:T(8,128)(2,1)S(1)}, f32[1024,768]{1,0:T(8,128)S(1)}, f32[1,768]{1,0:T(1,128)S(1)}) custom-call(f32[1]{0:T(128)} %bitcast.factor, bf16[2048,768]{1,0:T(8,128)(2,1)S(1)} %copy-done.7, bf16[2048,768]{1,0:T(8,128)(2,1)S(1)} %copy-done.22, s32[1,2048]{1,0:T(1,128)S(1)} %bitcast.19, ...), custom_call_target="tpu_custom_call" | custom-call | flops 100000000 | bytes 15000000 | tf_op jit(solution)/shard_map/pallas_call | solution.py:910
  132.4 8.8 %shard_map.310 = (f32[2048,384]{1,0:T(8,128)S(1)}, f32[1,2048]{1,0:T(1,128)S(1)}, f32[1,384]{1,0:T(1,128)S(1)}, f32[384,768]{1,0:T(8,128)S(1)}) custom-call(bf16[2048,768]{1,0:T(8,128)(2,1)S(1)} %get-tuple-element.118.d_branch, f32[2048,384]{1,0:T(8,128)S(1)} %get-tuple-element.115.mixer, f32[2048,384]{1,0:T(8,128)S(1)} %get-tuple-element.114.gate, ...), custom_call_target="tpu_custom_call" | custom-call | flops 2400000000 | bytes 15000000 | tf_op jit(solution)/shard_map/pallas_call | solution.py:910
  148.9 1.9 copy-done.2
  153.6 1.9 copy-done.24
  155.5 7.4 %shard_map.311 = (f32[2048,384]{1,0:T(8,128)S(1)}, bf16[2048,384]{1,0:T(8,128)(2,1)S(1)}, f32[16,128,384]{2,1,0:T(8,128)S(1)}, f32[16,8,384]{2,1,0:T(8,128)S(1)}, f32[136,384]{1,0:T(8,128)S(1)}) custom-call(f32[2048,384]{1,0:T(8,128)S(1)} %copy-done.24, f32[2048,384]{1,0:T(8,128)S(1)} %get-tuple-element.115.mixer, f32[2048,384]{1,0:T(8,128)S(1)} %copy-done.2, ...), custom_call_target="tpu_custom_call" | custom-call | flops 1000000000 | bytes 20000000 | tf_op jit(solution)/shard_map/pallas_call | solution.py:910
  165.2 9.8 %shard_map.312 = (f32[2048,384]{1,0:T(8,128)S(1)}, f32[2048,256]{1,0:T(8,128)S(1)}, f32[768,384]{1,0:T(8,128)S(1)}) custom-call(s32[2]{0:T(128)S(1)} %pad_add_fusion.idx, f32[2048,384]{1,0:T(8,128)S(1)} %get-tuple-element.121.d_mixer, f32[2048,384]{1,0:T(8,128)S(1)} %copy-done.14, f32[2048,256]{1,0:T(8,128)S(1)} %copy-done.5, f32[2048,128]{1,0:T(8,128)S(1)} %copy-done.10, ...), custom_call_target="tpu_custom_call" | custom-call | flops 6000000000 | bytes 20000000 | tf_op jit(solution)/shard_map/pallas_call | solution.py:910
  177.7 5.1 %collective-permute-done.13 = f32[136,384]{1,0:T(8,128)S(1)} collective-permute-done((f32[136,384]{1,0:T(8,128)S(1)}, f32[136,384]{1,0:T(8,128)S(1)}, u32[]{:S(2)}, u32[]{:S(2)}) %collective-permute-start.13) | collective-permute-done | bytes 208928 | tf_op jit(solution)/shard_map/ppermute | solution.py:929
  182.9 2.4 collective-permute-start.14
  185.3 7.8 %collective-permute-done.14 = f32[136,384]{1,0:T(8,128)S(1)} collective-permute-done((f32[136,384]{1,0:T(8,128)S(1)}, f32[136,384]{1,0:T(8,128)S(1)}, u32[]{:S(2)}, u32[]{:S(2)}) %collective-permute-start.14) | collective-permute-done | bytes 208928 | tf_op jit(solution)/shard_map/ppermute | solution.py:929
  193.9 106.0 %shard_map.313 = (bf16[2048,768]{1,0:T(8,128)(2,1)}, f32[2,768]{1,0:T(2,128)}, f32[384,768]{1,0:T(8,128)}, f32[768,384]{1,0:T(8,128)}, f32[768,384]{1,0:T(8,128)...) custom-call(f32[2048,384]{1,0:T(8,128)} %copy-done.19, f32[2048,256]{1,0:T(8,128)} %copy-done.26, ...), custom_call_target="tpu_custom_call" | custom-call | flops 8999999488 | bytes 80000000 | tf_op jit(solution)/shard_map/pallas_call | solution.py:910
  (207 shorter events, 65.2 us)
Async XLA Ops:
  1.4 14.7 %collective-permute-start.3 = (bf16[16,768]{1,0:T(8,128)(2,1)S(1)}, bf16[16,768]{1,0:T(8,128)(2,1)S(1)}, u32[]{:S(2)}, u32[]{:S(2)}) collective-permute-start(bf16[16,768]{1,0:T(8,128)(2,1)S(1)} %slice.273), channel_id=1, source_target_pairs={{0,4},{4,8},{8,12},{12,16},{16,20},{20,24},{24,28},{1,5},{5,9},{9,... | collective-permute-start | bytes 73736 | tf_op jit(solution)/shard_map/ppermute | solution.py:935
  12.5 28.3 %copy-start.47 = (f32[1,128]{1,0:T(1,128)}, f32[1,128]{1,0:T(1,128)S(1)}, u32[]{:S(2)}) copy-start(f32[1,128]{1,0:T(1,128)S(1)} %scatter.19.dlog) | copy-start | bytes 1540
  13.9 27.0 %copy-start.41 = (f32[1,768]{1,0:T(1,128)}, f32[1,768]{1,0:T(1,128)S(1)}, u32[]{:S(2)}) copy-start(f32[1,768]{1,0:T(1,128)S(1)} %broadcast_in_dim.29.gain) | copy-start | bytes 9220
  15.4 28.7 %copy-start.44 = (f32[1,384]{1,0:T(1,128)}, f32[1,384]{1,0:T(1,128)S(1)}, u32[]{:S(2)}) copy-start(f32[1,384]{1,0:T(1,128)S(1)} %broadcast_in_dim_reshape.3.skip) | copy-start | bytes 4612
  42.5 26.6 %copy-start.3 = (f32[2048,256]{1,0:T(8,128)}, f32[2048,256]{1,0:T(8,128)S(1)}, u32[]{:S(2)}) copy-start(f32[2048,256]{1,0:T(8,128)S(1)} %get-tuple-element.106.pre_p.pre_c) | copy-start | bytes 6291460
  42.5 9.0 %collective-permute-start.4 = (f32[136,384]{1,0:T(8,128)S(1)}, f32[136,384]{1,0:T(8,128)S(1)}, u32[]{:S(2)}, u32[]{:S(2)}) collective-permute-start(f32[136,384]{1,0:T(8,128)S(1)} %get-tuple-element.110), channel_id=1, source_target_pairs={{0,4},{4,0},{8,12},{12,8},{16,20},{20,16},{24,28},{28,24},{1,5},{5... | collective-permute-start | bytes 626696 | tf_op jit(solution)/shard_map/ppermute | solution.py:929
  51.4 81.0 %copy-start.1 = (f32[2048,384]{1,0:T(8,128)}, f32[2048,384]{1,0:T(8,128)S(1)}, u32[]{:S(2)}) copy-start(f32[2048,384]{1,0:T(8,128)S(1)} %get-tuple-element.114.gate) | copy-start | bytes 9437188
  51.6 6.4 %collective-permute-start.5 = (f32[136,384]{1,0:T(8,128)S(1)}, f32[136,384]{1,0:T(8,128)S(1)}, u32[]{:S(2)}, u32[]{:S(2)}) collective-permute-start(f32[136,384]{1,0:T(8,128)S(1)} %fusion.3), channel_id=1, source_target_pairs={{0,8},{4,12},{8,0},{12,4},{16,24},{20,28},{24,16},{28,20},{1,9},{5... | collective-permute-start | bytes 626696 | tf_op jit(solution)/shard_map/ppermute | solution.py:929
  58.1 10.9 %collective-permute-start.6 = (f32[136,384]{1,0:T(8,128)S(1)}, f32[136,384]{1,0:T(8,128)S(1)}, u32[]{:S(2)}, u32[]{:S(2)}) collective-permute-start(f32[136,384]{1,0:T(8,128)S(1)} %fusion.2), channel_id=1, source_target_pairs={{0,16},{4,20},{8,24},{12,28},{16,0},{20,4},{24,8},{28,12},{1,17},{... | collective-permute-start | bytes 626696 | tf_op jit(solution)/shard_map/ppermute | solution.py:929
  76.4 72.6 %copy-start = (f32[2048,384]{1,0:T(8,128)}, f32[2048,384]{1,0:T(8,128)S(1)}, u32[]{:S(2)}) copy-start(f32[2048,384]{1,0:T(8,128)S(1)} %get-tuple-element.115.mixer) | copy-start | bytes 9437188
  76.4 1.2 collective-permute-start.7
  77.6 3.7 %collective-permute-start.8 = (f32[1,2048]{1,0:T(1,128)S(1)}, f32[1,2048]{1,0:T(1,128)S(1)}, u32[]{:S(2)}, u32[]{:S(2)}) collective-permute-start(f32[1,2048]{1,0:T(1,128)S(1)} %add.82), channel_id=1, source_target_pairs={{0,2},{1,3},{2,0},{3,1},{4,6},{5,7},{6,4},{7,5},{8,10},{9,11},{10,... | collective-permute-start | bytes 24584 | tf_op jit(solution)/shard_map/ppermute | solution.py:929
  81.3 42.9 %copy-start.7 = (bf16[2048,768]{1,0:T(8,128)(2,1)S(1)}, bf16[2048,768]{1,0:T(8,128)(2,1)}, u32[]{:S(2)}) copy-start(bf16[2048,768]{1,0:T(8,128)(2,1)} %hid.5) | copy-start | bytes 9437188
  81.3 42.9 %copy-start.22 = (bf16[2048,768]{1,0:T(8,128)(2,1)S(1)}, bf16[2048,768]{1,0:T(8,128)(2,1)}, u32[]{:S(2)}) copy-start(bf16[2048,768]{1,0:T(8,128)(2,1)} %teacher.1) | copy-start | bytes 9437188
  87.8 36.4 %collective-permute-start.9 = (bf16[1024,768]{1,0:T(8,128)(2,1)S(1)}, bf16[1024,768]{1,0:T(8,128)(2,1)S(1)}, u32[]{:S(2)}, u32[]{:S(2)}) collective-permute-start(bf16[1024,768]{1,0:T(8,128)(2,1)S(1)} %shard_map.308.mine), channel_id=1, source_target_pairs={{0,2},{1,3},{2,0},{3,1},{4,6},{5,7},{6,4},{7,5},{8,10},{9,11},{10,... | collective-permute-start | bytes 4718600 | tf_op jit(solution)/shard_map/ppermute | solution.py:929
  90.6 3.7 %collective-permute-start = (f32[8,128]{1,0:T(8,128)S(1)}, f32[8,128]{1,0:T(8,128)S(1)}, u32[]{:S(2)}, u32[]{:S(2)}) collective-permute-start(f32[8,128]{1,0:T(8,128)S(1)} %broadcast_in_dim.27), channel_id=1, source_target_pairs={{0,4},{4,0},{8,12},{12,8},{16,20},{20,16},{24,28},{28,24},{1,5},{5... | collective-permute-start | bytes 12296 | tf_op jit(solution)/shard_map/ppermute | solution.py:929
  95.0 3.7 %collective-permute-start.1 = (f32[8,128]{1,0:T(8,128)S(1)}, f32[8,128]{1,0:T(8,128)S(1)}, u32[]{:S(2)}, u32[]{:S(2)}) collective-permute-start(f32[8,128]{1,0:T(8,128)S(1)} %broadcast_add_fusion), channel_id=1, source_target_pairs={{0,8},{4,12},{8,0},{12,4},{16,24},{20,28},{24,16},{28,20},{1,9},{5... | collective-permute-start | bytes 12296 | tf_op jit(solution)/shard_map/ppermute | solution.py:929
  99.3 4.6 %collective-permute-start.2 = (f32[8,128]{1,0:T(8,128)S(1)}, f32[8,128]{1,0:T(8,128)S(1)}, u32[]{:S(2)}, u32[]{:S(2)}) collective-permute-start(f32[8,128]{1,0:T(8,128)S(1)} %fusion.13), channel_id=1, source_target_pairs={{0,16},{4,20},{8,24},{12,28},{16,0},{20,4},{24,8},{28,12},{1,17},{... | collective-permute-start | bytes 12296 | tf_op jit(solution)/shard_map/ppermute | solution.py:929
  144.0 1.2 collective-permute-start.10
  145.2 3.7 %collective-permute-start.11 = (f32[1,2048]{1,0:T(1,128)S(1)}, f32[1,2048]{1,0:T(1,128)S(1)}, u32[]{:S(2)}, u32[]{:S(2)}) collective-permute-start(f32[1,2048]{1,0:T(1,128)S(1)} %add.84), channel_id=1, source_target_pairs={{0,2},{1,3},{2,0},{3,1},{4,6},{5,7},{6,4},{7,5},{8,10},{9,11},{10,... | collective-permute-start | bytes 24584 | tf_op jit(solution)/shard_map/ppermute | solution.py:929
  164.7 12.1 %collective-permute-start.12 = (f32[136,384]{1,0:T(8,128)S(1)}, f32[136,384]{1,0:T(8,128)S(1)}, u32[]{:S(2)}, u32[]{:S(2)}) collective-permute-start(f32[136,384]{1,0:T(8,128)S(1)} %get-tuple-element.132), channel_id=1, source_target_pairs={{0,4},{4,0},{8,12},{12,8},{16,20},{20,16},{24,28},{28,24},{1,5},{5... | collective-permute-start | bytes 626696 | tf_op jit(solution)/shard_map/ppermute | solution.py:929
  176.9 5.9 %collective-permute-start.13 = (f32[136,384]{1,0:T(8,128)S(1)}, f32[136,384]{1,0:T(8,128)S(1)}, u32[]{:S(2)}, u32[]{:S(2)}) collective-permute-start(f32[136,384]{1,0:T(8,128)S(1)} %fusion.1), channel_id=1, source_target_pairs={{0,8},{4,12},{8,0},{12,4},{16,24},{20,28},{24,16},{28,20},{1,9},{5... | collective-permute-start | bytes 626696 | tf_op jit(solution)/shard_map/ppermute | solution.py:929
  182.9 10.3 %collective-permute-start.14 = (f32[136,384]{1,0:T(8,128)S(1)}, f32[136,384]{1,0:T(8,128)S(1)}, u32[]{:S(2)}, u32[]{:S(2)}) collective-permute-start(f32[136,384]{1,0:T(8,128)S(1)} %fusion), channel_id=1, source_target_pairs={{0,16},{4,20},{8,24},{12,28},{16,0},{20,4},{24,8},{28,12},{1,17},{... | collective-permute-start | bytes 626696 | tf_op jit(solution)/shard_map/ppermute | solution.py:929
  193.9 116.6 %copy-start.21 = (bf16[2048,768]{1,0:T(8,128)(2,1)S(1)}, bf16[2048,768]{1,0:T(8,128)(2,1)}, u32[]{:S(2)}) copy-start(bf16[2048,768]{1,0:T(8,128)(2,1)} %copy-done.20) | copy-start | bytes 9437188
  (47 other events, 380.7 us)

commit v5 on v4

--- a/solution.py
+++ b/solution.py
@@ -36,13 +36,15 @@
 
 
 def column_sums(v):
-    high, low = halves(v)
-    ones = jnp.ones((8, v.shape[1]), BF16)
-    return (dot(ones, high, 1, 1) + dot(ones, low, 1, 1))[:1]
-
-
-def as_column(row):
-    return jnp.transpose(jnp.broadcast_to(row, (8, row.shape[1])))[:, :1]
+    folded = v[:, :LANES]
+    for at in range(LANES, v.shape[1], LANES):
+        folded = folded + v[:, at : at + LANES]
+    return jnp.sum(jnp.transpose(folded), axis=0, keepdims=True)
+
+
+def as_column(row, width=LANES):
+    column = jnp.transpose(jnp.broadcast_to(row, (LANES, row.shape[1])))
+    return jnp.concatenate([column] * (width // LANES), axis=1)
 
 
 def expand(table, base, width):
@@ -80,8 +82,8 @@
 
 
 def project_kernel(
-    idx, starts, hid, halo, tail, gain, wi, wp, ws, conv_i, conv_p, bias_i, bias_p, sbias, dlog,
-    low, in_i, in_p, pre_i, pre_p, aux, halo_low, halo_i, halo_p, sloc, pkl, fin, wide_i, wide_p, state, decay,
+    idx, given, valid, hid, halo, tail, gain, wi, wp, ws, conv_i, conv_p, bias_i, bias_p,
+    low, low_t, in_i, in_p, pre_i, pre_p, aux, halo_low, halo_i, halo_p, sloc, pkl, fin, wide_i, wide_p, state, decay, counted,
 ):
     step = pl.program_id(0)
     edge = tail.shape[0]
@@ -91,13 +93,16 @@
     def _():
         state[...] = jnp.zeros_like(state)
         decay[...] = jnp.ones_like(decay)
-
+        counted[...] = jnp.zeros_like(counted)
+
+    counted[...] += jnp.sum(valid[...].astype(F32), axis=1, keepdims=True)
     before = jnp.where(step == 0, tail[...].astype(F32), halo[...].astype(F32))
     rows = jnp.concatenate([before, hid[...].astype(F32)], axis=0)
     scale = lax.rsqrt(jnp.mean(rows * rows, axis=1, keepdims=True) + EPSILON)
     lowered = (rows * scale * gain[...]).astype(BF16)
     own = lowered[edge:]
     low[...] = own
+    low_t[...] = jnp.transpose(own)
     inner = dot(lowered, wi[...]).astype(BF16)
     pair = dot(lowered, wp[...]).astype(BF16)
     in_i[...] = inner[edge:]
@@ -113,16 +118,18 @@
 
     base = idx[1] + step * BLOCK
     pos = (base + lax.broadcasted_iota(jnp.int32, (BLOCK, LANES), 0)).astype(F32)
-    begun = starts[...] <= pos
-    start = jnp.max(jnp.where(begun, starts[...], -1.0), axis=1, keepdims=True)
-    end = jnp.min(jnp.where(begun, FAR, starts[...]), axis=1, keepdims=True)
+    starts = given[3:4]
+    begun = starts <= pos
+    start = jnp.max(jnp.where(begun, starts, -1.0), axis=1, keepdims=True)
+    end = jnp.min(jnp.where(begun, FAR, starts), axis=1, keepdims=True)
     within = pos[:, :1] - start
     keep = [(within >= float(3 - k)).astype(F32) for k in range(3)]
 
     def convolve(wide, weight, bias):
-        total = bias[...] + wide[edge : edge + BLOCK] * weight[3:4]
+        taps = weight[...].astype(F32)
+        total = bias[...].astype(F32) + wide[edge : edge + BLOCK] * taps[3:4]
         for k in range(3):
-            total = total + wide[edge - 3 + k : edge - 3 + k + BLOCK] * weight[k : k + 1] * keep[k]
+            total = total + wide[edge - 3 + k : edge - 3 + k + BLOCK] * taps[k : k + 1] * keep[k]
         return total
 
     conv_inner = convolve(wide_i, conv_i, bias_i)
@@ -133,10 +140,10 @@
     maps = conv_pair[:, :LANES]
     maps = maps * jax.nn.sigmoid(maps)
 
-    raw = dot(own, ws[...]) + sbias[...]
+    raw = dot(own, ws[...]) + given[0:1]
     dt = jnp.maximum(raw, 0.0) + jnp.log1p(jnp.exp(-jnp.abs(raw)))
     rate = jax.nn.sigmoid(raw)
-    logs = -dt * jnp.exp(dlog[...])
+    logs = -dt * jnp.exp(given[1:2])
     lane = lax.broadcasted_iota(jnp.int32, (CHUNK, LANES), 1)
     lower = triangle(False)
     for c in range(BLOCK // CHUNK):
@@ -160,7 +167,7 @@
         state[...] = state[...] * kept[:1] + added
         decay[...] = decay[...] * kept
     fin[:CHUNK] = state[...]
-    fin[CHUNK:] = decay[...]
+    fin[CHUNK:] = jnp.concatenate([decay[:7], jnp.broadcast_to(counted[...], (1, width))], axis=0)
 
 
 def masks(table, first, transposed):
@@ -180,8 +187,9 @@
     ).astype(BF16)
 
 
-def intra_kernel(idx, low, wg, pre_i, pre_p, aux, skip, gate, mixed):
+def intra_kernel(idx, low, wg, pre_i, pre_p, aux, given, gate, mixed):
     width = wg.shape[1]
+    skip = expand(given[...], 0, width)[2:3]
     gate[...] = dot(low[...], wg[...])
     base = idx[1] + pl.program_id(0) * BLOCK
     maps, _ = silu_parts(pre_p[...])
@@ -200,24 +208,7 @@
                 gap = table[:, CUM + h : CUM + h + 1] - rows[CUM + h : CUM + h + 1, :]
                 weights.append((scores * jnp.exp(jnp.where(joined, gap, -1e30))).astype(BF16))
             parts.append(dot(jnp.concatenate(weights, axis=1), head_split(scaled, pair)))
-        mixed[at, :] = jnp.concatenate(parts, axis=1) + values[at] * skip[...]
-
-
-def mix_kernel(pre_c, aux, sloc, pkl, sin, local, gate, mixer, states, square):
-    width = local.shape[1]
-    reads, _ = silu_parts(pre_c[...])
-    for c in range(BLOCK // CHUNK):
-        at = slice(c * CHUNK, (c + 1) * CHUNK)
-        state = sloc[c] + pkl[c, :1] * sin[...]
-        states[c] = state
-        mixer[at, :] = local[at, :] + expand(aux[at, :], INFLOW, width) * dot3(reads[at], state)
-    act, _ = silu_parts(gate[...])
-    gated = mixer[...] * act
-    square[...] = column_sums(gated * gated)
-
-
-def gate_scale(square, total):
-    return as_column(lax.rsqrt(square / total + EPSILON))
+        mixed[at, :] = jnp.concatenate(parts, axis=1) + values[at] * skip
 
 
 def core_bit():
@@ -228,161 +219,218 @@
     return lax.axis_index("head") + 1 - 2 * core_bit()
 
 
-def enter(peers):
-    barrier = pltpu.get_barrier_semaphore()
-    for peer in peers:
-        pl.semaphore_signal(barrier, inc=1, device_id=peer, device_id_type=pl.DeviceIdType.MESH)
-    pl.semaphore_wait(barrier, len(peers))
-
-
-def to_peer(src, dst, sends, lands, slot):
-    return pltpu.make_async_remote_copy(
-        src_ref=src, dst_ref=dst, send_sem=sends.at[slot], recv_sem=lands.at[slot],
-        device_id={"head": core_peer()}, device_id_type=pl.DeviceIdType.MESH,
-    )
-
-
-def add_halves(part, mine, away, land, send_sem, land_sem):
+def mid_kernel(
+    factor, pre_c, aux, sloc, pkl, sin, local, gate, gain, wo, hid, teacher, valid,
+    states, d_mixer, d_gate, gloc, pkb, fin, out, d_out, error, g_gain, g_wo,
+    mix, squares, square_land, crosses, cross_land, scales, parts, land, mine, other, d_branch, out_block, weighted, keeps,
+    state, wo_t, square_send, square_got, cross_send, cross_got, core_send, core_land, x_send, x_land, grad_send, grad_land,
+    out_local, out_send, out_land, *, total,
+):
     step = pl.program_id(0)
-    half = pl.num_programs(0) // 2
-
-    def copy(slot):
-        return to_peer(away.at[slot], land.at[slot], send_sem, land_sem, slot)
-
-    @pl.when(step < half)
-    def _():
-        away[step] = part.astype(away.dtype)
-        copy(step).start()
-
-    @pl.when(step >= half)
-    def _():
-        copy(step - half).wait_recv()
-        mine[...] = (part + land[step - half].astype(F32)).astype(mine.dtype)
-
-    @pl.when(step == 2 * half - 1)
-    def _():
-        def drain(slot, carry):
-            copy(slot).wait_send()
-            return carry
-
-        lax.fori_loop(0, half, drain, 0)
-
-
-def branch_kernel(mixer, gate, square, gain, wo, mine, away, land, send_sem, land_sem, *, total):
+    half = mine.shape[0]
+    blocks = 2 * half
+    width = local.shape[1]
+    head, core = lax.axis_index("head"), core_bit()
+    beside, across = {"head": core_peer()}, {"head": lax.rem(head + 2, 4)}
+
+    def to_head(distance):
+        return {"head": lax.rem(head + distance, 4)}
+
+    def square_copy(block, d):
+        return device_copy(squares.at[block], square_land.at[d, block], (square_send, square_got), 4 * block + d, to_head(d))
+
+    def cross_copy(block, d):
+        return device_copy(crosses.at[block], cross_land.at[d, block], (cross_send, cross_got), 4 * block + d, to_head(d))
+
+    def core_copy(slot):
+        return device_copy(parts.at[slot], land.at[slot], (core_send, core_land), slot, beside)
+
+    def x_copy(slot):
+        return device_copy(mine.at[slot], other.at[slot], (x_send, x_land), slot, across)
+
+    def grad_copy(block):
+        return device_copy(d_branch.at[block], d_branch.at[block], (grad_send, grad_land), block, beside)
+
+    def out_copies(slot):
+        rows = rows_at(out, core * half + slot, BLOCK)
+        here = pltpu.make_async_copy(out_block.at[slot], rows, out_local.at[slot])
+        return here, device_copy(out_block.at[slot], rows, (out_send, out_land), slot, beside)
+
+    def gate_rows(block):
+        return gate[pl.ds(pl.multiple_of(block * BLOCK, BLOCK), BLOCK), :]
+
+    def settle(slot):
+        core_copy(slot).wait_recv()
+        mine[slot] = (parts[slot] + land[slot]).astype(BF16)
+        x_copy(slot).start()
+
+    @pl.when(step == 0)
+    def _():
+        barrier = pltpu.get_barrier_semaphore()
+
+        def greet(d):
+            pl.semaphore_signal(barrier, inc=1, device_id=to_head(d), device_id_type=pl.DeviceIdType.MESH)
+
+        loop(1, 4, greet)
+        for ref in (error, g_gain, g_wo):
+            ref[...] = jnp.zeros_like(ref)
+        wo_t[...] = jnp.transpose(wo[...])
+        pl.semaphore_wait(barrier, 3)
+
+    @pl.when(step < blocks)
+    def _():
+        reads, _ = silu_parts(pre_c[...])
+        for c in range(BLOCK // CHUNK):
+            at = slice(c * CHUNK, (c + 1) * CHUNK)
+            now = sloc[c] + pkl[c, :1] * sin[...]
+            states[c] = now
+            mix[step, at, :] = local[at, :] + expand(aux[at, :], INFLOW, width) * dot3(reads[at], now)
+        act, _ = silu_parts(gate_rows(step))
+        gated = mix[step] * act
+        squares[step] = column_sums(gated * gated)
+        loop(1, 4, lambda d: square_copy(step, d).start())
+
+    @pl.when((step > blocks) & (step <= 2 * blocks) & ((step - blocks - 1) // half == core))
+    def _():
+        settle(lax.rem(step - blocks - 1, half))
+
+    @pl.when((step >= blocks) & (step < 2 * blocks))
+    def _():
+        block = step - blocks
+        slot = lax.rem(block, half)
+        own = block // half == core
+
+        def add(d, sum_row):
+            square_copy(block, d).wait_recv()
+            return sum_row + square_land[d, block]
+
+        row = lax.rsqrt(lax.fori_loop(1, 4, add, squares[block]) / total + EPSILON)
+        scales[block] = row
+        act, _ = silu_parts(gate_rows(block))
+        normed = (mix[block] * act * as_column(row, width) * gain[...]).astype(BF16)
+
+        @pl.when(own & (core == 1))
+        def _():
+            core_copy(slot).wait_send()
+
+        parts[slot] = dot(normed, wo[...])
+
+        @pl.when(jnp.logical_not(own))
+        def _():
+            core_copy(slot).start()
+
+    @pl.when((step >= 2 * blocks) & (step < 3 * blocks))
+    def _():
+        block = step - 2 * blocks
+        slot = lax.rem(block, half)
+        own = block // half == core
+
+        @pl.when(own)
+        def _():
+            x_copy(slot).wait_recv()
+            at = pl.ds(pl.multiple_of(slot * BLOCK, BLOCK), BLOCK)
+            outf = hid[at, :].astype(F32) + (mine[slot].astype(F32) + other[slot].astype(F32))
+            term = outf - teacher[at, :].astype(F32)
+            masked = as_column(valid[...].astype(F32), term.shape[1]) * term
+            error[...] += jnp.sum(masked * term, axis=0, keepdims=True)
+            grad = masked * factor[0]
+            d_out[...] = grad
+            d_branch[block] = grad.astype(BF16)
+            grad_copy(block).start()
+            out_block[slot] = outf.astype(BF16)
+            for copy in out_copies(slot):
+                copy.start()
+
+        @pl.when(jnp.logical_not(own))
+        def _():
+            grad_copy(block).wait_recv()
+
+        act, _ = silu_parts(gate_rows(block))
+        gated = mix[block] * act
+        scaled = gated * as_column(scales[block], width)
+        normed = (scaled * gain[...]).astype(BF16)
+        grads = d_branch[block]
+        g_wo[...] += dot(normed, grads, 0, 0)
+        d_normed = dot(grads, wo_t[...])
+        g_gain[...] += jnp.sum(d_normed * scaled, axis=0, keepdims=True)
+        pulled = d_normed * gain[...]
+        weighted[lax.rem(block, 2)] = pulled
+        crosses[block] = column_sums(pulled * gated)
+        loop(1, 4, lambda d: cross_copy(block, d).start())
+
+    @pl.when(step > 2 * blocks)
+    def _():
+        block = step - 2 * blocks - 1
+
+        def add(d, sum_row):
+            cross_copy(block, d).wait_recv()
+            return sum_row + cross_land[d, block]
+
+        cross = lax.fori_loop(1, 4, add, crosses[block])
+        act, slope = silu_parts(gate_rows(block))
+        gated = mix[block] * act
+        row = scales[block]
+        pull = as_column(row * row * row * cross / total, width)
+        d_gated = as_column(row, width) * weighted[lax.rem(block, 2)] - gated * pull
+        dy = d_gated * act
+        d_mixer[...] = dy
+        d_gate[...] = (d_gated * mix[block] * slope).astype(BF16)
+        reads, _ = silu_parts(pre_c[...])
+        for c in range(BLOCK // CHUNK):
+            at = slice(c * CHUNK, (c + 1) * CHUNK)
+            inflow = expand(aux[at, :], INFLOW, width)
+            keeps[block * (BLOCK // CHUNK) + c] = jnp.broadcast_to(inflow[CHUNK - 1 :], (8, width))
+            gloc[block * (BLOCK // CHUNK) + c] = dot3(reads[at], dy[at] * inflow, 0, 0)
+
+    @pl.when(step == 3 * blocks)
+    def _():
+        state[...] = jnp.zeros_like(state)
+        chunks = gloc.shape[0]
+
+        def back(i, decay):
+            c = chunks - 1 - i
+            added = gloc[c]
+            gloc[c] = state[...]
+            pkb[c] = decay
+            state[...] = state[...] * keeps[c, :1] + added
+            return decay * keeps[c]
+
+        decay = lax.fori_loop(0, chunks, back, jnp.ones((8, width), F32))
+        fin[:CHUNK] = state[...]
+        fin[CHUNK:] = decay
+
+        def drain(block):
+            def both(d):
+                square_copy(block, d).wait_send()
+                cross_copy(block, d).wait_send()
+
+            loop(1, 4, both)
+
+            @pl.when(block // half == core)
+            def _():
+                grad_copy(block).wait_send()
+
+        loop(0, blocks, drain)
+
+        @pl.when(core == 0)
+        def _():
+            loop(0, half, lambda slot: core_copy(slot).wait_send())
+
+        def finish(slot):
+            x_copy(slot).wait_send()
+            here, there = out_copies(slot)
+            here.wait()
+            there.wait()
+
+        loop(0, half, finish)
+
+
+def intra_back_kernel(idx, d_mixer, pre_i, pre_p, aux, low_t, d_gate, d_scaled, d_maps, g_wg):
     @pl.when(pl.program_id(0) == 0)
     def _():
-        enter([{"head": core_peer()}])
-
-    act, _ = silu_parts(gate[...])
-    gated = mixer[...] * act
-    normed = (gated * gate_scale(square[...], total) * gain[...]).astype(BF16)
-    add_halves(dot(normed, wo[...]), mine, away, land, send_sem, land_sem)
-
-
-def both_cores(buffers, wholes, sems):
-    step = pl.program_id(0)
-    half = pl.num_programs(0)
-    local, send, land = sems
-
-    def copies(k, slot):
-        rows = pl.ds(pl.multiple_of((core_bit() * half + slot) * BLOCK, BLOCK), BLOCK)
-        here = pltpu.make_async_copy(buffers[k].at[slot], wholes[k].at[rows], local.at[k * half + slot])
-        there = to_peer(buffers[k].at[slot], wholes[k].at[rows], send, land, k * half + slot)
-        return here, there
-
-    for k in range(len(wholes)):
-        for copy in copies(k, step):
-            copy.start()
-
-    @pl.when(step == half - 1)
-    def _():
-        for k in range(len(wholes)):
-
-            def drain(slot, carry, k=k):
-                here, there = copies(k, slot)
-                here.wait()
-                there.wait()
-                return carry
-
-            lax.fori_loop(0, half, drain, 0)
-
-
-def loss_kernel(factor, hid, teacher, valid, mine, other, out, d_branch, d_out, error, out_block, grad_block, *sems):
-    step = pl.program_id(0)
-
-    @pl.when(step == 0)
-    def _():
-        error[...] = jnp.zeros_like(error)
-        enter([{"head": core_peer()}])
-
-    outf = hid[...].astype(F32) + (mine[...].astype(F32) + other[...].astype(F32))
-    term = outf - teacher[...].astype(F32)
-    masked = as_column(valid[...].astype(F32)) * term
-    error[...] += jnp.sum(masked * term, axis=0, keepdims=True)
-    grad = masked * factor[0]
-    d_out[...] = grad
-    out_block[step] = outf.astype(BF16)
-    grad_block[step] = grad.astype(BF16)
-    both_cores([out_block, grad_block], [out, d_branch], sems)
-
-
-def branch_back_kernel(d_branch, mixer, gate, square, gain, wo, weighted, cross, g_gain, g_wo, *, total):
-    step = pl.program_id(0)
-
-    @pl.when(step == 0)
-    def _():
-        g_gain[...] = jnp.zeros_like(g_gain)
-        g_wo[...] = jnp.zeros_like(g_wo)
-
-    act, _ = silu_parts(gate[...])
-    gated = mixer[...] * act
-    scaled = gated * gate_scale(square[...], total)
-    normed = (scaled * gain[...]).astype(BF16)
-    g_wo[...] += dot(normed, d_branch[...], 0, 0)
-    d_normed = dot(d_branch[...], wo[...], 1, 1)
-    g_gain[...] += jnp.sum(d_normed * scaled, axis=0, keepdims=True)
-    grad = d_normed * gain[...]
-    weighted[...] = grad
-    cross[...] = column_sums(grad * gated)
-
-
-def gate_back_kernel(
-    weighted, mixer, gate, square, cross, pre_c, aux, d_mixer, d_gate, gloc, pkl, fin, state, decay, *, total
-):
-    @pl.when(pl.program_id(0) == 0)
-    def _():
-        state[...] = jnp.zeros_like(state)
-        decay[...] = jnp.ones_like(decay)
-
-    width = mixer.shape[1]
-    act, slope = silu_parts(gate[...])
-    gated = mixer[...] * act
-    row = lax.rsqrt(square[...] / total + EPSILON)
-    scale = as_column(row)
-    pull = as_column(row * row * row * cross[...] / total)
-    d_gated = scale * weighted[...] - gated * pull
-    dy = d_gated * act
-    d_mixer[...] = dy
-    d_gate[...] = (d_gated * mixer[...] * slope).astype(BF16)
-    reads, _ = silu_parts(pre_c[...])
-    for c in reversed(range(BLOCK // CHUNK)):
-        at = slice(c * CHUNK, (c + 1) * CHUNK)
-        inflow = expand(aux[at, :], INFLOW, width)
-        gloc[c] = state[...]
-        pkl[c] = decay[...]
-        kept = inflow[CHUNK - 1 :]
-        state[...] = state[...] * kept + dot3(reads[at], dy[at] * inflow, 0, 0)
-        decay[...] = decay[...] * kept
-    fin[:CHUNK] = state[...]
-    fin[CHUNK:] = decay[...]
-
-
-def intra_back_kernel(idx, d_mixer, pre_i, pre_p, aux, low, d_gate, d_scaled, d_maps, g_wg):
-    @pl.when(pl.program_id(0) == 0)
-    def _():
         g_wg[...] = jnp.zeros_like(g_wg)
 
-    g_wg[...] += dot(low[...], d_gate[...], 0, 0)
+    g_wg[...] += dot(low_t[...], d_gate[...])
     width = d_mixer.shape[1]
     base = idx[1] + pl.program_id(0) * BLOCK
     maps, _ = silu_parts(pre_p[...])
@@ -423,6 +471,7 @@
         for ref in shifted:
             ref[...] = jnp.zeros_like(ref)
 
+    weight = weight[...].astype(F32)
     total = grad * weight[3:4]
     edge = jnp.zeros((8, grad.shape[1]), F32)
     acc[3:4] += jnp.sum(grad * inputs, axis=0, keepdims=True)
@@ -610,12 +659,13 @@
 
 
 def finale_kernel(
-    d_scaled, d_maps, pre_i, pre_p, in_i, in_p, halo_low, halo_i, halo_p, aux, gloc, pkl, gin, states, d_mixer, mixer, skip, dlog,
-    conv_i, conv_p, low, d_gate, wg, wi, ws, wp, hid, d_out, gain, error, g_wo, g_wg, g_gain,
-    grad_all, sums, out_wo, out_wg, out_wi, out_pack, out_wp, out_small,
+    d_scaled, d_maps, pre_i, pre_p, in_i, in_p, halo_low, halo_i, halo_p, aux, gloc, pkl, gin, states, d_mixer, mixer, given,
+    conv_i, conv_p, low_t, d_gate, wg, wi, ws, wp, hid, d_out, gain, error, g_wo, g_wg, g_gain, factor,
+    grad_all, out_norm, out_loss, out_wo, out_wg, out_wi, out_wp, out_ws, out_conv_i, out_bias_i, out_conv_p, out_bias_p,
+    out_sbias, out_dlog, out_skip, out_gain,
     shift_i0, shift_i1, shift_i2, shift_p0, shift_p1, shift_p2, small, small_p, heads,
-    parts, land, mine, other, row, row_land, g_wi, g_ws, pack, g_wp, pair_small, sum_small, sum_wp, spread_wp, spread_small,
-    grad_own, grad_other, edge, edge_core, edge_plane, edge_ahead,
+    parts, land, mine, other, row, row_land, g_wi, g_ws, pack, g_wp, pair_small, sum_small, sum_wp, sum_pack, spread_wp, spread_small,
+    grad_own, grad_other, wg_t, wi_t, ws_t, wp_t, edge, edge_core, edge_plane, edge_ahead,
     core_send, core_land, x_send, x_land, edge_send, edge_land, grad_send, grad_land, row_send, row_arrive, *more,
 ):
     shifted = (shift_i0, shift_i1, shift_i2, shift_p0, shift_p1, shift_p2)
@@ -626,7 +676,7 @@
     seq, devices = lax.axis_index("seq"), lax.axis_size("seq")
     head, core = lax.axis_index("head"), core_bit()
     width = wi.shape[1]
-    model = low.shape[1]
+    model = low_t.shape[0]
     behind, ahead = lax.rem(seq + devices - 1, devices), lax.rem(seq + 1, devices)
     group = 2 * devices
     me = 2 * seq + core
@@ -646,10 +696,13 @@
         for source, out in ((g_wp, spread_wp), (pair_small, spread_small)):
             refs = take(HEAD_REFS)
             head_parts.append(HeadSum(source, out, *refs[:4], refs[4:]))
-        for source in (g_wo, g_wg, g_wi, pack, head_parts[0].quarter, head_parts[1].quarter):
+        third = model // 3
+        thirds = [g_wi.at[pl.ds(i * third, third)] for i in range(3)]
+        outs_wi = [out_wi.at[pl.ds(i * third, third)] for i in range(3)]
+        for source in (g_wo, g_wg, *thirds, pack, head_parts[0].quarter, head_parts[1].quarter):
             refs = take(SUM_REFS)
             seq_sums.append(SeqSum(source, *refs[:5], refs[5:]))
-        s_wo, s_wg, s_wi, s_pack, s_wp, s_small = seq_sums
+        s_wo, s_wg, *s_wi, s_pack, s_wp, s_small = seq_sums
         wide = list(zip(head_parts, (s_wp, s_small), (sum_wp, sum_small)))
 
     def device(distance):
@@ -684,6 +737,8 @@
             ref[...] = jnp.zeros_like(ref)
         row[:1] = jnp.zeros_like(row[:1])
         row[1:] = error[...]
+        for ref, weight in ((wg_t, wg), (wi_t, wi), (ws_t, ws), (wp_t, wp)):
+            ref[...] = jnp.transpose(weight[...])
         pl.semaphore_wait(barrier, group)
         if summing:
             s_wo.begin()
@@ -695,7 +750,8 @@
     dy = d_mixer[...]
     upper = triangle(True)
     lane = lax.broadcasted_iota(jnp.int32, (CHUNK, LANES), 1)
-    grown = jnp.exp(dlog[...])
+    grown = jnp.exp(given[1:2])
+    skip = expand(given[...], 0, width)[2:3]
     pieces, pieces_p, pieces_s = [], [], []
     for c in range(BLOCK // CHUNK):
         at = slice(c * CHUNK, (c + 1) * CHUNK)
@@ -712,7 +768,7 @@
         d_reads = d_maps[at, LANES:] + dot3(dy[at] * inflow, state, 1, 1)
         d_keys = d_maps[at, :LANES] + dot3(scaled * outflow, grad_state, 1, 1)
         pieces_p.append(jnp.concatenate([d_keys, d_reads], axis=1))
-        plain = mixer[at, :] - skip[...] * values[at]
+        plain = mixer[at, :] - skip * values[at]
         d_cum = head_sums(dy[at] * plain - scaled * total)
         carried = jnp.sum(grad_state * state, axis=0, keepdims=True) * inflow[CHUNK - 1 :]
         carried = carried + jnp.sum(scaled * passed, axis=0, keepdims=True)
@@ -724,7 +780,7 @@
         d_decay = jnp.where(lane < 8, -d_logs * table * grown, 0.0)
         heads[0:1] += jnp.sum(d_raw, axis=0, keepdims=True)
         heads[1:2] += jnp.sum(d_decay, axis=0, keepdims=True)
-        pieces.append(total * sizes + dy[at] * skip[...])
+        pieces.append(total * sizes + dy[at] * skip)
     small[5:6] += jnp.sum(dy * values, axis=0, keepdims=True)
     grad = jnp.concatenate(pieces, axis=0) * slope
     pos = (base + lax.broadcasted_iota(jnp.int32, (BLOCK, 1), 0)).astype(F32)
@@ -739,9 +795,9 @@
 
     inner = whole.astype(BF16)
     d_step = jnp.concatenate(pieces_s, axis=0)
-    part = dot(d_gate[...], wg[...], 1, 1) + dot(inner, wi[...], 1, 1) + dot(d_step, ws[...], 1, 1)
+    part = dot(d_gate[...], wg_t[...]) + dot(inner, wi_t[...]) + dot(d_step, ws_t[...])
     high, rest = halves(whole_p)
-    part = part + (dot(high, wp[...], 1, 1) + dot(rest, wp[...], 1, 1))
+    part = part + (dot(high, wp_t[...]) + dot(rest, wp_t[...]))
     upper = (step < half).astype(jnp.int32)
     slot = half - 1 - lax.rem(step, half)
     own = upper == core
@@ -765,9 +821,9 @@
     def _():
         core_copy(slot).start()
 
-    g_ws[...] += dot(d_step, low[...], 0, 0)[:8]
-    g_wp[...] += dot(low[...], high, 0, 0) + dot(low[...], rest, 0, 0)
-    g_wi[:model] += dot(low[...], inner, 0, 0)
+    g_ws[...] += dot(low_t[...], d_step)
+    g_wp[...] += dot(low_t[...], high) + dot(low_t[...], rest)
+    g_wi[:model] += dot(low_t[...], inner)
 
     def norm_back(at):
         x_copy(at).wait_recv()
@@ -789,13 +845,12 @@
 
     if summing:
 
-        @pl.when(step == half)
-        def _():
-            s_wo.pass_on()
-
-        @pl.when(step == blocks - 2)
-        def _():
-            s_wg.pass_on()
+        moves = (s_wo.pass_on, s_wg.pass_on, s_wo.finish, s_wg.finish, s_wo.collect)
+        for number, move in enumerate(moves):
+
+            @pl.when(step == number + 2)
+            def _(move=move):
+                move()
 
     @pl.when(last)
     def _():
@@ -804,20 +859,21 @@
         before_p = jnp.concatenate([jnp.zeros_like(outer_p), outer_p], axis=0)
         high_p, rest_p = halves(before_p)
         g_wp[...] += dot(halo_low[...], high_p, 0, 0) + dot(halo_low[...], rest_p, 0, 0)
-        edge_part = dot(before, wi[...], 1, 1) + (dot(high_p, wp[...], 1, 1) + dot(rest_p, wp[...], 1, 1))
+        edge_part = dot(before, wi_t[...]) + (dot(high_p, wp_t[...]) + dot(rest_p, wp_t[...]))
         edge[0] = edge_part[8:]
         edge_copy(0, edge_core, beside).start()
         pack[:6] = small[:6]
         pack[6:7] = g_gain[...]
-        pack[8:16] = g_ws[:, :width]
-        pack[16:24] = g_ws[:, width:]
+        step_rows = jnp.transpose(g_ws[...])[:8]
+        pack[8:16] = step_rows[:, :width]
+        pack[16:24] = step_rows[:, width:]
         pack[24:32, : heads.shape[1]] = heads[...]
         pair_small[:8] = small_p[...]
         if summing:
             for h_sum, _, _ in wide:
                 h_sum.fold_core().start()
-            s_wi.begin()
-            s_pack.begin()
+            s_wi[0].begin()
+            s_wi[1].begin()
 
         @pl.when(core == 0)
         def _():
@@ -826,14 +882,15 @@
         if summing:
             for h_sum, _, _ in wide:
                 h_sum.fold()
+            s_wi[2].begin()
+            s_pack.begin()
         edge_copy(0, edge_core, beside).wait_recv()
         edge[1] = edge[0] + edge_core[...]
         edge_copy(1, edge_plane, across).start()
         if summing:
-            s_wo.finish()
-            s_wi.pass_on()
-            s_wg.finish()
-            s_pack.pass_on()
+            s_wg.collect()
+            s_wi[0].pass_on()
+            s_wi[1].pass_on()
         edge_copy(1, edge_plane, across).wait_recv()
         edge[2] = edge[1] + edge_plane[...]
         edge_copy(2, edge_ahead, {"seq": behind}).start()
@@ -843,44 +900,62 @@
         norm_back(2)
         norm_back(1)
         if summing:
-            s_wo.collect()
-            s_wi.finish()
-            s_pack.finish()
+            s_wi[2].pass_on()
+            s_pack.pass_on()
+            s_wi[0].finish()
         for _, s_sum, _ in wide:
             s_sum.pass_on()
         norm_back(0)
         norm_back(3)
         loop(1, group, lambda d: hand(d).start())
         if summing:
-            s_wg.collect()
+            s_wi[1].finish()
+            s_wi[2].finish()
+            s_pack.finish()
             for _, s_sum, _ in wide:
                 s_sum.finish()
+            s_wi[0].collect()
             s_wo.store(out_wo)
+            s_wi[1].collect()
+            s_wi[2].collect()
             for _, s_sum, _ in wide:
                 s_sum.collect()
-            s_wi.collect()
             s_pack.collect()
+            s_wg.store(out_wg)
             for h_sum, s_sum, total in wide:
                 s_sum.store(total)
                 h_sum.spread(total)
-            s_wg.store(out_wg)
+            for s_sum, out in zip(s_wi, outs_wi):
+                s_sum.store(out)
             for h_sum, _, _ in wide:
                 h_sum.spread_more()
-            s_wi.store(out_wi)
-            s_pack.store(out_pack)
-            for (h_sum, _, _), out in zip(wide, (out_wp, out_small)):
+            s_pack.store(sum_pack)
+            for h_sum, _, _ in wide:
                 h_sum.finish()
-                out[...] = h_sum.out[...]
+            out_wp[...] = spread_wp[...]
+            totals, pair_totals = sum_pack[:32], spread_small[:8]
             for s_sum in seq_sums:
                 s_sum.drain()
         else:
-            for out, ref in (
-                (out_wo, g_wo), (out_wg, g_wg), (out_wi, g_wi), (out_pack, pack), (out_wp, g_wp), (out_small, pair_small),
-            ):
+            for out, ref in ((out_wo, g_wo), (out_wg, g_wg), (out_wi, g_wi), (out_wp, g_wp)):
                 out[...] = ref[...]
+            totals, pair_totals = pack[:32], pair_small[:8]
+        heads_here = out_sbias.shape[1]
+        out_conv_i[...] = totals[:4]
+        out_bias_i[...] = totals[4:5]
+        out_skip[...] = head_sums(totals[:8])[5:6, :heads_here]
+        out_gain[...] = totals[6:7]
+        out_ws[...] = jnp.transpose(jnp.concatenate([totals[8:16], totals[16:24]], axis=1))[:, :heads_here]
+        out_sbias[...] = totals[24:25, :heads_here]
+        out_dlog[...] = totals[25:26, :heads_here]
+        out_conv_p[...] = pair_totals[:4]
+        out_bias_p[...] = pair_totals[4:5]
         row_land[me] = row[...]
         loop(1, group, lambda d: hand(d).wait())
-        sums[...] = lax.fori_loop(1, group, lambda d, total: total + row_land[d], row_land[0])
+        both_rows = lax.fori_loop(1, group, lambda d, total: total + row_land[d], row_land[0])
+        out_norm[...] = both_rows[:1]
+        per_token = factor[0] / (group * half * BLOCK * model)
+        out_loss[...] = jnp.sum(both_rows[1:], axis=1, keepdims=True) * per_token
         for at, to in enumerate((beside, across, {"seq": behind})):
             edge_copy(at, edge_core, to).wait_send()
 
@@ -948,10 +1023,13 @@
 
 def carried(total, axis, backward):
     mine = lax.axis_index(axis)
+    decays = slice(CHUNK, total.shape[0] - 1)
 
     def join(early, late):
         decay = late[CHUNK : CHUNK + 1]
-        return jnp.concatenate([late[:CHUNK] + decay * early[:CHUNK], late[CHUNK:] * early[CHUNK:]])
+        return jnp.concatenate([
+            late[:CHUNK] + decay * early[:CHUNK], late[decays] * early[decays], late[-1:] + early[-1:],
+        ])
 
     reached = jnp.concatenate([jnp.zeros_like(total[:CHUNK]), jnp.ones_like(total[CHUNK:])])
     for bit in bits(axis):
@@ -959,11 +1037,7 @@
         later = ((mine & bit) == 0) if backward else ((mine & bit) != 0)
         reached = jnp.where(later, join(other, reached), reached)
         total = jnp.where(later, join(other, total), join(total, other))
-    return reached[:CHUNK]
-
-
-def padded(row, lanes=LANES):
-    return jnp.zeros((1, lanes), F32).at[0, : row.shape[0]].set(row)
+    return reached[:CHUNK], total[-1, 0]
 
 
 def shards(
@@ -983,18 +1057,17 @@
     idx = jnp.stack([core, offset]).astype(jnp.int32)
     edge_rows = 16
 
-    starts = jnp.full((1, LANES), FAR, F32).at[0, : doc_starts.shape[0]].set(doc_starts.astype(F32))
-    ws = jnp.zeros((model, LANES), BF16).at[:, :heads].set(w_step)
-    sbias, dlog = padded(step_bias), padded(decay_log)
-    skip = jnp.repeat(skip_gain, HEAD_DIM)[None, :]
+    given = jnp.stack([
+        jnp.pad(step_bias, (0, LANES - heads)), jnp.pad(decay_log, (0, LANES - heads)), jnp.pad(skip_gain, (0, LANES - heads)),
+        jnp.pad(doc_starts.astype(F32), (0, LANES - doc_starts.shape[0]), constant_values=FAR),
+        *[jnp.zeros((LANES,), F32)] * 4,
+    ])
+    ws = jnp.pad(w_step, ((0, 0), (0, LANES - heads)))
     gain, out_gain = norm_gain[None, :], gate_gain[None, :]
-    conv_i, conv_p = conv_inner.astype(F32), conv_pair.astype(F32)
-    bias_i, bias_p = bias_inner.astype(F32)[None, :], bias_pair.astype(F32)[None, :]
+    bias_i, bias_p = bias_inner[None, :], bias_pair[None, :]
     valid = valid_mask[None, :]
 
     tail = shifted(hidden[rows - edge_rows :], "seq", 1)
-    count = total_over(jnp.full((8, LANES), jnp.sum(valid_mask.astype(F32))), "seq")[0, 0]
-    factor = (rows * lax.axis_size("seq")) / count
 
     def by(w, column=0):
         return (BLOCK, w), lambda i, *_: (i, column)
@@ -1002,32 +1075,24 @@
     def back(w, column=0):
         return (BLOCK, w), lambda i, *_: (blocks - 1 - i, column)
 
-    row = ((1, BLOCK), lambda i, *_: (0, i))
-    row_back = ((1, BLOCK), lambda i, *_: (0, blocks - 1 - i))
     grid3 = lambda n: ((per, n, width), lambda i, *_: (i, 0, 0))
     back3 = lambda n: ((per, n, width), lambda i, *_: (blocks - 1 - i, 0, 0))
     whole = (None, None)
 
-    def send_order(w):
-        return (BLOCK, w), lambda i: (lax.rem(i + half * (1 - core_bit()), blocks), 0)
-
-    send_row = ((1, BLOCK), lambda i: (0, lax.rem(i + half * (1 - core_bit()), blocks)))
-    half_own = lambda w: ((BLOCK, w), lambda i: (i + half * core_bit(), 0))
-    tail_half = lambda w: ((BLOCK, w), lambda i: (jnp.maximum(i - half, 0), 0))
     dma = pltpu.SemaphoreType.DMA
-    swap_scratch = [pltpu.VMEM((half, BLOCK, model), F32)] * 2 + [dma((half,))] * 2
 
     halo_block = ((edge_rows, model), lambda i, *_: (jnp.maximum(i * (BLOCK // edge_rows) - 1, 0), 0))
-    (low, in_i, in_p, pre_i, pre_p, aux, halo_low, halo_i, halo_p, sloc, pkl, fin) = call(
+    (low, low_t, in_i, in_p, pre_i, pre_p, aux, halo_low, halo_i, halo_p, sloc, pkl, fin) = call(
         project_kernel,
         blocks,
         [
-            (idx, None, None), (starts, *whole), (hidden, *by(model)), (hidden, *halo_block), (tail, *whole),
-            (gain, *whole), (w_inner, *whole), (w_pair, *whole), (ws, *whole), (conv_i, *whole), (conv_p, *whole),
-            (bias_i, *whole), (bias_p, *whole), (sbias, *whole), (dlog, *whole),
+            (idx, None, None), (given, *whole), (valid, (1, BLOCK), lambda i, *_: (0, i)), (hidden, *by(model)), (hidden, *halo_block), (tail, *whole),
+            (gain, *whole), (w_inner, *whole), (w_pair, *whole), (ws, *whole), (conv_inner, *whole), (conv_pair, *whole),
+            (bias_i, *whole), (bias_p, *whole),
         ],
         [
-            ((rows, model), BF16, *by(model)), ((rows, width), BF16, *by(width)), ((rows, pair_width), BF16, *by(pair_width)),
+            ((rows, model), BF16, *by(model)), ((model, rows), BF16, (model, BLOCK), lambda i, *_: (0, i)),
+            ((rows, width), BF16, *by(width)), ((rows, pair_width), BF16, *by(pair_width)),
             ((rows, width), F32, *by(width)), ((rows, pair_width), F32, *by(pair_width)), ((rows, LANES), F32, *by(LANES)),
             ((edge_rows, model), BF16, *whole), ((edge_rows, width), BF16, *whole), ((edge_rows, pair_width), BF16, *whole),
             ((chunks, CHUNK, width), F32, *grid3(CHUNK)), ((chunks, 8, width), F32, *grid3(8)),
@@ -1035,107 +1100,79 @@
         ],
         [
             pltpu.VMEM((BLOCK + edge_rows, width), F32), pltpu.VMEM((BLOCK + edge_rows, pair_width), F32),
-            pltpu.VMEM((CHUNK, width), F32), pltpu.VMEM((8, width), F32),
+            pltpu.VMEM((CHUNK, width), F32), pltpu.VMEM((8, width), F32), pltpu.VMEM((1, 1), F32),
         ],
         prefetch=1, flops=3e9, moved=2e7,
     )
-    state_in = carried(fin, "seq", False)
+    state_in, count = carried(fin, "seq", False)
+    factor = (rows * lax.axis_size("seq")) / count
     gate, local = call(
         intra_kernel,
         blocks,
         [
             (idx, None, None), (low, *by(model)), (w_gate, *whole), (pre_i, *by(width)), (pre_p, *by(pair_width)),
-            (aux, *by(LANES)), (skip, *whole),
+            (aux, *by(LANES)), (given, *whole),
         ],
         [((rows, width), F32, *by(width)), ((rows, width), F32, *by(width))],
         prefetch=1, flops=4e9, moved=2e7,
     )
-    mixer, states, square = call(
-        mix_kernel,
-        blocks,
+    size = lax.axis_size("seq")
+    vmem = ("vmem", None)
+    once = lambda w: ((rows // 2, w), lambda i: (core_bit(), 0))
+    first_or_last = lambda i: jnp.where(i < blocks, i, jnp.clip(i - 2 * blocks - 1, 0, blocks - 1))
+    early = lambda i: jnp.minimum(i, blocks - 1)
+    late = lambda i: jnp.clip(i - 2 * blocks - 1, 0, blocks - 1)
+    own_slot = lambda i: jnp.clip(i - 2 * blocks - half * core_bit(), 0, half - 1)
+    early3 = lambda n: ((per, n, width), lambda i: (early(i), 0, 0))
+    states, d_mixer, d_gate, gloc, pkb, fin_back, output, d_out, error, g_gain, g_wo, mixer = call(
+        partial(mid_kernel, total=inner_total),
+        3 * blocks + 1,
         [
-            (pre_p, *by(LANES, 1)), (aux, *by(LANES)), (sloc, *grid3(CHUNK)), (pkl, *grid3(8)), (state_in, *whole),
-            (local, *by(width)), (gate, *by(width)),
-        ],
-        [((rows, width), F32, *by(width)), ((chunks, CHUNK, width), F32, *grid3(CHUNK)), ((1, rows), F32, *row)],
-        flops=1e9, moved=2e7,
-    )
-    square = total_over(square, "head")
-    (mine,) = call(
-        partial(branch_kernel, total=inner_total),
-        blocks,
-        [
-            (mixer, *send_order(width)), (gate, *send_order(width)), (square, *send_row), (out_gain, *whole), (w_output, *whole),
-        ],
-        [((rows // 2, model), BF16, *tail_half(model))],
-        swap_scratch,
-        flops=1.2e9, moved=1e7, collective=2,
-    )
-    other = swap(mine, "head", 2)
-    output, d_branch, d_out, error = call(
-        loss_kernel,
-        half,
-        [
-            (factor.reshape(1), "smem", None), (hidden, *half_own(model)), (teacher, *half_own(model)),
-            (valid, (1, BLOCK), lambda i: (0, i + half * core_bit())), (mine, *by(model)), (other, *by(model)),
+            (factor.reshape(1), "smem", None), (pre_p, (BLOCK, LANES), lambda i: (first_or_last(i), 1)),
+            (aux, (BLOCK, LANES), lambda i: (first_or_last(i), 0)), (sloc, *early3(CHUNK)), (pkl, *early3(8)), (state_in, *whole),
+            (local, (BLOCK, width), lambda i: (early(i), 0)), (gate, *vmem), (out_gain, *whole), (w_output, *whole),
+            (hidden, *once(model)), (teacher, *once(model)),
+            (valid, (1, BLOCK), lambda i: (0, own_slot(i) + half * core_bit())),
         ],
         [
-            ((rows, model), BF16, "any", None), ((rows, model), BF16, "any", None),
-            ((rows // 2, model), F32, *by(model)), ((1, model), F32, *whole),
-        ],
-        [pltpu.VMEM((half, BLOCK, model), BF16)] * 2 + [dma((2 * half,))] * 3,
-        flops=1e8, moved=1.5e7, collective=3,
-    )
-    weighted, cross, g_gain, g_wo = call(
-        partial(branch_back_kernel, total=inner_total),
-        blocks,
-        [
-            (d_branch, *by(model)), (mixer, *by(width)), (gate, *by(width)), (square, *row), (out_gain, *whole),
-            (w_output, *whole),
+            ((chunks, CHUNK, width), F32, *early3(CHUNK)), ((rows, width), F32, (BLOCK, width), lambda i: (late(i), 0)),
+            ((rows, width), BF16, (BLOCK, width), lambda i: (late(i), 0)), ((chunks, CHUNK, width), F32, *vmem),
+            ((chunks, 8, width), F32, *vmem), ((CHUNK + 8, width), F32, *vmem), ((rows, model), BF16, "any", None),
+            ((rows // 2, model), F32, (BLOCK, model), lambda i: (own_slot(i), 0)), ((1, model), F32, *whole),
+            ((1, width), F32, *whole), ((width, model), F32, *whole), ((blocks, BLOCK, width), F32, *vmem),
         ],
         [
-            ((rows, width), F32, *by(width)), ((1, rows), F32, *row), ((1, width), F32, *whole),
-            ((width, model), F32, *whole),
+            pltpu.VMEM((blocks, 1, BLOCK), F32), pltpu.VMEM((4, blocks, 1, BLOCK), F32),
+            pltpu.VMEM((blocks, 1, BLOCK), F32), pltpu.VMEM((4, blocks, 1, BLOCK), F32), pltpu.VMEM((blocks, 1, BLOCK), F32),
+            pltpu.VMEM((half, BLOCK, model), F32), pltpu.VMEM((half, BLOCK, model), F32),
+            pltpu.VMEM((half, BLOCK, model), BF16), pltpu.VMEM((half, BLOCK, model), BF16),
+            pltpu.VMEM((blocks, BLOCK, model), BF16), pltpu.VMEM((half, BLOCK, model), BF16),
+            pltpu.VMEM((2, BLOCK, width), F32), pltpu.VMEM((chunks, 8, width), F32), pltpu.VMEM((CHUNK, width), F32),
+            pltpu.VMEM((model, width), BF16), dma((4 * blocks,)), dma((4 * blocks,)), dma((4 * blocks,)), dma((4 * blocks,)), dma((half,)), dma((half,)),
+            dma((half,)), dma((half,)), dma((blocks,)), dma((blocks,)), dma((half,)), dma((half,)), dma((half,)),
         ],
-        flops=2.4e9, moved=1.5e7,
+        flops=6e9, moved=6e7, collective=2, vmem=44,
     )
-    cross = total_over(cross, "head")
-    d_mixer, d_gate, gloc, pkb, fin_back = call(
-        partial(gate_back_kernel, total=inner_total),
-        blocks,
-        [
-            (weighted, *back(width)), (mixer, *back(width)), (gate, *back(width)), (square, *row_back), (cross, *row_back),
-            (pre_p, *back(LANES, 1)), (aux, *back(LANES)),
-        ],
-        [
-            ((rows, width), F32, *back(width)), ((rows, width), BF16, *back(width)),
-            ((chunks, CHUNK, width), F32, *back3(CHUNK)), ((chunks, 8, width), F32, *back3(8)), ((CHUNK + 8, width), F32, *whole),
-        ],
-        [pltpu.VMEM((CHUNK, width), F32), pltpu.VMEM((8, width), F32)],
-        flops=1e9, moved=2e7,
-    )
-    grad_in = carried(fin_back, "seq", True)
+    mixer = mixer.reshape(rows, width)
+    grad_in, _ = carried(fin_back, "seq", True)
     d_scaled, d_maps, g_wg = call(
         intra_back_kernel,
         blocks,
         [
             (idx, None, None), (d_mixer, *by(width)), (pre_i, *by(width)), (pre_p, *by(pair_width)), (aux, *by(LANES)),
-            (low, *by(model)), (d_gate, *by(width)),
+            (low_t, (model, BLOCK), lambda i, *_: (0, i)), (d_gate, *by(width)),
         ],
         [((rows, width), F32, *by(width)), ((rows, pair_width), F32, *by(pair_width)), ((model, width), F32, *whole)],
         prefetch=1, flops=6e9, moved=2e7,
     )
-    size = lax.axis_size("seq")
     summing = size <= 8
 
     def piece(total_rows, tile):
         return -(-total_rows // (size * tile)) * tile
 
     r_wo, r_w, r_pack, r_wp, r_small = piece(width, 16), piece(model, 16), 8, piece(model // 4, 8), 8
-    vmem = ("vmem", None)
     core_wire = F32 if summing else BF16
-    once = lambda w: ((rows // 2, w), lambda i: (core_bit(), 0))
-    sum_shapes = [(r_wo, model, BF16), (r_w, width, BF16), (r_w, width, BF16), (r_pack, width, F32), (r_wp, pair_width, F32),
+    sum_shapes = [(r_wo, model, BF16), (r_w, width, BF16), *[(piece(model // 3, 16), width, BF16)] * 3, (r_pack, width, F32), (r_wp, pair_width, F32),
                   (r_small, pair_width, F32)]
     n_wo, n_w, n_pack = (r_wo * size, r_w * size, r_pack * size) if summing else (width, model, 64)
     scratch = [pltpu.VMEM((BLOCK + 16, width), F32)] * 3 + [pltpu.VMEM((BLOCK + 16, pair_width), F32)] * 3 + [
@@ -1143,11 +1180,13 @@
         pltpu.VMEM((half, BLOCK, model), core_wire), pltpu.VMEM((half, BLOCK, model), core_wire),
         pltpu.VMEM((half, BLOCK, model), BF16), pltpu.VMEM((half, BLOCK, model), BF16),
         pltpu.VMEM((2, model), F32), pltpu.VMEM((2 * size, 2, model), F32),
-        pltpu.VMEM((n_w, width), F32), pltpu.VMEM((8, model), F32), pltpu.VMEM((n_pack, width), F32),
+        pltpu.VMEM((n_w, width), F32), pltpu.VMEM((model, LANES), F32), pltpu.VMEM((n_pack, width), F32),
         pltpu.VMEM((model, pair_width), F32), pltpu.VMEM((32, pair_width), F32),
         pltpu.VMEM((r_small * size, pair_width), F32), pltpu.VMEM((r_wp * size, pair_width), F32),
-        pltpu.VMEM((model, pair_width), F32), pltpu.VMEM((32, pair_width), F32),
+        pltpu.VMEM((n_pack, width), F32), pltpu.VMEM((model, pair_width), F32), pltpu.VMEM((32, pair_width), F32),
         pltpu.VMEM((half, BLOCK, model), BF16), pltpu.VMEM((half, BLOCK, model), BF16),
+        pltpu.VMEM((width, model), BF16), pltpu.VMEM((width, model), BF16), pltpu.VMEM((LANES, model), BF16),
+        pltpu.VMEM((pair_width, model), BF16),
         pltpu.VMEM((3, 8, model), F32), pltpu.VMEM((8, model), F32), pltpu.VMEM((8, model), F32), pltpu.VMEM((8, model), F32),
         dma((half,)), dma((half,)), dma((half,)), dma((half,)), dma((3,)), dma((3,)), dma((half,)), dma((half,)),
         dma((2 * size,)), dma((2 * size,)),
@@ -1156,35 +1195,37 @@
         scratch += HeadSum.scratch(model, pair_width, r_wp * size) + HeadSum.scratch(32, pair_width, r_small * size)
         for r, lanes, wire in sum_shapes:
             scratch += SeqSum.scratch(r, lanes, wire, size)
-    grad_hidden, sums, g_wo, g_wg, g_wi, pack, g_wp, small_p = call(
+    grad_hidden, g_norm, loss, *grads, g_wp, g_ws, g_ci, g_bi, g_cp, g_bp, g_sb, g_dl, g_skip, g_gain = call(
         finale_kernel,
         blocks,
         [
             (d_scaled, *back(width)), (d_maps, *back(pair_width)), (pre_i, *back(width)), (pre_p, *back(pair_width)),
             (in_i, *back(width)), (in_p, *back(pair_width)), (halo_low, *whole), (halo_i, *whole), (halo_p, *whole),
             (aux, *back(LANES)), (gloc, *back3(CHUNK)), (pkb, *back3(8)), (grad_in, *whole), (states, *back3(CHUNK)),
-            (d_mixer, *back(width)), (mixer, *back(width)), (skip, *whole), (dlog, *whole), (conv_i, *whole), (conv_p, *whole),
-            (low, *back(model)), (d_gate, *back(width)), (w_gate, *whole), (w_inner, *whole), (ws, *whole), (w_pair, *whole),
+            (d_mixer, *back(width)), (mixer, *back(width)), (given, *whole), (conv_inner, *whole), (conv_pair, *whole),
+            (low_t, (model, BLOCK), lambda i, *_: (0, blocks - 1 - i)), (d_gate, *back(width)), (w_gate, *whole), (w_inner, *whole), (ws, *whole), (w_pair, *whole),
             (hidden, *once(model)), (d_out, *vmem), (gain, *whole), (error, *whole), (g_wo, *vmem), (g_wg, *vmem),
-            (g_gain, *whole),
+            (g_gain, *whole), (factor.reshape(1), "smem", None),
         ],
         [
-            ((rows, model), BF16, *vmem), ((2, model), F32, *vmem), ((n_wo, model), F32, *vmem),
-            ((n_w, width), F32, *vmem), ((n_w, width), F32, *vmem), ((n_pack, width), F32, *vmem),
-            ((model, pair_width), F32, *vmem), ((32, pair_width), F32, *vmem),
+            ((rows, model), BF16, *vmem), ((1, model), F32, *vmem), ((1, 1), F32, *vmem), ((n_wo, model), F32, *vmem),
+            ((n_w, width), F32, *vmem), ((n_w, width), F32, *vmem), ((model, pair_width), F32, *vmem),
+            ((model, heads), F32, *vmem), ((4, width), F32, *vmem), ((1, width), F32, *vmem), ((4, pair_width), F32, *vmem),
+            ((1, pair_width), F32, *vmem), ((1, heads), F32, *vmem), ((1, heads), F32, *vmem), ((1, heads), F32, *vmem),
+            ((1, width), F32, *vmem),
         ],
         scratch,
         flops=9e9, moved=8e7, collective=4, vmem=58,
     )
     if not summing:
-        g_wo, g_wg, g_wi, pack = lax.psum((g_wo, g_wg, g_wi, pack), "seq")
-        g_wp, small_p = lax.psum((g_wp, small_p), ("seq", "head"))
-    by_head, g_ws = pack[:8], jnp.concatenate([pack[8:16], pack[16:24]], axis=1)[:heads].T
-    pair_small, head_small = small_p[:8], pack[24:32, :LANES]
-    loss = jnp.sum(sums[1]) / (count * model)
+        *grads, g_ws, g_ci, g_bi, g_sb, g_dl, g_skip, g_gain = lax.psum(
+            (*grads, g_ws, g_ci, g_bi, g_sb, g_dl, g_skip, g_gain), "seq"
+        )
+        g_wp, g_cp, g_bp = lax.psum((g_wp, g_cp, g_bp), ("seq", "head"))
+    g_wo, g_wg, g_wi = grads
     return (
-        output, loss, grad_hidden, sums[0], g_wg, g_wi, g_wp, g_ws, by_head[:4], by_head[4], pair_small[:4], pair_small[4],
-        head_small[0, :heads], head_small[1, :heads], jnp.sum(by_head[5].reshape(heads, HEAD_DIM), axis=1), by_head[6], g_wo,
+        output, loss.reshape(()), grad_hidden, g_norm.reshape(-1), g_wg, g_wi, g_wp, g_ws, g_ci, g_bi.reshape(-1), g_cp,
+        g_bp.reshape(-1), g_sb.reshape(-1), g_dl.reshape(-1), g_skip.reshape(-1), g_gain.reshape(-1), g_wo,
     )
 
 

time: 322 us -> 308 us (0.957)
  Pallas kernels: 178 us -> 217 us
  waiting for transfers between devices: 60.7 us -> 29.7 us
  starting transfers between devices: 21.1 us -> 13.3 us
  local copies, waits for them, and re-layouts: 43.5 us -> 36.6 us
  other arithmetic: 12.5 us -> 5.91 us
    pallas_call x9 -> x5, Pallas kernels: 178 us -> 217 us  [call(): pl.pallas_call(kernel, grid_spec=pltpu.PrefetchScalarGridSpec(num_scalar_...]
    ppermute x14 -> x6, waiting for transfers between devices: 60.7 us -> 29.7 us  [swap(): return jax.tree.map(lambda v: lax.ppermute(v, axis, route), value)]
    ppermute x14 -> x6, starting transfers between devices: 16.3 us -> 8.42 us  [swap(): return jax.tree.map(lambda v: lax.ppermute(v, axis, route), value)]
    slice x18 -> x1, local copies, waits for them, and re-layouts: 6.75 us -> 0.51 us  [carried(): return (reached[:CHUNK], total[-1, 0])]
    another operation x5 -> x2, other arithmetic: 4.58 us -> 0.04 us  [join(): late[-1:] + early[-1:]]
    pallas_call x0 -> x3, other arithmetic: none -> 3.76 us  [call(): pl.pallas_call(kernel, grid_spec=pltpu.PrefetchScalarGridSpec(num_scalar_...]
    unnamed x119 -> x104, local copies, waits for them, and re-layouts: 31.7 us -> 31.2 us
  transfers between devices with their start and end apart: 15 -> 7, of which waited for: 12 -> 4; matrix products, arithmetic and copies ran while one was open for 4% -> 2% of each run, Pallas kernels for 5% -> 5%
where the time goes in v5:
time: 308 us; the launch traced here: 306 us
  Pallas kernels  217 us (70%)
  local copies, waits for them, and re-layouts  36.6 us (12%)
  waiting for transfers between devices  29.7 us (10%)
  starting transfers between devices  13.3 us (4%)
  other arithmetic  5.91 us (2%)
  between operations  4.28 us (1%)
    pallas_call x5, Pallas kernels, call(): pl.pallas_call(kernel, grid_spec=pltpu.PrefetchScalarGridSpec(num_scalar_...  217 us
    unnamed x104, local copies, waits for them, and re-layouts  31.2 us
    ppermute x6, waiting for transfers between devices, swap(): return jax.tree.map(lambda v: lax.ppermute(v, axis, route), value)  29.7 us
    ppermute x6, starting transfers between devices, swap(): return jax.tree.map(lambda v: lax.ppermute(v, axis, route), value)  8.42 us
  transfers between devices with their start and end apart: 7, of which 4 were waited for; matrix products, arithmetic and copies ran while one was open for 2% of the time, Pallas kernels for 5%

profile of v5, /device:TPU:0, one launch (start us, length us, event | category | flops | bytes accessed | tf_op | source)
XLA Modules:
  0.0 306.4 jit_solution(11235266173544767631)
XLA Ops:
  1.4 4.9 %collective-permute-start = (bf16[16,768]{1,0:T(8,128)(2,1)S(1)}, bf16[16,768]{1,0:T(8,128)(2,1)S(1)}, u32[]{:S(2)}, u32[]{:S(2)}) collective-permute-start(bf16[16,768]{1,0:T(8,128)(2,1)S(1)} %slice.240), channel_id=1, source_target_pairs={{0,4},{4,8},{8,12},{12,16},{16,20},{20,24},{24,28},{1,5},{5,9},{9,... | collective-permute-start | bytes 73736 | tf_op jit(solution)/shard_map/ppermute | solution.py:1010
  12.1 1.9 copy-done
  18.1 20.6 %shard_map.305 = (bf16[2048,768]{1,0:T(8,128)(2,1)S(1)}, bf16[768,2048]{1,0:T(8,128)(2,1)S(1)}, bf16[2048,384]{1,0:T(8,128)(2,1)S(1)}, bf16[2048,256]{1,0:T(8,12...) custom-call(s32[2]{0:T(128)S(1)} %pad_add_fusion.idx, ...), custom_call_target="tpu_custom_call" | custom-call | flops 3000000000 | bytes 20000000 | tf_op jit(solution)/shard_map/pallas_call | solution.py:985
  38.8 1.7 copy-done.30
  40.5 1.6 collective-permute-start.1
  42.1 7.1 %shard_map.306 = (f32[2048,384]{1,0:T(8,128)S(1)}, f32[2048,384]{1,0:T(8,128)S(1)}) custom-call(s32[2]{0:T(128)S(1)} %pad_add_fusion.idx, bf16[2048,768]{1,0:T(8,128)(2,1)S(1)} %get-tuple-element.68.low, bf16[768,384]{1,0:T(8,128)(2,1)S(1)} %copy-done.15, f32[2048,384]{1,0:T(8,128)S(1)} %get-tuple-element.69.pre_i, ...), custom_call_target="tpu_custom_call" | custom-call | flops 4000000000 | bytes 20000000 | tf_op jit(solution)/shard_map/pallas_call | solution.py:985
  49.2 1.7 copy-done.32
  51.0 1.7 collective-permute-start.2
  52.7 4.7 %collective-permute-done.2 = f32[136,384]{1,0:T(8,128)S(1)} collective-permute-done((f32[136,384]{1,0:T(8,128)S(1)}, f32[136,384]{1,0:T(8,128)S(1)}, u32[]{:S(2)}, u32[]{:S(2)}) %collective-permute-start.2) | collective-permute-done | bytes 208928 | tf_op jit(solution)/shard_map/ppermute | solution.py:1004
  57.6 2.7 collective-permute-start.3
  60.2 8.2 %collective-permute-done.3 = f32[136,384]{1,0:T(8,128)S(1)} collective-permute-done((f32[136,384]{1,0:T(8,128)S(1)}, f32[136,384]{1,0:T(8,128)S(1)}, u32[]{:S(2)}, u32[]{:S(2)}) %collective-permute-start.3) | collective-permute-done | bytes 208928 | tf_op jit(solution)/shard_map/ppermute | solution.py:1004
  70.4 77.8 %shard_map.307 = (f32[16,128,384]{2,1,0:T(8,128)}, f32[2048,384]{1,0:T(8,128)}, bf16[2048,384]{1,0:T(8,128)(2,1)S(1)}, f32[16,128,384]{2,1,0:T(8,128)}, f32[16,8...) custom-call(f32[1]{0:T(128)} %bitcast.7.factor, ...), custom_call_target="tpu_custom_call" | custom-call | flops 6000000000 | bytes 60000000 | tf_op jit(solution)/shard_map/pallas_call | solution.py:985
  148.8 2.3 copy-done.3
  151.1 9.6 %shard_map.308 = (f32[2048,384]{1,0:T(8,128)S(1)}, f32[2048,256]{1,0:T(8,128)S(1)}, f32[768,384]{1,0:T(8,128)S(1)}) custom-call(s32[2]{0:T(128)S(1)} %pad_add_fusion.idx, f32[2048,384]{1,0:T(8,128)S(1)} %copy-done.3, f32[2048,384]{1,0:T(8,128)S(1)} %get-tuple-element.69.pre_i, f32[2048,256]{1,0:T(8,128)S(1)} %get-tuple-element.64.pre_p.pre_c, ...), custom_call_target="tpu_custom_call" | custom-call | flops 6000000000 | bytes 20000000 | tf_op jit(solution)/shard_map/pallas_call | solution.py:985
  160.8 1.7 copy-done.4
  162.4 1.3 copy-done.6
  165.2 6.9 %collective-permute-done.5 = f32[136,384]{1,0:T(8,128)S(1)} collective-permute-done((f32[136,384]{1,0:T(8,128)S(1)}, f32[136,384]{1,0:T(8,128)S(1)}, u32[]{:S(2)}, u32[]{:S(2)}) %collective-permute-start.5) | collective-permute-done | bytes 208928 | tf_op jit(solution)/shard_map/ppermute | solution.py:1004
  172.3 1.7 collective-permute-start.6
  174.0 9.9 %collective-permute-done.6 = f32[136,384]{1,0:T(8,128)S(1)} collective-permute-done((f32[136,384]{1,0:T(8,128)S(1)}, f32[136,384]{1,0:T(8,128)S(1)}, u32[]{:S(2)}, u32[]{:S(2)}) %collective-permute-start.6) | collective-permute-done | bytes 208928 | tf_op jit(solution)/shard_map/ppermute | solution.py:1004
  184.6 101.6 %shard_map.309 = (bf16[2048,768]{1,0:T(8,128)(2,1)}, f32[1,768]{1,0:T(1,128)}, f32[1,1]{1,0:T(1,128)}, f32[384,768]{1,0:T(8,128)}, f32[768,384]{1,0:T(8,128)}, /...) custom-call(f32[2048,384]{1,0:T(8,128)} %copy-done.4, ...), custom_call_target="tpu_custom_call" | custom-call | flops 8999999488 | bytes 80000000 | tf_op jit(solution)/shard_map/pallas_call | solution.py:985
  288.7 1.3 reduce.14
  290.0 1.8 copy.36
  291.8 1.7 copy.50
  294.1 3.9 %copy.52 = bf16[2048,768]{1,0:T(8,128)(2,1)} copy(bf16[2048,768]{1,0:T(8,128)(2,1)} %get-tuple-element.186) | data formatting | bytes 6291456
  (143 shorter events, 24.3 us)
Async XLA Ops:
  1.4 10.7 %collective-permute-start = (bf16[16,768]{1,0:T(8,128)(2,1)S(1)}, bf16[16,768]{1,0:T(8,128)(2,1)S(1)}, u32[]{:S(2)}, u32[]{:S(2)}) collective-permute-start(bf16[16,768]{1,0:T(8,128)(2,1)S(1)} %slice.240), channel_id=1, source_target_pairs={{0,4},{4,8},{8,12},{12,16},{16,20},{20,24},{24,28},{1,5},{5,9},{9,... | collective-permute-start | bytes 73736 | tf_op jit(solution)/shard_map/ppermute | solution.py:1010
  11.1 27.7 %copy-start.21 = (f32[1,768]{1,0:T(1,128)}, f32[1,768]{1,0:T(1,128)S(1)}, u32[]{:S(2)}) copy-start(f32[1,768]{1,0:T(1,128)S(1)} %broadcast_in_dim.16.gain) | copy-start | bytes 9220
  12.0 26.8 %copy-start.13 = (bf16[768,128]{1,0:T(8,128)(2,1)}, bf16[768,128]{1,0:T(8,128)(2,1)S(1)}, u32[]{:S(2)}) copy-start(bf16[768,128]{1,0:T(8,128)(2,1)S(1)} %pad.22.ws) | copy-start | bytes 589828
  12.0 30.0 %copy-start.19 = (f32[8,128]{1,0:T(8,128)}, f32[8,128]{1,0:T(8,128)S(1)}, u32[]{:S(2)}) copy-start(f32[8,128]{1,0:T(8,128)S(1)} %stack.35.given) | copy-start | bytes 12292
  18.1 24.0 %copy-start.15 = (bf16[768,384]{1,0:T(8,128)(2,1)S(1)}, bf16[768,384]{1,0:T(8,128)(2,1)}, u32[]{:S(2)}) copy-start(bf16[768,384]{1,0:T(8,128)(2,1)} %wg.3) | copy-start | bytes 1769476
  40.5 108.4 %copy-start.1 = (bf16[768,2048]{1,0:T(8,128)(2,1)}, bf16[768,2048]{1,0:T(8,128)(2,1)S(1)}, u32[]{:S(2)}) copy-start(bf16[768,2048]{1,0:T(8,128)(2,1)S(1)} %get-tuple-element.74.low_t) | copy-start | bytes 9437188
  40.5 108.4 %copy-start.2 = (f32[2048,384]{1,0:T(8,128)}, f32[2048,384]{1,0:T(8,128)S(1)}, u32[]{:S(2)}) copy-start(f32[2048,384]{1,0:T(8,128)S(1)} %get-tuple-element.69.pre_i) | copy-start | bytes 9437188
  40.5 108.3 %copy-start.5 = (f32[2048,256]{1,0:T(8,128)}, f32[2048,256]{1,0:T(8,128)S(1)}, u32[]{:S(2)}) copy-start(f32[2048,256]{1,0:T(8,128)S(1)} %get-tuple-element.64.pre_p.pre_c) | copy-start | bytes 6291460
  40.5 108.3 %copy-start.12 = (f32[2048,128]{1,0:T(8,128)}, f32[2048,128]{1,0:T(8,128)S(1)}, u32[]{:S(2)}) copy-start(f32[2048,128]{1,0:T(8,128)S(1)} %get-tuple-element.65.aux) | copy-start | bytes 3145732
  40.5 10.4 %collective-permute-start.1 = (f32[136,384]{1,0:T(8,128)S(1)}, f32[136,384]{1,0:T(8,128)S(1)}, u32[]{:S(2)}, u32[]{:S(2)}) collective-permute-start(f32[136,384]{1,0:T(8,128)S(1)} %get-tuple-element.63), channel_id=1, source_target_pairs={{0,4},{4,0},{8,12},{12,8},{16,20},{20,16},{24,28},{28,24},{1,5},{5... | collective-permute-start | bytes 626696 | tf_op jit(solution)/shard_map/ppermute | solution.py:1004
  50.9 19.5 %copy-start.31 = (f32[2048,384]{1,0:T(8,128)}, f32[2048,384]{1,0:T(8,128)S(1)}, u32[]{:S(2)}) copy-start(f32[2048,384]{1,0:T(8,128)S(1)} %get-tuple-element.71.gate) | copy-start | bytes 9437188
  50.9 19.5 %copy-start.27 = (bf16[384,768]{1,0:T(8,128)(2,1)S(1)}, bf16[384,768]{1,0:T(8,128)(2,1)}, u32[]{:S(2)}) copy-start(bf16[384,768]{1,0:T(8,128)(2,1)} %wo.1) | copy-start | bytes 1769476
  50.9 19.5 %copy-start.29 = (s32[2048]{0:T(1024)S(1)}, s32[2048]{0:T(1024)}, u32[]{:S(2)}) copy-start(s32[2048]{0:T(1024)} %param.21) | copy-start | bytes 24580
  51.0 6.4 %collective-permute-start.2 = (f32[136,384]{1,0:T(8,128)S(1)}, f32[136,384]{1,0:T(8,128)S(1)}, u32[]{:S(2)}, u32[]{:S(2)}) collective-permute-start(f32[136,384]{1,0:T(8,128)S(1)} %fusion.3), channel_id=1, source_target_pairs={{0,8},{4,12},{8,0},{12,4},{16,24},{20,28},{24,16},{28,20},{1,9},{5... | collective-permute-start | bytes 626696 | tf_op jit(solution)/shard_map/ppermute | solution.py:1004
  57.6 10.9 %collective-permute-start.3 = (f32[136,384]{1,0:T(8,128)S(1)}, f32[136,384]{1,0:T(8,128)S(1)}, u32[]{:S(2)}, u32[]{:S(2)}) collective-permute-start(f32[136,384]{1,0:T(8,128)S(1)} %fusion.2), channel_id=1, source_target_pairs={{0,16},{4,20},{8,24},{12,28},{16,0},{20,4},{24,8},{28,12},{1,17},{... | collective-permute-start | bytes 626696 | tf_op jit(solution)/shard_map/ppermute | solution.py:1004
  148.2 12.5 %copy-start.8 = (bf16[2048,384]{1,0:T(8,128)(2,1)}, bf16[2048,384]{1,0:T(8,128)(2,1)S(1)}, u32[]{:S(2)}) copy-start(bf16[2048,384]{1,0:T(8,128)(2,1)S(1)} %get-tuple-element.75.d_gate) | copy-start | bytes 4718596
  148.2 12.5 %copy-start.9 = (f32[384,768]{1,0:T(8,128)}, f32[384,768]{1,0:T(8,128)S(1)}, u32[]{:S(2)}) copy-start(f32[384,768]{1,0:T(8,128)S(1)} %get-tuple-element.90.g_wo) | copy-start | bytes 3538948
  148.2 12.5 %copy-start.17 = (f32[16,8,384]{2,1,0:T(8,128)}, f32[16,8,384]{2,1,0:T(8,128)S(1)}, u32[]{:S(2)}) copy-start(f32[16,8,384]{2,1,0:T(8,128)S(1)} %get-tuple-element.84.pkl) | copy-start | bytes 589828
  148.2 12.5 %copy-start.24 = (f32[1,768]{1,0:T(1,128)}, f32[1,768]{1,0:T(1,128)S(1)}, u32[]{:S(2)}) copy-start(f32[1,768]{1,0:T(1,128)S(1)} %get-tuple-element.89.error) | copy-start | bytes 9220
  148.3 12.5 %copy-start.26 = (f32[1,384]{1,0:T(1,128)}, f32[1,384]{1,0:T(1,128)S(1)}, u32[]{:S(2)}) copy-start(f32[1,384]{1,0:T(1,128)S(1)} %get-tuple-element.92.g_gain) | copy-start | bytes 4612
  148.3 16.5 %collective-permute-start.4 = (f32[136,384]{1,0:T(8,128)S(1)}, f32[136,384]{1,0:T(8,128)S(1)}, u32[]{:S(2)}, u32[]{:S(2)}) collective-permute-start(f32[136,384]{1,0:T(8,128)S(1)} %get-tuple-element.85), channel_id=1, source_target_pairs={{0,4},{4,0},{8,12},{12,8},{16,20},{20,16},{24,28},{28,24},{1,5},{5... | collective-permute-start | bytes 626696 | tf_op jit(solution)/shard_map/ppermute | solution.py:1004
  164.9 7.3 %collective-permute-start.5 = (f32[136,384]{1,0:T(8,128)S(1)}, f32[136,384]{1,0:T(8,128)S(1)}, u32[]{:S(2)}, u32[]{:S(2)}) collective-permute-start(f32[136,384]{1,0:T(8,128)S(1)} %fusion.1), channel_id=1, source_target_pairs={{0,8},{4,12},{8,0},{12,4},{16,24},{20,28},{24,16},{28,20},{1,9},{5... | collective-permute-start | bytes 626696 | tf_op jit(solution)/shard_map/ppermute | solution.py:1004
  172.3 11.6 %collective-permute-start.6 = (f32[136,384]{1,0:T(8,128)S(1)}, f32[136,384]{1,0:T(8,128)S(1)}, u32[]{:S(2)}, u32[]{:S(2)}) collective-permute-start(f32[136,384]{1,0:T(8,128)S(1)} %fusion), channel_id=1, source_target_pairs={{0,16},{4,20},{8,24},{12,28},{16,0},{20,4},{24,8},{28,12},{1,17},{... | collective-permute-start | bytes 626696 | tf_op jit(solution)/shard_map/ppermute | solution.py:1004
  184.6 107.1 %copy-start.33 = (bf16[2048,768]{1,0:T(8,128)(2,1)S(1)}, bf16[2048,768]{1,0:T(8,128)(2,1)}, u32[]{:S(2)}) copy-start(bf16[2048,768]{1,0:T(8,128)(2,1)} %get-tuple-element.184) | copy-start | bytes 9437188
  (28 other events, 113.6 us)

commit v6 on v5

--- a/solution.py
+++ b/solution.py
@@ -15,7 +15,6 @@
 FAR = float(1 << 24)
 F32 = jnp.float32
 BF16 = jnp.bfloat16
-HIGHEST = lax.Precision.HIGHEST
 
 DT, CUM, INFLOW, TAIL, RATE, START, END = 0, 8, 16, 24, 32, 40, 41
 
@@ -58,6 +57,13 @@
     return jnp.concatenate(parts, axis=1)
 
 
+def triangle_sums(ones, v):
+    high, rest = halves(v)
+    low = (v - high.astype(F32) - rest.astype(F32)).astype(BF16)
+    sums = dot(ones, jnp.concatenate([high, rest, low], axis=1))
+    return sums[:, :LANES] + (sums[:, LANES : 2 * LANES] + sums[:, 2 * LANES :])
+
+
 def head_matrix(width):
     channel = lax.broadcasted_iota(jnp.int32, (width, LANES), 0)
     head = lax.broadcasted_iota(jnp.int32, (width, LANES), 1)
@@ -73,7 +79,7 @@
 def triangle(upper):
     row = lax.broadcasted_iota(jnp.int32, (CHUNK, CHUNK), 0)
     col = lax.broadcasted_iota(jnp.int32, (CHUNK, CHUNK), 1)
-    return ((col >= row) if upper else (col <= row)).astype(F32)
+    return ((col >= row) if upper else (col <= row)).astype(BF16)
 
 
 def silu_parts(pre):
@@ -148,7 +154,7 @@
     lower = triangle(False)
     for c in range(BLOCK // CHUNK):
         at = slice(c * CHUNK, (c + 1) * CHUNK)
-        cum = jnp.dot(lower, logs[at], precision=HIGHEST, preferred_element_type=F32)
+        cum = triangle_sums(lower, logs[at])
         last = cum[CHUNK - 1 :]
         first = (base + c * CHUNK).astype(F32)
         inflow = jnp.exp(cum) * (start[at] <= first - 1.0).astype(F32)
@@ -159,7 +165,7 @@
         table = jnp.where(lane < RATE, table, pltpu.roll(rate[at], RATE, 1))
         table = jnp.where(lane < START, table, jnp.where(lane < END, start[at], end[at]))
         aux[at, :] = table
-        scaled = values[at] * expand(table, DT, width) * expand(table, TAIL, width)
+        scaled = values[at] * expand(dt[at] * outflow, 0, width)
         added = dot3(maps[at], scaled, 0, 0)
         kept = expand(jnp.broadcast_to(inflow[CHUNK - 1 :], (8, LANES)), 0, width)
         sloc[c] = state[...]
@@ -665,7 +671,7 @@
     out_sbias, out_dlog, out_skip, out_gain,
     shift_i0, shift_i1, shift_i2, shift_p0, shift_p1, shift_p2, small, small_p, heads,
     parts, land, mine, other, row, row_land, g_wi, g_ws, pack, g_wp, pair_small, sum_small, sum_wp, sum_pack, spread_wp, spread_small,
-    grad_own, grad_other, wg_t, wi_t, ws_t, wp_t, edge, edge_core, edge_plane, edge_ahead,
+    grad_own, grad_other, w_t, edge, edge_core, edge_plane, edge_ahead,
     core_send, core_land, x_send, x_land, edge_send, edge_land, grad_send, grad_land, row_send, row_arrive, *more,
 ):
     shifted = (shift_i0, shift_i1, shift_i2, shift_p0, shift_p1, shift_p2)
@@ -737,8 +743,10 @@
             ref[...] = jnp.zeros_like(ref)
         row[:1] = jnp.zeros_like(row[:1])
         row[1:] = error[...]
-        for ref, weight in ((wg_t, wg), (wi_t, wi), (ws_t, ws), (wp_t, wp)):
-            ref[...] = jnp.transpose(weight[...])
+        filled = 0
+        for weight in (wg, wi, ws, wp, wp):
+            w_t[filled : filled + weight.shape[1]] = jnp.transpose(weight[...])
+            filled += weight.shape[1]
         pl.semaphore_wait(barrier, group)
         if summing:
             s_wo.begin()
@@ -773,7 +781,7 @@
         carried = jnp.sum(grad_state * state, axis=0, keepdims=True) * inflow[CHUNK - 1 :]
         carried = carried + jnp.sum(scaled * passed, axis=0, keepdims=True)
         after = head_sums(jnp.broadcast_to(carried, (8, width)))[:1]
-        d_logs = jnp.dot(upper, d_cum, precision=HIGHEST, preferred_element_type=F32) + after
+        d_logs = triangle_sums(upper, d_cum) + after
         d_raw = (head_sums(total * values[at]) - grown * d_logs) * pltpu.roll(table, LANES - RATE, 1)
         d_raw = jnp.where(lane < 8, d_raw, 0.0)
         pieces_s.append(d_raw.astype(BF16))
@@ -795,9 +803,8 @@
 
     inner = whole.astype(BF16)
     d_step = jnp.concatenate(pieces_s, axis=0)
-    part = dot(d_gate[...], wg_t[...]) + dot(inner, wi_t[...]) + dot(d_step, ws_t[...])
     high, rest = halves(whole_p)
-    part = part + (dot(high, wp_t[...]) + dot(rest, wp_t[...]))
+    part = dot(jnp.concatenate([d_gate[...], inner, d_step, high, rest], axis=1), w_t[...])
     upper = (step < half).astype(jnp.int32)
     slot = half - 1 - lax.rem(step, half)
     own = upper == core
@@ -821,9 +828,11 @@
     def _():
         core_copy(slot).start()
 
-    g_ws[...] += dot(low_t[...], d_step)
-    g_wp[...] += dot(low_t[...], high) + dot(low_t[...], rest)
-    g_wi[:model] += dot(low_t[...], inner)
+    products = dot(low_t[...], jnp.concatenate([inner, d_step, high, rest], axis=1))
+    g_wi[:model] += products[:, :width]
+    g_ws[...] += products[:, width : width + LANES]
+    to_pair = products[:, width + LANES :]
+    g_wp[...] += to_pair[:, : to_pair.shape[1] // 2] + to_pair[:, to_pair.shape[1] // 2 :]
 
     def norm_back(at):
         x_copy(at).wait_recv()
@@ -859,7 +868,8 @@
         before_p = jnp.concatenate([jnp.zeros_like(outer_p), outer_p], axis=0)
         high_p, rest_p = halves(before_p)
         g_wp[...] += dot(halo_low[...], high_p, 0, 0) + dot(halo_low[...], rest_p, 0, 0)
-        edge_part = dot(before, wi_t[...]) + (dot(high_p, wp_t[...]) + dot(rest_p, wp_t[...]))
+        edge_in = jnp.concatenate([before, jnp.zeros((16, LANES), BF16), high_p, rest_p], axis=1)
+        edge_part = dot(edge_in, w_t[width:])
         edge[0] = edge_part[8:]
         edge_copy(0, edge_core, beside).start()
         pack[:6] = small[:6]
@@ -875,13 +885,15 @@
             s_wi[0].begin()
             s_wi[1].begin()
 
+        if summing:
+            for h_sum, _, _ in wide:
+                h_sum.fold()
+
         @pl.when(core == 0)
         def _():
             settle(0)
 
         if summing:
-            for h_sum, _, _ in wide:
-                h_sum.fold()
             s_wi[2].begin()
             s_pack.begin()
         edge_copy(0, edge_core, beside).wait_recv()
@@ -972,9 +984,9 @@
 
 
 def call(kernel, grid, ins, outs, scratch=(), prefetch=0, flops=0, moved=0, collective=None, vmem=14):
-    def spec(shape, block, index):
+    def spec(shape, block, index, **single):
         if block is None:
-            return pl.BlockSpec(shape, lambda *_: (0,) * len(shape))
+            return pl.BlockSpec(shape, lambda *_: (0,) * len(shape), **single)
         if isinstance(block, str):
             return pl.BlockSpec(memory_space={"smem": pltpu.SMEM, "vmem": pltpu.VMEM, "any": pl.ANY}[block])
         return pl.BlockSpec(block, index)
@@ -987,7 +999,7 @@
         grid_spec=pltpu.PrefetchScalarGridSpec(
             num_scalar_prefetch=prefetch,
             grid=(grid,),
-            in_specs=[spec(a.shape, block, index) for a, block, index in arrays],
+            in_specs=[spec(a.shape, block, index, pipeline_mode=pl.Buffered(1)) for a, block, index in arrays],
             out_specs=[spec(shape, block, index) for shape, _, block, index in outs],
             scratch_shapes=list(scratch),
         ),
@@ -1185,8 +1197,7 @@
         pltpu.VMEM((r_small * size, pair_width), F32), pltpu.VMEM((r_wp * size, pair_width), F32),
         pltpu.VMEM((n_pack, width), F32), pltpu.VMEM((model, pair_width), F32), pltpu.VMEM((32, pair_width), F32),
         pltpu.VMEM((half, BLOCK, model), BF16), pltpu.VMEM((half, BLOCK, model), BF16),
-        pltpu.VMEM((width, model), BF16), pltpu.VMEM((width, model), BF16), pltpu.VMEM((LANES, model), BF16),
-        pltpu.VMEM((pair_width, model), BF16),
+        pltpu.VMEM((2 * width + LANES + 2 * pair_width, model), BF16),
         pltpu.VMEM((3, 8, model), F32), pltpu.VMEM((8, model), F32), pltpu.VMEM((8, model), F32), pltpu.VMEM((8, model), F32),
         dma((half,)), dma((half,)), dma((half,)), dma((half,)), dma((3,)), dma((3,)), dma((half,)), dma((half,)),
         dma((2 * size,)), dma((2 * size,)),

time: 308 us -> 304 us (0.987)
  no operation moved by 1% of the time
where the time goes in v6:
time: 304 us; the launch traced here: 303 us
  Pallas kernels  214 us (70%)
  local copies, waits for them, and re-layouts  36.5 us (12%)
  waiting for transfers between devices  29.7 us (10%)
  starting transfers between devices  13.3 us (4%)
  other arithmetic  5.91 us (2%)
  between operations  4.28 us (1%)
    pallas_call x5, Pallas kernels, call(): pl.pallas_call(kernel, grid_spec=pltpu.PrefetchScalarGridSpec(num_scalar_...  214 us
    unnamed x104, local copies, waits for them, and re-layouts  31.1 us
    ppermute x6, waiting for transfers between devices, swap(): return jax.tree.map(lambda v: lax.ppermute(v, axis, route), value)  29.7 us
    ppermute x6, starting transfers between devices, swap(): return jax.tree.map(lambda v: lax.ppermute(v, axis, route), value)  8.42 us
  transfers between devices with their start and end apart: 7, of which 4 were waited for; matrix products, arithmetic and copies ran while one was open for 2% of the time, Pallas kernels for 5%

profile of v6, /device:TPU:0, one launch (start us, length us, event | category | flops | bytes accessed | tf_op | source)
XLA Modules:
  0.0 303.3 jit_solution(6356577935709179074)
XLA Ops:
  1.4 4.9 %collective-permute-start = (bf16[16,768]{1,0:T(8,128)(2,1)S(1)}, bf16[16,768]{1,0:T(8,128)(2,1)S(1)}, u32[]{:S(2)}, u32[]{:S(2)}) collective-permute-start(bf16[16,768]{1,0:T(8,128)(2,1)S(1)} %slice.240), channel_id=1, source_target_pairs={{0,4},{4,8},{8,12},{12,16},{16,20},{20,24},{24,28},{1,5},{5,9},{9,... | collective-permute-start | bytes 73736 | tf_op jit(solution)/shard_map/ppermute | solution.py:1022
  12.1 1.9 copy-done
  18.1 18.7 %shard_map.305 = (bf16[2048,768]{1,0:T(8,128)(2,1)S(1)}, bf16[768,2048]{1,0:T(8,128)(2,1)S(1)}, bf16[2048,384]{1,0:T(8,128)(2,1)S(1)}, bf16[2048,256]{1,0:T(8,12...) custom-call(s32[2]{0:T(128)S(1)} %pad_add_fusion.idx, ...), custom_call_target="tpu_custom_call" | custom-call | flops 3000000000 | bytes 20000000 | tf_op jit(solution)/shard_map/pallas_call | solution.py:997
  36.9 1.7 copy-done.30
  38.6 1.6 collective-permute-start.1
  40.2 7.1 %shard_map.306 = (f32[2048,384]{1,0:T(8,128)S(1)}, f32[2048,384]{1,0:T(8,128)S(1)}) custom-call(s32[2]{0:T(128)S(1)} %pad_add_fusion.idx, bf16[2048,768]{1,0:T(8,128)(2,1)S(1)} %get-tuple-element.68.low, bf16[768,384]{1,0:T(8,128)(2,1)S(1)} %copy-done.15, f32[2048,384]{1,0:T(8,128)S(1)} %get-tuple-element.69.pre_i, ...), custom_call_target="tpu_custom_call" | custom-call | flops 4000000000 | bytes 20000000 | tf_op jit(solution)/shard_map/pallas_call | solution.py:997
  47.3 1.7 copy-done.32
  49.1 1.6 collective-permute-start.2
  50.8 4.7 %collective-permute-done.2 = f32[136,384]{1,0:T(8,128)S(1)} collective-permute-done((f32[136,384]{1,0:T(8,128)S(1)}, f32[136,384]{1,0:T(8,128)S(1)}, u32[]{:S(2)}, u32[]{:S(2)}) %collective-permute-start.2) | collective-permute-done | bytes 208928 | tf_op jit(solution)/shard_map/ppermute | solution.py:1016
  55.7 2.7 collective-permute-start.3
  58.4 8.1 %collective-permute-done.3 = f32[136,384]{1,0:T(8,128)S(1)} collective-permute-done((f32[136,384]{1,0:T(8,128)S(1)}, f32[136,384]{1,0:T(8,128)S(1)}, u32[]{:S(2)}, u32[]{:S(2)}) %collective-permute-start.3) | collective-permute-done | bytes 208928 | tf_op jit(solution)/shard_map/ppermute | solution.py:1016
  68.5 77.8 %shard_map.307 = (f32[16,128,384]{2,1,0:T(8,128)}, f32[2048,384]{1,0:T(8,128)}, bf16[2048,384]{1,0:T(8,128)(2,1)S(1)}, f32[16,128,384]{2,1,0:T(8,128)}, f32[16,8...) custom-call(f32[1]{0:T(128)} %bitcast.7.factor, ...), custom_call_target="tpu_custom_call" | custom-call | flops 6000000000 | bytes 60000000 | tf_op jit(solution)/shard_map/pallas_call | solution.py:997
  147.0 2.2 copy-done.3
  149.2 9.6 %shard_map.308 = (f32[2048,384]{1,0:T(8,128)S(1)}, f32[2048,256]{1,0:T(8,128)S(1)}, f32[768,384]{1,0:T(8,128)S(1)}) custom-call(s32[2]{0:T(128)S(1)} %pad_add_fusion.idx, f32[2048,384]{1,0:T(8,128)S(1)} %copy-done.3, f32[2048,384]{1,0:T(8,128)S(1)} %get-tuple-element.69.pre_i, f32[2048,256]{1,0:T(8,128)S(1)} %get-tuple-element.64.pre_p.pre_c, ...), custom_call_target="tpu_custom_call" | custom-call | flops 6000000000 | bytes 20000000 | tf_op jit(solution)/shard_map/pallas_call | solution.py:997
  158.9 1.7 copy-done.4
  160.6 1.3 copy-done.6
  163.3 6.9 %collective-permute-done.5 = f32[136,384]{1,0:T(8,128)S(1)} collective-permute-done((f32[136,384]{1,0:T(8,128)S(1)}, f32[136,384]{1,0:T(8,128)S(1)}, u32[]{:S(2)}, u32[]{:S(2)}) %collective-permute-start.5) | collective-permute-done | bytes 208928 | tf_op jit(solution)/shard_map/ppermute | solution.py:1016
  170.4 1.6 collective-permute-start.6
  172.0 9.9 %collective-permute-done.6 = f32[136,384]{1,0:T(8,128)S(1)} collective-permute-done((f32[136,384]{1,0:T(8,128)S(1)}, f32[136,384]{1,0:T(8,128)S(1)}, u32[]{:S(2)}, u32[]{:S(2)}) %collective-permute-start.6) | collective-permute-done | bytes 208928 | tf_op jit(solution)/shard_map/ppermute | solution.py:1016
  182.7 100.5 %shard_map.309 = (bf16[2048,768]{1,0:T(8,128)(2,1)}, f32[1,768]{1,0:T(1,128)}, f32[1,1]{1,0:T(1,128)}, f32[384,768]{1,0:T(8,128)}, f32[768,384]{1,0:T(8,128)}, /...) custom-call(f32[2048,384]{1,0:T(8,128)} %copy-done.4, ...), custom_call_target="tpu_custom_call" | custom-call | flops 8999999488 | bytes 80000000 | tf_op jit(solution)/shard_map/pallas_call | solution.py:997
  285.7 1.3 reduce.14
  286.9 1.8 copy.36
  288.7 1.7 copy.50
  291.0 3.9 %copy.52 = bf16[2048,768]{1,0:T(8,128)(2,1)} copy(bf16[2048,768]{1,0:T(8,128)(2,1)} %get-tuple-element.186) | data formatting | bytes 6291456
  (143 shorter events, 24.3 us)
Async XLA Ops:
  1.4 10.7 %collective-permute-start = (bf16[16,768]{1,0:T(8,128)(2,1)S(1)}, bf16[16,768]{1,0:T(8,128)(2,1)S(1)}, u32[]{:S(2)}, u32[]{:S(2)}) collective-permute-start(bf16[16,768]{1,0:T(8,128)(2,1)S(1)} %slice.240), channel_id=1, source_target_pairs={{0,4},{4,8},{8,12},{12,16},{16,20},{20,24},{24,28},{1,5},{5,9},{9,... | collective-permute-start | bytes 73736 | tf_op jit(solution)/shard_map/ppermute | solution.py:1022
  11.1 25.8 %copy-start.21 = (f32[1,768]{1,0:T(1,128)}, f32[1,768]{1,0:T(1,128)S(1)}, u32[]{:S(2)}) copy-start(f32[1,768]{1,0:T(1,128)S(1)} %broadcast_in_dim.16.gain) | copy-start | bytes 9220
  12.0 24.9 %copy-start.13 = (bf16[768,128]{1,0:T(8,128)(2,1)}, bf16[768,128]{1,0:T(8,128)(2,1)S(1)}, u32[]{:S(2)}) copy-start(bf16[768,128]{1,0:T(8,128)(2,1)S(1)} %pad.22.ws) | copy-start | bytes 589828
  12.0 28.1 %copy-start.19 = (f32[8,128]{1,0:T(8,128)}, f32[8,128]{1,0:T(8,128)S(1)}, u32[]{:S(2)}) copy-start(f32[8,128]{1,0:T(8,128)S(1)} %stack.35.given) | copy-start | bytes 12292
  18.1 22.1 %copy-start.15 = (bf16[768,384]{1,0:T(8,128)(2,1)S(1)}, bf16[768,384]{1,0:T(8,128)(2,1)}, u32[]{:S(2)}) copy-start(bf16[768,384]{1,0:T(8,128)(2,1)} %wg.3) | copy-start | bytes 1769476
  38.6 108.4 %copy-start.1 = (bf16[768,2048]{1,0:T(8,128)(2,1)}, bf16[768,2048]{1,0:T(8,128)(2,1)S(1)}, u32[]{:S(2)}) copy-start(bf16[768,2048]{1,0:T(8,128)(2,1)S(1)} %get-tuple-element.74.low_t) | copy-start | bytes 9437188
  38.6 108.4 %copy-start.2 = (f32[2048,384]{1,0:T(8,128)}, f32[2048,384]{1,0:T(8,128)S(1)}, u32[]{:S(2)}) copy-start(f32[2048,384]{1,0:T(8,128)S(1)} %get-tuple-element.69.pre_i) | copy-start | bytes 9437188
  38.6 108.4 %copy-start.5 = (f32[2048,256]{1,0:T(8,128)}, f32[2048,256]{1,0:T(8,128)S(1)}, u32[]{:S(2)}) copy-start(f32[2048,256]{1,0:T(8,128)S(1)} %get-tuple-element.64.pre_p.pre_c) | copy-start | bytes 6291460
  38.6 108.4 %copy-start.12 = (f32[2048,128]{1,0:T(8,128)}, f32[2048,128]{1,0:T(8,128)S(1)}, u32[]{:S(2)}) copy-start(f32[2048,128]{1,0:T(8,128)S(1)} %get-tuple-element.65.aux) | copy-start | bytes 3145732
  38.6 10.4 %collective-permute-start.1 = (f32[136,384]{1,0:T(8,128)S(1)}, f32[136,384]{1,0:T(8,128)S(1)}, u32[]{:S(2)}, u32[]{:S(2)}) collective-permute-start(f32[136,384]{1,0:T(8,128)S(1)} %get-tuple-element.63), channel_id=1, source_target_pairs={{0,4},{4,0},{8,12},{12,8},{16,20},{20,16},{24,28},{28,24},{1,5},{5... | collective-permute-start | bytes 626696 | tf_op jit(solution)/shard_map/ppermute | solution.py:1016
  49.0 19.5 %copy-start.31 = (f32[2048,384]{1,0:T(8,128)}, f32[2048,384]{1,0:T(8,128)S(1)}, u32[]{:S(2)}) copy-start(f32[2048,384]{1,0:T(8,128)S(1)} %get-tuple-element.71.gate) | copy-start | bytes 9437188
  49.0 19.5 %copy-start.27 = (bf16[384,768]{1,0:T(8,128)(2,1)S(1)}, bf16[384,768]{1,0:T(8,128)(2,1)}, u32[]{:S(2)}) copy-start(bf16[384,768]{1,0:T(8,128)(2,1)} %wo.1) | copy-start | bytes 1769476
  49.0 19.5 %copy-start.29 = (s32[2048]{0:T(1024)S(1)}, s32[2048]{0:T(1024)}, u32[]{:S(2)}) copy-start(s32[2048]{0:T(1024)} %param.21) | copy-start | bytes 24580
  49.1 6.4 %collective-permute-start.2 = (f32[136,384]{1,0:T(8,128)S(1)}, f32[136,384]{1,0:T(8,128)S(1)}, u32[]{:S(2)}, u32[]{:S(2)}) collective-permute-start(f32[136,384]{1,0:T(8,128)S(1)} %fusion.3), channel_id=1, source_target_pairs={{0,8},{4,12},{8,0},{12,4},{16,24},{20,28},{24,16},{28,20},{1,9},{5... | collective-permute-start | bytes 626696 | tf_op jit(solution)/shard_map/ppermute | solution.py:1016
  55.7 10.9 %collective-permute-start.3 = (f32[136,384]{1,0:T(8,128)S(1)}, f32[136,384]{1,0:T(8,128)S(1)}, u32[]{:S(2)}, u32[]{:S(2)}) collective-permute-start(f32[136,384]{1,0:T(8,128)S(1)} %fusion.2), channel_id=1, source_target_pairs={{0,16},{4,20},{8,24},{12,28},{16,0},{20,4},{24,8},{28,12},{1,17},{... | collective-permute-start | bytes 626696 | tf_op jit(solution)/shard_map/ppermute | solution.py:1016
  146.3 12.5 %copy-start.8 = (bf16[2048,384]{1,0:T(8,128)(2,1)}, bf16[2048,384]{1,0:T(8,128)(2,1)S(1)}, u32[]{:S(2)}) copy-start(bf16[2048,384]{1,0:T(8,128)(2,1)S(1)} %get-tuple-element.75.d_gate) | copy-start | bytes 4718596
  146.3 12.5 %copy-start.9 = (f32[384,768]{1,0:T(8,128)}, f32[384,768]{1,0:T(8,128)S(1)}, u32[]{:S(2)}) copy-start(f32[384,768]{1,0:T(8,128)S(1)} %get-tuple-element.90.g_wo) | copy-start | bytes 3538948
  146.3 12.5 %copy-start.17 = (f32[16,8,384]{2,1,0:T(8,128)}, f32[16,8,384]{2,1,0:T(8,128)S(1)}, u32[]{:S(2)}) copy-start(f32[16,8,384]{2,1,0:T(8,128)S(1)} %get-tuple-element.84.pkl) | copy-start | bytes 589828
  146.3 12.5 %copy-start.24 = (f32[1,768]{1,0:T(1,128)}, f32[1,768]{1,0:T(1,128)S(1)}, u32[]{:S(2)}) copy-start(f32[1,768]{1,0:T(1,128)S(1)} %get-tuple-element.89.error) | copy-start | bytes 9220
  146.4 12.5 %copy-start.26 = (f32[1,384]{1,0:T(1,128)}, f32[1,384]{1,0:T(1,128)S(1)}, u32[]{:S(2)}) copy-start(f32[1,384]{1,0:T(1,128)S(1)} %get-tuple-element.92.g_gain) | copy-start | bytes 4612
  146.4 16.5 %collective-permute-start.4 = (f32[136,384]{1,0:T(8,128)S(1)}, f32[136,384]{1,0:T(8,128)S(1)}, u32[]{:S(2)}, u32[]{:S(2)}) collective-permute-start(f32[136,384]{1,0:T(8,128)S(1)} %get-tuple-element.85), channel_id=1, source_target_pairs={{0,4},{4,0},{8,12},{12,8},{16,20},{20,16},{24,28},{28,24},{1,5},{5... | collective-permute-start | bytes 626696 | tf_op jit(solution)/shard_map/ppermute | solution.py:1016
  163.0 7.2 %collective-permute-start.5 = (f32[136,384]{1,0:T(8,128)S(1)}, f32[136,384]{1,0:T(8,128)S(1)}, u32[]{:S(2)}, u32[]{:S(2)}) collective-permute-start(f32[136,384]{1,0:T(8,128)S(1)} %fusion.1), channel_id=1, source_target_pairs={{0,8},{4,12},{8,0},{12,4},{16,24},{20,28},{24,16},{28,20},{1,9},{5... | collective-permute-start | bytes 626696 | tf_op jit(solution)/shard_map/ppermute | solution.py:1016
  170.4 11.6 %collective-permute-start.6 = (f32[136,384]{1,0:T(8,128)S(1)}, f32[136,384]{1,0:T(8,128)S(1)}, u32[]{:S(2)}, u32[]{:S(2)}) collective-permute-start(f32[136,384]{1,0:T(8,128)S(1)} %fusion), channel_id=1, source_target_pairs={{0,16},{4,20},{8,24},{12,28},{16,0},{20,4},{24,8},{28,12},{1,17},{... | collective-permute-start | bytes 626696 | tf_op jit(solution)/shard_map/ppermute | solution.py:1016
  182.7 106.0 %copy-start.33 = (bf16[2048,768]{1,0:T(8,128)(2,1)S(1)}, bf16[2048,768]{1,0:T(8,128)(2,1)}, u32[]{:S(2)}) copy-start(bf16[2048,768]{1,0:T(8,128)(2,1)} %get-tuple-element.184) | copy-start | bytes 9437188
  (28 other events, 113.5 us)

commit v7 on v6

--- a/solution.py
+++ b/solution.py
@@ -1163,7 +1163,7 @@
             pltpu.VMEM((model, width), BF16), dma((4 * blocks,)), dma((4 * blocks,)), dma((4 * blocks,)), dma((4 * blocks,)), dma((half,)), dma((half,)),
             dma((half,)), dma((half,)), dma((blocks,)), dma((blocks,)), dma((half,)), dma((half,)), dma((half,)),
         ],
-        flops=6e9, moved=6e7, collective=2, vmem=44,
+        flops=6e9, moved=6e7, collective=2, vmem=36,
     )
     mixer = mixer.reshape(rows, width)
     grad_in, _ = carried(fin_back, "seq", True)

time: 304 us -> 300 us (0.987)
    unnamed x104 -> x108, local copies, waits for them, and re-layouts: 31.1 us -> 28.9 us
  transfers between devices with their start and end apart: 7 -> 7, of which waited for: 4 -> 4; matrix products, arithmetic and copies ran while one was open for 2% -> 2% of each run, Pallas kernels for 5% -> 6%
where the time goes in v7:
time: 300 us; the launch traced here: 299 us
  Pallas kernels  212 us (71%)
  local copies, waits for them, and re-layouts  34.3 us (11%)
  waiting for transfers between devices  28.2 us (9%)
  starting transfers between devices  14.4 us (5%)
  other arithmetic  5.95 us (2%)
  between operations  4.34 us (1%)
    pallas_call x5, Pallas kernels, call(): pl.pallas_call(kernel, grid_spec=pltpu.PrefetchScalarGridSpec(num_scalar_...  212 us
    unnamed x108, local copies, waits for them, and re-layouts  28.9 us
    ppermute x6, waiting for transfers between devices, swap(): return jax.tree.map(lambda v: lax.ppermute(v, axis, route), value)  28.2 us
    ppermute x6, starting transfers between devices, swap(): return jax.tree.map(lambda v: lax.ppermute(v, axis, route), value)  9.5 us
  transfers between devices with their start and end apart: 7, of which 4 were waited for; matrix products, arithmetic and copies ran while one was open for 2% of the time, Pallas kernels for 6%

profile of v7, /device:TPU:0, one launch (start us, length us, event | category | flops | bytes accessed | tf_op | source)
XLA Modules:
  0.0 298.9 jit_solution(4884950831470693402)
XLA Ops:
  1.4 4.9 %collective-permute-start = (bf16[16,768]{1,0:T(8,128)(2,1)S(1)}, bf16[16,768]{1,0:T(8,128)(2,1)S(1)}, u32[]{:S(2)}, u32[]{:S(2)}) collective-permute-start(bf16[16,768]{1,0:T(8,128)(2,1)S(1)} %slice.240), channel_id=1, source_target_pairs={{0,4},{4,8},{8,12},{12,16},{16,20},{20,24},{24,28},{1,5},{5,9},{9,... | collective-permute-start | bytes 73736 | tf_op jit(solution)/shard_map/ppermute | solution.py:1022
  12.1 1.9 copy-done
  18.1 18.7 %shard_map.305 = (bf16[2048,768]{1,0:T(8,128)(2,1)S(1)}, bf16[768,2048]{1,0:T(8,128)(2,1)S(1)}, bf16[2048,384]{1,0:T(8,128)(2,1)S(1)}, bf16[2048,256]{1,0:T(8,12...) custom-call(s32[2]{0:T(128)S(1)} %pad_add_fusion.idx, ...), custom_call_target="tpu_custom_call" | custom-call | flops 3000000000 | bytes 20000000 | tf_op jit(solution)/shard_map/pallas_call | solution.py:997
  36.9 1.7 copy-done.32
  38.6 1.6 collective-permute-start.1
  40.2 7.1 %shard_map.306 = (f32[2048,384]{1,0:T(8,128)S(1)}, f32[2048,384]{1,0:T(8,128)S(1)}) custom-call(s32[2]{0:T(128)S(1)} %pad_add_fusion.idx, bf16[2048,768]{1,0:T(8,128)(2,1)S(1)} %get-tuple-element.68.low, bf16[768,384]{1,0:T(8,128)(2,1)S(1)} %copy-done.17, f32[2048,384]{1,0:T(8,128)S(1)} %get-tuple-element.69.pre_i, ...), custom_call_target="tpu_custom_call" | custom-call | flops 4000000000 | bytes 20000000 | tf_op jit(solution)/shard_map/pallas_call | solution.py:997
  47.3 1.7 copy-done.34
  49.1 1.6 collective-permute-start.2
  50.8 4.7 %collective-permute-done.2 = f32[136,384]{1,0:T(8,128)S(1)} collective-permute-done((f32[136,384]{1,0:T(8,128)S(1)}, f32[136,384]{1,0:T(8,128)S(1)}, u32[]{:S(2)}, u32[]{:S(2)}) %collective-permute-start.2) | collective-permute-done | bytes 208928 | tf_op jit(solution)/shard_map/ppermute | solution.py:1016
  55.7 2.7 collective-permute-start.3
  58.4 8.1 %collective-permute-done.3 = f32[136,384]{1,0:T(8,128)S(1)} collective-permute-done((f32[136,384]{1,0:T(8,128)S(1)}, f32[136,384]{1,0:T(8,128)S(1)}, u32[]{:S(2)}, u32[]{:S(2)}) %collective-permute-start.3) | collective-permute-done | bytes 208928 | tf_op jit(solution)/shard_map/ppermute | solution.py:1016
  68.5 76.2 %shard_map.307 = (f32[16,128,384]{2,1,0:T(8,128)S(1)}, f32[2048,384]{1,0:T(8,128)S(1)}, bf16[2048,384]{1,0:T(8,128)(2,1)S(1)}, f32[16,128,384]{2,1,0:T(8,128)S(1...) custom-call(f32[1]{0:T(128)} %bitcast.7.factor, ...), custom_call_target="tpu_custom_call" | custom-call | flops 6000000000 | bytes 60000000 | tf_op jit(solution)/shard_map/pallas_call | solution.py:997
  145.4 9.6 %shard_map.308 = (f32[2048,384]{1,0:T(8,128)S(1)}, f32[2048,256]{1,0:T(8,128)S(1)}, f32[768,384]{1,0:T(8,128)S(1)}) custom-call(s32[2]{0:T(128)S(1)} %pad_add_fusion.idx, f32[2048,384]{1,0:T(8,128)S(1)} %get-tuple-element.73.d_mixer, f32[2048,384]{1,0:T(8,128)S(1)} %get-tuple-element.69.pre_i, f32[2048,256]{1,0:T(8,128)S(1)} %get-tuple-element.64.pre_p.pre_c, ...), custom_call_target="tpu_custom_call" | custom-call | flops 6000000000 | bytes 20000000 | tf_op jit(solution)/shard_map/pallas_call | solution.py:997
  155.1 1.7 copy-done.6
  156.7 1.3 copy-done.8
  159.9 6.2 %collective-permute-done.5 = f32[136,384]{1,0:T(8,128)S(1)} collective-permute-done((f32[136,384]{1,0:T(8,128)S(1)}, f32[136,384]{1,0:T(8,128)S(1)}, u32[]{:S(2)}, u32[]{:S(2)}) %collective-permute-start.5) | collective-permute-done | bytes 208928 | tf_op jit(solution)/shard_map/ppermute | solution.py:1016
  166.3 2.3 collective-permute-start.6
  168.7 9.1 %collective-permute-done.6 = f32[136,384]{1,0:T(8,128)S(1)} collective-permute-done((f32[136,384]{1,0:T(8,128)S(1)}, f32[136,384]{1,0:T(8,128)S(1)}, u32[]{:S(2)}, u32[]{:S(2)}) %collective-permute-start.6) | collective-permute-done | bytes 208928 | tf_op jit(solution)/shard_map/ppermute | solution.py:1016
  178.5 100.1 %shard_map.309 = (bf16[2048,768]{1,0:T(8,128)(2,1)}, f32[1,768]{1,0:T(1,128)}, f32[1,1]{1,0:T(1,128)}, f32[384,768]{1,0:T(8,128)}, f32[768,384]{1,0:T(8,128)}, /...) custom-call(f32[2048,384]{1,0:T(8,128)} %copy-done.6, ...), custom_call_target="tpu_custom_call" | custom-call | flops 8999999488 | bytes 80000000 | tf_op jit(solution)/shard_map/pallas_call | solution.py:997
  278.6 1.3 reduce.15
  279.9 1.3 reduce.16
  282.4 1.8 copy.36
  284.2 1.7 copy.50
  286.5 3.9 %copy.52 = bf16[2048,768]{1,0:T(8,128)(2,1)} copy(bf16[2048,768]{1,0:T(8,128)(2,1)} %get-tuple-element.186) | data formatting | bytes 6291456
  (147 shorter events, 23.4 us)
Async XLA Ops:
  1.4 10.7 %collective-permute-start = (bf16[16,768]{1,0:T(8,128)(2,1)S(1)}, bf16[16,768]{1,0:T(8,128)(2,1)S(1)}, u32[]{:S(2)}, u32[]{:S(2)}) collective-permute-start(bf16[16,768]{1,0:T(8,128)(2,1)S(1)} %slice.240), channel_id=1, source_target_pairs={{0,4},{4,8},{8,12},{12,16},{16,20},{20,24},{24,28},{1,5},{5,9},{9,... | collective-permute-start | bytes 73736 | tf_op jit(solution)/shard_map/ppermute | solution.py:1022
  11.1 25.8 %copy-start.23 = (f32[1,768]{1,0:T(1,128)}, f32[1,768]{1,0:T(1,128)S(1)}, u32[]{:S(2)}) copy-start(f32[1,768]{1,0:T(1,128)S(1)} %broadcast_in_dim.16.gain) | copy-start | bytes 9220
  12.0 24.9 %copy-start.15 = (bf16[768,128]{1,0:T(8,128)(2,1)}, bf16[768,128]{1,0:T(8,128)(2,1)S(1)}, u32[]{:S(2)}) copy-start(bf16[768,128]{1,0:T(8,128)(2,1)S(1)} %pad.22.ws) | copy-start | bytes 589828
  12.0 28.1 %copy-start.21 = (f32[8,128]{1,0:T(8,128)}, f32[8,128]{1,0:T(8,128)S(1)}, u32[]{:S(2)}) copy-start(f32[8,128]{1,0:T(8,128)S(1)} %stack.35.given) | copy-start | bytes 12292
  18.1 22.1 %copy-start.17 = (bf16[768,384]{1,0:T(8,128)(2,1)S(1)}, bf16[768,384]{1,0:T(8,128)(2,1)}, u32[]{:S(2)}) copy-start(bf16[768,384]{1,0:T(8,128)(2,1)} %wg.3) | copy-start | bytes 1769476
  38.6 106.8 %copy-start.1 = (bf16[768,2048]{1,0:T(8,128)(2,1)}, bf16[768,2048]{1,0:T(8,128)(2,1)S(1)}, u32[]{:S(2)}) copy-start(bf16[768,2048]{1,0:T(8,128)(2,1)S(1)} %get-tuple-element.74.low_t) | copy-start | bytes 9437188
  38.6 106.8 %copy-start.2 = (f32[2048,384]{1,0:T(8,128)}, f32[2048,384]{1,0:T(8,128)S(1)}, u32[]{:S(2)}) copy-start(f32[2048,384]{1,0:T(8,128)S(1)} %get-tuple-element.69.pre_i) | copy-start | bytes 9437188
  38.6 106.8 %copy-start.7 = (f32[2048,256]{1,0:T(8,128)}, f32[2048,256]{1,0:T(8,128)S(1)}, u32[]{:S(2)}) copy-start(f32[2048,256]{1,0:T(8,128)S(1)} %get-tuple-element.64.pre_p.pre_c) | copy-start | bytes 6291460
  38.6 106.8 %copy-start.14 = (f32[2048,128]{1,0:T(8,128)}, f32[2048,128]{1,0:T(8,128)S(1)}, u32[]{:S(2)}) copy-start(f32[2048,128]{1,0:T(8,128)S(1)} %get-tuple-element.65.aux) | copy-start | bytes 3145732
  38.6 10.4 %collective-permute-start.1 = (f32[136,384]{1,0:T(8,128)S(1)}, f32[136,384]{1,0:T(8,128)S(1)}, u32[]{:S(2)}, u32[]{:S(2)}) collective-permute-start(f32[136,384]{1,0:T(8,128)S(1)} %get-tuple-element.63), channel_id=1, source_target_pairs={{0,4},{4,0},{8,12},{12,8},{16,20},{20,16},{24,28},{28,24},{1,5},{5... | collective-permute-start | bytes 626696 | tf_op jit(solution)/shard_map/ppermute | solution.py:1016
  40.2 10.6 %copy-start.39 = (f32[136,384]{1,0:T(8,128)S(1)}, f32[136,384]{1,0:T(8,128)}, u32[]{:S(2)}) copy-start(f32[136,384]{1,0:T(8,128)} %constant.32.clone.1) | copy-start | bytes 626692
  49.0 19.5 %copy-start.33 = (f32[2048,384]{1,0:T(8,128)}, f32[2048,384]{1,0:T(8,128)S(1)}, u32[]{:S(2)}) copy-start(f32[2048,384]{1,0:T(8,128)S(1)} %get-tuple-element.71.gate) | copy-start | bytes 9437188
  49.0 19.5 %copy-start.29 = (bf16[384,768]{1,0:T(8,128)(2,1)S(1)}, bf16[384,768]{1,0:T(8,128)(2,1)}, u32[]{:S(2)}) copy-start(bf16[384,768]{1,0:T(8,128)(2,1)} %wo.1) | copy-start | bytes 1769476
  49.0 19.5 %copy-start.31 = (s32[2048]{0:T(1024)S(1)}, s32[2048]{0:T(1024)}, u32[]{:S(2)}) copy-start(s32[2048]{0:T(1024)} %param.21) | copy-start | bytes 24580
  49.1 6.4 %collective-permute-start.2 = (f32[136,384]{1,0:T(8,128)S(1)}, f32[136,384]{1,0:T(8,128)S(1)}, u32[]{:S(2)}, u32[]{:S(2)}) collective-permute-start(f32[136,384]{1,0:T(8,128)S(1)} %fusion.3), channel_id=1, source_target_pairs={{0,8},{4,12},{8,0},{12,4},{16,24},{20,28},{24,16},{28,20},{1,9},{5... | collective-permute-start | bytes 626696 | tf_op jit(solution)/shard_map/ppermute | solution.py:1016
  55.7 10.9 %collective-permute-start.3 = (f32[136,384]{1,0:T(8,128)S(1)}, f32[136,384]{1,0:T(8,128)S(1)}, u32[]{:S(2)}, u32[]{:S(2)}) collective-permute-start(f32[136,384]{1,0:T(8,128)S(1)} %fusion.2), channel_id=1, source_target_pairs={{0,16},{4,20},{8,24},{12,28},{16,0},{20,4},{24,8},{28,12},{1,17},{... | collective-permute-start | bytes 626696 | tf_op jit(solution)/shard_map/ppermute | solution.py:1016
  144.7 10.3 %copy-start.3 = (f32[16,128,384]{2,1,0:T(8,128)}, f32[16,128,384]{2,1,0:T(8,128)S(1)}, u32[]{:S(2)}) copy-start(f32[16,128,384]{2,1,0:T(8,128)S(1)} %get-tuple-element.86.states) | copy-start | bytes 9437188
  144.7 10.3 %copy-start.4 = (f32[2048,384]{1,0:T(8,128)}, f32[2048,384]{1,0:T(8,128)S(1)}, u32[]{:S(2)}) copy-start(f32[2048,384]{1,0:T(8,128)S(1)} %get-tuple-element.73.d_mixer) | copy-start | bytes 9437188
  144.7 10.3 %copy-start.5 = (f32[16,128,384]{2,1,0:T(8,128)}, f32[16,128,384]{2,1,0:T(8,128)S(1)}, u32[]{:S(2)}) copy-start(f32[16,128,384]{2,1,0:T(8,128)S(1)} %get-tuple-element.83.gloc) | copy-start | bytes 9437188
  144.7 10.3 %copy-start.10 = (bf16[2048,384]{1,0:T(8,128)(2,1)}, bf16[2048,384]{1,0:T(8,128)(2,1)S(1)}, u32[]{:S(2)}) copy-start(bf16[2048,384]{1,0:T(8,128)(2,1)S(1)} %get-tuple-element.75.d_gate) | copy-start | bytes 4718596
  144.8 14.3 %collective-permute-start.4 = (f32[136,384]{1,0:T(8,128)S(1)}, f32[136,384]{1,0:T(8,128)S(1)}, u32[]{:S(2)}, u32[]{:S(2)}) collective-permute-start(f32[136,384]{1,0:T(8,128)S(1)} %get-tuple-element.85), channel_id=1, source_target_pairs={{0,4},{4,0},{8,12},{12,8},{16,20},{20,16},{24,28},{28,24},{1,5},{5... | collective-permute-start | bytes 626696 | tf_op jit(solution)/shard_map/ppermute | solution.py:1016
  159.2 7.0 %collective-permute-start.5 = (f32[136,384]{1,0:T(8,128)S(1)}, f32[136,384]{1,0:T(8,128)S(1)}, u32[]{:S(2)}, u32[]{:S(2)}) collective-permute-start(f32[136,384]{1,0:T(8,128)S(1)} %fusion.1), channel_id=1, source_target_pairs={{0,8},{4,12},{8,0},{12,4},{16,24},{20,28},{24,16},{28,20},{1,9},{5... | collective-permute-start | bytes 626696 | tf_op jit(solution)/shard_map/ppermute | solution.py:1016
  166.3 11.5 %collective-permute-start.6 = (f32[136,384]{1,0:T(8,128)S(1)}, f32[136,384]{1,0:T(8,128)S(1)}, u32[]{:S(2)}, u32[]{:S(2)}) collective-permute-start(f32[136,384]{1,0:T(8,128)S(1)} %fusion), channel_id=1, source_target_pairs={{0,16},{4,20},{8,24},{12,28},{16,0},{20,4},{24,8},{28,12},{1,17},{... | collective-permute-start | bytes 626696 | tf_op jit(solution)/shard_map/ppermute | solution.py:1016
  178.5 105.7 %copy-start.35 = (bf16[2048,768]{1,0:T(8,128)(2,1)S(1)}, bf16[2048,768]{1,0:T(8,128)(2,1)}, u32[]{:S(2)}) copy-start(bf16[2048,768]{1,0:T(8,128)(2,1)} %get-tuple-element.184) | copy-start | bytes 9437188
  (30 other events, 141.9 us)
